TPU v7x, 256 devices: a whole 4x4x8 slice. The times are simulated.
256 devices in a mesh: dp: 32 (over y, x, core), tensor: 8 (over z).
Axes of the slice: x: 4, y: 4, z: 8, core: 2. Of those that a mesh axis runs over, the one named last changes fastest.
Arguments:
- rank_query: bfloat16 [256, 32, 5120], P('dp', None, 'tensor'), may hold values from -4.5 to 4.5
- rank_key: bfloat16 [256, 32, 5120], P('dp', None, 'tensor'), may hold values from -4.5 to 4.5
- rank_value: bfloat16 [256, 32, 5120], P('dp', None, 'tensor'), may hold values from -6 to 6
- rank_resid: bfloat16 [256, 32, 5120], P(('dp', 'tensor')), may hold values from -4 to 4
- out_weight: bfloat16 [5120, 5120], P('tensor', 'dp'), may hold values from -0.25 to 0.25
- rank_gain: bfloat16 [5120], replicated, may hold values from 0.099609375 to 1.8984375
- score_weight: bfloat16 [5120], replicated, may hold values from -0.078125 to 0.078125
- pair_index: int32 [256, 3], P(('dp', 'tensor')), may hold values from 0 to 31, as said below
- cand_rank: int32 [1024, 8], P('dp'), may hold values from 0 to 7, each once within a row
- cand_len: int32 [1024, 8], P('dp'), may hold values from 1 to 8, 39 in all within a row
- blend_owner: int32 [32, 32], P('dp'), may hold values from 0 to 31, each once within a row
- blend_rows: bfloat16 [1024, 8, 8, 4096], P('dp', None, None, 'tensor'), may hold values from -6 to 6
- blend_gain: bfloat16 [4096], replicated, may hold values from 0.099609375 to 1.8984375
- blend_weight: bfloat16 [4096, 3, 2048], P('dp', None, 'tensor'), may hold values from -0.09375 to 0.09375
Outputs:
- rank_hidden: bfloat16 [256, 32, 5120], P(('dp', 'tensor'))
- cand_score: float32 [1024, 8], P('dp')
- blended_qkv: bfloat16 [1024, 24, 3, 2048], P('dp', None, None, 'tensor')
Inputs may be any that keep to these rules, and one draw needn't show every extreme that they name: `pair_index`: column 0 is a prompt of the pair's own group of 32 prompts (pair p belongs to group p // 8); columns 1 and 2 are two different candidates of that prompt. `cand_rank`: each row gives every rank once. `blend_owner`: each row names every group once.
All inputs are finite; a program needn't handle non-finite values.
Results may differ from a plain program's by a relative error of at most 0.024.
Values may be sent and summed in bfloat16 or wider, within the bound.
No kernel may reach another device: no remote copies, remote signals or barrier semaphores. Data moves between devices by JAX's collectives and lax.ppermute only.
A program may use at most 128 MiB of HBM per device.

v0:
```python
import math

import jax
import jax.numpy as jnp
from jax import lax
from jax.sharding import PartitionSpec as P

HR = 40
HDR = 128


def pair_attention(queries, keys_in, values_in, head_count):
    pair_count, length, row_width = queries.shape
    head_size = row_width // head_count
    query_heads = queries.reshape(pair_count, length, head_count, head_size)
    key_heads = keys_in.reshape(pair_count, length, head_count, head_size)
    value_heads = values_in.reshape(pair_count, length, head_count, head_size)
    scores = jnp.einsum(
        "pihd,pjhd->phij", query_heads, key_heads, preferred_element_type=jnp.float32
    ) * (1.0 / math.sqrt(HDR))
    highest = jnp.max(scores, axis=-1, keepdims=True)
    weights = jnp.exp(scores - highest)
    soft_weights = (weights / jnp.sum(weights, axis=-1, keepdims=True)).astype(jnp.bfloat16)
    context = jnp.einsum(
        "phij,pjhd->pihd", soft_weights, value_heads, preferred_element_type=jnp.float32
    )
    return context.astype(jnp.bfloat16).reshape(pair_count * length, row_width)


def encode(rows_in, blend_gain, blend_weight):
    whole_rows = lax.all_gather(rows_in, "tensor", axis=3, tiled=True)
    prompts, pick_count, length, features = whole_rows.shape
    flat_rows = whole_rows.reshape(prompts * pick_count * length, features)
    as_float = flat_rows.astype(jnp.float32)
    scale_rows = lax.rsqrt(jnp.mean(as_float * as_float, axis=-1, keepdims=True) + 1e-06)
    blend_normed = (as_float * scale_rows * blend_gain.astype(jnp.float32)).astype(jnp.bfloat16)
    columns = blend_weight.shape[1] * blend_weight.shape[2]
    portion = lax.all_gather(blend_weight, "dp", axis=0, tiled=True)
    projected = jnp.dot(
        blend_normed, portion.reshape(portion.shape[0], columns), preferred_element_type=jnp.float32
    )
    return projected.astype(jnp.bfloat16).reshape(
        prompts, pick_count * length, blend_weight.shape[1], blend_weight.shape[2]
    )


def body(
    rank_query,
    rank_key,
    rank_value,
    rank_resid,
    out_weight,
    rank_gain,
    score_weight,
    pair_index,
    cand_rank,
    cand_len,
    blend_owner,
    blend_rows,
    blend_gain,
    blend_weight,
):
    tensor_count = lax.axis_size("tensor")
    local_heads = HR // tensor_count
    length = rank_query.shape[1]
    context = pair_attention(rank_query, rank_key, rank_value, local_heads)
    own_pairs = rank_resid.shape[0]
    own_rows = own_pairs * length
    term_rows = jnp.dot(
        context,
        lax.all_gather(out_weight, "dp", axis=1, tiled=True),
        preferred_element_type=jnp.float32,
    )
    summed = lax.psum(term_rows.astype(jnp.bfloat16), "tensor").astype(jnp.float32)
    part_sum = lax.dynamic_slice_in_dim(summed, lax.axis_index("tensor") * own_rows, own_rows, 0)
    mixed_rows = rank_resid.reshape(own_rows, -1).astype(jnp.float32) + part_sum
    mean_square = jnp.mean(mixed_rows * mixed_rows, axis=-1, keepdims=True)
    normed = mixed_rows * lax.rsqrt(mean_square + 1e-05) * rank_gain.astype(jnp.float32)
    rank_hidden = normed.astype(jnp.bfloat16).reshape(rank_resid.shape)
    leading = normed.reshape(own_pairs, length, -1)[:, 0, :]
    pair_logit = jnp.sum(leading * score_weight.astype(jnp.float32), axis=-1)
    prompt_count = cand_rank.shape[0]
    cand_count = cand_rank.shape[1]
    slot_ids = jnp.arange(prompt_count * cand_count, dtype=jnp.int32)
    base_slot = pair_index[:, 0] * cand_count
    upward = jnp.where(
        (base_slot + pair_index[:, 1])[:, None] == slot_ids[None, :], pair_logit[:, None], 0.0
    )
    downward = jnp.where(
        (base_slot + pair_index[:, 2])[:, None] == slot_ids[None, :], pair_logit[:, None], 0.0
    )
    vote_sums = jnp.sum(upward - downward, axis=0).reshape(prompt_count, cand_count)
    cand_score = lax.psum(vote_sums, "tensor")
    places = jnp.arange(3, dtype=jnp.int32)
    matched = cand_rank[:, None, :] == places[None, :, None]
    labels = jnp.arange(cand_count, dtype=jnp.int32)
    chosen = jnp.sum(jnp.where(matched, labels[None, None, :], 0), axis=-1)
    chosen_len = jnp.sum(jnp.where(matched, cand_len[:, None, :], 0), axis=-1)
    prompt_ids = jnp.arange(prompt_count, dtype=jnp.int32)
    picked = blend_rows[prompt_ids[:, None], chosen]
    positions = jnp.arange(blend_rows.shape[2], dtype=jnp.int32)
    live_rows = positions[None, None, :] < chosen_len[:, :, None]
    picked = jnp.where(live_rows[..., None], picked, jnp.zeros((), jnp.bfloat16))
    owners = blend_owner[0]
    sender = jnp.sum(
        jnp.where(owners[None, :] == prompt_ids[:, None], prompt_ids[None, :], 0), axis=1
    )
    outgoing = picked[sender]
    arrived = lax.all_to_all(outgoing, "dp", split_axis=0, concat_axis=0, tiled=True)
    blended_qkv = encode(arrived, blend_gain, blend_weight)
    return (rank_hidden, cand_score, blended_qkv)


def solution(mesh):
    placed = (
        P("dp", None, "tensor"),
        P("dp", None, "tensor"),
        P("dp", None, "tensor"),
        P(("dp", "tensor"), None, None),
        P("tensor", "dp"),
        P(),
        P(),
        P(("dp", "tensor"), None),
        P("dp", None),
        P("dp", None),
        P("dp", None),
        P("dp", None, None, "tensor"),
        P(),
        P("dp", None, "tensor"),
    )
    return jax.shard_map(
        body,
        mesh=mesh,
        in_specs=placed,
        out_specs=(P(("dp", "tensor"), None, None), P("dp", None), P("dp", None, None, "tensor")),
        check_vma=False,
    )
```

profile of v0, /device:TPU:2, one launch (start us, length us, event | category | flops | bytes accessed | tf_op | source)
XLA Modules:
  0.0 343.9 jit_solution(1360914309973684097)
XLA Ops:
  7.2 0.9 select_reduce_fusion.2
  8.2 0.1 reshape.142
  8.4 0.1 iota_compare_fusion
  8.5 0.8 select_reduce_fusion
  9.3 0.6 pad_clamp_fusion
  9.9 2.0 gather_fusion
  11.9 1.3 broadcast_select_fusion
  13.3 1.7 gather_fusion.1
  15.0 21.0 %all_to_all.5 = bf16[32,3,8,512]{3,2,1,0:T(8,128)(2,1)} all-to-all(bf16[32,3,8,512]{3,2,1,0:T(8,128)(2,1)} %gather_fusion.1), channel_id=1, replica_groups=mesh['dp'=32,'tensor'=8] {'dp'}, dimensions={0} | all-to-all | bytes 1572864 | tf_op jit(solution)/shard_map/all_to_all | solution.py:109
  36.1 0.7 all-gather.4.cloned.1.call-update
  36.9 1.7 copy.63
  38.7 1.0 fusion.32
  39.7 0.3 convolution_multiply_fusion
  40.0 1.3 fusion.6
  41.3 0.2 copy.58
  41.5 0.6 fusion.31
  44.0 0.7 convert_element_type.58
  44.7 66.2 %all-gather.6.cloned.1.call-done = bf16[32,3,8,4096]{3,2,1,0:T(8,128)(2,1)} async-done(((bf16[32,3,8,512]{3,2,1,0:T(8,128)(2,1)}), bf16[32,3,8,4096]{3,2,1,0:T(8,128)(2,1)}) %all-gather.6.cloned.1.call-update) | async-done | bytes 6291472 | tf_op jit(solution)/shard_map/all_gather | solution.py:31
  110.9 4.1 %fusion.1 = f32[32,3,8]{2,1,0:T(4,128)S(1)} fusion(bf16[32,3,8,4096]{3,2,1,0:T(8,128)(2,1)} %all-gather.6.cloned.1.call-done), kind=kLoop, calls=%fused_computation.5 | loop fusion | flops 9436416 | bytes 6294528 | tf_op jit(solution)/shard_map/reduce_sum | solution.py:35
  115.2 50.6 %all-gather.4.cloned.1.call-done = bf16[640,5120]{0,1:T(8,128)(2,1)} async-done(((bf16[640,160]{0,1:T(8,128)(2,1)}), bf16[640,5120]{0,1:T(8,128)(2,1)}) %all-gather.4.cloned.1.call-update) | async-done | bytes 6553616 | tf_op jit(solution)/shard_map/all_gather | solution.py:71
  165.7 6.6 %convolution_convert_fusion = bf16[256,5120]{1,0:T(8,128)(2,1)} fusion(bf16[640,5120]{0,1:T(8,128)(2,1)} %all-gather.4.cloned.1.call-done, bf16[32,8,5,128]{3,2,1,0:T(8,128)(2,1)S(1)} %bitcast.74), kind=kOutput, calls=%fused_computation.8 | convolution fusion | flops 1679032320 | bytes 9502720 | tf_op jit(solution)/shard_map/dot_general | solution.py:69
  172.4 8.2 %fusion.3 = bf16[32,3,8,4096]{3,2,1,0:T(8,128)(2,1)} fusion(bf16[32,3,8,4096]{3,2,1,0:T(8,128)(2,1)} %all-gather.6.cloned.1.call-done, f32[4096]{0:T(1024)S(1)} %convert_element_type.58, f32[32,3,8]{2,1,0:T(4,128)S(1)} %copy.62), kind=kLoop, calls=%fused_computation.7 | loop fusion | flops 12582912 | bytes 12602368 | tf_op jit(solution)/shard_map/convert_element_type | solution.py:36
  180.5 47.1 %all-gather.8.cloned.1.call-done = bf16[4096,3,256]{0,2,1:T(8,128)(2,1)} async-done(((bf16[128,3,256]{0,2,1:T(8,128)(2,1)}), bf16[4096,3,256]{0,2,1:T(8,128)(2,1)}) %all-gather.8.cloned.1.call-update) | async-done | bytes 6291472 | tf_op jit(solution)/shard_map/all_gather | solution.py:38
  227.7 9.9 %convolution_convert_fusion.1 = bf16[768,768]{1,0:T(8,128)(2,1)} fusion(bf16[768,4096]{1,0:T(8,128)(2,1)} %bitcast.72, bf16[4096,768]{0,1:T(8,128)(2,1)} %bitcast.76), kind=kOutput, calls=%fused_computation.9 | convolution fusion | flops 4832428032 | bytes 13762560 | tf_op jit(solution)/shard_map/dot_general | solution.py:39
  237.6 3.7 %reshape.140 = bf16[32,24,3,256]{3,2,1,0:T(4,128)(2,1)} reshape(bf16[768,768]{1,0:T(8,128)(2,1)} %convolution_convert_fusion.1) | data formatting | bytes 2359296 | tf_op jit(solution)/shard_map/reshape | solution.py:42
  241.3 2.6 copy.64
  243.9 72.1 %all-reduce.2.cloned.1.call-done = bf16[256,5120]{1,0:T(8,128)(2,1)} async-done(((bf16[256,5120]{1,0:T(8,128)(2,1)}), bf16[256,5120]{1,0:T(8,128)(2,1)}) %all-reduce.2.cloned.1.call-update) | async-done | bytes 2621456 | tf_op jit(solution)/shard_map/psum | solution.py:74
  316.0 1.2 multiply_reduce_fusion
  317.2 1.8 fusion.7
  319.1 0.6 multiply_reduce_fusion.1
  319.7 0.6 select_subtract_fusion
  320.2 17.1 %psum.15 = f32[32,8]{0,1:T(8,128)} all-reduce(f32[32,8]{0,1:T(8,128)S(1)} %select_subtract_fusion), channel_id=1, replica_groups=mesh['dp'=32,'tensor'=8] {'tensor'}, use_global_device_ids=true, to_apply=%region_5.6 | all-reduce | flops 256 | bytes 2048 | tf_op jit(solution)/shard_map/psum | solution.py:93
  (31 shorter events, 0.6 us)
Async XLA Ops:
  7.2 2.7 copy-start
  7.2 31.5 %copy-start.3 = (bf16[8,32,640]{2,1,0:T(8,128)(2,1)S(1)}, bf16[8,32,640]{2,1,0:T(8,128)(2,1)}, u32[]{:S(2)}) copy-start(bf16[8,32,640]{2,1,0:T(8,128)(2,1)} %param.14) | copy-start | bytes 983044
  7.2 31.5 %copy-start.2 = (bf16[8,32,640]{2,1,0:T(8,128)(2,1)S(1)}, bf16[8,32,640]{2,1,0:T(8,128)(2,1)}, u32[]{:S(2)}) copy-start(bf16[8,32,640]{2,1,0:T(8,128)(2,1)} %param.15) | copy-start | bytes 983044
  7.2 103.7 %all-gather.6.cloned.1.call-start = ((), (), s32[]{:S(2)}) async-start(), calls=%async_computation.3 | async-start | bytes 7077888 | tf_op jit(solution)/shard_map/all_gather | solution.py:31
  13.3 28.3 %copy-start.5 = (bf16[5120]{0:T(1024)(128)(2,1)S(1)}, bf16[5120]{0:T(1024)(128)(2,1)}, u32[]{:S(2)}) copy-start(bf16[5120]{0:T(1024)(128)(2,1)} %param.19) | copy-start | bytes 30724
  13.3 28.3 %copy-start.6 = (s32[1,3]{1,0:T(1,128)S(1)}, s32[1,3]{1,0:T(1,128)}, u32[]{:S(2)}) copy-start(s32[1,3]{1,0:T(1,128)} %param.21) | copy-start | bytes 40
  36.1 129.7 %all-gather.4.cloned.1.call-start = ((), (), s32[]{:S(2)}) async-start(), calls=%async_computation.1 | async-start | bytes 6758400 | tf_op jit(solution)/shard_map/all_gather | solution.py:71
  36.8 190.9 %all-gather.8.cloned.1.call-start = ((), (), s32[]{:S(2)}) async-start(), calls=%async_computation.4 | async-start | bytes 6488064 | tf_op jit(solution)/shard_map/all_gather | solution.py:38
  38.6 277.4 %all-reduce.2.cloned.1.call-start = ((), (), s32[]{:S(2)}) async-start(), calls=%async_computation.2 | async-start | bytes 5242880 | tf_op jit(solution)/shard_map/psum | solution.py:74
  227.7 88.3 %copy-start.1 = (bf16[1,32,5120]{2,1,0:T(8,128)(2,1)S(1)}, bf16[1,32,5120]{2,1,0:T(8,128)(2,1)}, u32[]{:S(2)}) copy-start(bf16[1,32,5120]{2,1,0:T(8,128)(2,1)} %param.17) | copy-start | bytes 983044
  237.6 81.5 %copy-start.4 = (bf16[5120]{0:T(1024)(128)(2,1)S(1)}, bf16[5120]{0:T(1024)(128)(2,1)}, u32[]{:S(2)}) copy-start(bf16[5120]{0:T(1024)(128)(2,1)} %param.20) | copy-start | bytes 30724
Sparse Core Ops, SparseCore 0:
  36.2 74.6 all-gather.5
  113.4 52.2 all-gather.3
  168.8 58.8 all-gather.7
  229.9 86.0 all-reduce.1
where the time goes:
time: 345 us; the launch traced here: 344 us
  waiting for transfers between devices  237 us (69%)
  blocking collectives  38.1 us (11%)
  other arithmetic  20.9 us (6%)
  matrix products  19.1 us (6%)
  between operations  15.8 us (5%)
  local copies, waits for them, and re-layouts  13.1 us (4%)
    psum x1, waiting for transfers between devices, body(): lax.psum(term_rows.astype(jnp.bfloat16), 'tensor').astype(jnp.float32)  72.1 us
    all_gather x1, waiting for transfers between devices, encode(): whole_rows = lax.all_gather(rows_in, 'tensor', axis=3, tiled=True)  66.2 us
    all_gather x1, waiting for transfers between devices, body(): lax.all_gather(out_weight, 'dp', axis=1, tiled=True)  50.6 us
    all_gather x1, waiting for transfers between devices, encode(): portion = lax.all_gather(blend_weight, 'dp', axis=0, tiled=True)  47.1 us
    all_to_all x1, blocking collectives, body(): lax.all_to_all(outgoing, 'dp', split_axis=0, concat_axis=0, tiled=True)  21 us
    psum x1, blocking collectives, body(): cand_score = lax.psum(vote_sums, 'tensor')  17.1 us
    dot_general x1, matrix products, encode(): jnp.dot(blend_normed, portion.reshape(portion.shape[0], columns), preferr...  9.89 us
    convert_element_type x1, other arithmetic, encode(): (as_float * scale_rows * blend_gain.astype(jnp.float32)).astype(jnp.bfloa...  8.16 us
  transfers between devices with their start and end apart: 4, of which 4 were waited for; matrix products, arithmetic and copies ran while one was open for 12% of the time, Pallas kernels for 0%

commit v1 on v0

v1 whole, which is shorter than its diff:
```python
import math

import jax
import jax.numpy as jnp
from jax import lax
from jax.experimental import pallas as pl
from jax.experimental.pallas import tpu as pltpu
from jax.sharding import Mesh, PartitionSpec as P

HR = 40
HDR = 128
NY, NX, NC, NZ = 4, 4, 2, 8
PLANE = ("y", "x", "core")


def ring(count, step):
    return [(i, (i + step) % count) for i in range(count)]


def pair_attention(queries, keys_in, values_in, head_count):
    pair_count, length, row_width = queries.shape
    head_size = row_width // head_count
    query_heads = queries.reshape(pair_count, length, head_count, head_size)
    key_heads = keys_in.reshape(pair_count, length, head_count, head_size)
    value_heads = values_in.reshape(pair_count, length, head_count, head_size)
    scores = jnp.einsum(
        "pihd,pjhd->phij", query_heads, key_heads, preferred_element_type=jnp.float32
    ) * (1.0 / math.sqrt(HDR))
    highest = jnp.max(scores, axis=-1, keepdims=True)
    weights = jnp.exp(scores - highest)
    soft_weights = (weights / jnp.sum(weights, axis=-1, keepdims=True)).astype(jnp.bfloat16)
    context = jnp.einsum(
        "phij,pjhd->pihd", soft_weights, value_heads, preferred_element_type=jnp.float32
    )
    return context.astype(jnp.bfloat16).reshape(pair_count * length, row_width)


def select_kernel(owner_ref, rank_ref, len_ref, rows_ref, out_ref):
    places = rank_ref.shape[0]
    position = lax.broadcasted_iota(jnp.int32, rows_ref.shape[1:], 0)

    def one_prompt(prompt, carry):
        owner = owner_ref[0, prompt]
        for rank in range(3):
            cand = jnp.int32(0)
            live = jnp.int32(0)
            for place in range(places):
                hit = rank_ref[place, prompt] == rank
                cand = jnp.where(hit, place, cand)
                live = jnp.where(hit, len_ref[place, prompt], live)
            picked = rows_ref[prompt * places + cand].astype(jnp.float32)
            out_ref[owner * 3 + rank] = jnp.where(position < live, picked, 0.0).astype(out_ref.dtype)
        return carry

    lax.fori_loop(0, owner_ref.shape[1], one_prompt, 0)


def select_rows(blend_owner, cand_rank, cand_len, blend_rows):
    prompts, cands, length, features = blend_rows.shape
    smem = pl.BlockSpec(memory_space=pltpu.SMEM)
    vmem = pl.BlockSpec(memory_space=pltpu.VMEM)
    return pl.pallas_call(
        select_kernel,
        out_shape=jax.ShapeDtypeStruct((prompts * 3, length, features), blend_rows.dtype),
        in_specs=[smem, smem, smem, vmem],
        out_specs=vmem,
        cost_estimate=pl.CostEstimate(flops=0, bytes_accessed=3 << 20, transcendentals=0),
    )(blend_owner, cand_rank.T, cand_len.T, blend_rows.reshape(prompts * cands, length, features))


def encode_kernel(where_ref, *refs):
    row_refs = refs[:NZ]
    mine_ref, other_ref, out_ref, weight_ref = refs[NZ:]
    third, depth, width = mine_ref.shape[1:]
    my_y, my_x, my_core, my_z = where_ref[0], where_ref[1], where_ref[2], where_ref[3]
    features = row_refs[0].shape[1]

    @pl.when(pl.program_id(0) == 0)
    def _():
        def one_source(order, carry):
            source = lax.rem(my_z + order, NZ)
            for piece in range(4):
                slab_y = source // 2
                slab_x = lax.rem(source, 2) * 2 + piece // 2
                slot = lax.rem(my_y - slab_y + NY, NY) * NX + lax.rem(my_x - slab_x + NX, NX)
                place = pl.ds(pl.multiple_of(order * features + piece * depth, depth), depth)

                @pl.when(my_core == piece % 2)
                def _():
                    for part in range(third):
                        weight_ref[part, place, :] = mine_ref[slot, part]

                @pl.when(my_core != piece % 2)
                def _():
                    for part in range(third):
                        weight_ref[part, place, :] = other_ref[slot, part]

            return carry

        lax.fori_loop(0, NZ, one_source, 0)

    squares = None
    for rows in row_refs:
        value = rows[...].astype(jnp.float32)
        term = jnp.sum(value * value, axis=-1, keepdims=True)
        squares = term if squares is None else squares + term
    scale = lax.rsqrt(squares * (1.0 / (NZ * features)) + 1e-06)
    prompts, length = out_ref.shape[0], out_ref.shape[2]
    for part in range(third):
        total = None
        for order, rows in enumerate(row_refs):
            term = jnp.dot(
                rows[...],
                weight_ref[part, order * features : (order + 1) * features, :],
                preferred_element_type=jnp.float32,
            )
            total = term if total is None else total + term
        total = (total * scale).astype(out_ref.dtype)
        out_ref[:, part] = total.reshape(prompts, length, width)


def encode(where, blocks, mine, other, prompts, length):
    rows, features = blocks[0].shape
    third, depth, width = mine.shape[1:]
    steps = 4
    step_rows = rows // steps
    step_prompts = prompts // steps
    row_spec = pl.BlockSpec((step_rows, features), lambda i, w: (i, 0))
    slab_spec = pl.BlockSpec(
        mine.shape, lambda i, w: (0, 0, 0, 0), pipeline_mode=pl.Buffered(1)
    )
    out = pl.pallas_call(
        encode_kernel,
        out_shape=jax.ShapeDtypeStruct((prompts, third, length, width), jnp.bfloat16),
        grid_spec=pltpu.PrefetchScalarGridSpec(
            num_scalar_prefetch=1,
            grid=(steps,),
            in_specs=[row_spec] * NZ + [slab_spec] * 2,
            out_specs=pl.BlockSpec(
                (step_prompts, third, length, width), lambda i, w: (i, 0, 0, 0)
            ),
            scratch_shapes=[pltpu.VMEM((third, NZ * features, width), jnp.bfloat16)],
        ),
        compiler_params=pltpu.CompilerParams(vmem_limit_bytes=40 << 20),
        cost_estimate=pl.CostEstimate(
            flops=2 * rows * NZ * features * third * width,
            bytes_accessed=16 << 20,
            transcendentals=rows,
        ),
    )(where, *blocks, mine, other)
    return out.transpose(0, 2, 1, 3)


def gather_axis(block, axis, count):
    before = lax.ppermute(block, axis, ring(count, 1))
    after = lax.ppermute(block, axis, ring(count, -1))
    across = lax.ppermute(before, axis, ring(count, 1))
    return jnp.concatenate([block, before, across, after], axis=0)


def body(
    rank_query,
    rank_key,
    rank_value,
    rank_resid,
    out_weight,
    rank_gain,
    score_weight,
    pair_index,
    cand_rank,
    cand_len,
    blend_owner,
    blend_rows,
    blend_gain,
    blend_weight,
):
    local_heads = HR // NZ
    length = rank_query.shape[1]
    my_y, my_x, my_core, my_z = (lax.axis_index(a) for a in ("y", "x", "core", "z"))

    outgoing = select_rows(blend_owner, cand_rank, cand_len, blend_rows)
    prompts = blend_rows.shape[0]
    features = blend_rows.shape[3]
    arrived = lax.all_to_all(
        outgoing.reshape(prompts, -1, features), PLANE, split_axis=0, concat_axis=0, tiled=True
    )
    picked_rows = arrived.shape[1]
    own = arrived.reshape(prompts * picked_rows, features)

    depth = blend_weight.shape[0]
    slab = (my_y * NX + my_x) * NC + my_core
    gain = lax.dynamic_slice_in_dim(blend_gain, slab * depth, depth, 0).astype(jnp.float32)
    own_slab = (blend_weight.transpose(1, 0, 2).astype(jnp.float32) * gain[None, :, None]).astype(
        jnp.bfloat16
    )
    mine = gather_axis(own_slab[None], "x", NX)
    mine = gather_axis(mine, "y", NY)
    other = lax.ppermute(mine, "core", ring(NC, 1))

    lower, upper = [own], [own]
    for step in range(3):
        lower.append(lax.ppermute(lower[-1], "z", ring(NZ, 1)))
        upper.append(lax.ppermute(upper[-1], "z", ring(NZ, -1)))
    half = own.shape[0] // 2
    across = jnp.concatenate(
        [
            lax.ppermute(lower[3][:half], "z", ring(NZ, 1)),
            lax.ppermute(upper[3][half:], "z", ring(NZ, -1)),
        ],
        axis=0,
    )
    blocks = [own, upper[1], upper[2], upper[3], across, lower[3], lower[2], lower[1]]
    where = jnp.stack([my_y, my_x, my_core, my_z]).astype(jnp.int32)
    blended_qkv = encode(where, blocks, mine, other, prompts, picked_rows)

    context = pair_attention(rank_query, rank_key, rank_value, local_heads)
    own_pairs = rank_resid.shape[0]
    own_rows = own_pairs * length
    term_rows = jnp.dot(
        context,
        lax.all_gather(out_weight, PLANE, axis=1, tiled=True),
        preferred_element_type=jnp.float32,
    )
    part_sum = lax.psum_scatter(
        term_rows.astype(jnp.bfloat16), "z", scatter_dimension=0, tiled=True
    ).astype(jnp.float32)
    mixed_rows = rank_resid.reshape(own_rows, -1).astype(jnp.float32) + part_sum
    mean_square = jnp.mean(mixed_rows * mixed_rows, axis=-1, keepdims=True)
    normed = mixed_rows * lax.rsqrt(mean_square + 1e-05) * rank_gain.astype(jnp.float32)
    rank_hidden = normed.astype(jnp.bfloat16).reshape(rank_resid.shape)
    leading = normed.reshape(own_pairs, length, -1)[:, 0, :]
    pair_logit = jnp.sum(leading * score_weight.astype(jnp.float32), axis=-1)
    prompt_count = cand_rank.shape[0]
    cand_count = cand_rank.shape[1]
    slot_ids = jnp.arange(prompt_count * cand_count, dtype=jnp.int32)
    base_slot = pair_index[:, 0] * cand_count
    upward = jnp.where(
        (base_slot + pair_index[:, 1])[:, None] == slot_ids[None, :], pair_logit[:, None], 0.0
    )
    downward = jnp.where(
        (base_slot + pair_index[:, 2])[:, None] == slot_ids[None, :], pair_logit[:, None], 0.0
    )
    cand_score = jnp.sum(upward - downward, axis=0).reshape(prompt_count, cand_count)
    for bit in (1, 2, 4):
        cand_score = cand_score + lax.ppermute(cand_score, "z", [(i, i ^ bit) for i in range(NZ)])
    return (rank_hidden, cand_score, blended_qkv)


def solution(mesh):
    grid = Mesh(mesh.devices.reshape(NY, NX, NC, NZ), ("y", "x", "core", "z"))
    whole = ("y", "x", "core", "z")
    placed = (
        P(PLANE, None, "z"),
        P(PLANE, None, "z"),
        P(PLANE, None, "z"),
        P(whole, None, None),
        P("z", PLANE),
        P(),
        P(),
        P(whole, None),
        P(PLANE, None),
        P(PLANE, None),
        P(PLANE, None),
        P(PLANE, None, None, "z"),
        P(),
        P(PLANE, None, "z"),
    )
    return jax.shard_map(
        body,
        mesh=grid,
        in_specs=placed,
        out_specs=(P(whole, None, None), P(PLANE, None), P(PLANE, None, None, "z")),
        check_vma=False,
    )
```

time: 345 us -> 211 us (0.61)
  waiting for transfers between devices: 237 us -> 118 us
  blocking collectives: 38.1 us -> 0 us
  starting transfers between devices: 0.16 us -> 34.8 us
  Pallas kernels: 0 us -> 14.3 us
  other arithmetic: 20.9 us -> 10.3 us
  matrix products: 19.1 us -> 9.79 us
  local copies, waits for them, and re-layouts: 13.1 us -> 7.28 us
    all_gather x3 -> x1, waiting for transfers between devices: 164 us -> 55.9 us  [body(): lax.all_gather(out_weight, PLANE, axis=1, tiled=True)]
    psum x1 -> x0, waiting for transfers between devices: 72.1 us -> none  [body(): lax.psum(term_rows.astype(jnp.bfloat16), 'tensor').astype(jnp.float32)]
    ppermute x0 -> x18, waiting for transfers between devices: none -> 61.2 us  [the longest x2 26 us: gather_axis(): before = lax.ppermute(block, axis, ring(count, 1))]
    ppermute x0 -> x18, starting transfers between devices: none -> 28.8 us  [the longest x3 9.63 us: body(): upper.append(lax.ppermute(upper[-1], 'z', ring(NZ, -1)))]
    all_to_all x1 -> x0, blocking collectives: 21 us -> none  [body(): lax.all_to_all(outgoing, 'dp', split_axis=0, concat_axis=0, tiled=True)]
    psum x1 -> x0, blocking collectives: 17.1 us -> none  [body(): cand_score = lax.psum(vote_sums, 'tensor')]
    pallas_call x0 -> x2, Pallas kernels: none -> 14.3 us  [the longest x1 10.2 us: encode(): pl.pallas_call(encode_kernel, out_shape=jax.ShapeDtypeStruct((prompts, th...]
    dot_general x2 -> x1, matrix products: 16.5 us -> 6.64 us  [body(): jnp.dot(context, lax.all_gather(out_weight, PLANE, axis=1, tiled=True), p...]
  transfers between devices with their start and end apart: 4 -> 21, of which waited for: 4 -> 10; matrix products, arithmetic and copies ran while one was open for 12% -> 10% of each run, Pallas kernels for 0% -> 7%
where the time goes in v1:
time: 211 us; the launch traced here: 210 us
  waiting for transfers between devices  118 us (56%)
  starting transfers between devices  34.8 us (16%)
  between operations  16.1 us (8%)
  Pallas kernels  14.3 us (7%)
  other arithmetic  10.3 us (5%)
  matrix products  9.79 us (5%)
  local copies, waits for them, and re-layouts  7.28 us (3%)
    all_gather x1, waiting for transfers between devices, body(): lax.all_gather(out_weight, PLANE, axis=1, tiled=True)  55.9 us
    ppermute x2, waiting for transfers between devices, gather_axis(): before = lax.ppermute(block, axis, ring(count, 1))  26 us
    ppermute x3, waiting for transfers between devices, body(): upper.append(lax.ppermute(upper[-1], 'z', ring(NZ, -1)))  17.6 us
    ppermute x2, waiting for transfers between devices, gather_axis(): across = lax.ppermute(before, axis, ring(count, 1))  13.7 us
    pallas_call x1, Pallas kernels, encode(): pl.pallas_call(encode_kernel, out_shape=jax.ShapeDtypeStruct((prompts, th...  10.2 us
    ppermute x3, starting transfers between devices, body(): upper.append(lax.ppermute(upper[-1], 'z', ring(NZ, -1)))  9.63 us
    ppermute x3, starting transfers between devices, body(): lax.ppermute(cand_score, 'z', [(i, i ^ bit) for i in range(NZ)])  7.98 us
    dot_general x1, matrix products, body(): jnp.dot(context, lax.all_gather(out_weight, PLANE, axis=1, tiled=True), p...  6.64 us
  transfers between devices with their start and end apart: 21, of which 10 were waited for; matrix products, arithmetic and copies ran while one was open for 10% of the time, Pallas kernels for 7%

profile of v1, /device:TPU:2, one launch (start us, length us, event | category | flops | bytes accessed | tf_op | source)
XLA Modules:
  0.0 210.5 jit_solution(16420410880875387235)
XLA Ops:
  8.0 1.4 fusion.28
  9.4 1.4 convolution_multiply_fusion
  11.3 55.9 %all-gather.2.cloned.1.call-done = bf16[640,5120]{0,1:T(8,128)(2,1)} async-done(((bf16[640,160]{0,1:T(8,128)(2,1)}), bf16[640,5120]{0,1:T(8,128)(2,1)}) %all-gather.2.cloned.1.call-update) | async-done | bytes 6553616 | tf_op jit(solution)/shard_map/all_gather | solution.py:221
  67.3 6.6 %convolution_convert_fusion = bf16[256,5120]{1,0:T(8,128)(2,1)} fusion(bf16[640,5120]{0,1:T(8,128)(2,1)} %all-gather.2.cloned.1.call-done, bf16[32,8,5,128]{3,2,1,0:T(8,128)(2,1)S(1)} %bitcast.78), kind=kOutput, calls=%fused_computation.1 | convolution fusion | flops 1679032320 | bytes 9502720 | tf_op jit(solution)/shard_map/dot_general | solution.py:219
  73.9 4.1 %shard_map.157 = bf16[96,8,512]{2,1,0:T(8,128)(2,1)} custom-call(s32[1,32]{1,0:T(1,128)} %owner_ref.1, s32[8,32]{1,0:T(8,128)} %bitcast.80, s32[8,32]{1,0:T(8,128)} %bitcast.81, bf16[256,8,512]{2,1,0:T(8,128)(2,1)} %bitcast.77), custom_call_target="tpu_custom_call" | custom-call | bytes 3145728 | tf_op jit(solution)/shard_map/pallas_call | solution.py:62
  78.0 5.9 %all-to-all-start = ((bf16[32,24,512]{2,1,0:T(8,128)(2,1)}), bf16[32,24,512]{2,1,0:T(8,128)(2,1)S(1)}, u32[]{:S(2)}, u32[]{:S(2)}) async-start(bf16[32,24,512]{2,1,0:T(8,128)(2,1)} %bitcast.76), calls=%async_computation.1 | async-start | bytes 1572864 | tf_op jit(solution)/shard_map/all_to_all | solution.py:184
  85.5 1.5 collective-permute-start.11
  87.5 10.5 %collective-permute-done.11 = bf16[1,3,128,256]{3,2,1,0:T(8,128)(2,1)S(1)} collective-permute-done((bf16[1,3,128,256]{3,2,1,0:T(8,128)(2,1)S(1)}, bf16[1,3,128,256]{3,2,1,0:T(8,128)(2,1)S(1)}, u32[]{:S(2)}, u32[]{:S(2)}) %collective-permute-start.11) | collective-permute-done | bytes 196640 | tf_op jit(solution)/shard_map/ppermute | solution.py:155
  98.0 1.5 collective-permute-start.12
  99.5 6.4 %collective-permute-done.12 = bf16[1,3,128,256]{3,2,1,0:T(8,128)(2,1)S(1)} collective-permute-done((bf16[1,3,128,256]{3,2,1,0:T(8,128)(2,1)S(1)}, bf16[1,3,128,256]{3,2,1,0:T(8,128)(2,1)S(1)}, u32[]{:S(2)}, u32[]{:S(2)}) %collective-permute-start.12) | collective-permute-done | bytes 196640 | tf_op jit(solution)/shard_map/ppermute | solution.py:157
  105.9 1.0 pad_maximum_fusion.1
  106.9 1.5 collective-permute-start.14
  108.3 3.3 %collective-permute-start.3 = (bf16[768,512]{1,0:T(8,128)(2,1)S(1)}, bf16[768,512]{1,0:T(8,128)(2,1)S(1)}, u32[]{:S(2)}, u32[]{:S(2)}) collective-permute-start(bf16[768,512]{1,0:T(8,128)(2,1)S(1)} %bitcast.73), channel_id=1, source_target_pairs={{0,7},{1,0},{2,1},{3,2},{4,3},{5,4},{6,5},{7,6},{8,15},{9,8},{10,9... | collective-permute-start | bytes 2359304 | tf_op jit(solution)/shard_map/ppermute | solution.py:203
  111.6 15.5 %collective-permute-done.14 = bf16[4,3,128,256]{3,2,1,0:T(8,128)(2,1)S(1)} collective-permute-done((bf16[4,3,128,256]{3,2,1,0:T(8,128)(2,1)}, bf16[4,3,128,256]{3,2,1,0:T(8,128)(2,1)S(1)}, u32[]{:S(2)}, u32[]{:S(2)}) %collective-permute-start.14) | collective-permute-done | bytes 786464 | tf_op jit(solution)/shard_map/ppermute | solution.py:155
  127.3 3.5 %collective-permute-done.3.refs_1_ = bf16[768,512]{1,0:T(8,128)(2,1)S(1)} collective-permute-done((bf16[768,512]{1,0:T(8,128)(2,1)S(1)}, bf16[768,512]{1,0:T(8,128)(2,1)S(1)}, u32[]{:S(2)}, u32[]{:S(2)}) %collective-permute-start.3) | collective-permute-done | bytes 786464 | tf_op jit(solution)/shard_map/ppermute | solution.py:203
  130.8 2.7 %collective-permute-start.4 = (bf16[768,512]{1,0:T(8,128)(2,1)S(1)}, bf16[768,512]{1,0:T(8,128)(2,1)}, u32[]{:S(2)}, u32[]{:S(2)}) collective-permute-start(bf16[768,512]{1,0:T(8,128)(2,1)S(1)} %collective-permute-done.3.refs_1_), channel_id=1, source_target_pairs={{0,7},{1,0},{2,1},{3,2},{4,3},{5,4},{6,5},{7,6},{8,15},{9,8},{10,9... | collective-permute-start | bytes 2359304 | tf_op jit(solution)/shard_map/ppermute | solution.py:203
  133.5 2.5 %collective-permute-start.16 = (bf16[4,3,128,256]{3,2,1,0:T(8,128)(2,1)}, bf16[4,3,128,256]{3,2,1,0:T(8,128)(2,1)S(1)}, u32[]{:S(2)}, u32[]{:S(2)}) collective-permute-start(bf16[4,3,128,256]{3,2,1,0:T(8,128)(2,1)} %pad_maximum_fusion.1), channel_id=1, source_target_pairs={{0,192},{64,0},{128,64},{192,128},{1,193},{65,1},{129,65},{193,129... | collective-permute-start | bytes 2359304 | tf_op jit(solution)/shard_map/ppermute | solution.py:156
  138.0 0.9 constant_dynamic-update-slice_fusion.2
  139.0 7.4 %collective-permute-done.15 = bf16[4,3,128,256]{3,2,1,0:T(8,128)(2,1)S(1)} collective-permute-done((bf16[4,3,128,256]{3,2,1,0:T(8,128)(2,1)S(1)}, bf16[4,3,128,256]{3,2,1,0:T(8,128)(2,1)S(1)}, u32[]{:S(2)}, u32[]{:S(2)}) %collective-permute-start.15) | collective-permute-done | bytes 786464 | tf_op jit(solution)/shard_map/ppermute | solution.py:157
  146.3 1.0 constant_dynamic-update-slice_fusion.1
  147.3 2.3 %collective-permute-done.4.refs_2_ = bf16[768,512]{1,0:T(8,128)(2,1)} collective-permute-done((bf16[768,512]{1,0:T(8,128)(2,1)S(1)}, bf16[768,512]{1,0:T(8,128)(2,1)}, u32[]{:S(2)}, u32[]{:S(2)}) %collective-permute-start.4) | collective-permute-done | bytes 786464 | tf_op jit(solution)/shard_map/ppermute | solution.py:203
  149.6 3.6 %collective-permute-start.5 = (bf16[768,512]{1,0:T(8,128)(2,1)}, bf16[768,512]{1,0:T(8,128)(2,1)S(1)}, u32[]{:S(2)}, u32[]{:S(2)}) collective-permute-start(bf16[768,512]{1,0:T(8,128)(2,1)} %collective-permute-done.4.refs_2_), channel_id=1, source_target_pairs={{0,7},{1,0},{2,1},{3,2},{4,3},{5,4},{6,5},{7,6},{8,15},{9,8},{10,9... | collective-permute-start | bytes 2359304 | tf_op jit(solution)/shard_map/ppermute | solution.py:203
  153.3 1.0 constant_dynamic-update-slice_fusion.refs_8_
  156.8 11.8 %collective-permute-done.5.refs_3_ = bf16[768,512]{1,0:T(8,128)(2,1)S(1)} collective-permute-done((bf16[768,512]{1,0:T(8,128)(2,1)}, bf16[768,512]{1,0:T(8,128)(2,1)S(1)}, u32[]{:S(2)}, u32[]{:S(2)}) %collective-permute-start.5) | collective-permute-done | bytes 786464 | tf_op jit(solution)/shard_map/ppermute | solution.py:203
  169.4 3.6 %collective-permute-start.10 = (bf16[384,512]{1,0:T(8,128)(2,1)}, bf16[384,512]{1,0:T(8,128)(2,1)}, u32[]{:S(2)}, u32[]{:S(2)}) collective-permute-start(bf16[384,512]{1,0:T(8,128)(2,1)} %slice.26), channel_id=1, source_target_pairs={{0,7},{1,0},{2,1},{3,2},{4,3},{5,4},{6,5},{7,6},{8,15},{9,8},{10,9... | collective-permute-start | bytes 1179656 | tf_op jit(solution)/shard_map/ppermute | solution.py:208
  173.8 1.4 multiply_reduce_fusion
  175.2 1.9 fusion.4
  178.8 3.4 %collective-permute-done = f32[32,8]{0,1:T(8,128)S(1)} collective-permute-done((f32[32,8]{0,1:T(8,128)S(1)}, f32[32,8]{0,1:T(8,128)S(1)}, u32[]{:S(2)}, u32[]{:S(2)}) %collective-permute-start) | collective-permute-done | bytes 1056 | tf_op jit(solution)/shard_map/ppermute | solution.py:245
  182.8 3.8 %collective-permute-start.1 = (f32[32,8]{0,1:T(8,128)S(1)}, f32[32,8]{0,1:T(8,128)S(1)}, u32[]{:S(2)}, u32[]{:S(2)}) collective-permute-start(f32[32,8]{0,1:T(8,128)S(1)} %fusion.19), channel_id=1, source_target_pairs={{0,2},{1,3},{2,0},{3,1},{4,6},{5,7},{6,4},{7,5},{8,10},{9,11},{10,... | collective-permute-start | bytes 3080 | tf_op jit(solution)/shard_map/ppermute | solution.py:245
  186.7 1.2 pad_maximum_fusion.refs_4_
  188.9 3.9 %collective-permute-start.2 = (f32[32,8]{0,1:T(8,128)S(1)}, f32[32,8]{0,1:T(8,128)S(1)}, u32[]{:S(2)}, u32[]{:S(2)}) collective-permute-start(f32[32,8]{0,1:T(8,128)S(1)} %fusion.35), channel_id=1, source_target_pairs={{0,4},{1,5},{2,6},{3,7},{4,0},{5,1},{6,2},{7,3},{8,12},{9,13},{10,... | collective-permute-start | bytes 3080 | tf_op jit(solution)/shard_map/ppermute | solution.py:245
  192.8 10.2 %shard_map.158 = bf16[32,3,24,256]{3,2,1,0:T(8,128)(2,1)} custom-call(s32[4]{0:T(128)S(1)} %pad_add_fusion.where_ref, bf16[768,512]{1,0:T(8,128)(2,1)S(1)} %bitcast.75, bf16[768,512]{1,0:T(8,128)(2,1)S(1)} %collective-permute-done.3.refs_1_, bf16[768,512]{1,0:T(8,128)(2,1)} %collective-permute-done.4.refs_2_, ...), custom_call_target="tpu_custom_call" | custom-call | flops 4831838208 | bytes 16777216 | tf_op jit(solution)/shard_map/pallas_call | solution.py:132
  (59 shorter events, 11.7 us)
Async XLA Ops:
  7.2 3.6 %copy-start = (bf16[8,32,640]{2,1,0:T(8,128)(2,1)S(1)}, bf16[8,32,640]{2,1,0:T(8,128)(2,1)}, u32[]{:S(2)}) copy-start(bf16[8,32,640]{2,1,0:T(8,128)(2,1)} %param.16) | copy-start | bytes 983044
  7.2 60.1 %all-gather.2.cloned.1.call-start = ((), (), s32[]{:S(2)}) async-start(), calls=%async_computation.2 | async-start | bytes 6758400 | tf_op jit(solution)/shard_map/all_gather | solution.py:221
  7.9 165.9 %reduce-scatter.2.cloned.1.call-start = ((), (), s32[]{:S(2)}) async-start(), calls=%async_computation.3 | async-start | bytes 2949120 | tf_op jit(solution)/shard_map/reduce_scatter | solution.py:224
  73.9 10.8 %copy-start.4 = (bf16[128,3,256]{2,0,1:T(8,128)(2,1)S(1)}, bf16[128,3,256]{2,0,1:T(8,128)(2,1)}, u32[]{:S(2)}) copy-start(bf16[128,3,256]{2,0,1:T(8,128)(2,1)} %param.27) | copy-start | bytes 589828
  78.0 30.3 %all-to-all-start = ((bf16[32,24,512]{2,1,0:T(8,128)(2,1)}), bf16[32,24,512]{2,1,0:T(8,128)(2,1)S(1)}, u32[]{:S(2)}, u32[]{:S(2)}) async-start(bf16[32,24,512]{2,1,0:T(8,128)(2,1)} %bitcast.76), calls=%async_computation.1 | async-start | bytes 1572864 | tf_op jit(solution)/shard_map/all_to_all | solution.py:184
  85.5 12.5 %collective-permute-start.11 = (bf16[1,3,128,256]{3,2,1,0:T(8,128)(2,1)S(1)}, bf16[1,3,128,256]{3,2,1,0:T(8,128)(2,1)S(1)}, u32[]{:S(2)}, u32[]{:S(2)}) collective-permute-start(bf16[1,3,128,256]{3,2,1,0:T(8,128)(2,1)S(1)} %get-tuple-element.4), channel_id=1, source_target_pairs={{0,16},{16,32},{32,48},{48,0},{1,17},{17,33},{33,49},{49,1},{2,18}... | collective-permute-start | bytes 589832 | tf_op jit(solution)/shard_map/ppermute | solution.py:155
  86.9 12.5 %collective-permute-start.13 = (bf16[1,3,128,256]{3,2,1,0:T(8,128)(2,1)S(1)}, bf16[1,3,128,256]{3,2,1,0:T(8,128)(2,1)S(1)}, u32[]{:S(2)}, u32[]{:S(2)}) collective-permute-start(bf16[1,3,128,256]{3,2,1,0:T(8,128)(2,1)S(1)} %get-tuple-element.4), channel_id=1, source_target_pairs={{0,48},{16,0},{32,16},{48,32},{1,49},{17,1},{33,17},{49,33},{2,50}... | collective-permute-start | bytes 589832 | tf_op jit(solution)/shard_map/ppermute | solution.py:156
  98.0 7.8 %collective-permute-start.12 = (bf16[1,3,128,256]{3,2,1,0:T(8,128)(2,1)S(1)}, bf16[1,3,128,256]{3,2,1,0:T(8,128)(2,1)S(1)}, u32[]{:S(2)}, u32[]{:S(2)}) collective-permute-start(bf16[1,3,128,256]{3,2,1,0:T(8,128)(2,1)S(1)} %collective-permute-done.11), channel_id=1, source_target_pairs={{0,16},{16,32},{32,48},{48,0},{1,17},{17,33},{33,49},{49,1},{2,18}... | collective-permute-start | bytes 589832 | tf_op jit(solution)/shard_map/ppermute | solution.py:157
  106.8 47.4 %copy-start.7 = (s32[1,3]{1,0:T(1,128)S(1)}, s32[1,3]{1,0:T(1,128)}, u32[]{:S(2)}) copy-start(s32[1,3]{1,0:T(1,128)} %param.21) | copy-start | bytes 40
  106.9 49.9 %copy-start.6 = (bf16[5120]{0:T(1024)(128)(2,1)S(1)}, bf16[5120]{0:T(1024)(128)(2,1)}, u32[]{:S(2)}) copy-start(bf16[5120]{0:T(1024)(128)(2,1)} %param.19) | copy-start | bytes 30724
  106.9 20.3 %collective-permute-start.14 = (bf16[4,3,128,256]{3,2,1,0:T(8,128)(2,1)}, bf16[4,3,128,256]{3,2,1,0:T(8,128)(2,1)S(1)}, u32[]{:S(2)}, u32[]{:S(2)}) collective-permute-start(bf16[4,3,128,256]{3,2,1,0:T(8,128)(2,1)} %pad_maximum_fusion.1), channel_id=1, source_target_pairs={{0,64},{64,128},{128,192},{192,0},{1,65},{65,129},{129,193},{193,1... | collective-permute-start | bytes 2359304 | tf_op jit(solution)/shard_map/ppermute | solution.py:155
  108.3 22.5 %collective-permute-start.3 = (bf16[768,512]{1,0:T(8,128)(2,1)S(1)}, bf16[768,512]{1,0:T(8,128)(2,1)S(1)}, u32[]{:S(2)}, u32[]{:S(2)}) collective-permute-start(bf16[768,512]{1,0:T(8,128)(2,1)S(1)} %bitcast.73), channel_id=1, source_target_pairs={{0,7},{1,0},{2,1},{3,2},{4,3},{5,4},{6,5},{7,6},{8,15},{9,8},{10,9... | collective-permute-start | bytes 2359304 | tf_op jit(solution)/shard_map/ppermute | solution.py:203
  111.6 21.9 %collective-permute-start.6 = (bf16[768,512]{1,0:T(8,128)(2,1)S(1)}, bf16[768,512]{1,0:T(8,128)(2,1)S(1)}, u32[]{:S(2)}, u32[]{:S(2)}) collective-permute-start(bf16[768,512]{1,0:T(8,128)(2,1)S(1)} %bitcast.74), channel_id=1, source_target_pairs={{0,1},{1,2},{2,3},{3,4},{4,5},{5,6},{6,7},{7,0},{8,9},{9,10},{10,1... | collective-permute-start | bytes 2359304 | tf_op jit(solution)/shard_map/ppermute | solution.py:202
  127.2 19.2 %collective-permute-start.15 = (bf16[4,3,128,256]{3,2,1,0:T(8,128)(2,1)S(1)}, bf16[4,3,128,256]{3,2,1,0:T(8,128)(2,1)S(1)}, u32[]{:S(2)}, u32[]{:S(2)}) collective-permute-start(bf16[4,3,128,256]{3,2,1,0:T(8,128)(2,1)S(1)} %collective-permute-done.14), channel_id=1, source_target_pairs={{0,64},{64,128},{128,192},{192,0},{1,65},{65,129},{129,193},{193,1... | collective-permute-start | bytes 2359304 | tf_op jit(solution)/shard_map/ppermute | solution.py:157
  130.8 18.8 %collective-permute-start.4 = (bf16[768,512]{1,0:T(8,128)(2,1)S(1)}, bf16[768,512]{1,0:T(8,128)(2,1)}, u32[]{:S(2)}, u32[]{:S(2)}) collective-permute-start(bf16[768,512]{1,0:T(8,128)(2,1)S(1)} %collective-permute-done.3.refs_1_), channel_id=1, source_target_pairs={{0,7},{1,0},{2,1},{3,2},{4,3},{5,4},{6,5},{7,6},{8,15},{9,8},{10,9... | collective-permute-start | bytes 2359304 | tf_op jit(solution)/shard_map/ppermute | solution.py:203
  133.5 19.8 %copy-start.2 = (bf16[768,512]{1,0:T(8,128)(2,1)}, bf16[768,512]{1,0:T(8,128)(2,1)S(1)}, u32[]{:S(2)}) copy-start(bf16[768,512]{1,0:T(8,128)(2,1)S(1)} %collective-permute-done.6.refs_7_) | copy-start | bytes 2359300
  133.5 19.8 %collective-permute-start.7 = (bf16[768,512]{1,0:T(8,128)(2,1)S(1)}, bf16[768,512]{1,0:T(8,128)(2,1)}, u32[]{:S(2)}, u32[]{:S(2)}) collective-permute-start(bf16[768,512]{1,0:T(8,128)(2,1)S(1)} %collective-permute-done.6.refs_7_), channel_id=1, source_target_pairs={{0,1},{1,2},{2,3},{3,4},{4,5},{5,6},{6,7},{7,0},{8,9},{9,10},{10,1... | collective-permute-start | bytes 2359304 | tf_op jit(solution)/shard_map/ppermute | solution.py:202
  133.5 19.8 %collective-permute-start.16 = (bf16[4,3,128,256]{3,2,1,0:T(8,128)(2,1)}, bf16[4,3,128,256]{3,2,1,0:T(8,128)(2,1)S(1)}, u32[]{:S(2)}, u32[]{:S(2)}) collective-permute-start(bf16[4,3,128,256]{3,2,1,0:T(8,128)(2,1)} %pad_maximum_fusion.1), channel_id=1, source_target_pairs={{0,192},{64,0},{128,64},{192,128},{1,193},{65,1},{129,65},{193,129... | collective-permute-start | bytes 2359304 | tf_op jit(solution)/shard_map/ppermute | solution.py:156
  147.3 29.9 %copy-start.5 = (bf16[5120]{0:T(1024)(128)(2,1)S(1)}, bf16[5120]{0:T(1024)(128)(2,1)}, u32[]{:S(2)}) copy-start(bf16[5120]{0:T(1024)(128)(2,1)} %param.20) | copy-start | bytes 30724
  149.6 19.0 %collective-permute-start.5 = (bf16[768,512]{1,0:T(8,128)(2,1)}, bf16[768,512]{1,0:T(8,128)(2,1)S(1)}, u32[]{:S(2)}, u32[]{:S(2)}) collective-permute-start(bf16[768,512]{1,0:T(8,128)(2,1)} %collective-permute-done.4.refs_2_), channel_id=1, source_target_pairs={{0,7},{1,0},{2,1},{3,2},{4,3},{5,4},{6,5},{7,6},{8,15},{9,8},{10,9... | collective-permute-start | bytes 2359304 | tf_op jit(solution)/shard_map/ppermute | solution.py:203
  153.3 19.7 %collective-permute-start.8 = (bf16[768,512]{1,0:T(8,128)(2,1)}, bf16[768,512]{1,0:T(8,128)(2,1)S(1)}, u32[]{:S(2)}, u32[]{:S(2)}) collective-permute-start(bf16[768,512]{1,0:T(8,128)(2,1)} %collective-permute-done.7.refs_6_), channel_id=1, source_target_pairs={{0,1},{1,2},{2,3},{3,4},{4,5},{5,6},{6,7},{7,0},{8,9},{9,10},{10,1... | collective-permute-start | bytes 2359304 | tf_op jit(solution)/shard_map/ppermute | solution.py:202
  154.2 38.6 %collective-permute-start.17 = (bf16[16,3,128,256]{3,2,1,0:T(8,128)(2,1)}, bf16[16,3,128,256]{3,2,1,0:T(8,128)(2,1)}, u32[]{:S(2)}, u32[]{:S(2)}) collective-permute-start(bf16[16,3,128,256]{3,2,1,0:T(8,128)(2,1)} %constant_dynamic-update-slice_fusion.refs_8_), channel_id=1, source_target_pairs={{0,8},{8,0},{1,9},{9,1},{2,10},{10,2},{3,11},{11,3},{4,12},{12,4},... | collective-permute-start | bytes 9437192 | tf_op jit(solution)/shard_map/ppermute | solution.py:198
  169.4 17.3 %collective-permute-start.10 = (bf16[384,512]{1,0:T(8,128)(2,1)}, bf16[384,512]{1,0:T(8,128)(2,1)}, u32[]{:S(2)}, u32[]{:S(2)}) collective-permute-start(bf16[384,512]{1,0:T(8,128)(2,1)} %slice.26), channel_id=1, source_target_pairs={{0,7},{1,0},{2,1},{3,2},{4,3},{5,4},{6,5},{7,6},{8,15},{9,8},{10,9... | collective-permute-start | bytes 1179656 | tf_op jit(solution)/shard_map/ppermute | solution.py:208
  173.8 12.9 %collective-permute-start.9 = (bf16[384,512]{1,0:T(8,128)(2,1)}, bf16[384,512]{1,0:T(8,128)(2,1)}, u32[]{:S(2)}, u32[]{:S(2)}) collective-permute-start(bf16[384,512]{1,0:T(8,128)(2,1)} %slice.25), channel_id=1, source_target_pairs={{0,1},{1,2},{2,3},{3,4},{4,5},{5,6},{6,7},{7,0},{8,9},{9,10},{10,1... | collective-permute-start | bytes 1179656 | tf_op jit(solution)/shard_map/ppermute | solution.py:207
  173.8 19.0 %copy-start.1 = (bf16[16,3,128,256]{3,2,1,0:T(8,128)(2,1)S(1)}, bf16[16,3,128,256]{3,2,1,0:T(8,128)(2,1)}, u32[]{:S(2)}) copy-start(bf16[16,3,128,256]{3,2,1,0:T(8,128)(2,1)} %constant_dynamic-update-slice_fusion.refs_8_) | copy-start | bytes 9437188
  173.8 19.0 %copy-start.3 = (bf16[768,512]{1,0:T(8,128)(2,1)S(1)}, bf16[768,512]{1,0:T(8,128)(2,1)}, u32[]{:S(2)}) copy-start(bf16[768,512]{1,0:T(8,128)(2,1)} %copy-done.2) | copy-start | bytes 2359300
  178.5 3.7 %collective-permute-start = (f32[32,8]{0,1:T(8,128)S(1)}, f32[32,8]{0,1:T(8,128)S(1)}, u32[]{:S(2)}, u32[]{:S(2)}) collective-permute-start(f32[32,8]{0,1:T(8,128)S(1)} %select_subtract_fusion), channel_id=1, source_target_pairs={{0,1},{1,0},{2,3},{3,2},{4,5},{5,4},{6,7},{7,6},{8,9},{9,8},{10,11... | collective-permute-start | bytes 3080 | tf_op jit(solution)/shard_map/ppermute | solution.py:245
  182.8 5.4 %collective-permute-start.1 = (f32[32,8]{0,1:T(8,128)S(1)}, f32[32,8]{0,1:T(8,128)S(1)}, u32[]{:S(2)}, u32[]{:S(2)}) collective-permute-start(f32[32,8]{0,1:T(8,128)S(1)} %fusion.19), channel_id=1, source_target_pairs={{0,2},{1,3},{2,0},{3,1},{4,6},{5,7},{6,4},{7,5},{8,10},{9,11},{10,... | collective-permute-start | bytes 3080 | tf_op jit(solution)/shard_map/ppermute | solution.py:245
  188.9 14.1 %collective-permute-start.2 = (f32[32,8]{0,1:T(8,128)S(1)}, f32[32,8]{0,1:T(8,128)S(1)}, u32[]{:S(2)}, u32[]{:S(2)}) collective-permute-start(f32[32,8]{0,1:T(8,128)S(1)} %fusion.35), channel_id=1, source_target_pairs={{0,4},{1,5},{2,6},{3,7},{4,0},{5,1},{6,2},{7,3},{8,12},{9,13},{10,... | collective-permute-start | bytes 3080 | tf_op jit(solution)/shard_map/ppermute | solution.py:245
Sparse Core Ops, SparseCore 0:
  10.6 56.6 all-gather.1
  74.0 45.9 reduce-scatter.1

commit v2 on v1

v2 whole, which is shorter than its diff:
```python
import math

import jax
import jax.numpy as jnp
from jax import lax
from jax.experimental import pallas as pl
from jax.experimental.pallas import tpu as pltpu
from jax.sharding import Mesh, PartitionSpec as P

HR = 40
HDR = 128
NY, NX, NC, NZ = 4, 4, 2, 8
PLANE = ("y", "x", "core")


def ring(count, step):
    return [(i, (i + step) % count) for i in range(count)]


def pair_attention(queries, keys_in, values_in, head_count):
    pair_count, length, row_width = queries.shape
    head_size = row_width // head_count
    query_heads = queries.reshape(pair_count, length, head_count, head_size)
    key_heads = keys_in.reshape(pair_count, length, head_count, head_size)
    value_heads = values_in.reshape(pair_count, length, head_count, head_size)
    scores = jnp.einsum(
        "pihd,pjhd->phij", query_heads, key_heads, preferred_element_type=jnp.float32
    ) * (1.0 / math.sqrt(HDR))
    highest = jnp.max(scores, axis=-1, keepdims=True)
    weights = jnp.exp(scores - highest)
    soft_weights = (weights / jnp.sum(weights, axis=-1, keepdims=True)).astype(jnp.bfloat16)
    context = jnp.einsum(
        "phij,pjhd->pihd", soft_weights, value_heads, preferred_element_type=jnp.float32
    )
    return context.astype(jnp.bfloat16).reshape(pair_count * length, row_width)


def select_kernel(owner_ref, rank_ref, len_ref, rows_ref, out_ref):
    places = rank_ref.shape[0]
    position = lax.broadcasted_iota(jnp.int32, rows_ref.shape[1:], 0)

    def one_prompt(prompt, carry):
        owner = owner_ref[0, prompt]
        for rank in range(3):
            cand = jnp.int32(0)
            live = jnp.int32(0)
            for place in range(places):
                hit = rank_ref[place, prompt] == rank
                cand = jnp.where(hit, place, cand)
                live = jnp.where(hit, len_ref[place, prompt], live)
            picked = rows_ref[prompt * places + cand].astype(jnp.float32)
            out_ref[owner * 3 + rank] = jnp.where(position < live, picked, 0.0).astype(out_ref.dtype)
        return carry

    lax.fori_loop(0, owner_ref.shape[1], one_prompt, 0)


def select_rows(blend_owner, cand_rank, cand_len, blend_rows):
    prompts, cands, length, features = blend_rows.shape
    smem = pl.BlockSpec(memory_space=pltpu.SMEM)
    vmem = pl.BlockSpec(memory_space=pltpu.VMEM)
    return pl.pallas_call(
        select_kernel,
        out_shape=jax.ShapeDtypeStruct((prompts * 3, length, features), blend_rows.dtype),
        in_specs=[smem, smem, smem, vmem],
        out_specs=vmem,
        cost_estimate=pl.CostEstimate(flops=0, bytes_accessed=3 << 20, transcendentals=0),
    )(blend_owner, cand_rank.T, cand_len.T, blend_rows.reshape(prompts * cands, length, features))


def arrange_kernel(where_ref, *refs):
    slab_refs, out_ref = refs[:-1], refs[-1]
    third, depth = slab_refs[0].shape[1:3]
    my_y, my_x, my_core, my_z = where_ref[0], where_ref[1], where_ref[2], where_ref[3]
    for swapped in range(NC):
        for back in range(NY):
            slabs = slab_refs[swapped * NY + back]
            for left in range(NX):
                slab_y = lax.rem(my_y - back + NY, NY)
                slab_x = lax.rem(my_x - left + NX, NX)
                slab_core = lax.rem(my_core + swapped, NC)
                slab = (slab_y * NX + slab_x) * NC + slab_core
                order = lax.rem(slab // 4 - my_z + NZ, NZ)
                start = pl.multiple_of((order * 4 + lax.rem(slab, 4)) * depth, depth)
                for part in range(third):
                    out_ref[part, pl.ds(start, depth), :] = slabs[left, part]


def arrange(where, slabs):
    third, depth, width = slabs[0].shape[1:]
    vmem = pl.BlockSpec(memory_space=pltpu.VMEM)
    return pl.pallas_call(
        arrange_kernel,
        out_shape=jax.ShapeDtypeStruct((third, NC * NY * NX * depth, width), jnp.bfloat16),
        in_specs=[pl.BlockSpec(memory_space=pltpu.SMEM)] + [vmem] * len(slabs),
        out_specs=vmem,
        compiler_params=pltpu.CompilerParams(vmem_limit_bytes=32 << 20),
        cost_estimate=pl.CostEstimate(flops=0, bytes_accessed=12 << 20, transcendentals=0),
    )(where, *slabs)


def project_kernel(rows_ref, columns_ref, out_ref):
    out_ref[...] = lax.dot_general(
        rows_ref[...], columns_ref[...], (((1,), (1,)), ((), ())), preferred_element_type=jnp.float32
    ).astype(out_ref.dtype)


def project(rows, columns):
    count, depth = rows.shape
    width = columns.shape[0]
    steps = 4
    return pl.pallas_call(
        project_kernel,
        out_shape=jax.ShapeDtypeStruct((count, width), jnp.bfloat16),
        grid=(steps,),
        in_specs=[
            pl.BlockSpec((count, depth), lambda i: (0, 0)),
            pl.BlockSpec((width // steps, depth), lambda i: (i, 0)),
        ],
        out_specs=pl.BlockSpec((count, width // steps), lambda i: (0, i)),
        compiler_params=pltpu.CompilerParams(vmem_limit_bytes=16 << 20),
        cost_estimate=pl.CostEstimate(
            flops=2 * count * width * depth, bytes_accessed=9 << 20, transcendentals=0
        ),
    )(rows, columns)


def squares_of(values):
    value = values.astype(jnp.float32)
    return jnp.sum(value * value, axis=-1, keepdims=True)


def first_kernel(orders, *refs):
    row_refs = refs[: len(orders)]
    weight_ref, total_ref, squares_ref = refs[len(orders) :]
    features = row_refs[0].shape[1]
    squares = sum(squares_of(rows[...]) for rows in row_refs)
    squares_ref[...] = jnp.broadcast_to(squares, squares_ref.shape)
    for part in range(weight_ref.shape[0]):
        total_ref[part] = sum(
            jnp.dot(
                rows[...],
                weight_ref[part, order * features : (order + 1) * features, :],
                preferred_element_type=jnp.float32,
            )
            for order, rows in zip(orders, row_refs)
        )


def last_kernel(orders, row_a, row_b, low_ref, high_ref, weight_ref, total_ref, squares_ref, out_ref):
    features = row_a.shape[1]
    half_steps = pl.num_programs(0) // 2
    across = jnp.where(pl.program_id(0) < half_steps, low_ref[...], high_ref[...])
    values = [row_a[...], row_b[...], across]
    squares = squares_ref[:, :1] + sum(squares_of(value) for value in values)
    scale = lax.rsqrt(squares * (1.0 / (NZ * features)) + 1e-06)
    prompts, third, length, width = out_ref.shape
    for part in range(third):
        total = total_ref[part] + sum(
            jnp.dot(
                value,
                weight_ref[part, order * features : (order + 1) * features, :],
                preferred_element_type=jnp.float32,
            )
            for order, value in zip(orders, values)
        )
        out_ref[:, part] = (total * scale).astype(out_ref.dtype).reshape(prompts, length, width)


def whole_spec(array):
    return pl.BlockSpec(array.shape, lambda i: (0,) * array.ndim, pipeline_mode=pl.Buffered(1))


def encode_first(orders, blocks, weights):
    rows, features = blocks[0].shape
    third, _, width = weights.shape
    steps = 4
    step_rows = rows // steps
    return pl.pallas_call(
        lambda *refs: first_kernel(orders, *refs),
        out_shape=(
            jax.ShapeDtypeStruct((third, rows, width), jnp.float32),
            jax.ShapeDtypeStruct((rows, 128), jnp.float32),
        ),
        grid=(steps,),
        in_specs=[pl.BlockSpec((step_rows, features), lambda i: (i, 0))] * len(blocks)
        + [whole_spec(weights)],
        out_specs=(
            pl.BlockSpec((third, step_rows, width), lambda i: (0, i, 0)),
            pl.BlockSpec((step_rows, 128), lambda i: (i, 0)),
        ),
        compiler_params=pltpu.CompilerParams(vmem_limit_bytes=24 << 20),
        cost_estimate=pl.CostEstimate(
            flops=2 * rows * len(blocks) * features * third * width,
            bytes_accessed=12 << 20,
            transcendentals=0,
        ),
    )(*blocks, weights)


def encode_last(orders, row_a, row_b, low, high, weights, total, squares, prompts):
    rows, features = row_a.shape
    third, _, width = weights.shape
    length = rows // prompts
    steps = 4
    step_rows = rows // steps
    step_prompts = prompts // steps
    out = pl.pallas_call(
        lambda *refs: last_kernel(orders, *refs),
        out_shape=jax.ShapeDtypeStruct((prompts, third, length, width), jnp.bfloat16),
        grid=(steps,),
        in_specs=[
            pl.BlockSpec((step_rows, features), lambda i: (i, 0)),
            pl.BlockSpec((step_rows, features), lambda i: (i, 0)),
            pl.BlockSpec((step_rows, features), lambda i: (jnp.minimum(i, steps // 2 - 1), 0)),
            pl.BlockSpec((step_rows, features), lambda i: (jnp.maximum(i - steps // 2, 0), 0)),
            whole_spec(weights),
            pl.BlockSpec((third, step_rows, width), lambda i: (0, i, 0)),
            pl.BlockSpec((step_rows, 128), lambda i: (i, 0)),
        ],
        out_specs=pl.BlockSpec((step_prompts, third, length, width), lambda i: (i, 0, 0, 0)),
        compiler_params=pltpu.CompilerParams(vmem_limit_bytes=24 << 20),
        cost_estimate=pl.CostEstimate(
            flops=40 * rows * 3 * features * third * width,
            bytes_accessed=12 << 20,
            transcendentals=rows,
        ),
    )(row_a, row_b, low, high, weights, total, squares)
    return out.transpose(0, 2, 1, 3)


def norm_kernel(pair_ref, resid_ref, gain_ref, score_ref, sum_ref, hidden_ref, votes_ref):
    mixed = resid_ref[...].astype(jnp.float32) + sum_ref[...].astype(jnp.float32)
    squares = jnp.sum(mixed * mixed, axis=-1, keepdims=True)
    scale = lax.rsqrt(squares * (1.0 / mixed.shape[1]) + 1e-05)
    normed = mixed * scale * gain_ref[...].astype(jnp.float32)
    hidden_ref[...] = normed.astype(hidden_ref.dtype)
    logit = jnp.sum(normed[:1] * score_ref[...].astype(jnp.float32), axis=-1, keepdims=True)
    cand = lax.broadcasted_iota(jnp.int32, votes_ref.shape, 0)
    prompt = lax.broadcasted_iota(jnp.int32, votes_ref.shape, 1)
    own = prompt == pair_ref[0, 0]
    upward = jnp.where(own & (cand == pair_ref[0, 1]), logit, 0.0)
    downward = jnp.where(own & (cand == pair_ref[0, 2]), logit, 0.0)
    votes_ref[...] = upward - downward


def norm_and_vote(pair_index, resid, gain, score, part_sum, prompts, cands):
    rows, width = resid.shape
    vmem = pl.BlockSpec(memory_space=pltpu.VMEM)
    return pl.pallas_call(
        norm_kernel,
        out_shape=(
            jax.ShapeDtypeStruct((rows, width), jnp.bfloat16),
            jax.ShapeDtypeStruct((cands, prompts), jnp.float32),
        ),
        in_specs=[pl.BlockSpec(memory_space=pltpu.SMEM)] + [vmem] * 4,
        out_specs=(vmem, vmem),
        cost_estimate=pl.CostEstimate(
            flops=rows * width * 8, bytes_accessed=2 << 20, transcendentals=rows
        ),
    )(pair_index, resid, gain, score, part_sum)


def together(*values):
    return lax.optimization_barrier(values)


def body(
    rank_query,
    rank_key,
    rank_value,
    rank_resid,
    out_weight,
    rank_gain,
    score_weight,
    pair_index,
    cand_rank,
    cand_len,
    blend_owner,
    blend_rows,
    blend_gain,
    blend_weight,
):
    local_heads = HR // NZ
    length = rank_query.shape[1]
    my_y, my_x, my_core, my_z = (lax.axis_index(a) for a in ("y", "x", "core", "z"))

    where = jnp.stack([my_y, my_x, my_core, my_z]).astype(jnp.int32)
    columns = lax.all_gather(out_weight.T, PLANE, axis=0, tiled=True)

    outgoing = select_rows(blend_owner, cand_rank, cand_len, blend_rows)
    rank_query, blend_weight, outgoing = together(rank_query, blend_weight, outgoing)
    prompts = blend_rows.shape[0]
    features = blend_rows.shape[3]
    arrived = lax.all_to_all(
        outgoing.reshape(prompts, -1, features), PLANE, split_axis=0, concat_axis=0, tiled=True
    )
    own = arrived.reshape(prompts * arrived.shape[1], features)

    context = pair_attention(rank_query, rank_key, rank_value, local_heads)
    depth = blend_weight.shape[0]
    slab = (my_y * NX + my_x) * NC + my_core
    gain = lax.dynamic_slice_in_dim(blend_gain, slab * depth, depth, 0).astype(jnp.float32)
    own_slab = (blend_weight.transpose(1, 0, 2).astype(jnp.float32) * gain[None, :, None]).astype(
        jnp.bfloat16
    )[None]
    gain_row = rank_gain.reshape(1, -1)
    score_row = score_weight.reshape(1, -1)
    own, context, own_slab, gain_row, score_row, where = together(
        own, context, own_slab, gain_row, score_row, where
    )

    lower = lax.ppermute(own, "z", ring(NZ, 1))
    upper = lax.ppermute(own, "z", ring(NZ, -1))
    x_before = lax.ppermute(own_slab, "x", ring(NX, 1))
    x_after = lax.ppermute(own_slab, "x", ring(NX, -1))
    x_across = lax.ppermute(x_before, "x", ring(NX, 1))
    strip = jnp.concatenate([own_slab, x_before, x_across, x_after], axis=0)
    lower, upper, strip = together(lower, upper, strip)
    blocks = {1: upper, NZ - 1: lower, 0: own}

    lower = lax.ppermute(lower, "z", ring(NZ, 1))
    upper = lax.ppermute(upper, "z", ring(NZ, -1))
    y_before = lax.ppermute(strip, "y", ring(NY, 1))
    y_after = lax.ppermute(strip, "y", ring(NY, -1))
    term_rows = project(context, columns)
    lower, upper, y_before, y_after, term_rows = together(
        lower, upper, y_before, y_after, term_rows
    )
    blocks.update({2: upper, NZ - 2: lower})
    part_sum = lax.psum_scatter(term_rows, "z", scatter_dimension=0, tiled=True)

    lower = lax.ppermute(lower, "z", ring(NZ, 1))
    upper = lax.ppermute(upper, "z", ring(NZ, -1))
    y_across = jnp.concatenate(
        [
            lax.ppermute(y_before[:2], "y", ring(NY, 1)),
            lax.ppermute(y_after[2:], "y", ring(NY, -1)),
        ],
        axis=0,
    )
    lower, upper, y_across = together(lower, upper, y_across)

    slabs = [strip, y_before, y_across, y_after]
    weights = arrange(where, slabs + [lax.ppermute(s, "core", ring(NC, 1)) for s in slabs])
    near = (0, 1, 2, NZ - 2, NZ - 1)
    half = own.shape[0] // 2
    total, squares = encode_first(near, [blocks[i] for i in near], weights)
    low = lax.ppermute(lower[:half], "z", ring(NZ, 1))
    high = lax.ppermute(upper[half:], "z", ring(NZ, -1))
    blended_qkv = encode_last(
        (3, NZ - 3, 4), upper, lower, low, high, weights, total, squares, prompts
    )

    part_sum, blended_qkv = together(part_sum, blended_qkv)
    own_pairs = rank_resid.shape[0]
    rank_hidden, votes = norm_and_vote(
        pair_index,
        rank_resid.reshape(own_pairs * length, -1),
        gain_row,
        score_row,
        part_sum,
        prompts,
        cand_rank.shape[1],
    )
    rank_hidden = rank_hidden.reshape(rank_resid.shape)
    for bit in (1, 2, 4):
        votes = votes + lax.ppermute(votes, "z", [(i, i ^ bit) for i in range(NZ)])
    cand_score = votes.T
    return (rank_hidden, cand_score, blended_qkv)


def solution(mesh):
    grid = Mesh(mesh.devices.reshape(NY, NX, NC, NZ), ("y", "x", "core", "z"))
    whole = ("y", "x", "core", "z")
    placed = (
        P(PLANE, None, "z"),
        P(PLANE, None, "z"),
        P(PLANE, None, "z"),
        P(whole, None, None),
        P("z", PLANE),
        P(),
        P(),
        P(whole, None),
        P(PLANE, None),
        P(PLANE, None),
        P(PLANE, None),
        P(PLANE, None, None, "z"),
        P(),
        P(PLANE, None, "z"),
    )
    return jax.shard_map(
        body,
        mesh=grid,
        in_specs=placed,
        out_specs=(P(whole, None, None), P(PLANE, None), P(PLANE, None, None, "z")),
        check_vma=False,
    )
```

time: 211 us -> 169 us (0.80)
  waiting for transfers between devices: 118 us -> 83.1 us
  matrix products: 9.79 us -> 1.02 us
  other arithmetic: 10.3 us -> 2.39 us
  Pallas kernels: 14.3 us -> 21.4 us
  starting transfers between devices: 34.8 us -> 41.3 us
    all_gather x1, waiting for transfers between devices: 55.9 us -> 3.63 us  [body(): columns = lax.all_gather(out_weight.T, PLANE, axis=0, tiled=True)]
    all_to_all x1, waiting for transfers between devices: 0.01 us -> 10.9 us  [body(): lax.all_to_all(outgoing.reshape(prompts, -1, features), PLANE, split_axis...]
    pallas_call x1 -> x5, Pallas kernels: 10.2 us -> 17.3 us  [the longest x1 5.46 us: encode_first(): pl.pallas_call(lambda *refs: first_kernel(orders, *refs), out_shape=(jax....]
    dot_general x1 -> x0, matrix products: 6.64 us -> none  [body(): jnp.dot(context, lax.all_gather(out_weight, PLANE, axis=1, tiled=True), p...]
    ppermute x18 -> x22, starting transfers between devices: 28.8 us -> 33.4 us  [the longest x3 9.61 us: body(): votes = votes + lax.ppermute(votes, 'z', [(i, i ^ bit) for i in range(NZ)])]
    ppermute x18 -> x22, waiting for transfers between devices: 61.2 us -> 65.6 us  [the longest x2 12.5 us: body(): lower = lax.ppermute(lower, 'z', ring(NZ, 1))]
    reduce_scatter x1, waiting for transfers between devices: 0.01 us -> 2.26 us  [body(): part_sum = lax.psum_scatter(term_rows, 'z', scatter_dimension=0, tiled=True)]
  transfers between devices with their start and end apart: 21 -> 25, of which waited for: 10 -> 18; matrix products, arithmetic and copies ran while one was open for 10% -> 3% of each run, Pallas kernels for 7% -> 11%
where the time goes in v2:
time: 169 us
  waiting for transfers between devices  83.1 us (49%)
  starting transfers between devices  41.3 us (24%)
  Pallas kernels  21.4 us (13%)
  between operations  14.2 us (8%)
  local copies, waits for them, and re-layouts  5.45 us (3%)
  other arithmetic  2.39 us (1%)
    ppermute x2, waiting for transfers between devices, body(): lower = lax.ppermute(lower, 'z', ring(NZ, 1))  12.5 us
    ppermute x1, waiting for transfers between devices, body(): low = lax.ppermute(lower[:half], 'z', ring(NZ, 1))  11.5 us
    all_to_all x1, waiting for transfers between devices, body(): lax.all_to_all(outgoing.reshape(prompts, -1, features), PLANE, split_axis...  10.9 us
    ppermute x3, starting transfers between devices, body(): votes = votes + lax.ppermute(votes, 'z', [(i, i ^ bit) for i in range(NZ)])  9.61 us
    ppermute x1, waiting for transfers between devices, body(): lax.ppermute(y_after[2:], 'y', ring(NY, -1))  7.87 us
    all_to_all x1, starting transfers between devices, body(): lax.all_to_all(outgoing.reshape(prompts, -1, features), PLANE, split_axis...  7.75 us
    ppermute x1, waiting for transfers between devices, body(): x_across = lax.ppermute(x_before, 'x', ring(NX, 1))  7 us
    ppermute x1, starting transfers between devices, body(): upper = lax.ppermute(own, 'z', ring(NZ, -1))  6.7 us
  transfers between devices with their start and end apart: 25, of which 18 were waited for; matrix products, arithmetic and copies ran while one was open for 3% of the time, Pallas kernels for 11%

profile of v2, /device:TPU:2, one launch (start us, length us, event | category | flops | bytes accessed | tf_op | source)
XLA Modules:
  0.0 168.8 jit_solution(6484460539441012325)
XLA Ops:
  7.9 4.1 %shard_map.157 = bf16[96,8,512]{2,1,0:T(8,128)(2,1)} custom-call(s32[1,32]{1,0:T(1,128)} %owner_ref.1, s32[8,32]{1,0:T(8,128)} %bitcast.73, s32[8,32]{1,0:T(8,128)} %bitcast.74, bf16[256,8,512]{2,1,0:T(8,128)(2,1)} %bitcast.69), custom_call_target="tpu_custom_call" | custom-call | bytes 3145728 | tf_op jit(solution)/shard_map/pallas_call | solution.py:62
  12.0 7.7 %all-to-all-start = ((bf16[32,24,512]{2,1,0:T(8,128)(2,1)}), bf16[32,24,512]{2,1,0:T(8,128)(2,1)S(1)}, u32[]{:S(2)}, u32[]{:S(2)}) async-start(bf16[32,24,512]{2,1,0:T(8,128)(2,1)} %bitcast.68), calls=%async_computation | async-start | bytes 1572864 | tf_op jit(solution)/shard_map/all_to_all | solution.py:295
  23.3 10.9 %all-to-all-done = bf16[32,24,512]{2,1,0:T(8,128)(2,1)S(1)} async-done(((bf16[32,24,512]{2,1,0:T(8,128)(2,1)}), bf16[32,24,512]{2,1,0:T(8,128)(2,1)S(1)}, u32[]{:S(2)}, u32[]{:S(2)}) %all-to-all-start) | async-done | bytes 786464 | tf_op jit(solution)/shard_map/all_to_all | solution.py:295
  34.2 6.7 %collective-permute-start.1 = (bf16[768,512]{1,0:T(8,128)(2,1)S(1)}, bf16[768,512]{1,0:T(8,128)(2,1)}, u32[]{:S(2)}, u32[]{:S(2)}) collective-permute-start(bf16[768,512]{1,0:T(8,128)(2,1)S(1)} %bitcast.65), channel_id=1, source_target_pairs={{0,7},{1,0},{2,1},{3,2},{4,3},{5,4},{6,5},{7,6},{8,15},{9,8},{10,9... | collective-permute-start | bytes 2359304 | tf_op jit(solution)/shard_map/ppermute | solution.py:314
  41.1 1.8 %collective-permute-start.4 = (bf16[1,3,128,256]{3,2,1,0:T(8,128)(2,1)S(1)}, bf16[1,3,128,256]{3,2,1,0:T(8,128)(2,1)S(1)}, u32[]{:S(2)}, u32[]{:S(2)}) collective-permute-start(bf16[1,3,128,256]{3,2,1,0:T(8,128)(2,1)S(1)} %fusion.11), channel_id=1, source_target_pairs={{0,48},{16,0},{32,16},{48,32},{1,49},{17,1},{33,17},{49,33},{2,50}... | collective-permute-start | bytes 589832 | tf_op jit(solution)/shard_map/ppermute | solution.py:316
  42.9 4.9 %collective-permute-done.2 = bf16[1,3,128,256]{3,2,1,0:T(8,128)(2,1)S(1)} collective-permute-done((bf16[1,3,128,256]{3,2,1,0:T(8,128)(2,1)S(1)}, bf16[1,3,128,256]{3,2,1,0:T(8,128)(2,1)S(1)}, u32[]{:S(2)}, u32[]{:S(2)}) %collective-permute-start.2) | collective-permute-done | bytes 196640 | tf_op jit(solution)/shard_map/ppermute | solution.py:315
  48.0 7.0 %collective-permute-done.3 = bf16[1,3,128,256]{3,2,1,0:T(8,128)(2,1)S(1)} collective-permute-done((bf16[1,3,128,256]{3,2,1,0:T(8,128)(2,1)S(1)}, bf16[1,3,128,256]{3,2,1,0:T(8,128)(2,1)S(1)}, u32[]{:S(2)}, u32[]{:S(2)}) %collective-permute-start.3) | collective-permute-done | bytes 196640 | tf_op jit(solution)/shard_map/ppermute | solution.py:317
  55.1 3.0 %collective-permute-done.1.refs_1_ = bf16[768,512]{1,0:T(8,128)(2,1)} collective-permute-done((bf16[768,512]{1,0:T(8,128)(2,1)S(1)}, bf16[768,512]{1,0:T(8,128)(2,1)}, u32[]{:S(2)}, u32[]{:S(2)}) %collective-permute-start.1) | collective-permute-done | bytes 786464 | tf_op jit(solution)/shard_map/ppermute | solution.py:314
  58.2 3.5 %collective-permute-done.refs_4_ = bf16[768,512]{1,0:T(8,128)(2,1)} collective-permute-done((bf16[768,512]{1,0:T(8,128)(2,1)S(1)}, bf16[768,512]{1,0:T(8,128)(2,1)}, u32[]{:S(2)}, u32[]{:S(2)}) %collective-permute-start) | collective-permute-done | bytes 786464 | tf_op jit(solution)/shard_map/ppermute | solution.py:313
  61.7 3.2 %collective-permute-start.6 = (bf16[768,512]{1,0:T(8,128)(2,1)}, bf16[768,512]{1,0:T(8,128)(2,1)}, u32[]{:S(2)}, u32[]{:S(2)}) collective-permute-start(bf16[768,512]{1,0:T(8,128)(2,1)} %collective-permute-done.1.refs_1_), channel_id=1, source_target_pairs={{0,7},{1,0},{2,1},{3,2},{4,3},{5,4},{6,5},{7,6},{8,15},{9,8},{10,9... | collective-permute-start | bytes 2359304 | tf_op jit(solution)/shard_map/ppermute | solution.py:323
  67.0 3.6 %all-gather.2.cloned.1.call-done.columns_ref = bf16[5120,640]{1,0:T(8,128)(2,1)} async-done(((bf16[160,640]{1,0:T(8,128)(2,1)}), bf16[5120,640]{1,0:T(8,128)(2,1)}) %all-gather.2.cloned.1.call-update) | async-done | bytes 6553616 | tf_op jit(solution)/shard_map/all_gather | solution.py:289
  70.6 2.9 %copy-done.1 = bf16[5120,640]{1,0:T(8,128)(2,1)S(1)} copy-done((bf16[5120,640]{1,0:T(8,128)(2,1)S(1)}, bf16[5120,640]{1,0:T(8,128)(2,1)}, u32[]{:S(2)}) %copy-start.1) | copy-done | bytes 6553624
  73.5 3.9 %shard_map.158 = bf16[256,5120]{1,0:T(8,128)(2,1)} custom-call(bf16[256,640]{1,0:T(8,128)(2,1)S(1)} %bitcast.64, bf16[5120,640]{1,0:T(8,128)(2,1)S(1)} %copy-done.1), custom_call_target="tpu_custom_call" | custom-call | flops 1677721600 | bytes 9437184 | tf_op jit(solution)/shard_map/pallas_call | solution.py:112
  77.4 4.5 %collective-permute-done.5.refs_3_ = bf16[768,512]{1,0:T(8,128)(2,1)} collective-permute-done((bf16[768,512]{1,0:T(8,128)(2,1)}, bf16[768,512]{1,0:T(8,128)(2,1)}, u32[]{:S(2)}, u32[]{:S(2)}) %collective-permute-start.5) | collective-permute-done | bytes 786464 | tf_op jit(solution)/shard_map/ppermute | solution.py:322
  81.9 2.4 %collective-permute-done.8.refs_3_ = bf16[4,3,128,256]{3,2,1,0:T(8,128)(2,1)S(1)} collective-permute-done((bf16[4,3,128,256]{3,2,1,0:T(8,128)(2,1)S(1)}, bf16[4,3,128,256]{3,2,1,0:T(8,128)(2,1)S(1)}, u32[]{:S(2)}, u32[]{:S(2)}) %collective-permute-start.8) | collective-permute-done | bytes 786464 | tf_op jit(solution)/shard_map/ppermute | solution.py:325
  87.1 1.8 %collective-permute-start.10 = (bf16[768,512]{1,0:T(8,128)(2,1)}, bf16[768,512]{1,0:T(8,128)(2,1)}, u32[]{:S(2)}, u32[]{:S(2)}) collective-permute-start(bf16[768,512]{1,0:T(8,128)(2,1)} %collective-permute-done.6.refs_2_), channel_id=1, source_target_pairs={{0,7},{1,0},{2,1},{3,2},{4,3},{5,4},{6,5},{7,6},{8,15},{9,8},{10,9... | collective-permute-start | bytes 2359304 | tf_op jit(solution)/shard_map/ppermute | solution.py:334
  91.3 7.9 %collective-permute-done.12 = bf16[2,3,128,256]{3,2,1,0:T(8,128)(2,1)S(1)} collective-permute-done((bf16[2,3,128,256]{3,2,1,0:T(8,128)(2,1)S(1)}, bf16[2,3,128,256]{3,2,1,0:T(8,128)(2,1)S(1)}, u32[]{:S(2)}, u32[]{:S(2)}) %collective-permute-start.12) | collective-permute-done | bytes 393248 | tf_op jit(solution)/shard_map/ppermute | solution.py:338
  99.2 2.7 %collective-permute-done.11 = bf16[2,3,128,256]{3,2,1,0:T(8,128)(2,1)S(1)} collective-permute-done((bf16[2,3,128,256]{3,2,1,0:T(8,128)(2,1)S(1)}, bf16[2,3,128,256]{3,2,1,0:T(8,128)(2,1)S(1)}, u32[]{:S(2)}, u32[]{:S(2)}) %collective-permute-start.11) | collective-permute-done | bytes 393248 | tf_op jit(solution)/shard_map/ppermute | solution.py:337
  102.0 8.0 %collective-permute-done.9.refs_1_ = bf16[768,512]{1,0:T(8,128)(2,1)S(1)} collective-permute-done((bf16[768,512]{1,0:T(8,128)(2,1)}, bf16[768,512]{1,0:T(8,128)(2,1)S(1)}, u32[]{:S(2)}, u32[]{:S(2)}) %collective-permute-start.9) | collective-permute-done | bytes 786464 | tf_op jit(solution)/shard_map/ppermute | solution.py:333
  110.0 2.7 %collective-permute-done.10.refs_0_ = bf16[768,512]{1,0:T(8,128)(2,1)} collective-permute-done((bf16[768,512]{1,0:T(8,128)(2,1)}, bf16[768,512]{1,0:T(8,128)(2,1)}, u32[]{:S(2)}, u32[]{:S(2)}) %collective-permute-start.10) | collective-permute-done | bytes 786464 | tf_op jit(solution)/shard_map/ppermute | solution.py:334
  114.7 3.0 %collective-permute-start.14 = (bf16[384,512]{1,0:T(8,128)(2,1)S(1)}, bf16[384,512]{1,0:T(8,128)(2,1)S(1)}, u32[]{:S(2)}, u32[]{:S(2)}) collective-permute-start(bf16[384,512]{1,0:T(8,128)(2,1)S(1)} %slice.15), channel_id=1, source_target_pairs={{0,7},{1,0},{2,1},{3,2},{4,3},{5,4},{6,5},{7,6},{8,15},{9,8},{10,9... | collective-permute-start | bytes 1179656 | tf_op jit(solution)/shard_map/ppermute | solution.py:350
  118.7 5.5 %shard_map.160 = (f32[3,768,256]{2,1,0:T(8,128)S(1)}, f32[768,128]{1,0:T(8,128)S(1)}) custom-call(bf16[768,512]{1,0:T(8,128)(2,1)S(1)} %bitcast.67, bf16[768,512]{1,0:T(8,128)(2,1)} %collective-permute-done.1.refs_1_, bf16[768,512]{1,0:T(8,128)(2,1)} %collective-permute-done.6.refs_2_, bf16[768,512]{1,0:T(8,128)(2,1)} %collective-permute-done.5.refs_3_, ...), custom_call_target="tpu_custom_call" | custom-call | flops 3019898880 | bytes 12582912 | tf_op jit(solution)/shard_map/pallas_call | solution.py:179
  124.2 11.5 %collective-permute-done.13.refs_2_ = bf16[384,512]{1,0:T(8,128)(2,1)S(1)} collective-permute-done((bf16[384,512]{1,0:T(8,128)(2,1)S(1)}, bf16[384,512]{1,0:T(8,128)(2,1)S(1)}, u32[]{:S(2)}, u32[]{:S(2)}) %collective-permute-start.13) | collective-permute-done | bytes 393248 | tf_op jit(solution)/shard_map/ppermute | solution.py:349
  135.7 4.8 %shard_map.161 = bf16[32,3,24,256]{3,2,1,0:T(8,128)(2,1)} custom-call(bf16[768,512]{1,0:T(8,128)(2,1)} %collective-permute-done.10.refs_0_, bf16[768,512]{1,0:T(8,128)(2,1)S(1)} %collective-permute-done.9.refs_1_, bf16[384,512]{1,0:T(8,128)(2,1)S(1)} %collective-permute-done.13.refs_2_, bf16[384,512]{1,0:T(8,128)(2,1)S(1)} %collective-permute-done.14.refs_3_, ...), custom_call_target="tpu_custom_call" | custom-call | flops 36238786560 | bytes 12582912 | tf_op jit(solution)/shard_map/pallas_call | solution.py:208
  140.5 2.3 %reduce-scatter.2.cloned.1.call-done.sum_ref = bf16[32,5120]{1,0:T(8,128)(2,1)} async-done(((bf16[256,5120]{1,0:T(8,128)(2,1)}), bf16[32,5120]{1,0:T(8,128)(2,1)}) %reduce-scatter.2.cloned.1.call-update) | async-done | bytes 327696 | tf_op jit(solution)/shard_map/reduce_scatter | solution.py:331
  142.8 2.1 %shard_map.162 = (bf16[32,5120]{1,0:T(8,128)(2,1)}, f32[8,32]{1,0:T(8,128)}) custom-call(s32[1,3]{1,0:T(1,128)} %pair_ref.1, bf16[32,5120]{1,0:T(8,128)(2,1)} %bitcast.71, bf16[1,5120]{1,0:T(2,128)(2,1)} %reshape.50.gain_ref, bf16[1,5120]{1,0:T(2,128)(2,1)} %reshape.51.score_ref, bf16[32,5120]{1,0:T(8,128)(2,1)} %reduce-scatter.2.cloned.1.call-done.sum_ref), custom_call_target="tpu_custom_call" | custom-call | flops 1310720 | bytes 2097152 | tf_op jit(solution)/shard_map/pallas_call | solution.py:250
  144.9 1.8 %collective-permute-start.19 = (f32[8,32]{1,0:T(8,128)}, f32[8,32]{1,0:T(8,128)S(1)}, u32[]{:S(2)}, u32[]{:S(2)}) collective-permute-start(f32[8,32]{1,0:T(8,128)} %get-tuple-element.53), channel_id=1, source_target_pairs={{0,1},{1,0},{2,3},{3,2},{4,5},{5,4},{6,7},{7,6},{8,9},{9,8},{10,11... | collective-permute-start | bytes 3080 | tf_op jit(solution)/shard_map/ppermute | solution.py:368
  146.7 2.0 %collective-permute-done.19 = f32[8,32]{1,0:T(8,128)S(1)} collective-permute-done((f32[8,32]{1,0:T(8,128)}, f32[8,32]{1,0:T(8,128)S(1)}, u32[]{:S(2)}, u32[]{:S(2)}) %collective-permute-start.19) | collective-permute-done | bytes 1056 | tf_op jit(solution)/shard_map/ppermute | solution.py:368
  149.4 2.9 %collective-permute-start.20 = (f32[8,32]{1,0:T(8,128)S(1)}, f32[8,32]{1,0:T(8,128)S(1)}, u32[]{:S(2)}, u32[]{:S(2)}) collective-permute-start(f32[8,32]{1,0:T(8,128)S(1)} %add.23), channel_id=1, source_target_pairs={{0,2},{1,3},{2,0},{3,1},{4,6},{5,7},{6,4},{7,5},{8,10},{9,11},{10,... | collective-permute-start | bytes 3080 | tf_op jit(solution)/shard_map/ppermute | solution.py:368
  152.2 1.7 collective-permute-done.20
  153.9 5.0 %collective-permute-start.21 = (f32[8,32]{1,0:T(8,128)S(1)}, f32[8,32]{1,0:T(8,128)S(1)}, u32[]{:S(2)}, u32[]{:S(2)}) collective-permute-start(f32[8,32]{1,0:T(8,128)S(1)} %add.24), channel_id=1, source_target_pairs={{0,4},{1,5},{2,6},{3,7},{4,0},{5,1},{6,2},{7,3},{8,12},{9,13},{10,... | collective-permute-start | bytes 3080 | tf_op jit(solution)/shard_map/ppermute | solution.py:368
  158.8 2.6 %collective-permute-done.21 = f32[8,32]{1,0:T(8,128)S(1)} collective-permute-done((f32[8,32]{1,0:T(8,128)S(1)}, f32[8,32]{1,0:T(8,128)S(1)}, u32[]{:S(2)}, u32[]{:S(2)}) %collective-permute-start.21) | collective-permute-done | bytes 1056 | tf_op jit(solution)/shard_map/ppermute | solution.py:368
  (63 shorter events, 16.4 us)
Async XLA Ops:
  7.2 14.6 %copy-start = (bf16[8,32,640]{2,1,0:T(8,128)(2,1)S(1)}, bf16[8,32,640]{2,1,0:T(8,128)(2,1)}, u32[]{:S(2)}) copy-start(bf16[8,32,640]{2,1,0:T(8,128)(2,1)} %param.16) | copy-start | bytes 983044
  7.2 12.6 %copy-start.5 = (bf16[8,32,640]{2,1,0:T(8,128)(2,1)S(1)}, bf16[8,32,640]{2,1,0:T(8,128)(2,1)}, u32[]{:S(2)}) copy-start(bf16[8,32,640]{2,1,0:T(8,128)(2,1)} %param.14) | copy-start | bytes 983044
  7.2 12.6 %copy-start.4 = (bf16[8,32,640]{2,1,0:T(8,128)(2,1)S(1)}, bf16[8,32,640]{2,1,0:T(8,128)(2,1)}, u32[]{:S(2)}) copy-start(bf16[8,32,640]{2,1,0:T(8,128)(2,1)} %param.15) | copy-start | bytes 983044
  7.2 63.4 %all-gather.2.cloned.1.call-start = ((), (), s32[]{:S(2)}) async-start(), calls=%async_computation.2 | async-start | bytes 6758400 | tf_op jit(solution)/shard_map/all_gather | solution.py:289
  12.0 8.5 %copy-start.7 = (bf16[5120]{0:T(1024)(128)(2,1)S(1)}, bf16[5120]{0:T(1024)(128)(2,1)}, u32[]{:S(2)}) copy-start(bf16[5120]{0:T(1024)(128)(2,1)} %param.19) | copy-start | bytes 30724
  12.0 9.1 %copy-start.8 = (bf16[5120]{0:T(1024)(128)(2,1)S(1)}, bf16[5120]{0:T(1024)(128)(2,1)}, u32[]{:S(2)}) copy-start(bf16[5120]{0:T(1024)(128)(2,1)} %param.20) | copy-start | bytes 30724
  12.0 22.2 %all-to-all-start = ((bf16[32,24,512]{2,1,0:T(8,128)(2,1)}), bf16[32,24,512]{2,1,0:T(8,128)(2,1)S(1)}, u32[]{:S(2)}, u32[]{:S(2)}) async-start(bf16[32,24,512]{2,1,0:T(8,128)(2,1)} %bitcast.68), calls=%async_computation | async-start | bytes 1572864 | tf_op jit(solution)/shard_map/all_to_all | solution.py:295
  19.7 123.0 %reduce-scatter.2.cloned.1.call-start = ((), (), s32[]{:S(2)}) async-start(), calls=%async_computation.3 | async-start | bytes 2949120 | tf_op jit(solution)/shard_map/reduce_scatter | solution.py:331
  34.2 27.6 %copy-start.2 = (bf16[32,24,512]{2,1,0:T(8,128)(2,1)}, bf16[32,24,512]{2,1,0:T(8,128)(2,1)S(1)}, u32[]{:S(2)}) copy-start(bf16[32,24,512]{2,1,0:T(8,128)(2,1)S(1)} %all-to-all-done) | copy-start | bytes 2359300
  34.2 24.0 %collective-permute-start.1 = (bf16[768,512]{1,0:T(8,128)(2,1)S(1)}, bf16[768,512]{1,0:T(8,128)(2,1)}, u32[]{:S(2)}, u32[]{:S(2)}) collective-permute-start(bf16[768,512]{1,0:T(8,128)(2,1)S(1)} %bitcast.65), channel_id=1, source_target_pairs={{0,7},{1,0},{2,1},{3,2},{4,3},{5,4},{6,5},{7,6},{8,15},{9,8},{10,9... | collective-permute-start | bytes 2359304 | tf_op jit(solution)/shard_map/ppermute | solution.py:314
  40.9 20.8 %collective-permute-start = (bf16[768,512]{1,0:T(8,128)(2,1)S(1)}, bf16[768,512]{1,0:T(8,128)(2,1)}, u32[]{:S(2)}, u32[]{:S(2)}) collective-permute-start(bf16[768,512]{1,0:T(8,128)(2,1)S(1)} %bitcast.66), channel_id=1, source_target_pairs={{0,1},{1,2},{2,3},{3,4},{4,5},{5,6},{6,7},{7,0},{8,9},{9,10},{10,1... | collective-permute-start | bytes 2359304 | tf_op jit(solution)/shard_map/ppermute | solution.py:313
  40.9 6.9 %collective-permute-start.2 = (bf16[1,3,128,256]{3,2,1,0:T(8,128)(2,1)S(1)}, bf16[1,3,128,256]{3,2,1,0:T(8,128)(2,1)S(1)}, u32[]{:S(2)}, u32[]{:S(2)}) collective-permute-start(bf16[1,3,128,256]{3,2,1,0:T(8,128)(2,1)S(1)} %fusion.11), channel_id=1, source_target_pairs={{0,16},{16,32},{32,48},{48,0},{1,17},{17,33},{33,49},{49,1},{2,18}... | collective-permute-start | bytes 589832 | tf_op jit(solution)/shard_map/ppermute | solution.py:315
  41.1 7.0 %collective-permute-start.4 = (bf16[1,3,128,256]{3,2,1,0:T(8,128)(2,1)S(1)}, bf16[1,3,128,256]{3,2,1,0:T(8,128)(2,1)S(1)}, u32[]{:S(2)}, u32[]{:S(2)}) collective-permute-start(bf16[1,3,128,256]{3,2,1,0:T(8,128)(2,1)S(1)} %fusion.11), channel_id=1, source_target_pairs={{0,48},{16,0},{32,16},{48,32},{1,49},{17,1},{33,17},{49,33},{2,50}... | collective-permute-start | bytes 589832 | tf_op jit(solution)/shard_map/ppermute | solution.py:316
  47.7 7.3 %collective-permute-start.3 = (bf16[1,3,128,256]{3,2,1,0:T(8,128)(2,1)S(1)}, bf16[1,3,128,256]{3,2,1,0:T(8,128)(2,1)S(1)}, u32[]{:S(2)}, u32[]{:S(2)}) collective-permute-start(bf16[1,3,128,256]{3,2,1,0:T(8,128)(2,1)S(1)} %collective-permute-done.2), channel_id=1, source_target_pairs={{0,16},{16,32},{32,48},{48,0},{1,17},{17,33},{33,49},{49,1},{2,18}... | collective-permute-start | bytes 589832 | tf_op jit(solution)/shard_map/ppermute | solution.py:317
  61.7 20.2 %collective-permute-start.5 = (bf16[768,512]{1,0:T(8,128)(2,1)}, bf16[768,512]{1,0:T(8,128)(2,1)}, u32[]{:S(2)}, u32[]{:S(2)}) collective-permute-start(bf16[768,512]{1,0:T(8,128)(2,1)} %collective-permute-done.refs_4_), channel_id=1, source_target_pairs={{0,1},{1,2},{2,3},{3,4},{4,5},{5,6},{6,7},{7,0},{8,9},{9,10},{10,1... | collective-permute-start | bytes 2359304 | tf_op jit(solution)/shard_map/ppermute | solution.py:322
  61.7 20.2 %collective-permute-start.6 = (bf16[768,512]{1,0:T(8,128)(2,1)}, bf16[768,512]{1,0:T(8,128)(2,1)}, u32[]{:S(2)}, u32[]{:S(2)}) collective-permute-start(bf16[768,512]{1,0:T(8,128)(2,1)} %collective-permute-done.1.refs_1_), channel_id=1, source_target_pairs={{0,7},{1,0},{2,1},{3,2},{4,3},{5,4},{6,5},{7,6},{8,15},{9,8},{10,9... | collective-permute-start | bytes 2359304 | tf_op jit(solution)/shard_map/ppermute | solution.py:323
  64.9 19.4 %collective-permute-start.8 = (bf16[4,3,128,256]{3,2,1,0:T(8,128)(2,1)S(1)}, bf16[4,3,128,256]{3,2,1,0:T(8,128)(2,1)S(1)}, u32[]{:S(2)}, u32[]{:S(2)}) collective-permute-start(bf16[4,3,128,256]{3,2,1,0:T(8,128)(2,1)S(1)} %pad_maximum_fusion.refs_0_), channel_id=1, source_target_pairs={{0,192},{64,0},{128,64},{192,128},{1,193},{65,1},{129,65},{193,129... | collective-permute-start | bytes 2359304 | tf_op jit(solution)/shard_map/ppermute | solution.py:325
  66.1 19.5 %collective-permute-start.7 = (bf16[4,3,128,256]{3,2,1,0:T(8,128)(2,1)S(1)}, bf16[4,3,128,256]{3,2,1,0:T(8,128)(2,1)S(1)}, u32[]{:S(2)}, u32[]{:S(2)}) collective-permute-start(bf16[4,3,128,256]{3,2,1,0:T(8,128)(2,1)S(1)} %pad_maximum_fusion.refs_0_), channel_id=1, source_target_pairs={{0,64},{64,128},{128,192},{192,0},{1,65},{65,129},{129,193},{193,1... | collective-permute-start | bytes 2359304 | tf_op jit(solution)/shard_map/ppermute | solution.py:324
  85.5 24.4 %collective-permute-start.9 = (bf16[768,512]{1,0:T(8,128)(2,1)}, bf16[768,512]{1,0:T(8,128)(2,1)S(1)}, u32[]{:S(2)}, u32[]{:S(2)}) collective-permute-start(bf16[768,512]{1,0:T(8,128)(2,1)} %collective-permute-done.5.refs_3_), channel_id=1, source_target_pairs={{0,1},{1,2},{2,3},{3,4},{4,5},{5,6},{6,7},{7,0},{8,9},{9,10},{10,1... | collective-permute-start | bytes 2359304 | tf_op jit(solution)/shard_map/ppermute | solution.py:333
  87.1 25.6 %collective-permute-start.10 = (bf16[768,512]{1,0:T(8,128)(2,1)}, bf16[768,512]{1,0:T(8,128)(2,1)}, u32[]{:S(2)}, u32[]{:S(2)}) collective-permute-start(bf16[768,512]{1,0:T(8,128)(2,1)} %collective-permute-done.6.refs_2_), channel_id=1, source_target_pairs={{0,7},{1,0},{2,1},{3,2},{4,3},{5,4},{6,5},{7,6},{8,15},{9,8},{10,9... | collective-permute-start | bytes 2359304 | tf_op jit(solution)/shard_map/ppermute | solution.py:334
  88.9 10.3 %collective-permute-start.12 = (bf16[2,3,128,256]{3,2,1,0:T(8,128)(2,1)S(1)}, bf16[2,3,128,256]{3,2,1,0:T(8,128)(2,1)S(1)}, u32[]{:S(2)}, u32[]{:S(2)}) collective-permute-start(bf16[2,3,128,256]{3,2,1,0:T(8,128)(2,1)S(1)} %slice.13), channel_id=1, source_target_pairs={{0,192},{64,0},{128,64},{192,128},{1,193},{65,1},{129,65},{193,129... | collective-permute-start | bytes 1179656 | tf_op jit(solution)/shard_map/ppermute | solution.py:338
  90.5 11.4 %collective-permute-start.11 = (bf16[2,3,128,256]{3,2,1,0:T(8,128)(2,1)S(1)}, bf16[2,3,128,256]{3,2,1,0:T(8,128)(2,1)S(1)}, u32[]{:S(2)}, u32[]{:S(2)}) collective-permute-start(bf16[2,3,128,256]{3,2,1,0:T(8,128)(2,1)S(1)} %slice.12), channel_id=1, source_target_pairs={{0,64},{64,128},{128,192},{192,0},{1,65},{65,129},{129,193},{193,1... | collective-permute-start | bytes 1179656 | tf_op jit(solution)/shard_map/ppermute | solution.py:337
  91.3 23.4 %collective-permute-start.15 = (bf16[4,3,128,256]{3,2,1,0:T(8,128)(2,1)S(1)}, bf16[4,3,128,256]{3,2,1,0:T(8,128)(2,1)S(1)}, u32[]{:S(2)}, u32[]{:S(2)}) collective-permute-start(bf16[4,3,128,256]{3,2,1,0:T(8,128)(2,1)S(1)} %pad_maximum_fusion.refs_0_), channel_id=1, source_target_pairs={{0,8},{8,0},{1,9},{9,1},{2,10},{10,2},{3,11},{11,3},{4,12},{12,4},... | collective-permute-start | bytes 2359304 | tf_op jit(solution)/shard_map/ppermute | solution.py:345
  99.2 18.5 %collective-permute-start.16 = (bf16[4,3,128,256]{3,2,1,0:T(8,128)(2,1)S(1)}, bf16[4,3,128,256]{3,2,1,0:T(8,128)(2,1)S(1)}, u32[]{:S(2)}, u32[]{:S(2)}) collective-permute-start(bf16[4,3,128,256]{3,2,1,0:T(8,128)(2,1)S(1)} %collective-permute-done.7.refs_1_), channel_id=1, source_target_pairs={{0,8},{8,0},{1,9},{9,1},{2,10},{10,2},{3,11},{11,3},{4,12},{12,4},... | collective-permute-start | bytes 2359304 | tf_op jit(solution)/shard_map/ppermute | solution.py:345
  101.9 15.7 %collective-permute-start.18 = (bf16[4,3,128,256]{3,2,1,0:T(8,128)(2,1)S(1)}, bf16[4,3,128,256]{3,2,1,0:T(8,128)(2,1)S(1)}, u32[]{:S(2)}, u32[]{:S(2)}) collective-permute-start(bf16[4,3,128,256]{3,2,1,0:T(8,128)(2,1)S(1)} %collective-permute-done.8.refs_3_), channel_id=1, source_target_pairs={{0,8},{8,0},{1,9},{9,1},{2,10},{10,2},{3,11},{11,3},{4,12},{12,4},... | collective-permute-start | bytes 2359304 | tf_op jit(solution)/shard_map/ppermute | solution.py:345
  112.7 5.0 %collective-permute-start.17 = (bf16[4,3,128,256]{3,2,1,0:T(8,128)(2,1)S(1)}, bf16[4,3,128,256]{3,2,1,0:T(8,128)(2,1)S(1)}, u32[]{:S(2)}, u32[]{:S(2)}) collective-permute-start(bf16[4,3,128,256]{3,2,1,0:T(8,128)(2,1)S(1)} %pad_maximum_fusion.1.refs_2_), channel_id=1, source_target_pairs={{0,8},{8,0},{1,9},{9,1},{2,10},{10,2},{3,11},{11,3},{4,12},{12,4},... | collective-permute-start | bytes 2359304 | tf_op jit(solution)/shard_map/ppermute | solution.py:345
  113.8 4.9 %copy-start.3 = (bf16[32,24,512]{2,1,0:T(8,128)(2,1)S(1)}, bf16[32,24,512]{2,1,0:T(8,128)(2,1)}, u32[]{:S(2)}) copy-start(bf16[32,24,512]{2,1,0:T(8,128)(2,1)} %copy-done.2) | copy-start | bytes 2359300
  113.8 21.9 %collective-permute-start.13 = (bf16[384,512]{1,0:T(8,128)(2,1)S(1)}, bf16[384,512]{1,0:T(8,128)(2,1)S(1)}, u32[]{:S(2)}, u32[]{:S(2)}) collective-permute-start(bf16[384,512]{1,0:T(8,128)(2,1)S(1)} %slice.14), channel_id=1, source_target_pairs={{0,1},{1,2},{2,3},{3,4},{4,5},{5,6},{6,7},{7,0},{8,9},{9,10},{10,1... | collective-permute-start | bytes 1179656 | tf_op jit(solution)/shard_map/ppermute | solution.py:349
  114.7 21.0 %collective-permute-start.14 = (bf16[384,512]{1,0:T(8,128)(2,1)S(1)}, bf16[384,512]{1,0:T(8,128)(2,1)S(1)}, u32[]{:S(2)}, u32[]{:S(2)}) collective-permute-start(bf16[384,512]{1,0:T(8,128)(2,1)S(1)} %slice.15), channel_id=1, source_target_pairs={{0,7},{1,0},{2,1},{3,2},{4,3},{5,4},{6,5},{7,6},{8,15},{9,8},{10,9... | collective-permute-start | bytes 1179656 | tf_op jit(solution)/shard_map/ppermute | solution.py:350
  144.9 3.8 %collective-permute-start.19 = (f32[8,32]{1,0:T(8,128)}, f32[8,32]{1,0:T(8,128)S(1)}, u32[]{:S(2)}, u32[]{:S(2)}) collective-permute-start(f32[8,32]{1,0:T(8,128)} %get-tuple-element.53), channel_id=1, source_target_pairs={{0,1},{1,0},{2,3},{3,2},{4,5},{5,4},{6,7},{7,6},{8,9},{9,8},{10,11... | collective-permute-start | bytes 3080 | tf_op jit(solution)/shard_map/ppermute | solution.py:368
  149.4 4.5 %collective-permute-start.20 = (f32[8,32]{1,0:T(8,128)S(1)}, f32[8,32]{1,0:T(8,128)S(1)}, u32[]{:S(2)}, u32[]{:S(2)}) collective-permute-start(f32[8,32]{1,0:T(8,128)S(1)} %add.23), channel_id=1, source_target_pairs={{0,2},{1,3},{2,0},{3,1},{4,6},{5,7},{6,4},{7,5},{8,10},{9,11},{10,... | collective-permute-start | bytes 3080 | tf_op jit(solution)/shard_map/ppermute | solution.py:368
  153.9 7.5 %collective-permute-start.21 = (f32[8,32]{1,0:T(8,128)S(1)}, f32[8,32]{1,0:T(8,128)S(1)}, u32[]{:S(2)}, u32[]{:S(2)}) collective-permute-start(f32[8,32]{1,0:T(8,128)S(1)} %add.24), channel_id=1, source_target_pairs={{0,4},{1,5},{2,6},{3,7},{4,0},{5,1},{6,2},{7,3},{8,12},{9,13},{10,... | collective-permute-start | bytes 3080 | tf_op jit(solution)/shard_map/ppermute | solution.py:368
  (2 other events, 5.6 us)
Sparse Core Ops, SparseCore 0:
  10.6 59.9 all-gather.1
  89.0 53.7 reduce-scatter.1

commit v3 on v2

--- a/solution.py
+++ b/solution.py
@@ -99,25 +99,37 @@
     )(where, *slabs)
 
 
-def project_kernel(rows_ref, columns_ref, out_ref):
-    out_ref[...] = lax.dot_general(
+def project_kernel(rows_ref, columns_ref, out_ref, lead_ref):
+    product = lax.dot_general(
         rows_ref[...], columns_ref[...], (((1,), (1,)), ((), ())), preferred_element_type=jnp.float32
-    ).astype(out_ref.dtype)
-
-
-def project(rows, columns):
+    )
+    out_ref[...] = product.astype(out_ref.dtype)
+    pairs = lead_ref.shape[0]
+    length = product.shape[0] // pairs
+    for pair in range(pairs):
+        row = product[pair * length : pair * length + 1].astype(out_ref.dtype)
+        lead_ref[pair : pair + 1] = row.astype(lead_ref.dtype)
+
+
+def project(rows, columns, pairs):
     count, depth = rows.shape
     width = columns.shape[0]
     steps = 4
     return pl.pallas_call(
         project_kernel,
-        out_shape=jax.ShapeDtypeStruct((count, width), jnp.bfloat16),
+        out_shape=(
+            jax.ShapeDtypeStruct((count, width), jnp.bfloat16),
+            jax.ShapeDtypeStruct((pairs, width), jnp.float32),
+        ),
         grid=(steps,),
         in_specs=[
             pl.BlockSpec((count, depth), lambda i: (0, 0)),
             pl.BlockSpec((width // steps, depth), lambda i: (i, 0)),
         ],
-        out_specs=pl.BlockSpec((count, width // steps), lambda i: (0, i)),
+        out_specs=(
+            pl.BlockSpec((count, width // steps), lambda i: (0, i)),
+            pl.BlockSpec((pairs, width // steps), lambda i: (0, i)),
+        ),
         compiler_params=pltpu.CompilerParams(vmem_limit_bytes=16 << 20),
         cost_estimate=pl.CostEstimate(
             flops=2 * count * width * depth, bytes_accessed=9 << 20, transcendentals=0
@@ -229,36 +241,60 @@
     return out.transpose(0, 2, 1, 3)
 
 
-def norm_kernel(pair_ref, resid_ref, gain_ref, score_ref, sum_ref, hidden_ref, votes_ref):
+def norm_kernel(resid_ref, gain_ref, sum_ref, hidden_ref):
     mixed = resid_ref[...].astype(jnp.float32) + sum_ref[...].astype(jnp.float32)
     squares = jnp.sum(mixed * mixed, axis=-1, keepdims=True)
     scale = lax.rsqrt(squares * (1.0 / mixed.shape[1]) + 1e-05)
     normed = mixed * scale * gain_ref[...].astype(jnp.float32)
     hidden_ref[...] = normed.astype(hidden_ref.dtype)
-    logit = jnp.sum(normed[:1] * score_ref[...].astype(jnp.float32), axis=-1, keepdims=True)
-    cand = lax.broadcasted_iota(jnp.int32, votes_ref.shape, 0)
-    prompt = lax.broadcasted_iota(jnp.int32, votes_ref.shape, 1)
-    own = prompt == pair_ref[0, 0]
-    upward = jnp.where(own & (cand == pair_ref[0, 1]), logit, 0.0)
-    downward = jnp.where(own & (cand == pair_ref[0, 2]), logit, 0.0)
-    votes_ref[...] = upward - downward
-
-
-def norm_and_vote(pair_index, resid, gain, score, part_sum, prompts, cands):
+
+
+def norm(resid, gain, part_sum):
     rows, width = resid.shape
     vmem = pl.BlockSpec(memory_space=pltpu.VMEM)
     return pl.pallas_call(
         norm_kernel,
-        out_shape=(
-            jax.ShapeDtypeStruct((rows, width), jnp.bfloat16),
-            jax.ShapeDtypeStruct((cands, prompts), jnp.float32),
-        ),
-        in_specs=[pl.BlockSpec(memory_space=pltpu.SMEM)] + [vmem] * 4,
-        out_specs=(vmem, vmem),
+        out_shape=jax.ShapeDtypeStruct((rows, width), jnp.bfloat16),
+        in_specs=[vmem] * 3,
+        out_specs=vmem,
         cost_estimate=pl.CostEstimate(
             flops=rows * width * 8, bytes_accessed=2 << 20, transcendentals=rows
         ),
-    )(pair_index, resid, gain, score, part_sum)
+    )(resid, gain, part_sum)
+
+
+def vote_kernel(gain_ref, score_ref, lead_ref, votes_ref):
+    pairs, width = lead_ref.shape[0], gain_ref.shape[1]
+    mixed = lead_ref[:, :width].astype(jnp.float32)
+    squares = jnp.sum(mixed * mixed, axis=-1, keepdims=True)
+    scale = lax.rsqrt(squares * (1.0 / width) + 1e-05)
+    normed = mixed * scale * gain_ref[...].astype(jnp.float32)
+    logits = jnp.sum(normed * score_ref[...].astype(jnp.float32), axis=-1, keepdims=True)
+    index = lead_ref[:, width:].astype(jnp.float32)
+    cand = lax.broadcasted_iota(jnp.int32, votes_ref.shape, 0).astype(jnp.float32)
+    prompt = lax.broadcasted_iota(jnp.int32, votes_ref.shape, 1).astype(jnp.float32)
+    votes = jnp.zeros(votes_ref.shape, jnp.float32)
+    for pair in range(pairs):
+        own = prompt == index[pair : pair + 1, 0:1]
+        logit = logits[pair : pair + 1]
+        votes = votes + jnp.where(own & (cand == index[pair : pair + 1, 1:2]), logit, 0.0)
+        votes = votes - jnp.where(own & (cand == index[pair : pair + 1, 2:3]), logit, 0.0)
+    votes_ref[...] = votes
+
+
+def vote(gain, score, lead, prompts, cands):
+    vmem = pl.BlockSpec(memory_space=pltpu.VMEM)
+    return pl.pallas_call(
+        vote_kernel,
+        out_shape=jax.ShapeDtypeStruct((cands, prompts), jnp.float32),
+        in_specs=[vmem] * 3,
+        out_specs=vmem,
+    )(gain, score, lead)
+
+
+def exchange(partial, bit):
+    sent = lax.ppermute(partial.astype(jnp.bfloat16), "z", [(i, i ^ bit) for i in range(NZ)])
+    return partial + sent.astype(jnp.float32)
 
 
 def together(*values):
@@ -323,10 +359,8 @@
     upper = lax.ppermute(upper, "z", ring(NZ, -1))
     y_before = lax.ppermute(strip, "y", ring(NY, 1))
     y_after = lax.ppermute(strip, "y", ring(NY, -1))
-    term_rows = project(context, columns)
-    lower, upper, y_before, y_after, term_rows = together(
-        lower, upper, y_before, y_after, term_rows
-    )
+    term_rows, lead = project(context, columns, NZ)
+    lower, upper, y_before, y_after, lead = together(lower, upper, y_before, y_after, lead)
     blocks.update({2: upper, NZ - 2: lower})
     part_sum = lax.psum_scatter(term_rows, "z", scatter_dimension=0, tiled=True)
 
@@ -339,7 +373,14 @@
         ],
         axis=0,
     )
-    lower, upper, y_across = together(lower, upper, y_across)
+    pair = lax.broadcasted_iota(jnp.int32, (NZ, 1), 0)
+    own_lead = jnp.concatenate(
+        [rank_resid[:, 0].astype(jnp.float32), jnp.pad(pair_index, ((0, 0), (0, 125))).astype(jnp.float32)],
+        axis=1,
+    )
+    lead = jnp.pad(lead, ((0, 0), (0, 128))) + jnp.where(pair == my_z, own_lead, 0.0)
+    lead = exchange(lead, 1)
+    lower, upper, y_across, lead = together(lower, upper, y_across, lead)
 
     slabs = [strip, y_before, y_across, y_after]
     weights = arrange(where, slabs + [lax.ppermute(s, "core", ring(NC, 1)) for s in slabs])
@@ -348,25 +389,19 @@
     total, squares = encode_first(near, [blocks[i] for i in near], weights)
     low = lax.ppermute(lower[:half], "z", ring(NZ, 1))
     high = lax.ppermute(upper[half:], "z", ring(NZ, -1))
+    lead = exchange(lead, 2)
+    low, high, lead, part_sum = together(low, high, lead, part_sum)
     blended_qkv = encode_last(
         (3, NZ - 3, 4), upper, lower, low, high, weights, total, squares, prompts
     )
 
-    part_sum, blended_qkv = together(part_sum, blended_qkv)
+    lead = exchange(lead, 4)
+    votes = vote(gain_row, score_row, lead, prompts, cand_rank.shape[1])
+
+    cand_score = votes.T
     own_pairs = rank_resid.shape[0]
-    rank_hidden, votes = norm_and_vote(
-        pair_index,
-        rank_resid.reshape(own_pairs * length, -1),
-        gain_row,
-        score_row,
-        part_sum,
-        prompts,
-        cand_rank.shape[1],
-    )
+    rank_hidden = norm(rank_resid.reshape(own_pairs * length, -1), gain_row, part_sum)
     rank_hidden = rank_hidden.reshape(rank_resid.shape)
-    for bit in (1, 2, 4):
-        votes = votes + lax.ppermute(votes, "z", [(i, i ^ bit) for i in range(NZ)])
-    cand_score = votes.T
     return (rank_hidden, cand_score, blended_qkv)
 
 

time: 169 us -> 175 us (1.036)
  local copies, waits for them, and re-layouts: 5.45 us -> 13.6 us
  waiting for transfers between devices: 83.1 us -> 78.8 us
    ppermute x1, waiting for transfers between devices: 11.5 us -> 0.01 us  [body(): low = lax.ppermute(lower[:half], 'z', ring(NZ, 1))]
    unnamed x19 -> x43, local copies, waits for them, and re-layouts: 2.95 us -> 12.1 us
    ppermute x2, waiting for transfers between devices: 12.5 us -> 21.1 us  [body(): lower = lax.ppermute(lower, 'z', ring(NZ, 1))]
    ppermute x3, waiting for transfers between devices: 6.23 us -> 3.2 us  [exchange(): lax.ppermute(partial.astype(jnp.bfloat16), 'z', [(i, i ^ bit) for i in ra...]
    ppermute x1, waiting for transfers between devices: 7.87 us -> 4.97 us  [body(): lax.ppermute(y_after[2:], 'y', ring(NY, -1))]
    ppermute x1, starting transfers between devices: 2.98 us -> 0.08 us  [body(): high = lax.ppermute(upper[half:], 'z', ring(NZ, -1))]
    ppermute x1, waiting for transfers between devices: 0.01 us -> 2.62 us  [body(): high = lax.ppermute(upper[half:], 'z', ring(NZ, -1))]
    all_gather x1, waiting for transfers between devices: 3.63 us -> 6.1 us  [body(): columns = lax.all_gather(out_weight.T, PLANE, axis=0, tiled=True)]
  transfers between devices with their start and end apart: 25 -> 25, of which waited for: 18 -> 17; matrix products, arithmetic and copies ran while one was open for 3% -> 3% of each run, Pallas kernels for 11% -> 12%
where the time goes in v3:
time: 175 us; the launch traced here: 173 us
  waiting for transfers between devices  78.8 us (45%)
  starting transfers between devices  40.3 us (23%)
  Pallas kernels  22.1 us (13%)
  between operations  14.4 us (8%)
  local copies, waits for them, and re-layouts  13.6 us (8%)
  other arithmetic  2.98 us (2%)
    ppermute x2, waiting for transfers between devices, body(): lower = lax.ppermute(lower, 'z', ring(NZ, 1))  21.1 us
    unnamed x43, local copies, waits for them, and re-layouts  12.1 us
    all_to_all x1, waiting for transfers between devices, body(): lax.all_to_all(outgoing.reshape(prompts, -1, features), PLANE, split_axis...  10.9 us
    ppermute x3, starting transfers between devices, exchange(): lax.ppermute(partial.astype(jnp.bfloat16), 'z', [(i, i ^ bit) for i in ra...  9.35 us
    all_to_all x1, starting transfers between devices, body(): lax.all_to_all(outgoing.reshape(prompts, -1, features), PLANE, split_axis...  7.75 us
    ppermute x1, waiting for transfers between devices, body(): x_across = lax.ppermute(x_before, 'x', ring(NX, 1))  7 us
    ppermute x2, starting transfers between devices, body(): upper = lax.ppermute(upper, 'z', ring(NZ, -1))  6.93 us
    ppermute x1, starting transfers between devices, body(): upper = lax.ppermute(own, 'z', ring(NZ, -1))  6.7 us
  transfers between devices with their start and end apart: 25, of which 17 were waited for; matrix products, arithmetic and copies ran while one was open for 3% of the time, Pallas kernels for 12%

profile of v3, /device:TPU:2, one launch (start us, length us, event | category | flops | bytes accessed | tf_op | source)
XLA Modules:
  0.0 173.2 jit_solution(9857449310328119386)
XLA Ops:
  7.9 4.0 %shard_map.157 = bf16[96,8,512]{2,1,0:T(8,128)(2,1)} custom-call(s32[1,32]{1,0:T(1,128)} %owner_ref.1, s32[8,32]{1,0:T(8,128)} %bitcast.76, s32[8,32]{1,0:T(8,128)} %bitcast.77, bf16[256,8,512]{2,1,0:T(8,128)(2,1)} %bitcast.71), custom_call_target="tpu_custom_call" | custom-call | bytes 3145728 | tf_op jit(solution)/shard_map/pallas_call | solution.py:62
  12.0 7.8 %all-to-all-start = ((bf16[32,24,512]{2,1,0:T(8,128)(2,1)}), bf16[32,24,512]{2,1,0:T(8,128)(2,1)S(1)}, u32[]{:S(2)}, u32[]{:S(2)}) async-start(bf16[32,24,512]{2,1,0:T(8,128)(2,1)} %bitcast.70), calls=%async_computation | async-start | bytes 1572864 | tf_op jit(solution)/shard_map/all_to_all | solution.py:331
  23.3 10.9 %all-to-all-done = bf16[32,24,512]{2,1,0:T(8,128)(2,1)S(1)} async-done(((bf16[32,24,512]{2,1,0:T(8,128)(2,1)}), bf16[32,24,512]{2,1,0:T(8,128)(2,1)S(1)}, u32[]{:S(2)}, u32[]{:S(2)}) %all-to-all-start) | async-done | bytes 786464 | tf_op jit(solution)/shard_map/all_to_all | solution.py:331
  34.2 6.7 %collective-permute-start.1 = (bf16[768,512]{1,0:T(8,128)(2,1)S(1)}, bf16[768,512]{1,0:T(8,128)(2,1)}, u32[]{:S(2)}, u32[]{:S(2)}) collective-permute-start(bf16[768,512]{1,0:T(8,128)(2,1)S(1)} %bitcast.67), channel_id=1, source_target_pairs={{0,7},{1,0},{2,1},{3,2},{4,3},{5,4},{6,5},{7,6},{8,15},{9,8},{10,9... | collective-permute-start | bytes 2359304 | tf_op jit(solution)/shard_map/ppermute | solution.py:350
  41.1 1.8 %collective-permute-start.4 = (bf16[1,3,128,256]{3,2,1,0:T(8,128)(2,1)S(1)}, bf16[1,3,128,256]{3,2,1,0:T(8,128)(2,1)S(1)}, u32[]{:S(2)}, u32[]{:S(2)}) collective-permute-start(bf16[1,3,128,256]{3,2,1,0:T(8,128)(2,1)S(1)} %fusion.11), channel_id=1, source_target_pairs={{0,48},{16,0},{32,16},{48,32},{1,49},{17,1},{33,17},{49,33},{2,50}... | collective-permute-start | bytes 589832 | tf_op jit(solution)/shard_map/ppermute | solution.py:352
  42.9 4.9 %collective-permute-done.2 = bf16[1,3,128,256]{3,2,1,0:T(8,128)(2,1)S(1)} collective-permute-done((bf16[1,3,128,256]{3,2,1,0:T(8,128)(2,1)S(1)}, bf16[1,3,128,256]{3,2,1,0:T(8,128)(2,1)S(1)}, u32[]{:S(2)}, u32[]{:S(2)}) %collective-permute-start.2) | collective-permute-done | bytes 196640 | tf_op jit(solution)/shard_map/ppermute | solution.py:351
  48.0 7.0 %collective-permute-done.3 = bf16[1,3,128,256]{3,2,1,0:T(8,128)(2,1)S(1)} collective-permute-done((bf16[1,3,128,256]{3,2,1,0:T(8,128)(2,1)S(1)}, bf16[1,3,128,256]{3,2,1,0:T(8,128)(2,1)S(1)}, u32[]{:S(2)}, u32[]{:S(2)}) %collective-permute-start.3) | collective-permute-done | bytes 196640 | tf_op jit(solution)/shard_map/ppermute | solution.py:353
  55.1 3.0 %collective-permute-done.1.refs_1_ = bf16[768,512]{1,0:T(8,128)(2,1)} collective-permute-done((bf16[768,512]{1,0:T(8,128)(2,1)S(1)}, bf16[768,512]{1,0:T(8,128)(2,1)}, u32[]{:S(2)}, u32[]{:S(2)}) %collective-permute-start.1) | collective-permute-done | bytes 786464 | tf_op jit(solution)/shard_map/ppermute | solution.py:350
  58.2 3.5 %collective-permute-done.refs_4_ = bf16[768,512]{1,0:T(8,128)(2,1)} collective-permute-done((bf16[768,512]{1,0:T(8,128)(2,1)S(1)}, bf16[768,512]{1,0:T(8,128)(2,1)}, u32[]{:S(2)}, u32[]{:S(2)}) %collective-permute-start) | collective-permute-done | bytes 786464 | tf_op jit(solution)/shard_map/ppermute | solution.py:349
  63.7 3.2 %collective-permute-start.6 = (bf16[768,512]{1,0:T(8,128)(2,1)}, bf16[768,512]{1,0:T(8,128)(2,1)}, u32[]{:S(2)}, u32[]{:S(2)}) collective-permute-start(bf16[768,512]{1,0:T(8,128)(2,1)} %collective-permute-done.1.refs_1_), channel_id=1, source_target_pairs={{0,7},{1,0},{2,1},{3,2},{4,3},{5,4},{6,5},{7,6},{8,15},{9,8},{10,9... | collective-permute-start | bytes 2359304 | tf_op jit(solution)/shard_map/ppermute | solution.py:359
  67.0 6.1 %all-gather.2.cloned.1.call-done.columns_ref = bf16[5120,640]{1,0:T(8,128)(2,1)} async-done(((bf16[160,640]{1,0:T(8,128)(2,1)}), bf16[5120,640]{1,0:T(8,128)(2,1)}) %all-gather.2.cloned.1.call-update) | async-done | bytes 6553616 | tf_op jit(solution)/shard_map/all_gather | solution.py:325
  73.1 2.9 %copy-done.1 = bf16[5120,640]{1,0:T(8,128)(2,1)S(1)} copy-done((bf16[5120,640]{1,0:T(8,128)(2,1)S(1)}, bf16[5120,640]{1,0:T(8,128)(2,1)}, u32[]{:S(2)}) %copy-start.1) | copy-done | bytes 6553624
  75.9 3.0 %shard_map.158 = (bf16[256,5120]{1,0:T(8,128)(2,1)S(1)}, f32[8,5120]{1,0:T(8,128)S(1)}) custom-call(bf16[256,640]{1,0:T(8,128)(2,1)S(1)} %bitcast.66, bf16[5120,640]{1,0:T(8,128)(2,1)S(1)} %copy-done.1), custom_call_target="tpu_custom_call" | custom-call | flops 1677721600 | bytes 9437184 | tf_op jit(solution)/shard_map/pallas_call | solution.py:118
  81.6 1.8 %collective-permute-done.5.refs_3_ = bf16[768,512]{1,0:T(8,128)(2,1)} collective-permute-done((bf16[768,512]{1,0:T(8,128)(2,1)}, bf16[768,512]{1,0:T(8,128)(2,1)}, u32[]{:S(2)}, u32[]{:S(2)}) %collective-permute-start.5) | collective-permute-done | bytes 786464 | tf_op jit(solution)/shard_map/ppermute | solution.py:358
  85.6 1.6 collective-permute-start.13
  90.2 3.7 %collective-permute-start.10 = (bf16[768,512]{1,0:T(8,128)(2,1)}, bf16[768,512]{1,0:T(8,128)(2,1)S(1)}, u32[]{:S(2)}, u32[]{:S(2)}) collective-permute-start(bf16[768,512]{1,0:T(8,128)(2,1)} %collective-permute-done.6.refs_2_), channel_id=1, source_target_pairs={{0,7},{1,0},{2,1},{3,2},{4,3},{5,4},{6,5},{7,6},{8,15},{9,8},{10,9... | collective-permute-start | bytes 2359304 | tf_op jit(solution)/shard_map/ppermute | solution.py:368
  94.0 5.0 %collective-permute-done.12 = bf16[2,3,128,256]{3,2,1,0:T(8,128)(2,1)S(1)} collective-permute-done((bf16[2,3,128,256]{3,2,1,0:T(8,128)(2,1)S(1)}, bf16[2,3,128,256]{3,2,1,0:T(8,128)(2,1)S(1)}, u32[]{:S(2)}, u32[]{:S(2)}) %collective-permute-start.12) | collective-permute-done | bytes 393248 | tf_op jit(solution)/shard_map/ppermute | solution.py:372
  98.9 2.5 %collective-permute-done.11 = bf16[2,3,128,256]{3,2,1,0:T(8,128)(2,1)S(1)} collective-permute-done((bf16[2,3,128,256]{3,2,1,0:T(8,128)(2,1)S(1)}, bf16[2,3,128,256]{3,2,1,0:T(8,128)(2,1)S(1)}, u32[]{:S(2)}, u32[]{:S(2)}) %collective-permute-start.11) | collective-permute-done | bytes 393248 | tf_op jit(solution)/shard_map/ppermute | solution.py:371
  101.5 19.3 %collective-permute-done.9.refs_1_ = bf16[768,512]{1,0:T(8,128)(2,1)S(1)} collective-permute-done((bf16[768,512]{1,0:T(8,128)(2,1)}, bf16[768,512]{1,0:T(8,128)(2,1)S(1)}, u32[]{:S(2)}, u32[]{:S(2)}) %collective-permute-start.9) | collective-permute-done | bytes 786464 | tf_op jit(solution)/shard_map/ppermute | solution.py:367
  120.7 4.0 %collective-permute-done.10.refs_0_ = bf16[768,512]{1,0:T(8,128)(2,1)S(1)} collective-permute-done((bf16[768,512]{1,0:T(8,128)(2,1)}, bf16[768,512]{1,0:T(8,128)(2,1)S(1)}, u32[]{:S(2)}, u32[]{:S(2)}) %collective-permute-start.10) | collective-permute-done | bytes 786464 | tf_op jit(solution)/shard_map/ppermute | solution.py:368
  124.8 4.0 %collective-permute-start.16 = (bf16[8,5248]{1,0:T(8,128)(2,1)S(1)}, bf16[8,5248]{1,0:T(8,128)(2,1)S(1)}, u32[]{:S(2)}, u32[]{:S(2)}) collective-permute-start(bf16[8,5248]{1,0:T(8,128)(2,1)S(1)} %convert_element_type.71), channel_id=1, source_target_pairs={{0,2},{1,3},{2,0},{3,1},{4,6},{5,7},{6,4},{7,5},{8,10},{9,11},{10,... | collective-permute-start | bytes 251912 | tf_op jit(solution)/shard_map/ppermute | solution.py:296
  129.5 2.0 %collective-permute-start.14 = (bf16[384,512]{1,0:T(8,128)(2,1)S(1)}, bf16[384,512]{1,0:T(8,128)(2,1)S(1)}, u32[]{:S(2)}, u32[]{:S(2)}) collective-permute-start(bf16[384,512]{1,0:T(8,128)(2,1)S(1)} %slice.18), channel_id=1, source_target_pairs={{0,1},{1,2},{2,3},{3,4},{4,5},{5,6},{6,7},{7,0},{8,9},{9,10},{10,1... | collective-permute-start | bytes 1179656 | tf_op jit(solution)/shard_map/ppermute | solution.py:390
  131.5 2.9 %collective-permute-done.16 = bf16[8,5248]{1,0:T(8,128)(2,1)S(1)} collective-permute-done((bf16[8,5248]{1,0:T(8,128)(2,1)S(1)}, bf16[8,5248]{1,0:T(8,128)(2,1)S(1)}, u32[]{:S(2)}, u32[]{:S(2)}) %collective-permute-start.16) | collective-permute-done | bytes 84000 | tf_op jit(solution)/shard_map/ppermute | solution.py:296
  134.5 2.2 %collective-permute-done.20.refs_6_ = bf16[4,3,128,256]{3,2,1,0:T(8,128)(2,1)S(1)} collective-permute-done((bf16[4,3,128,256]{3,2,1,0:T(8,128)(2,1)S(1)}, bf16[4,3,128,256]{3,2,1,0:T(8,128)(2,1)S(1)}, u32[]{:S(2)}, u32[]{:S(2)}) %collective-permute-start.20) | collective-permute-done | bytes 786464 | tf_op jit(solution)/shard_map/ppermute | solution.py:386
  137.7 6.5 %shard_map.162 = (f32[3,768,256]{2,1,0:T(8,128)S(1)}, f32[768,128]{1,0:T(8,128)S(1)}) custom-call(bf16[768,512]{1,0:T(8,128)(2,1)S(1)} %bitcast.69, bf16[768,512]{1,0:T(8,128)(2,1)} %collective-permute-done.1.refs_1_, bf16[768,512]{1,0:T(8,128)(2,1)} %collective-permute-done.6.refs_2_, bf16[768,512]{1,0:T(8,128)(2,1)} %collective-permute-done.5.refs_3_, ...), custom_call_target="tpu_custom_call" | custom-call | flops 3019898880 | bytes 12582912 | tf_op jit(solution)/shard_map/pallas_call | solution.py:191
  145.6 2.6 %collective-permute-done.15.refs_3_ = bf16[384,512]{1,0:T(8,128)(2,1)S(1)} collective-permute-done((bf16[384,512]{1,0:T(8,128)(2,1)S(1)}, bf16[384,512]{1,0:T(8,128)(2,1)S(1)}, u32[]{:S(2)}, u32[]{:S(2)}) %collective-permute-start.15) | collective-permute-done | bytes 393248 | tf_op jit(solution)/shard_map/ppermute | solution.py:391
  149.1 3.7 %collective-permute-start.17 = (bf16[8,5248]{1,0:T(8,128)(2,1)S(1)}, bf16[8,5248]{1,0:T(8,128)(2,1)S(1)}, u32[]{:S(2)}, u32[]{:S(2)}) collective-permute-start(bf16[8,5248]{1,0:T(8,128)(2,1)S(1)} %convert_element_type.73), channel_id=1, source_target_pairs={{0,4},{1,5},{2,6},{3,7},{4,0},{5,1},{6,2},{7,3},{8,12},{9,13},{10,... | collective-permute-start | bytes 251912 | tf_op jit(solution)/shard_map/ppermute | solution.py:296
  152.8 2.8 %copy-done.3 = bf16[3,4096,256]{2,1,0:T(8,128)(2,1)S(1)} copy-done((bf16[3,4096,256]{2,1,0:T(8,128)(2,1)S(1)}, bf16[3,4096,256]{2,1,0:T(8,128)(2,1)}, u32[]{:S(2)}) %copy-start.3) | copy-done | bytes 6291480
  156.6 1.7 copy-done.14
  158.2 3.6 %shard_map.163 = bf16[32,3,24,256]{3,2,1,0:T(8,128)(2,1)} custom-call(bf16[768,512]{1,0:T(8,128)(2,1)S(1)} %copy-done.10, bf16[768,512]{1,0:T(8,128)(2,1)S(1)} %copy-done.8, bf16[384,512]{1,0:T(8,128)(2,1)S(1)} %copy-done.12, bf16[384,512]{1,0:T(8,128)(2,1)S(1)} %collective-permute-done.15.refs_3_, bf16[3,4096,256]{2,1,0:T(8,128)(2,1)S(1)} %copy-done.3, ...), custom_call_target="tpu_custom_call" | custom-call | flops 36238786560 | bytes 12582912 | tf_op jit(solution)/shard_map/pallas_call | solution.py:220
  161.8 2.0 %shard_map.159 = bf16[32,5120]{1,0:T(8,128)(2,1)} custom-call(bf16[32,5120]{1,0:T(8,128)(2,1)} %bitcast.73, bf16[1,5120]{1,0:T(2,128)(2,1)} %reshape.69.gain_ref, bf16[32,5120]{1,0:T(8,128)(2,1)} %reduce-scatter.2.cloned.1.call-done.sum_ref), custom_call_target="tpu_custom_call" | custom-call | flops 1310720 | bytes 2097152 | tf_op jit(solution)/shard_map/pallas_call | solution.py:255
  164.6 1.8 %shard_map.160 = f32[8,32]{1,0:T(8,128)} custom-call(bf16[1,5120]{1,0:T(2,128)(2,1)} %reshape.69.gain_ref, bf16[1,5120]{1,0:T(2,128)(2,1)} %reshape.70.score_ref, f32[8,5248]{1,0:T(8,128)} %convert_add_fusion.lead_ref), custom_call_target="tpu_custom_call" | custom-call | tf_op jit(solution)/shard_map/pallas_call | solution.py:287
  (95 shorter events, 20.2 us)
Async XLA Ops:
  7.2 14.6 %copy-start = (bf16[8,32,640]{2,1,0:T(8,128)(2,1)S(1)}, bf16[8,32,640]{2,1,0:T(8,128)(2,1)}, u32[]{:S(2)}) copy-start(bf16[8,32,640]{2,1,0:T(8,128)(2,1)} %param.16) | copy-start | bytes 983044
  7.2 12.6 %copy-start.16 = (bf16[8,32,640]{2,1,0:T(8,128)(2,1)S(1)}, bf16[8,32,640]{2,1,0:T(8,128)(2,1)}, u32[]{:S(2)}) copy-start(bf16[8,32,640]{2,1,0:T(8,128)(2,1)} %param.14) | copy-start | bytes 983044
  7.2 12.6 %copy-start.15 = (bf16[8,32,640]{2,1,0:T(8,128)(2,1)S(1)}, bf16[8,32,640]{2,1,0:T(8,128)(2,1)}, u32[]{:S(2)}) copy-start(bf16[8,32,640]{2,1,0:T(8,128)(2,1)} %param.15) | copy-start | bytes 983044
  7.2 65.9 %all-gather.2.cloned.1.call-start = ((), (), s32[]{:S(2)}) async-start(), calls=%async_computation.2 | async-start | bytes 6758400 | tf_op jit(solution)/shard_map/all_gather | solution.py:325
  12.0 22.2 %all-to-all-start = ((bf16[32,24,512]{2,1,0:T(8,128)(2,1)}), bf16[32,24,512]{2,1,0:T(8,128)(2,1)S(1)}, u32[]{:S(2)}, u32[]{:S(2)}) async-start(bf16[32,24,512]{2,1,0:T(8,128)(2,1)} %bitcast.70), calls=%async_computation | async-start | bytes 1572864 | tf_op jit(solution)/shard_map/all_to_all | solution.py:331
  19.7 129.3 %reduce-scatter.2.cloned.1.call-start = ((), (), s32[]{:S(2)}) async-start(), calls=%async_computation.3 | async-start | bytes 2949120 | tf_op jit(solution)/shard_map/reduce_scatter | solution.py:365
  34.2 24.0 %copy-start.5 = (bf16[32,24,512]{2,1,0:T(8,128)(2,1)}, bf16[32,24,512]{2,1,0:T(8,128)(2,1)S(1)}, u32[]{:S(2)}) copy-start(bf16[32,24,512]{2,1,0:T(8,128)(2,1)S(1)} %all-to-all-done) | copy-start | bytes 2359300
  34.2 24.0 %collective-permute-start.1 = (bf16[768,512]{1,0:T(8,128)(2,1)S(1)}, bf16[768,512]{1,0:T(8,128)(2,1)}, u32[]{:S(2)}, u32[]{:S(2)}) collective-permute-start(bf16[768,512]{1,0:T(8,128)(2,1)S(1)} %bitcast.67), channel_id=1, source_target_pairs={{0,7},{1,0},{2,1},{3,2},{4,3},{5,4},{6,5},{7,6},{8,15},{9,8},{10,9... | collective-permute-start | bytes 2359304 | tf_op jit(solution)/shard_map/ppermute | solution.py:350
  40.9 20.8 %collective-permute-start = (bf16[768,512]{1,0:T(8,128)(2,1)S(1)}, bf16[768,512]{1,0:T(8,128)(2,1)}, u32[]{:S(2)}, u32[]{:S(2)}) collective-permute-start(bf16[768,512]{1,0:T(8,128)(2,1)S(1)} %bitcast.68), channel_id=1, source_target_pairs={{0,1},{1,2},{2,3},{3,4},{4,5},{5,6},{6,7},{7,0},{8,9},{9,10},{10,1... | collective-permute-start | bytes 2359304 | tf_op jit(solution)/shard_map/ppermute | solution.py:349
  40.9 6.9 %collective-permute-start.2 = (bf16[1,3,128,256]{3,2,1,0:T(8,128)(2,1)S(1)}, bf16[1,3,128,256]{3,2,1,0:T(8,128)(2,1)S(1)}, u32[]{:S(2)}, u32[]{:S(2)}) collective-permute-start(bf16[1,3,128,256]{3,2,1,0:T(8,128)(2,1)S(1)} %fusion.11), channel_id=1, source_target_pairs={{0,16},{16,32},{32,48},{48,0},{1,17},{17,33},{33,49},{49,1},{2,18}... | collective-permute-start | bytes 589832 | tf_op jit(solution)/shard_map/ppermute | solution.py:351
  41.1 7.0 %collective-permute-start.4 = (bf16[1,3,128,256]{3,2,1,0:T(8,128)(2,1)S(1)}, bf16[1,3,128,256]{3,2,1,0:T(8,128)(2,1)S(1)}, u32[]{:S(2)}, u32[]{:S(2)}) collective-permute-start(bf16[1,3,128,256]{3,2,1,0:T(8,128)(2,1)S(1)} %fusion.11), channel_id=1, source_target_pairs={{0,48},{16,0},{32,16},{48,32},{1,49},{17,1},{33,17},{49,33},{2,50}... | collective-permute-start | bytes 589832 | tf_op jit(solution)/shard_map/ppermute | solution.py:352
  47.8 7.3 %collective-permute-start.3 = (bf16[1,3,128,256]{3,2,1,0:T(8,128)(2,1)S(1)}, bf16[1,3,128,256]{3,2,1,0:T(8,128)(2,1)S(1)}, u32[]{:S(2)}, u32[]{:S(2)}) collective-permute-start(bf16[1,3,128,256]{3,2,1,0:T(8,128)(2,1)S(1)} %collective-permute-done.2), channel_id=1, source_target_pairs={{0,16},{16,32},{32,48},{48,0},{1,17},{17,33},{33,49},{49,1},{2,18}... | collective-permute-start | bytes 589832 | tf_op jit(solution)/shard_map/ppermute | solution.py:353
  61.7 22.6 %collective-permute-start.8 = (bf16[4,3,128,256]{3,2,1,0:T(8,128)(2,1)S(1)}, bf16[4,3,128,256]{3,2,1,0:T(8,128)(2,1)S(1)}, u32[]{:S(2)}, u32[]{:S(2)}) collective-permute-start(bf16[4,3,128,256]{3,2,1,0:T(8,128)(2,1)S(1)} %pad_maximum_fusion.refs_0_), channel_id=1, source_target_pairs={{0,192},{64,0},{128,64},{192,128},{1,193},{65,1},{129,65},{193,129... | collective-permute-start | bytes 2359304 | tf_op jit(solution)/shard_map/ppermute | solution.py:361
  62.8 22.7 %collective-permute-start.7 = (bf16[4,3,128,256]{3,2,1,0:T(8,128)(2,1)S(1)}, bf16[4,3,128,256]{3,2,1,0:T(8,128)(2,1)S(1)}, u32[]{:S(2)}, u32[]{:S(2)}) collective-permute-start(bf16[4,3,128,256]{3,2,1,0:T(8,128)(2,1)S(1)} %pad_maximum_fusion.refs_0_), channel_id=1, source_target_pairs={{0,64},{64,128},{128,192},{192,0},{1,65},{65,129},{129,193},{193,1... | collective-permute-start | bytes 2359304 | tf_op jit(solution)/shard_map/ppermute | solution.py:360
  63.7 19.7 %collective-permute-start.5 = (bf16[768,512]{1,0:T(8,128)(2,1)}, bf16[768,512]{1,0:T(8,128)(2,1)}, u32[]{:S(2)}, u32[]{:S(2)}) collective-permute-start(bf16[768,512]{1,0:T(8,128)(2,1)} %collective-permute-done.refs_4_), channel_id=1, source_target_pairs={{0,1},{1,2},{2,3},{3,4},{4,5},{5,6},{6,7},{7,0},{8,9},{9,10},{10,1... | collective-permute-start | bytes 2359304 | tf_op jit(solution)/shard_map/ppermute | solution.py:358
  63.7 19.7 %collective-permute-start.6 = (bf16[768,512]{1,0:T(8,128)(2,1)}, bf16[768,512]{1,0:T(8,128)(2,1)}, u32[]{:S(2)}, u32[]{:S(2)}) collective-permute-start(bf16[768,512]{1,0:T(8,128)(2,1)} %collective-permute-done.1.refs_1_), channel_id=1, source_target_pairs={{0,7},{1,0},{2,1},{3,2},{4,3},{5,4},{6,5},{7,6},{8,15},{9,8},{10,9... | collective-permute-start | bytes 2359304 | tf_op jit(solution)/shard_map/ppermute | solution.py:359
  85.6 4.6 %collective-permute-start.13 = (bf16[8,5248]{1,0:T(8,128)(2,1)S(1)}, bf16[8,5248]{1,0:T(8,128)(2,1)S(1)}, u32[]{:S(2)}, u32[]{:S(2)}) collective-permute-start(bf16[8,5248]{1,0:T(8,128)(2,1)S(1)} %fusion.12), channel_id=1, source_target_pairs={{0,1},{1,0},{2,3},{3,2},{4,5},{5,4},{6,7},{7,6},{8,9},{9,8},{10,11... | collective-permute-start | bytes 251912 | tf_op jit(solution)/shard_map/ppermute | solution.py:296
  87.3 42.2 %collective-permute-start.18 = (bf16[4,3,128,256]{3,2,1,0:T(8,128)(2,1)S(1)}, bf16[4,3,128,256]{3,2,1,0:T(8,128)(2,1)S(1)}, u32[]{:S(2)}, u32[]{:S(2)}) collective-permute-start(bf16[4,3,128,256]{3,2,1,0:T(8,128)(2,1)S(1)} %pad_maximum_fusion.refs_0_), channel_id=1, source_target_pairs={{0,8},{8,0},{1,9},{9,1},{2,10},{10,2},{3,11},{11,3},{4,12},{12,4},... | collective-permute-start | bytes 2359304 | tf_op jit(solution)/shard_map/ppermute | solution.py:386
  87.3 11.6 %collective-permute-start.12 = (bf16[2,3,128,256]{3,2,1,0:T(8,128)(2,1)S(1)}, bf16[2,3,128,256]{3,2,1,0:T(8,128)(2,1)S(1)}, u32[]{:S(2)}, u32[]{:S(2)}) collective-permute-start(bf16[2,3,128,256]{3,2,1,0:T(8,128)(2,1)S(1)} %slice.16), channel_id=1, source_target_pairs={{0,192},{64,0},{128,64},{192,128},{1,193},{65,1},{129,65},{193,129... | collective-permute-start | bytes 1179656 | tf_op jit(solution)/shard_map/ppermute | solution.py:372
  88.9 12.5 %collective-permute-start.11 = (bf16[2,3,128,256]{3,2,1,0:T(8,128)(2,1)S(1)}, bf16[2,3,128,256]{3,2,1,0:T(8,128)(2,1)S(1)}, u32[]{:S(2)}, u32[]{:S(2)}) collective-permute-start(bf16[2,3,128,256]{3,2,1,0:T(8,128)(2,1)S(1)} %slice.15), channel_id=1, source_target_pairs={{0,64},{64,128},{128,192},{192,0},{1,65},{65,129},{129,193},{193,1... | collective-permute-start | bytes 1179656 | tf_op jit(solution)/shard_map/ppermute | solution.py:371
  89.4 31.3 %collective-permute-start.9 = (bf16[768,512]{1,0:T(8,128)(2,1)}, bf16[768,512]{1,0:T(8,128)(2,1)S(1)}, u32[]{:S(2)}, u32[]{:S(2)}) collective-permute-start(bf16[768,512]{1,0:T(8,128)(2,1)} %collective-permute-done.5.refs_3_), channel_id=1, source_target_pairs={{0,1},{1,2},{2,3},{3,4},{4,5},{5,6},{6,7},{7,0},{8,9},{9,10},{10,1... | collective-permute-start | bytes 2359304 | tf_op jit(solution)/shard_map/ppermute | solution.py:367
  90.2 34.6 %collective-permute-start.10 = (bf16[768,512]{1,0:T(8,128)(2,1)}, bf16[768,512]{1,0:T(8,128)(2,1)S(1)}, u32[]{:S(2)}, u32[]{:S(2)}) collective-permute-start(bf16[768,512]{1,0:T(8,128)(2,1)} %collective-permute-done.6.refs_2_), channel_id=1, source_target_pairs={{0,7},{1,0},{2,1},{3,2},{4,3},{5,4},{6,5},{7,6},{8,15},{9,8},{10,9... | collective-permute-start | bytes 2359304 | tf_op jit(solution)/shard_map/ppermute | solution.py:368
  120.7 13.7 %copy-start.7 = (bf16[768,512]{1,0:T(8,128)(2,1)}, bf16[768,512]{1,0:T(8,128)(2,1)S(1)}, u32[]{:S(2)}) copy-start(bf16[768,512]{1,0:T(8,128)(2,1)S(1)} %collective-permute-done.9.refs_1_) | copy-start | bytes 2359300
  124.8 9.6 %collective-permute-start.16 = (bf16[8,5248]{1,0:T(8,128)(2,1)S(1)}, bf16[8,5248]{1,0:T(8,128)(2,1)S(1)}, u32[]{:S(2)}, u32[]{:S(2)}) collective-permute-start(bf16[8,5248]{1,0:T(8,128)(2,1)S(1)} %convert_element_type.71), channel_id=1, source_target_pairs={{0,2},{1,3},{2,0},{3,1},{4,6},{5,7},{6,4},{7,5},{8,10},{9,11},{10,... | collective-permute-start | bytes 251912 | tf_op jit(solution)/shard_map/ppermute | solution.py:296
  128.8 5.7 %collective-permute-start.19 = (bf16[4,3,128,256]{3,2,1,0:T(8,128)(2,1)S(1)}, bf16[4,3,128,256]{3,2,1,0:T(8,128)(2,1)S(1)}, u32[]{:S(2)}, u32[]{:S(2)}) collective-permute-start(bf16[4,3,128,256]{3,2,1,0:T(8,128)(2,1)S(1)} %collective-permute-done.7.refs_1_), channel_id=1, source_target_pairs={{0,8},{8,0},{1,9},{9,1},{2,10},{10,2},{3,11},{11,3},{4,12},{12,4},... | collective-permute-start | bytes 2359304 | tf_op jit(solution)/shard_map/ppermute | solution.py:386
  128.8 5.7 %collective-permute-start.21 = (bf16[4,3,128,256]{3,2,1,0:T(8,128)(2,1)S(1)}, bf16[4,3,128,256]{3,2,1,0:T(8,128)(2,1)S(1)}, u32[]{:S(2)}, u32[]{:S(2)}) collective-permute-start(bf16[4,3,128,256]{3,2,1,0:T(8,128)(2,1)S(1)} %collective-permute-done.8.refs_3_), channel_id=1, source_target_pairs={{0,8},{8,0},{1,9},{9,1},{2,10},{10,2},{3,11},{11,3},{4,12},{12,4},... | collective-permute-start | bytes 2359304 | tf_op jit(solution)/shard_map/ppermute | solution.py:386
  129.4 18.9 %collective-permute-start.15 = (bf16[384,512]{1,0:T(8,128)(2,1)S(1)}, bf16[384,512]{1,0:T(8,128)(2,1)S(1)}, u32[]{:S(2)}, u32[]{:S(2)}) collective-permute-start(bf16[384,512]{1,0:T(8,128)(2,1)S(1)} %slice.19), channel_id=1, source_target_pairs={{0,7},{1,0},{2,1},{3,2},{4,3},{5,4},{6,5},{7,6},{8,15},{9,8},{10,9... | collective-permute-start | bytes 1179656 | tf_op jit(solution)/shard_map/ppermute | solution.py:391
  129.5 18.8 %collective-permute-start.14 = (bf16[384,512]{1,0:T(8,128)(2,1)S(1)}, bf16[384,512]{1,0:T(8,128)(2,1)S(1)}, u32[]{:S(2)}, u32[]{:S(2)}) collective-permute-start(bf16[384,512]{1,0:T(8,128)(2,1)S(1)} %slice.18), channel_id=1, source_target_pairs={{0,1},{1,2},{2,3},{3,4},{4,5},{5,6},{6,7},{7,0},{8,9},{9,10},{10,1... | collective-permute-start | bytes 1179656 | tf_op jit(solution)/shard_map/ppermute | solution.py:390
  134.4 2.3 %collective-permute-start.20 = (bf16[4,3,128,256]{3,2,1,0:T(8,128)(2,1)S(1)}, bf16[4,3,128,256]{3,2,1,0:T(8,128)(2,1)S(1)}, u32[]{:S(2)}, u32[]{:S(2)}) collective-permute-start(bf16[4,3,128,256]{3,2,1,0:T(8,128)(2,1)S(1)} %pad_maximum_fusion.1.refs_2_), channel_id=1, source_target_pairs={{0,8},{8,0},{1,9},{9,1},{2,10},{10,2},{3,11},{11,3},{4,12},{12,4},... | collective-permute-start | bytes 2359304 | tf_op jit(solution)/shard_map/ppermute | solution.py:386
  137.7 15.1 %copy-start.8 = (bf16[768,512]{1,0:T(8,128)(2,1)S(1)}, bf16[768,512]{1,0:T(8,128)(2,1)}, u32[]{:S(2)}) copy-start(bf16[768,512]{1,0:T(8,128)(2,1)} %copy-done.7) | copy-start | bytes 2359300
  137.7 15.1 %copy-start.10 = (bf16[768,512]{1,0:T(8,128)(2,1)S(1)}, bf16[768,512]{1,0:T(8,128)(2,1)}, u32[]{:S(2)}) copy-start(bf16[768,512]{1,0:T(8,128)(2,1)} %copy-done.9) | copy-start | bytes 2359300
  149.1 14.8 %collective-permute-start.17 = (bf16[8,5248]{1,0:T(8,128)(2,1)S(1)}, bf16[8,5248]{1,0:T(8,128)(2,1)S(1)}, u32[]{:S(2)}, u32[]{:S(2)}) collective-permute-start(bf16[8,5248]{1,0:T(8,128)(2,1)S(1)} %convert_element_type.73), channel_id=1, source_target_pairs={{0,4},{1,5},{2,6},{3,7},{4,0},{5,1},{6,2},{7,3},{8,12},{9,13},{10,... | collective-permute-start | bytes 251912 | tf_op jit(solution)/shard_map/ppermute | solution.py:296
  (14 other events, 52.8 us)
Sparse Core Ops, SparseCore 0:
  10.6 62.4 all-gather.1
  80.7 68.2 reduce-scatter.1

commit v4 on v2

--- a/solution.py
+++ b/solution.py
@@ -35,24 +35,23 @@
     return context.astype(jnp.bfloat16).reshape(pair_count * length, row_width)
 
 
-def select_kernel(owner_ref, rank_ref, len_ref, rows_ref, out_ref):
+def select_kernel(owner_ref, rank_ref, len_ref, rows_ref, out_ref, cand_ref, live_ref):
     places = rank_ref.shape[0]
     position = lax.broadcasted_iota(jnp.int32, rows_ref.shape[1:], 0)
 
     def one_prompt(prompt, carry):
         owner = owner_ref[0, prompt]
+        for place in range(places):
+            rank = rank_ref[place, prompt]
+            cand_ref[prompt, rank] = place
+            live_ref[prompt, rank] = len_ref[place, prompt]
         for rank in range(3):
-            cand = jnp.int32(0)
-            live = jnp.int32(0)
-            for place in range(places):
-                hit = rank_ref[place, prompt] == rank
-                cand = jnp.where(hit, place, cand)
-                live = jnp.where(hit, len_ref[place, prompt], live)
-            picked = rows_ref[prompt * places + cand].astype(jnp.float32)
-            out_ref[owner * 3 + rank] = jnp.where(position < live, picked, 0.0).astype(out_ref.dtype)
+            picked = rows_ref[prompt * places + cand_ref[prompt, rank]].astype(jnp.float32)
+            chosen = jnp.where(position < live_ref[prompt, rank], picked, 0.0)
+            out_ref[owner * 3 + rank] = chosen.astype(out_ref.dtype)
         return carry
 
-    lax.fori_loop(0, owner_ref.shape[1], one_prompt, 0)
+    lax.fori_loop(0, owner_ref.shape[1], one_prompt, 0, unroll=4)
 
 
 def select_rows(blend_owner, cand_rank, cand_len, blend_rows):
@@ -64,11 +63,12 @@
         out_shape=jax.ShapeDtypeStruct((prompts * 3, length, features), blend_rows.dtype),
         in_specs=[smem, smem, smem, vmem],
         out_specs=vmem,
+        scratch_shapes=[pltpu.SMEM((prompts, cands), jnp.int32)] * 2,
         cost_estimate=pl.CostEstimate(flops=0, bytes_accessed=3 << 20, transcendentals=0),
     )(blend_owner, cand_rank.T, cand_len.T, blend_rows.reshape(prompts * cands, length, features))
 
 
-def arrange_kernel(where_ref, *refs):
+def arrange_kernel(where_ref, token_ref, *refs):
     slab_refs, out_ref = refs[:-1], refs[-1]
     third, depth = slab_refs[0].shape[1:3]
     my_y, my_x, my_core, my_z = where_ref[0], where_ref[1], where_ref[2], where_ref[3]
@@ -86,20 +86,21 @@
                     out_ref[part, pl.ds(start, depth), :] = slabs[left, part]
 
 
-def arrange(where, slabs):
+def arrange(where, token, slabs):
     third, depth, width = slabs[0].shape[1:]
     vmem = pl.BlockSpec(memory_space=pltpu.VMEM)
     return pl.pallas_call(
         arrange_kernel,
         out_shape=jax.ShapeDtypeStruct((third, NC * NY * NX * depth, width), jnp.bfloat16),
-        in_specs=[pl.BlockSpec(memory_space=pltpu.SMEM)] + [vmem] * len(slabs),
+        in_specs=[pl.BlockSpec(memory_space=pltpu.SMEM)] + [vmem] * (len(slabs) + 1),
         out_specs=vmem,
         compiler_params=pltpu.CompilerParams(vmem_limit_bytes=32 << 20),
         cost_estimate=pl.CostEstimate(flops=0, bytes_accessed=12 << 20, transcendentals=0),
-    )(where, *slabs)
-
-
-def project_kernel(rows_ref, columns_ref, out_ref):
+    )(where, token, *slabs)
+
+
+def project_kernel(rows_ref, columns_ref, out_ref, token_ref):
+    token_ref[...] = jnp.zeros_like(token_ref)
     out_ref[...] = lax.dot_general(
         rows_ref[...], columns_ref[...], (((1,), (1,)), ((), ())), preferred_element_type=jnp.float32
     ).astype(out_ref.dtype)
@@ -111,13 +112,19 @@
     steps = 4
     return pl.pallas_call(
         project_kernel,
-        out_shape=jax.ShapeDtypeStruct((count, width), jnp.bfloat16),
+        out_shape=(
+            jax.ShapeDtypeStruct((count, width), jnp.bfloat16),
+            jax.ShapeDtypeStruct((8, 128), jnp.float32),
+        ),
         grid=(steps,),
         in_specs=[
             pl.BlockSpec((count, depth), lambda i: (0, 0)),
             pl.BlockSpec((width // steps, depth), lambda i: (i, 0)),
         ],
-        out_specs=pl.BlockSpec((count, width // steps), lambda i: (0, i)),
+        out_specs=(
+            pl.BlockSpec((count, width // steps), lambda i: (0, i)),
+            pl.BlockSpec((8, 128), lambda i: (0, 0)),
+        ),
         compiler_params=pltpu.CompilerParams(vmem_limit_bytes=16 << 20),
         cost_estimate=pl.CostEstimate(
             flops=2 * count * width * depth, bytes_accessed=9 << 20, transcendentals=0
@@ -316,17 +323,15 @@
     x_after = lax.ppermute(own_slab, "x", ring(NX, -1))
     x_across = lax.ppermute(x_before, "x", ring(NX, 1))
     strip = jnp.concatenate([own_slab, x_before, x_across, x_after], axis=0)
-    lower, upper, strip = together(lower, upper, strip)
+    lower, upper, strip, context = together(lower, upper, strip, context)
     blocks = {1: upper, NZ - 1: lower, 0: own}
 
     lower = lax.ppermute(lower, "z", ring(NZ, 1))
     upper = lax.ppermute(upper, "z", ring(NZ, -1))
     y_before = lax.ppermute(strip, "y", ring(NY, 1))
     y_after = lax.ppermute(strip, "y", ring(NY, -1))
-    term_rows = project(context, columns)
-    lower, upper, y_before, y_after, term_rows = together(
-        lower, upper, y_before, y_after, term_rows
-    )
+    term_rows, token = project(context, columns)
+    lower, upper, y_before, y_after, token = together(lower, upper, y_before, y_after, token)
     blocks.update({2: upper, NZ - 2: lower})
     part_sum = lax.psum_scatter(term_rows, "z", scatter_dimension=0, tiled=True)
 
@@ -342,7 +347,7 @@
     lower, upper, y_across = together(lower, upper, y_across)
 
     slabs = [strip, y_before, y_across, y_after]
-    weights = arrange(where, slabs + [lax.ppermute(s, "core", ring(NC, 1)) for s in slabs])
+    weights = arrange(where, token, slabs + [lax.ppermute(s, "core", ring(NC, 1)) for s in slabs])
     near = (0, 1, 2, NZ - 2, NZ - 1)
     half = own.shape[0] // 2
     total, squares = encode_first(near, [blocks[i] for i in near], weights)
@@ -364,9 +369,9 @@
         cand_rank.shape[1],
     )
     rank_hidden = rank_hidden.reshape(rank_resid.shape)
-    for bit in (1, 2, 4):
-        votes = votes + lax.ppermute(votes, "z", [(i, i ^ bit) for i in range(NZ)])
-    cand_score = votes.T
+    votes = jnp.broadcast_to(votes[None], (NZ,) + votes.shape)
+    votes = lax.all_to_all(votes, "z", split_axis=0, concat_axis=0, tiled=True)
+    cand_score = jnp.sum(votes, axis=0).T
     return (rank_hidden, cand_score, blended_qkv)
 
 

time: 169 us -> 169 us (level)
  blocking collectives: 0 us -> 13.7 us
  starting transfers between devices: 41.3 us -> 32.5 us
  waiting for transfers between devices: 83.1 us -> 75.2 us
  local copies, waits for them, and re-layouts: 5.45 us -> 8.35 us
    all_to_all x0 -> x1, blocking collectives: none -> 13.7 us  [body(): votes = lax.all_to_all(votes, 'z', split_axis=0, concat_axis=0, tiled=True)]
    ppermute x3 -> x0, starting transfers between devices: 9.61 us -> none  [body(): votes = votes + lax.ppermute(votes, 'z', [(i, i ^ bit) for i in range(NZ)])]
    ppermute x3 -> x0, waiting for transfers between devices: 6.23 us -> none  [body(): votes = votes + lax.ppermute(votes, 'z', [(i, i ^ bit) for i in range(NZ)])]
    all_gather x1, waiting for transfers between devices: 3.63 us -> 8.12 us  [body(): columns = lax.all_gather(out_weight.T, PLANE, axis=0, tiled=True)]
    ppermute x2, waiting for transfers between devices: 12.5 us -> 8.05 us  [body(): lower = lax.ppermute(lower, 'z', ring(NZ, 1))]
    ppermute x1, waiting for transfers between devices: 1.25 us -> 4.62 us  [body(): y_before = lax.ppermute(strip, 'y', ring(NY, 1))]
    ppermute x1, waiting for transfers between devices: 3.05 us -> 0.01 us  [body(): upper = lax.ppermute(own, 'z', ring(NZ, -1))]
    ppermute x1, waiting for transfers between devices: 2.37 us -> 0.01 us  [body(): y_after = lax.ppermute(strip, 'y', ring(NY, -1))]
  transfers between devices with their start and end apart: 25 -> 22, of which waited for: 18 -> 13; matrix products, arithmetic and copies ran while one was open for 3% -> 3% of each run, Pallas kernels for 11% -> 11%
where the time goes in v4:
time: 169 us; the launch traced here: 168 us
  waiting for transfers between devices  75.2 us (44%)
  starting transfers between devices  32.5 us (19%)
  Pallas kernels  20.1 us (12%)
  between operations  14.3 us (8%)
  blocking collectives  13.7 us (8%)
  local copies, waits for them, and re-layouts  8.35 us (5%)
  other arithmetic  2.37 us (1%)
    all_to_all x1, blocking collectives, body(): votes = lax.all_to_all(votes, 'z', split_axis=0, concat_axis=0, tiled=True)  13.7 us
    all_to_all x1, waiting for transfers between devices, body(): lax.all_to_all(outgoing.reshape(prompts, -1, features), PLANE, split_axis...  10.7 us
    ppermute x1, waiting for transfers between devices, body(): low = lax.ppermute(lower[:half], 'z', ring(NZ, 1))  10.6 us
    all_gather x1, waiting for transfers between devices, body(): columns = lax.all_gather(out_weight.T, PLANE, axis=0, tiled=True)  8.12 us
    ppermute x2, waiting for transfers between devices, body(): lower = lax.ppermute(lower, 'z', ring(NZ, 1))  8.05 us
    ppermute x1, waiting for transfers between devices, body(): lax.ppermute(y_after[2:], 'y', ring(NY, -1))  7.92 us
    all_to_all x1, starting transfers between devices, body(): lax.all_to_all(outgoing.reshape(prompts, -1, features), PLANE, split_axis...  7.62 us
    ppermute x1, waiting for transfers between devices, body(): x_across = lax.ppermute(x_before, 'x', ring(NX, 1))  7.22 us
  transfers between devices with their start and end apart: 22, of which 13 were waited for; matrix products, arithmetic and copies ran while one was open for 3% of the time, Pallas kernels for 11%

profile of v4, /device:TPU:2, one launch (start us, length us, event | category | flops | bytes accessed | tf_op | source)
XLA Modules:
  0.0 167.6 jit_solution(12882968270853750333)
XLA Ops:
  7.9 3.8 %shard_map.157 = bf16[96,8,512]{2,1,0:T(8,128)(2,1)} custom-call(s32[1,32]{1,0:T(1,128)} %owner_ref.1, s32[8,32]{1,0:T(8,128)} %bitcast.72, s32[8,32]{1,0:T(8,128)} %bitcast.73, bf16[256,8,512]{2,1,0:T(8,128)(2,1)} %bitcast.68), custom_call_target="tpu_custom_call" | custom-call | bytes 3145728 | tf_op jit(solution)/shard_map/pallas_call | solution.py:61
  11.7 7.6 %all-to-all-start = ((bf16[32,24,512]{2,1,0:T(8,128)(2,1)}), bf16[32,24,512]{2,1,0:T(8,128)(2,1)S(1)}, u32[]{:S(2)}, u32[]{:S(2)}) async-start(bf16[32,24,512]{2,1,0:T(8,128)(2,1)} %bitcast.67), calls=%async_computation | async-start | bytes 1572864 | tf_op jit(solution)/shard_map/all_to_all | solution.py:302
  23.0 10.7 %all-to-all-done = bf16[32,24,512]{2,1,0:T(8,128)(2,1)S(1)} async-done(((bf16[32,24,512]{2,1,0:T(8,128)(2,1)}), bf16[32,24,512]{2,1,0:T(8,128)(2,1)S(1)}, u32[]{:S(2)}, u32[]{:S(2)}) %all-to-all-start) | async-done | bytes 786464 | tf_op jit(solution)/shard_map/all_to_all | solution.py:302
  33.7 2.0 %collective-permute-start = (bf16[768,512]{1,0:T(8,128)(2,1)S(1)}, bf16[768,512]{1,0:T(8,128)(2,1)}, u32[]{:S(2)}, u32[]{:S(2)}) collective-permute-start(bf16[768,512]{1,0:T(8,128)(2,1)S(1)} %bitcast.64), channel_id=1, source_target_pairs={{0,1},{1,2},{2,3},{3,4},{4,5},{5,6},{6,7},{7,0},{8,9},{9,10},{10,1... | collective-permute-start | bytes 2359304 | tf_op jit(solution)/shard_map/ppermute | solution.py:320
  35.7 4.5 %collective-permute-start.1 = (bf16[768,512]{1,0:T(8,128)(2,1)S(1)}, bf16[768,512]{1,0:T(8,128)(2,1)}, u32[]{:S(2)}, u32[]{:S(2)}) collective-permute-start(bf16[768,512]{1,0:T(8,128)(2,1)S(1)} %bitcast.65), channel_id=1, source_target_pairs={{0,7},{1,0},{2,1},{3,2},{4,3},{5,4},{6,5},{7,6},{8,15},{9,8},{10,9... | collective-permute-start | bytes 2359304 | tf_op jit(solution)/shard_map/ppermute | solution.py:321
  40.3 1.9 %collective-permute-start.4 = (bf16[1,3,128,256]{3,2,1,0:T(8,128)(2,1)S(1)}, bf16[1,3,128,256]{3,2,1,0:T(8,128)(2,1)S(1)}, u32[]{:S(2)}, u32[]{:S(2)}) collective-permute-start(bf16[1,3,128,256]{3,2,1,0:T(8,128)(2,1)S(1)} %fusion.11), channel_id=1, source_target_pairs={{0,48},{16,0},{32,16},{48,32},{1,49},{17,1},{33,17},{49,33},{2,50}... | collective-permute-start | bytes 589832 | tf_op jit(solution)/shard_map/ppermute | solution.py:323
  42.2 5.0 %collective-permute-done.2 = bf16[1,3,128,256]{3,2,1,0:T(8,128)(2,1)S(1)} collective-permute-done((bf16[1,3,128,256]{3,2,1,0:T(8,128)(2,1)S(1)}, bf16[1,3,128,256]{3,2,1,0:T(8,128)(2,1)S(1)}, u32[]{:S(2)}, u32[]{:S(2)}) %collective-permute-start.2) | collective-permute-done | bytes 196640 | tf_op jit(solution)/shard_map/ppermute | solution.py:322
  47.5 7.2 %collective-permute-done.3 = bf16[1,3,128,256]{3,2,1,0:T(8,128)(2,1)S(1)} collective-permute-done((bf16[1,3,128,256]{3,2,1,0:T(8,128)(2,1)S(1)}, bf16[1,3,128,256]{3,2,1,0:T(8,128)(2,1)S(1)}, u32[]{:S(2)}, u32[]{:S(2)}) %collective-permute-start.3) | collective-permute-done | bytes 196640 | tf_op jit(solution)/shard_map/ppermute | solution.py:324
  54.8 3.7 %collective-permute-done.refs_4_ = bf16[768,512]{1,0:T(8,128)(2,1)} collective-permute-done((bf16[768,512]{1,0:T(8,128)(2,1)S(1)}, bf16[768,512]{1,0:T(8,128)(2,1)}, u32[]{:S(2)}, u32[]{:S(2)}) %collective-permute-start) | collective-permute-done | bytes 786464 | tf_op jit(solution)/shard_map/ppermute | solution.py:320
  58.5 3.2 %collective-permute-start.6 = (bf16[768,512]{1,0:T(8,128)(2,1)}, bf16[768,512]{1,0:T(8,128)(2,1)}, u32[]{:S(2)}, u32[]{:S(2)}) collective-permute-start(bf16[768,512]{1,0:T(8,128)(2,1)} %collective-permute-done.1.refs_1_), channel_id=1, source_target_pairs={{0,7},{1,0},{2,1},{3,2},{4,3},{5,4},{6,5},{7,6},{8,15},{9,8},{10,9... | collective-permute-start | bytes 2359304 | tf_op jit(solution)/shard_map/ppermute | solution.py:330
  61.7 3.2 %collective-permute-start.8 = (bf16[4,3,128,256]{3,2,1,0:T(8,128)(2,1)S(1)}, bf16[4,3,128,256]{3,2,1,0:T(8,128)(2,1)S(1)}, u32[]{:S(2)}, u32[]{:S(2)}) collective-permute-start(bf16[4,3,128,256]{3,2,1,0:T(8,128)(2,1)S(1)} %pad_maximum_fusion.refs_0_), channel_id=1, source_target_pairs={{0,192},{64,0},{128,64},{192,128},{1,193},{65,1},{129,65},{193,129... | collective-permute-start | bytes 2359304 | tf_op jit(solution)/shard_map/ppermute | solution.py:332
  65.0 8.1 %all-gather.2.cloned.1.call-done.columns_ref = bf16[5120,640]{1,0:T(8,128)(2,1)} async-done(((bf16[160,640]{1,0:T(8,128)(2,1)}), bf16[5120,640]{1,0:T(8,128)(2,1)}) %all-gather.2.cloned.1.call-update) | async-done | bytes 6553616 | tf_op jit(solution)/shard_map/all_gather | solution.py:296
  73.1 2.9 %copy-done.1 = bf16[5120,640]{1,0:T(8,128)(2,1)S(1)} copy-done((bf16[5120,640]{1,0:T(8,128)(2,1)S(1)}, bf16[5120,640]{1,0:T(8,128)(2,1)}, u32[]{:S(2)}) %copy-start.1) | copy-done | bytes 6553624
  75.9 3.0 %shard_map.158 = (bf16[256,5120]{1,0:T(8,128)(2,1)S(1)}, f32[8,128]{1,0:T(8,128)S(1)}) custom-call(bf16[256,640]{1,0:T(8,128)(2,1)S(1)} %bitcast.63, bf16[5120,640]{1,0:T(8,128)(2,1)S(1)} %copy-done.1), custom_call_target="tpu_custom_call" | custom-call | flops 1677721600 | bytes 9437184 | tf_op jit(solution)/shard_map/pallas_call | solution.py:113
  79.0 1.5 copy-done.2
  80.5 4.6 %collective-permute-done.7.refs_1_ = bf16[4,3,128,256]{3,2,1,0:T(8,128)(2,1)S(1)} collective-permute-done((bf16[4,3,128,256]{3,2,1,0:T(8,128)(2,1)S(1)}, bf16[4,3,128,256]{3,2,1,0:T(8,128)(2,1)S(1)}, u32[]{:S(2)}, u32[]{:S(2)}) %collective-permute-start.7) | collective-permute-done | bytes 786464 | tf_op jit(solution)/shard_map/ppermute | solution.py:331
  85.1 1.6 collective-permute-start.9
  86.6 1.8 %collective-permute-start.10 = (bf16[768,512]{1,0:T(8,128)(2,1)}, bf16[768,512]{1,0:T(8,128)(2,1)}, u32[]{:S(2)}, u32[]{:S(2)}) collective-permute-start(bf16[768,512]{1,0:T(8,128)(2,1)} %collective-permute-done.6.refs_2_), channel_id=1, source_target_pairs={{0,7},{1,0},{2,1},{3,2},{4,3},{5,4},{6,5},{7,6},{8,15},{9,8},{10,9... | collective-permute-start | bytes 2359304 | tf_op jit(solution)/shard_map/ppermute | solution.py:339
  88.5 1.6 collective-permute-start.12
  90.9 7.9 %collective-permute-done.12 = bf16[2,3,128,256]{3,2,1,0:T(8,128)(2,1)S(1)} collective-permute-done((bf16[2,3,128,256]{3,2,1,0:T(8,128)(2,1)S(1)}, bf16[2,3,128,256]{3,2,1,0:T(8,128)(2,1)S(1)}, u32[]{:S(2)}, u32[]{:S(2)}) %collective-permute-start.12) | collective-permute-done | bytes 393248 | tf_op jit(solution)/shard_map/ppermute | solution.py:343
  98.8 2.6 %collective-permute-done.11 = bf16[2,3,128,256]{3,2,1,0:T(8,128)(2,1)S(1)} collective-permute-done((bf16[2,3,128,256]{3,2,1,0:T(8,128)(2,1)S(1)}, bf16[2,3,128,256]{3,2,1,0:T(8,128)(2,1)S(1)}, u32[]{:S(2)}, u32[]{:S(2)}) %collective-permute-start.11) | collective-permute-done | bytes 393248 | tf_op jit(solution)/shard_map/ppermute | solution.py:342
  101.5 8.1 %collective-permute-done.9.refs_1_ = bf16[768,512]{1,0:T(8,128)(2,1)S(1)} collective-permute-done((bf16[768,512]{1,0:T(8,128)(2,1)}, bf16[768,512]{1,0:T(8,128)(2,1)S(1)}, u32[]{:S(2)}, u32[]{:S(2)}) %collective-permute-start.9) | collective-permute-done | bytes 786464 | tf_op jit(solution)/shard_map/ppermute | solution.py:338
  109.5 2.7 %collective-permute-done.10.refs_0_ = bf16[768,512]{1,0:T(8,128)(2,1)} collective-permute-done((bf16[768,512]{1,0:T(8,128)(2,1)}, bf16[768,512]{1,0:T(8,128)(2,1)}, u32[]{:S(2)}, u32[]{:S(2)}) %collective-permute-start.10) | collective-permute-done | bytes 786464 | tf_op jit(solution)/shard_map/ppermute | solution.py:339
  113.0 1.0 slice.15
  114.1 3.1 %collective-permute-start.14 = (bf16[384,512]{1,0:T(8,128)(2,1)S(1)}, bf16[384,512]{1,0:T(8,128)(2,1)S(1)}, u32[]{:S(2)}, u32[]{:S(2)}) collective-permute-start(bf16[384,512]{1,0:T(8,128)(2,1)S(1)} %slice.15), channel_id=1, source_target_pairs={{0,7},{1,0},{2,1},{3,2},{4,3},{5,4},{6,5},{7,6},{8,15},{9,8},{10,9... | collective-permute-start | bytes 1179656 | tf_op jit(solution)/shard_map/ppermute | solution.py:355
  117.2 1.0 shard_map.159.refs_5_.refs_4_
  118.2 5.4 %shard_map.160 = (f32[3,768,256]{2,1,0:T(8,128)S(1)}, f32[768,128]{1,0:T(8,128)S(1)}) custom-call(bf16[768,512]{1,0:T(8,128)(2,1)S(1)} %bitcast.66, bf16[768,512]{1,0:T(8,128)(2,1)} %collective-permute-done.1.refs_1_, bf16[768,512]{1,0:T(8,128)(2,1)} %collective-permute-done.6.refs_2_, bf16[768,512]{1,0:T(8,128)(2,1)} %collective-permute-done.5.refs_3_, ...), custom_call_target="tpu_custom_call" | custom-call | flops 3019898880 | bytes 12582912 | tf_op jit(solution)/shard_map/pallas_call | solution.py:186
  123.7 10.6 %collective-permute-done.13.refs_2_ = bf16[384,512]{1,0:T(8,128)(2,1)S(1)} collective-permute-done((bf16[384,512]{1,0:T(8,128)(2,1)S(1)}, bf16[384,512]{1,0:T(8,128)(2,1)S(1)}, u32[]{:S(2)}, u32[]{:S(2)}) %collective-permute-start.13) | collective-permute-done | bytes 393248 | tf_op jit(solution)/shard_map/ppermute | solution.py:354
  135.1 4.8 %shard_map.161 = bf16[32,3,24,256]{3,2,1,0:T(8,128)(2,1)} custom-call(bf16[768,512]{1,0:T(8,128)(2,1)} %collective-permute-done.10.refs_0_, bf16[768,512]{1,0:T(8,128)(2,1)S(1)} %collective-permute-done.9.refs_1_, bf16[384,512]{1,0:T(8,128)(2,1)S(1)} %collective-permute-done.13.refs_2_, bf16[384,512]{1,0:T(8,128)(2,1)S(1)} %collective-permute-done.14.refs_3_, ...), custom_call_target="tpu_custom_call" | custom-call | flops 36238786560 | bytes 12582912 | tf_op jit(solution)/shard_map/pallas_call | solution.py:215
  139.9 2.4 %reduce-scatter.2.cloned.1.call-done.sum_ref = bf16[32,5120]{1,0:T(8,128)(2,1)} async-done(((bf16[256,5120]{1,0:T(8,128)(2,1)}), bf16[32,5120]{1,0:T(8,128)(2,1)}) %reduce-scatter.2.cloned.1.call-update) | async-done | bytes 327696 | tf_op jit(solution)/shard_map/reduce_scatter | solution.py:336
  142.3 2.1 %shard_map.162 = (bf16[32,5120]{1,0:T(8,128)(2,1)}, f32[8,32]{1,0:T(8,128)}) custom-call(s32[1,3]{1,0:T(1,128)} %pair_ref.1, bf16[32,5120]{1,0:T(8,128)(2,1)} %bitcast.70, bf16[1,5120]{1,0:T(2,128)(2,1)} %reshape.51.gain_ref, bf16[1,5120]{1,0:T(2,128)(2,1)} %reshape.52.score_ref, bf16[32,5120]{1,0:T(8,128)(2,1)} %reduce-scatter.2.cloned.1.call-done.sum_ref), custom_call_target="tpu_custom_call" | custom-call | flops 1310720 | bytes 2097152 | tf_op jit(solution)/shard_map/pallas_call | solution.py:257
  145.2 13.7 %all_to_all.10 = f32[8,1,256]{2,1,0:T(1,128)S(1)} all-to-all(f32[8,1,256]{2,1,0:T(1,128)S(1)} %reshape.54), channel_id=1, replica_groups=mesh['y'=4,'x'=4,'core'=2,'z'=8] {'z'}, dimensions={0} | all-to-all | bytes 16384 | tf_op jit(solution)/shard_map/all_to_all | solution.py:373
  (63 shorter events, 10.0 us)
Async XLA Ops:
  7.2 13.0 %copy-start = (bf16[8,32,640]{2,1,0:T(8,128)(2,1)S(1)}, bf16[8,32,640]{2,1,0:T(8,128)(2,1)}, u32[]{:S(2)}) copy-start(bf16[8,32,640]{2,1,0:T(8,128)(2,1)} %param.16) | copy-start | bytes 983044
  7.2 12.2 %copy-start.6 = (bf16[8,32,640]{2,1,0:T(8,128)(2,1)S(1)}, bf16[8,32,640]{2,1,0:T(8,128)(2,1)}, u32[]{:S(2)}) copy-start(bf16[8,32,640]{2,1,0:T(8,128)(2,1)} %param.14) | copy-start | bytes 983044
  7.2 12.2 %copy-start.5 = (bf16[8,32,640]{2,1,0:T(8,128)(2,1)S(1)}, bf16[8,32,640]{2,1,0:T(8,128)(2,1)}, u32[]{:S(2)}) copy-start(bf16[8,32,640]{2,1,0:T(8,128)(2,1)} %param.15) | copy-start | bytes 983044
  7.2 65.9 %all-gather.2.cloned.1.call-start = ((), (), s32[]{:S(2)}) async-start(), calls=%async_computation.3 | async-start | bytes 6758400 | tf_op jit(solution)/shard_map/all_gather | solution.py:296
  11.7 22.0 %all-to-all-start = ((bf16[32,24,512]{2,1,0:T(8,128)(2,1)}), bf16[32,24,512]{2,1,0:T(8,128)(2,1)S(1)}, u32[]{:S(2)}, u32[]{:S(2)}) async-start(bf16[32,24,512]{2,1,0:T(8,128)(2,1)} %bitcast.67), calls=%async_computation | async-start | bytes 1572864 | tf_op jit(solution)/shard_map/all_to_all | solution.py:302
  19.4 122.9 %reduce-scatter.2.cloned.1.call-start = ((), (), s32[]{:S(2)}) async-start(), calls=%async_computation.4 | async-start | bytes 2949120 | tf_op jit(solution)/shard_map/reduce_scatter | solution.py:336
  20.1 0.7 copy-start.8
  20.1 1.3 copy-start.9
  20.1 2.7 %copy-start.7 = (bf16[128,3,256]{2,0,1:T(8,128)(2,1)S(1)}, bf16[128,3,256]{2,0,1:T(8,128)(2,1)}, u32[]{:S(2)}) copy-start(bf16[128,3,256]{2,0,1:T(8,128)(2,1)} %param.27) | copy-start | bytes 589828
  33.7 24.8 %copy-start.3 = (bf16[32,24,512]{2,1,0:T(8,128)(2,1)}, bf16[32,24,512]{2,1,0:T(8,128)(2,1)S(1)}, u32[]{:S(2)}) copy-start(bf16[32,24,512]{2,1,0:T(8,128)(2,1)S(1)} %all-to-all-done) | copy-start | bytes 2359300
  33.7 24.8 %collective-permute-start = (bf16[768,512]{1,0:T(8,128)(2,1)S(1)}, bf16[768,512]{1,0:T(8,128)(2,1)}, u32[]{:S(2)}, u32[]{:S(2)}) collective-permute-start(bf16[768,512]{1,0:T(8,128)(2,1)S(1)} %bitcast.64), channel_id=1, source_target_pairs={{0,1},{1,2},{2,3},{3,4},{4,5},{5,6},{6,7},{7,0},{8,9},{9,10},{10,1... | collective-permute-start | bytes 2359304 | tf_op jit(solution)/shard_map/ppermute | solution.py:320
  35.7 22.8 %collective-permute-start.1 = (bf16[768,512]{1,0:T(8,128)(2,1)S(1)}, bf16[768,512]{1,0:T(8,128)(2,1)}, u32[]{:S(2)}, u32[]{:S(2)}) collective-permute-start(bf16[768,512]{1,0:T(8,128)(2,1)S(1)} %bitcast.65), channel_id=1, source_target_pairs={{0,7},{1,0},{2,1},{3,2},{4,3},{5,4},{6,5},{7,6},{8,15},{9,8},{10,9... | collective-permute-start | bytes 2359304 | tf_op jit(solution)/shard_map/ppermute | solution.py:321
  40.2 7.0 %collective-permute-start.2 = (bf16[1,3,128,256]{3,2,1,0:T(8,128)(2,1)S(1)}, bf16[1,3,128,256]{3,2,1,0:T(8,128)(2,1)S(1)}, u32[]{:S(2)}, u32[]{:S(2)}) collective-permute-start(bf16[1,3,128,256]{3,2,1,0:T(8,128)(2,1)S(1)} %fusion.11), channel_id=1, source_target_pairs={{0,16},{16,32},{32,48},{48,0},{1,17},{17,33},{33,49},{49,1},{2,18}... | collective-permute-start | bytes 589832 | tf_op jit(solution)/shard_map/ppermute | solution.py:322
  40.3 7.1 %collective-permute-start.4 = (bf16[1,3,128,256]{3,2,1,0:T(8,128)(2,1)S(1)}, bf16[1,3,128,256]{3,2,1,0:T(8,128)(2,1)S(1)}, u32[]{:S(2)}, u32[]{:S(2)}) collective-permute-start(bf16[1,3,128,256]{3,2,1,0:T(8,128)(2,1)S(1)} %fusion.11), channel_id=1, source_target_pairs={{0,48},{16,0},{32,16},{48,32},{1,49},{17,1},{33,17},{49,33},{2,50}... | collective-permute-start | bytes 589832 | tf_op jit(solution)/shard_map/ppermute | solution.py:323
  47.2 7.5 %collective-permute-start.3 = (bf16[1,3,128,256]{3,2,1,0:T(8,128)(2,1)S(1)}, bf16[1,3,128,256]{3,2,1,0:T(8,128)(2,1)S(1)}, u32[]{:S(2)}, u32[]{:S(2)}) collective-permute-start(bf16[1,3,128,256]{3,2,1,0:T(8,128)(2,1)S(1)} %collective-permute-done.2), channel_id=1, source_target_pairs={{0,16},{16,32},{32,48},{48,0},{1,17},{17,33},{33,49},{49,1},{2,18}... | collective-permute-start | bytes 589832 | tf_op jit(solution)/shard_map/ppermute | solution.py:324
  58.5 22.0 %collective-permute-start.5 = (bf16[768,512]{1,0:T(8,128)(2,1)}, bf16[768,512]{1,0:T(8,128)(2,1)}, u32[]{:S(2)}, u32[]{:S(2)}) collective-permute-start(bf16[768,512]{1,0:T(8,128)(2,1)} %collective-permute-done.refs_4_), channel_id=1, source_target_pairs={{0,1},{1,2},{2,3},{3,4},{4,5},{5,6},{6,7},{7,0},{8,9},{9,10},{10,1... | collective-permute-start | bytes 2359304 | tf_op jit(solution)/shard_map/ppermute | solution.py:329
  58.5 22.0 %collective-permute-start.6 = (bf16[768,512]{1,0:T(8,128)(2,1)}, bf16[768,512]{1,0:T(8,128)(2,1)}, u32[]{:S(2)}, u32[]{:S(2)}) collective-permute-start(bf16[768,512]{1,0:T(8,128)(2,1)} %collective-permute-done.1.refs_1_), channel_id=1, source_target_pairs={{0,7},{1,0},{2,1},{3,2},{4,3},{5,4},{6,5},{7,6},{8,15},{9,8},{10,9... | collective-permute-start | bytes 2359304 | tf_op jit(solution)/shard_map/ppermute | solution.py:330
  61.7 23.4 %collective-permute-start.7 = (bf16[4,3,128,256]{3,2,1,0:T(8,128)(2,1)S(1)}, bf16[4,3,128,256]{3,2,1,0:T(8,128)(2,1)S(1)}, u32[]{:S(2)}, u32[]{:S(2)}) collective-permute-start(bf16[4,3,128,256]{3,2,1,0:T(8,128)(2,1)S(1)} %pad_maximum_fusion.refs_0_), channel_id=1, source_target_pairs={{0,64},{64,128},{128,192},{192,0},{1,65},{65,129},{129,193},{193,1... | collective-permute-start | bytes 2359304 | tf_op jit(solution)/shard_map/ppermute | solution.py:331
  61.7 23.4 %collective-permute-start.8 = (bf16[4,3,128,256]{3,2,1,0:T(8,128)(2,1)S(1)}, bf16[4,3,128,256]{3,2,1,0:T(8,128)(2,1)S(1)}, u32[]{:S(2)}, u32[]{:S(2)}) collective-permute-start(bf16[4,3,128,256]{3,2,1,0:T(8,128)(2,1)S(1)} %pad_maximum_fusion.refs_0_), channel_id=1, source_target_pairs={{0,192},{64,0},{128,64},{192,128},{1,193},{65,1},{129,65},{193,129... | collective-permute-start | bytes 2359304 | tf_op jit(solution)/shard_map/ppermute | solution.py:332
  73.1 2.9 %copy-start.1 = (bf16[5120,640]{1,0:T(8,128)(2,1)S(1)}, bf16[5120,640]{1,0:T(8,128)(2,1)}, u32[]{:S(2)}) copy-start(bf16[5120,640]{1,0:T(8,128)(2,1)} %all-gather.2.cloned.1.call-done.columns_ref) | copy-start | bytes 19660804
  78.9 1.5 copy-start.2
  85.1 24.4 %collective-permute-start.9 = (bf16[768,512]{1,0:T(8,128)(2,1)}, bf16[768,512]{1,0:T(8,128)(2,1)S(1)}, u32[]{:S(2)}, u32[]{:S(2)}) collective-permute-start(bf16[768,512]{1,0:T(8,128)(2,1)} %collective-permute-done.5.refs_3_), channel_id=1, source_target_pairs={{0,1},{1,2},{2,3},{3,4},{4,5},{5,6},{6,7},{7,0},{8,9},{9,10},{10,1... | collective-permute-start | bytes 2359304 | tf_op jit(solution)/shard_map/ppermute | solution.py:338
  86.6 25.6 %collective-permute-start.10 = (bf16[768,512]{1,0:T(8,128)(2,1)}, bf16[768,512]{1,0:T(8,128)(2,1)}, u32[]{:S(2)}, u32[]{:S(2)}) collective-permute-start(bf16[768,512]{1,0:T(8,128)(2,1)} %collective-permute-done.6.refs_2_), channel_id=1, source_target_pairs={{0,7},{1,0},{2,1},{3,2},{4,3},{5,4},{6,5},{7,6},{8,15},{9,8},{10,9... | collective-permute-start | bytes 2359304 | tf_op jit(solution)/shard_map/ppermute | solution.py:339
  88.5 10.3 %collective-permute-start.12 = (bf16[2,3,128,256]{3,2,1,0:T(8,128)(2,1)S(1)}, bf16[2,3,128,256]{3,2,1,0:T(8,128)(2,1)S(1)}, u32[]{:S(2)}, u32[]{:S(2)}) collective-permute-start(bf16[2,3,128,256]{3,2,1,0:T(8,128)(2,1)S(1)} %slice.13), channel_id=1, source_target_pairs={{0,192},{64,0},{128,64},{192,128},{1,193},{65,1},{129,65},{193,129... | collective-permute-start | bytes 1179656 | tf_op jit(solution)/shard_map/ppermute | solution.py:343
  90.1 11.3 %collective-permute-start.11 = (bf16[2,3,128,256]{3,2,1,0:T(8,128)(2,1)S(1)}, bf16[2,3,128,256]{3,2,1,0:T(8,128)(2,1)S(1)}, u32[]{:S(2)}, u32[]{:S(2)}) collective-permute-start(bf16[2,3,128,256]{3,2,1,0:T(8,128)(2,1)S(1)} %slice.12), channel_id=1, source_target_pairs={{0,64},{64,128},{128,192},{192,0},{1,65},{65,129},{129,193},{193,1... | collective-permute-start | bytes 1179656 | tf_op jit(solution)/shard_map/ppermute | solution.py:342
  90.8 23.2 %collective-permute-start.15 = (bf16[4,3,128,256]{3,2,1,0:T(8,128)(2,1)S(1)}, bf16[4,3,128,256]{3,2,1,0:T(8,128)(2,1)S(1)}, u32[]{:S(2)}, u32[]{:S(2)}) collective-permute-start(bf16[4,3,128,256]{3,2,1,0:T(8,128)(2,1)S(1)} %pad_maximum_fusion.refs_0_), channel_id=1, source_target_pairs={{0,8},{8,0},{1,9},{9,1},{2,10},{10,2},{3,11},{11,3},{4,12},{12,4},... | collective-permute-start | bytes 2359304 | tf_op jit(solution)/shard_map/ppermute | solution.py:350
  98.8 18.4 %collective-permute-start.16 = (bf16[4,3,128,256]{3,2,1,0:T(8,128)(2,1)S(1)}, bf16[4,3,128,256]{3,2,1,0:T(8,128)(2,1)S(1)}, u32[]{:S(2)}, u32[]{:S(2)}) collective-permute-start(bf16[4,3,128,256]{3,2,1,0:T(8,128)(2,1)S(1)} %collective-permute-done.7.refs_1_), channel_id=1, source_target_pairs={{0,8},{8,0},{1,9},{9,1},{2,10},{10,2},{3,11},{11,3},{4,12},{12,4},... | collective-permute-start | bytes 2359304 | tf_op jit(solution)/shard_map/ppermute | solution.py:350
  101.4 15.8 %collective-permute-start.18 = (bf16[4,3,128,256]{3,2,1,0:T(8,128)(2,1)S(1)}, bf16[4,3,128,256]{3,2,1,0:T(8,128)(2,1)S(1)}, u32[]{:S(2)}, u32[]{:S(2)}) collective-permute-start(bf16[4,3,128,256]{3,2,1,0:T(8,128)(2,1)S(1)} %collective-permute-done.8.refs_3_), channel_id=1, source_target_pairs={{0,8},{8,0},{1,9},{9,1},{2,10},{10,2},{3,11},{11,3},{4,12},{12,4},... | collective-permute-start | bytes 2359304 | tf_op jit(solution)/shard_map/ppermute | solution.py:350
  112.2 5.0 %collective-permute-start.17 = (bf16[4,3,128,256]{3,2,1,0:T(8,128)(2,1)S(1)}, bf16[4,3,128,256]{3,2,1,0:T(8,128)(2,1)S(1)}, u32[]{:S(2)}, u32[]{:S(2)}) collective-permute-start(bf16[4,3,128,256]{3,2,1,0:T(8,128)(2,1)S(1)} %pad_maximum_fusion.1.refs_2_), channel_id=1, source_target_pairs={{0,8},{8,0},{1,9},{9,1},{2,10},{10,2},{3,11},{11,3},{4,12},{12,4},... | collective-permute-start | bytes 2359304 | tf_op jit(solution)/shard_map/ppermute | solution.py:350
  112.3 22.0 %collective-permute-start.13 = (bf16[384,512]{1,0:T(8,128)(2,1)S(1)}, bf16[384,512]{1,0:T(8,128)(2,1)S(1)}, u32[]{:S(2)}, u32[]{:S(2)}) collective-permute-start(bf16[384,512]{1,0:T(8,128)(2,1)S(1)} %slice.14), channel_id=1, source_target_pairs={{0,1},{1,2},{2,3},{3,4},{4,5},{5,6},{6,7},{7,0},{8,9},{9,10},{10,1... | collective-permute-start | bytes 1179656 | tf_op jit(solution)/shard_map/ppermute | solution.py:354
  114.0 4.2 %copy-start.4 = (bf16[32,24,512]{2,1,0:T(8,128)(2,1)S(1)}, bf16[32,24,512]{2,1,0:T(8,128)(2,1)}, u32[]{:S(2)}) copy-start(bf16[32,24,512]{2,1,0:T(8,128)(2,1)} %copy-done.3) | copy-start | bytes 2359300
  114.1 21.0 %collective-permute-start.14 = (bf16[384,512]{1,0:T(8,128)(2,1)S(1)}, bf16[384,512]{1,0:T(8,128)(2,1)S(1)}, u32[]{:S(2)}, u32[]{:S(2)}) collective-permute-start(bf16[384,512]{1,0:T(8,128)(2,1)S(1)} %slice.15), channel_id=1, source_target_pairs={{0,7},{1,0},{2,1},{3,2},{4,3},{5,4},{6,5},{7,6},{8,15},{9,8},{10,9... | collective-permute-start | bytes 1179656 | tf_op jit(solution)/shard_map/ppermute | solution.py:355
Sparse Core Ops, SparseCore 0:
  10.6 62.4 all-gather.1
  88.5 53.7 reduce-scatter.1

commit v5 on v4

--- a/solution.py
+++ b/solution.py
@@ -236,13 +236,20 @@
     return out.transpose(0, 2, 1, 3)
 
 
-def norm_kernel(pair_ref, resid_ref, gain_ref, score_ref, sum_ref, hidden_ref, votes_ref):
+def normed_rows(resid_ref, gain_ref, sum_ref):
     mixed = resid_ref[...].astype(jnp.float32) + sum_ref[...].astype(jnp.float32)
     squares = jnp.sum(mixed * mixed, axis=-1, keepdims=True)
     scale = lax.rsqrt(squares * (1.0 / mixed.shape[1]) + 1e-05)
-    normed = mixed * scale * gain_ref[...].astype(jnp.float32)
-    hidden_ref[...] = normed.astype(hidden_ref.dtype)
-    logit = jnp.sum(normed[:1] * score_ref[...].astype(jnp.float32), axis=-1, keepdims=True)
+    return mixed * scale * gain_ref[...].astype(jnp.float32)
+
+
+def norm_kernel(resid_ref, gain_ref, sum_ref, hidden_ref):
+    hidden_ref[...] = normed_rows(resid_ref, gain_ref, sum_ref).astype(hidden_ref.dtype)
+
+
+def vote_kernel(pair_ref, resid_ref, gain_ref, score_ref, sum_ref, votes_ref):
+    normed = normed_rows(resid_ref, gain_ref, sum_ref)[:1]
+    logit = jnp.sum(normed * score_ref[...].astype(jnp.float32), axis=-1, keepdims=True)
     cand = lax.broadcasted_iota(jnp.int32, votes_ref.shape, 0)
     prompt = lax.broadcasted_iota(jnp.int32, votes_ref.shape, 1)
     own = prompt == pair_ref[0, 0]
@@ -251,19 +258,32 @@
     votes_ref[...] = upward - downward
 
 
-def norm_and_vote(pair_index, resid, gain, score, part_sum, prompts, cands):
+def norm(resid, gain, part_sum):
     rows, width = resid.shape
     vmem = pl.BlockSpec(memory_space=pltpu.VMEM)
     return pl.pallas_call(
         norm_kernel,
-        out_shape=(
-            jax.ShapeDtypeStruct((rows, width), jnp.bfloat16),
-            jax.ShapeDtypeStruct((cands, prompts), jnp.float32),
-        ),
-        in_specs=[pl.BlockSpec(memory_space=pltpu.SMEM)] + [vmem] * 4,
-        out_specs=(vmem, vmem),
+        out_shape=jax.ShapeDtypeStruct((rows, width), jnp.bfloat16),
+        in_specs=[vmem] * 3,
+        out_specs=vmem,
         cost_estimate=pl.CostEstimate(
             flops=rows * width * 8, bytes_accessed=2 << 20, transcendentals=rows
+        ),
+    )(resid, gain, part_sum)
+
+
+def vote(pair_index, resid, gain, score, part_sum, prompts, cands):
+    width = resid.shape[1]
+    lead = pl.BlockSpec((16, width), lambda i: (0, 0))
+    row = pl.BlockSpec((1, width), lambda i: (0, 0))
+    return pl.pallas_call(
+        vote_kernel,
+        out_shape=jax.ShapeDtypeStruct((cands, prompts), jnp.float32),
+        grid=(1,),
+        in_specs=[pl.BlockSpec(memory_space=pltpu.SMEM), lead, row, row, lead],
+        out_specs=pl.BlockSpec((cands, prompts), lambda i: (0, 0)),
+        cost_estimate=pl.CostEstimate(
+            flops=width * 128, bytes_accessed=1 << 18, transcendentals=16
         ),
     )(pair_index, resid, gain, score, part_sum)
 
@@ -323,16 +343,16 @@
     x_after = lax.ppermute(own_slab, "x", ring(NX, -1))
     x_across = lax.ppermute(x_before, "x", ring(NX, 1))
     strip = jnp.concatenate([own_slab, x_before, x_across, x_after], axis=0)
-    lower, upper, strip, context = together(lower, upper, strip, context)
+    lower, upper, strip = together(lower, upper, strip)
     blocks = {1: upper, NZ - 1: lower, 0: own}
 
     lower = lax.ppermute(lower, "z", ring(NZ, 1))
     upper = lax.ppermute(upper, "z", ring(NZ, -1))
     y_before = lax.ppermute(strip, "y", ring(NY, 1))
     y_after = lax.ppermute(strip, "y", ring(NY, -1))
+    lower, upper, y_before, y_after, context = together(lower, upper, y_before, y_after, context)
+    blocks.update({2: upper, NZ - 2: lower})
     term_rows, token = project(context, columns)
-    lower, upper, y_before, y_after, token = together(lower, upper, y_before, y_after, token)
-    blocks.update({2: upper, NZ - 2: lower})
     part_sum = lax.psum_scatter(term_rows, "z", scatter_dimension=0, tiled=True)
 
     lower = lax.ppermute(lower, "z", ring(NZ, 1))
@@ -344,7 +364,7 @@
         ],
         axis=0,
     )
-    lower, upper, y_across = together(lower, upper, y_across)
+    lower, upper, y_across, token = together(lower, upper, y_across, token)
 
     slabs = [strip, y_before, y_across, y_after]
     weights = arrange(where, token, slabs + [lax.ppermute(s, "core", ring(NC, 1)) for s in slabs])
@@ -359,19 +379,15 @@
 
     part_sum, blended_qkv = together(part_sum, blended_qkv)
     own_pairs = rank_resid.shape[0]
-    rank_hidden, votes = norm_and_vote(
-        pair_index,
-        rank_resid.reshape(own_pairs * length, -1),
-        gain_row,
-        score_row,
-        part_sum,
-        prompts,
-        cand_rank.shape[1],
-    )
-    rank_hidden = rank_hidden.reshape(rank_resid.shape)
-    votes = jnp.broadcast_to(votes[None], (NZ,) + votes.shape)
-    votes = lax.all_to_all(votes, "z", split_axis=0, concat_axis=0, tiled=True)
-    cand_score = jnp.sum(votes, axis=0).T
+    resid = rank_resid.reshape(own_pairs * length, -1)
+    votes = vote(
+        pair_index, resid, gain_row, score_row, part_sum, prompts, cand_rank.shape[1]
+    )
+    shifts = [[(i, i // 4 * 4 + (i + step) % 4) for i in range(NZ)] for step in (1, 2, 3)]
+    votes = votes + sum([lax.ppermute(votes, "z", shift) for shift in shifts])
+    votes = votes + lax.ppermute(votes, "z", ring(NZ, NZ // 2))
+    cand_score = votes.T
+    rank_hidden = norm(resid, gain_row, part_sum).reshape(rank_resid.shape)
     return (rank_hidden, cand_score, blended_qkv)
 
 

time: 169 us -> 173 us (1.024)
  blocking collectives: 13.7 us -> 0 us
  waiting for transfers between devices: 75.2 us -> 84.8 us
  starting transfers between devices: 32.5 us -> 38.7 us
    all_to_all x1 -> x0, blocking collectives: 13.7 us -> none  [body(): votes = lax.all_to_all(votes, 'z', split_axis=0, concat_axis=0, tiled=True)]
    all_gather x1, waiting for transfers between devices: 8.12 us -> 0.01 us  [body(): columns = lax.all_gather(out_weight.T, PLANE, axis=0, tiled=True)]
    ppermute x0 -> x4, starting transfers between devices: none -> 7.15 us  [the longest x3 4.21 us: body(): votes = votes + sum([lax.ppermute(votes, 'z', shift) for shift in shifts])]
    ppermute x0 -> x4, waiting for transfers between devices: none -> 7.12 us  [the longest x3 4.59 us: body(): votes = votes + sum([lax.ppermute(votes, 'z', shift) for shift in shifts])]
    reduce_scatter x1, waiting for transfers between devices: 2.43 us -> 8.09 us  [body(): part_sum = lax.psum_scatter(term_rows, 'z', scatter_dimension=0, tiled=True)]
    ppermute x2, waiting for transfers between devices: 8.05 us -> 12.8 us  [body(): lower = lax.ppermute(lower, 'z', ring(NZ, 1))]
    ppermute x1, waiting for transfers between devices: 0.01 us -> 3.98 us  [body(): upper = lax.ppermute(own, 'z', ring(NZ, -1))]
    ppermute x1, waiting for transfers between devices: 0.01 us -> 3.1 us  [body(): y_after = lax.ppermute(strip, 'y', ring(NY, -1))]
  transfers between devices with their start and end apart: 22 -> 26, of which waited for: 13 -> 17; matrix products, arithmetic and copies ran while one was open for 3% -> 3% of each run, Pallas kernels for 11% -> 12%
where the time goes in v5:
time: 173 us
  waiting for transfers between devices  84.8 us (49%)
  starting transfers between devices  38.7 us (22%)
  Pallas kernels  21.8 us (13%)
  between operations  14.3 us (8%)
  local copies, waits for them, and re-layouts  9.71 us (6%)
  other arithmetic  2.39 us (1%)
    ppermute x2, waiting for transfers between devices, body(): lower = lax.ppermute(lower, 'z', ring(NZ, 1))  12.8 us
    ppermute x1, waiting for transfers between devices, body(): low = lax.ppermute(lower[:half], 'z', ring(NZ, 1))  11.9 us
    all_to_all x1, waiting for transfers between devices, body(): lax.all_to_all(outgoing.reshape(prompts, -1, features), PLANE, split_axis...  10.9 us
    reduce_scatter x1, waiting for transfers between devices, body(): part_sum = lax.psum_scatter(term_rows, 'z', scatter_dimension=0, tiled=True)  8.09 us
    all_to_all x1, starting transfers between devices, body(): lax.all_to_all(outgoing.reshape(prompts, -1, features), PLANE, split_axis...  7.75 us
    ppermute x1, starting transfers between devices, body(): upper = lax.ppermute(own, 'z', ring(NZ, -1))  6.66 us
    ppermute x2, starting transfers between devices, body(): upper = lax.ppermute(upper, 'z', ring(NZ, -1))  6.47 us
    ppermute x1, waiting for transfers between devices, body(): lax.ppermute(y_after[2:], 'y', ring(NY, -1))  6.41 us
  transfers between devices with their start and end apart: 26, of which 17 were waited for; matrix products, arithmetic and copies ran while one was open for 3% of the time, Pallas kernels for 12%

profile of v5, /device:TPU:2, one launch (start us, length us, event | category | flops | bytes accessed | tf_op | source)
XLA Modules:
  0.0 172.7 jit_solution(10042272077137949096)
XLA Ops:
  7.9 3.8 %shard_map.157 = bf16[96,8,512]{2,1,0:T(8,128)(2,1)} custom-call(s32[1,32]{1,0:T(1,128)} %owner_ref.1, s32[8,32]{1,0:T(8,128)} %bitcast.75, s32[8,32]{1,0:T(8,128)} %bitcast.76, bf16[256,8,512]{2,1,0:T(8,128)(2,1)} %bitcast.69), custom_call_target="tpu_custom_call" | custom-call | bytes 3145728 | tf_op jit(solution)/shard_map/pallas_call | solution.py:61
  11.7 7.8 %all-to-all-start = ((bf16[32,24,512]{2,1,0:T(8,128)(2,1)}), bf16[32,24,512]{2,1,0:T(8,128)(2,1)S(1)}, u32[]{:S(2)}, u32[]{:S(2)}) async-start(bf16[32,24,512]{2,1,0:T(8,128)(2,1)} %bitcast.68), calls=%async_computation | async-start | bytes 1572864 | tf_op jit(solution)/shard_map/all_to_all | solution.py:322
  23.1 10.9 %all-to-all-done = bf16[32,24,512]{2,1,0:T(8,128)(2,1)S(1)} async-done(((bf16[32,24,512]{2,1,0:T(8,128)(2,1)}), bf16[32,24,512]{2,1,0:T(8,128)(2,1)S(1)}, u32[]{:S(2)}, u32[]{:S(2)}) %all-to-all-start) | async-done | bytes 786464 | tf_op jit(solution)/shard_map/all_to_all | solution.py:322
  33.9 6.7 %collective-permute-start.1 = (bf16[768,512]{1,0:T(8,128)(2,1)S(1)}, bf16[768,512]{1,0:T(8,128)(2,1)S(1)}, u32[]{:S(2)}, u32[]{:S(2)}) collective-permute-start(bf16[768,512]{1,0:T(8,128)(2,1)S(1)} %bitcast.65), channel_id=1, source_target_pairs={{0,7},{1,0},{2,1},{3,2},{4,3},{5,4},{6,5},{7,6},{8,15},{9,8},{10,9... | collective-permute-start | bytes 2359304 | tf_op jit(solution)/shard_map/ppermute | solution.py:341
  40.6 2.0 %collective-permute-start.4 = (bf16[1,3,128,256]{3,2,1,0:T(8,128)(2,1)S(1)}, bf16[1,3,128,256]{3,2,1,0:T(8,128)(2,1)S(1)}, u32[]{:S(2)}, u32[]{:S(2)}) collective-permute-start(bf16[1,3,128,256]{3,2,1,0:T(8,128)(2,1)S(1)} %fusion.11), channel_id=1, source_target_pairs={{0,48},{16,0},{32,16},{48,32},{1,49},{17,1},{33,17},{49,33},{2,50}... | collective-permute-start | bytes 589832 | tf_op jit(solution)/shard_map/ppermute | solution.py:343
  42.6 4.7 %collective-permute-done.2 = bf16[1,3,128,256]{3,2,1,0:T(8,128)(2,1)S(1)} collective-permute-done((bf16[1,3,128,256]{3,2,1,0:T(8,128)(2,1)S(1)}, bf16[1,3,128,256]{3,2,1,0:T(8,128)(2,1)S(1)}, u32[]{:S(2)}, u32[]{:S(2)}) %collective-permute-start.2) | collective-permute-done | bytes 196640 | tf_op jit(solution)/shard_map/ppermute | solution.py:342
  47.6 6.1 %collective-permute-done.3 = bf16[1,3,128,256]{3,2,1,0:T(8,128)(2,1)S(1)} collective-permute-done((bf16[1,3,128,256]{3,2,1,0:T(8,128)(2,1)S(1)}, bf16[1,3,128,256]{3,2,1,0:T(8,128)(2,1)S(1)}, u32[]{:S(2)}, u32[]{:S(2)}) %collective-permute-start.3) | collective-permute-done | bytes 196640 | tf_op jit(solution)/shard_map/ppermute | solution.py:344
  53.7 4.0 %collective-permute-done.1.refs_1_ = bf16[768,512]{1,0:T(8,128)(2,1)S(1)} collective-permute-done((bf16[768,512]{1,0:T(8,128)(2,1)S(1)}, bf16[768,512]{1,0:T(8,128)(2,1)S(1)}, u32[]{:S(2)}, u32[]{:S(2)}) %collective-permute-start.1) | collective-permute-done | bytes 786464 | tf_op jit(solution)/shard_map/ppermute | solution.py:341
  57.7 3.4 %collective-permute-done.refs_4_ = bf16[768,512]{1,0:T(8,128)(2,1)S(1)} collective-permute-done((bf16[768,512]{1,0:T(8,128)(2,1)S(1)}, bf16[768,512]{1,0:T(8,128)(2,1)S(1)}, u32[]{:S(2)}, u32[]{:S(2)}) %collective-permute-start) | collective-permute-done | bytes 786464 | tf_op jit(solution)/shard_map/ppermute | solution.py:340
  62.0 3.2 %collective-permute-start.6 = (bf16[768,512]{1,0:T(8,128)(2,1)S(1)}, bf16[768,512]{1,0:T(8,128)(2,1)}, u32[]{:S(2)}, u32[]{:S(2)}) collective-permute-start(bf16[768,512]{1,0:T(8,128)(2,1)S(1)} %collective-permute-done.1.refs_1_), channel_id=1, source_target_pairs={{0,7},{1,0},{2,1},{3,2},{4,3},{5,4},{6,5},{7,6},{8,15},{9,8},{10,9... | collective-permute-start | bytes 2359304 | tf_op jit(solution)/shard_map/ppermute | solution.py:350
  66.1 1.2 collective-permute-start.8
  68.2 12.8 %collective-permute-done.5.refs_3_ = bf16[768,512]{1,0:T(8,128)(2,1)} collective-permute-done((bf16[768,512]{1,0:T(8,128)(2,1)S(1)}, bf16[768,512]{1,0:T(8,128)(2,1)}, u32[]{:S(2)}, u32[]{:S(2)}) %collective-permute-start.5) | collective-permute-done | bytes 786464 | tf_op jit(solution)/shard_map/ppermute | solution.py:349
  81.1 3.1 %collective-permute-done.8.refs_3_ = bf16[4,3,128,256]{3,2,1,0:T(8,128)(2,1)S(1)} collective-permute-done((bf16[4,3,128,256]{3,2,1,0:T(8,128)(2,1)S(1)}, bf16[4,3,128,256]{3,2,1,0:T(8,128)(2,1)S(1)}, u32[]{:S(2)}, u32[]{:S(2)}) %collective-permute-start.8) | collective-permute-done | bytes 786464 | tf_op jit(solution)/shard_map/ppermute | solution.py:352
  84.2 2.7 %collective-permute-done.7.refs_1_ = bf16[4,3,128,256]{3,2,1,0:T(8,128)(2,1)S(1)} collective-permute-done((bf16[4,3,128,256]{3,2,1,0:T(8,128)(2,1)S(1)}, bf16[4,3,128,256]{3,2,1,0:T(8,128)(2,1)S(1)}, u32[]{:S(2)}, u32[]{:S(2)}) %collective-permute-start.7) | collective-permute-done | bytes 786464 | tf_op jit(solution)/shard_map/ppermute | solution.py:351
  86.9 3.2 %collective-permute-start.10 = (bf16[768,512]{1,0:T(8,128)(2,1)}, bf16[768,512]{1,0:T(8,128)(2,1)}, u32[]{:S(2)}, u32[]{:S(2)}) collective-permute-start(bf16[768,512]{1,0:T(8,128)(2,1)} %collective-permute-done.6.refs_2_), channel_id=1, source_target_pairs={{0,7},{1,0},{2,1},{3,2},{4,3},{5,4},{6,5},{7,6},{8,15},{9,8},{10,9... | collective-permute-start | bytes 2359304 | tf_op jit(solution)/shard_map/ppermute | solution.py:359
  90.1 2.9 %copy-done.1 = bf16[5120,640]{1,0:T(8,128)(2,1)S(1)} copy-done((bf16[5120,640]{1,0:T(8,128)(2,1)S(1)}, bf16[5120,640]{1,0:T(8,128)(2,1)}, u32[]{:S(2)}) %copy-start.1) | copy-done | bytes 6553624
  93.0 3.0 %shard_map.158 = (bf16[256,5120]{1,0:T(8,128)(2,1)S(1)}, f32[8,128]{1,0:T(8,128)S(1)}) custom-call(bf16[256,640]{1,0:T(8,128)(2,1)S(1)} %bitcast.64, bf16[5120,640]{1,0:T(8,128)(2,1)S(1)} %copy-done.1), custom_call_target="tpu_custom_call" | custom-call | flops 1677721600 | bytes 9437184 | tf_op jit(solution)/shard_map/pallas_call | solution.py:113
  96.1 1.5 copy-done.2
  98.0 2.0 %collective-permute-start.11 = (bf16[2,3,128,256]{3,2,1,0:T(8,128)(2,1)S(1)}, bf16[2,3,128,256]{3,2,1,0:T(8,128)(2,1)S(1)}, u32[]{:S(2)}, u32[]{:S(2)}) collective-permute-start(bf16[2,3,128,256]{3,2,1,0:T(8,128)(2,1)S(1)} %slice.12), channel_id=1, source_target_pairs={{0,64},{64,128},{128,192},{192,0},{1,65},{65,129},{129,193},{193,1... | collective-permute-start | bytes 1179656 | tf_op jit(solution)/shard_map/ppermute | solution.py:362
  100.0 6.4 %collective-permute-done.12 = bf16[2,3,128,256]{3,2,1,0:T(8,128)(2,1)S(1)} collective-permute-done((bf16[2,3,128,256]{3,2,1,0:T(8,128)(2,1)S(1)}, bf16[2,3,128,256]{3,2,1,0:T(8,128)(2,1)S(1)}, u32[]{:S(2)}, u32[]{:S(2)}) %collective-permute-start.12) | collective-permute-done | bytes 393248 | tf_op jit(solution)/shard_map/ppermute | solution.py:363
  106.4 2.8 %collective-permute-done.11 = bf16[2,3,128,256]{3,2,1,0:T(8,128)(2,1)S(1)} collective-permute-done((bf16[2,3,128,256]{3,2,1,0:T(8,128)(2,1)S(1)}, bf16[2,3,128,256]{3,2,1,0:T(8,128)(2,1)S(1)}, u32[]{:S(2)}, u32[]{:S(2)}) %collective-permute-start.11) | collective-permute-done | bytes 393248 | tf_op jit(solution)/shard_map/ppermute | solution.py:362
  112.1 3.2 %collective-permute-start.14 = (bf16[384,512]{1,0:T(8,128)(2,1)S(1)}, bf16[384,512]{1,0:T(8,128)(2,1)S(1)}, u32[]{:S(2)}, u32[]{:S(2)}) collective-permute-start(bf16[384,512]{1,0:T(8,128)(2,1)S(1)} %slice.15), channel_id=1, source_target_pairs={{0,7},{1,0},{2,1},{3,2},{4,3},{5,4},{6,5},{7,6},{8,15},{9,8},{10,9... | collective-permute-start | bytes 1179656 | tf_op jit(solution)/shard_map/ppermute | solution.py:375
  116.4 5.0 %shard_map.160 = (f32[3,768,256]{2,1,0:T(8,128)S(1)}, f32[768,128]{1,0:T(8,128)S(1)}) custom-call(bf16[768,512]{1,0:T(8,128)(2,1)S(1)} %bitcast.67, bf16[768,512]{1,0:T(8,128)(2,1)S(1)} %copy-done.6, bf16[768,512]{1,0:T(8,128)(2,1)} %collective-permute-done.6.refs_2_, bf16[768,512]{1,0:T(8,128)(2,1)} %collective-permute-done.5.refs_3_, ...), custom_call_target="tpu_custom_call" | custom-call | flops 3019898880 | bytes 12582912 | tf_op jit(solution)/shard_map/pallas_call | solution.py:186
  121.4 11.9 %collective-permute-done.13.refs_2_ = bf16[384,512]{1,0:T(8,128)(2,1)S(1)} collective-permute-done((bf16[384,512]{1,0:T(8,128)(2,1)S(1)}, bf16[384,512]{1,0:T(8,128)(2,1)S(1)}, u32[]{:S(2)}, u32[]{:S(2)}) %collective-permute-start.13) | collective-permute-done | bytes 393248 | tf_op jit(solution)/shard_map/ppermute | solution.py:374
  133.3 5.0 %shard_map.161 = bf16[32,3,24,256]{3,2,1,0:T(8,128)(2,1)} custom-call(bf16[768,512]{1,0:T(8,128)(2,1)} %collective-permute-done.10.refs_0_, bf16[768,512]{1,0:T(8,128)(2,1)} %collective-permute-done.9.refs_1_, bf16[384,512]{1,0:T(8,128)(2,1)S(1)} %collective-permute-done.13.refs_2_, bf16[384,512]{1,0:T(8,128)(2,1)S(1)} %collective-permute-done.14.refs_3_, ...), custom_call_target="tpu_custom_call" | custom-call | flops 36238786560 | bytes 12582912 | tf_op jit(solution)/shard_map/pallas_call | solution.py:215
  138.3 8.1 %reduce-scatter.2.cloned.1.call-done.sum_ref = bf16[32,5120]{1,0:T(8,128)(2,1)} async-done(((bf16[256,5120]{1,0:T(8,128)(2,1)}), bf16[32,5120]{1,0:T(8,128)(2,1)}) %reduce-scatter.2.cloned.1.call-update) | async-done | bytes 327696 | tf_op jit(solution)/shard_map/reduce_scatter | solution.py:356
  146.4 1.9 %shard_map.163 = f32[8,32]{1,0:T(8,128)} custom-call(s32[1,3]{1,0:T(1,128)} %pair_ref.1, bf16[32,5120]{1,0:T(8,128)(2,1)} %bitcast.71, bf16[1,5120]{1,0:T(2,128)(2,1)} %reshape.50.gain_ref, bf16[1,5120]{1,0:T(2,128)(2,1)} %reshape.51.score_ref, bf16[32,5120]{1,0:T(8,128)(2,1)} %reduce-scatter.2.cloned.1.call-done.sum_ref), custom_call_target="tpu_custom_call" | custom-call | flops 655360 | bytes 262144 | tf_op jit(solution)/shard_map/pallas_call | solution.py:279
  148.3 3.2 %collective-permute-start.21 = (f32[8,32]{1,0:T(8,128)}, f32[8,32]{1,0:T(8,128)S(1)}, u32[]{:S(2)}, u32[]{:S(2)}) collective-permute-start(f32[8,32]{1,0:T(8,128)} %shard_map.163), channel_id=1, source_target_pairs={{0,3},{1,0},{2,1},{3,2},{4,7},{5,4},{6,5},{7,6},{8,11},{9,8},{10,9... | collective-permute-start | bytes 3080 | tf_op jit(solution)/shard_map/ppermute | solution.py:387
  153.0 3.2 %collective-permute-done.20 = f32[8,32]{1,0:T(8,128)S(1)} collective-permute-done((f32[8,32]{1,0:T(8,128)}, f32[8,32]{1,0:T(8,128)S(1)}, u32[]{:S(2)}, u32[]{:S(2)}) %collective-permute-start.20) | collective-permute-done | bytes 1056 | tf_op jit(solution)/shard_map/ppermute | solution.py:387
  157.8 2.9 %collective-permute-start.22 = (f32[8,32]{1,0:T(8,128)S(1)}, f32[8,32]{1,0:T(8,128)S(1)}, u32[]{:S(2)}, u32[]{:S(2)}) collective-permute-start(f32[8,32]{1,0:T(8,128)S(1)} %add_add_fusion), channel_id=1, source_target_pairs={{0,4},{1,5},{2,6},{3,7},{4,0},{5,1},{6,2},{7,3},{8,12},{9,13},{10,... | collective-permute-start | bytes 3080 | tf_op jit(solution)/shard_map/ppermute | solution.py:388
  160.7 2.0 %shard_map.162 = bf16[32,5120]{1,0:T(8,128)(2,1)} custom-call(bf16[32,5120]{1,0:T(8,128)(2,1)} %bitcast.72, bf16[1,5120]{1,0:T(2,128)(2,1)} %reshape.50.gain_ref, bf16[32,5120]{1,0:T(8,128)(2,1)} %reduce-scatter.2.cloned.1.call-done.sum_ref), custom_call_target="tpu_custom_call" | custom-call | flops 1310720 | bytes 2097152 | tf_op jit(solution)/shard_map/pallas_call | solution.py:264
  162.8 2.5 %collective-permute-done.22 = f32[8,32]{1,0:T(8,128)S(1)} collective-permute-done((f32[8,32]{1,0:T(8,128)S(1)}, f32[8,32]{1,0:T(8,128)S(1)}, u32[]{:S(2)}, u32[]{:S(2)}) %collective-permute-start.22) | collective-permute-done | bytes 1056 | tf_op jit(solution)/shard_map/ppermute | solution.py:388
  (75 shorter events, 15.3 us)
Async XLA Ops:
  7.2 14.3 %copy-start = (bf16[8,32,640]{2,1,0:T(8,128)(2,1)S(1)}, bf16[8,32,640]{2,1,0:T(8,128)(2,1)}, u32[]{:S(2)}) copy-start(bf16[8,32,640]{2,1,0:T(8,128)(2,1)} %param.16) | copy-start | bytes 983044
  7.2 12.4 %copy-start.10 = (bf16[8,32,640]{2,1,0:T(8,128)(2,1)S(1)}, bf16[8,32,640]{2,1,0:T(8,128)(2,1)}, u32[]{:S(2)}) copy-start(bf16[8,32,640]{2,1,0:T(8,128)(2,1)} %param.14) | copy-start | bytes 983044
  7.2 12.4 %copy-start.9 = (bf16[8,32,640]{2,1,0:T(8,128)(2,1)S(1)}, bf16[8,32,640]{2,1,0:T(8,128)(2,1)}, u32[]{:S(2)}) copy-start(bf16[8,32,640]{2,1,0:T(8,128)(2,1)} %param.15) | copy-start | bytes 983044
  7.2 82.9 %all-gather.2.cloned.1.call-start = ((), (), s32[]{:S(2)}) async-start(), calls=%async_computation.2 | async-start | bytes 6758400 | tf_op jit(solution)/shard_map/all_gather | solution.py:316
  11.7 8.5 %copy-start.12 = (bf16[5120]{0:T(1024)(128)(2,1)S(1)}, bf16[5120]{0:T(1024)(128)(2,1)}, u32[]{:S(2)}) copy-start(bf16[5120]{0:T(1024)(128)(2,1)} %param.19) | copy-start | bytes 30724
  11.7 9.1 %copy-start.13 = (bf16[5120]{0:T(1024)(128)(2,1)S(1)}, bf16[5120]{0:T(1024)(128)(2,1)}, u32[]{:S(2)}) copy-start(bf16[5120]{0:T(1024)(128)(2,1)} %param.20) | copy-start | bytes 30724
  11.7 22.2 %all-to-all-start = ((bf16[32,24,512]{2,1,0:T(8,128)(2,1)}), bf16[32,24,512]{2,1,0:T(8,128)(2,1)S(1)}, u32[]{:S(2)}, u32[]{:S(2)}) async-start(bf16[32,24,512]{2,1,0:T(8,128)(2,1)} %bitcast.68), calls=%async_computation | async-start | bytes 1572864 | tf_op jit(solution)/shard_map/all_to_all | solution.py:322
  19.5 126.9 %reduce-scatter.2.cloned.1.call-start = ((), (), s32[]{:S(2)}) async-start(), calls=%async_computation.3 | async-start | bytes 2949120 | tf_op jit(solution)/shard_map/reduce_scatter | solution.py:356
  33.9 27.2 %copy-start.3 = (bf16[32,24,512]{2,1,0:T(8,128)(2,1)}, bf16[32,24,512]{2,1,0:T(8,128)(2,1)S(1)}, u32[]{:S(2)}) copy-start(bf16[32,24,512]{2,1,0:T(8,128)(2,1)S(1)} %all-to-all-done) | copy-start | bytes 2359300
  33.9 23.8 %collective-permute-start.1 = (bf16[768,512]{1,0:T(8,128)(2,1)S(1)}, bf16[768,512]{1,0:T(8,128)(2,1)S(1)}, u32[]{:S(2)}, u32[]{:S(2)}) collective-permute-start(bf16[768,512]{1,0:T(8,128)(2,1)S(1)} %bitcast.65), channel_id=1, source_target_pairs={{0,7},{1,0},{2,1},{3,2},{4,3},{5,4},{6,5},{7,6},{8,15},{9,8},{10,9... | collective-permute-start | bytes 2359304 | tf_op jit(solution)/shard_map/ppermute | solution.py:341
  40.6 20.5 %collective-permute-start = (bf16[768,512]{1,0:T(8,128)(2,1)S(1)}, bf16[768,512]{1,0:T(8,128)(2,1)S(1)}, u32[]{:S(2)}, u32[]{:S(2)}) collective-permute-start(bf16[768,512]{1,0:T(8,128)(2,1)S(1)} %bitcast.66), channel_id=1, source_target_pairs={{0,1},{1,2},{2,3},{3,4},{4,5},{5,6},{6,7},{7,0},{8,9},{9,10},{10,1... | collective-permute-start | bytes 2359304 | tf_op jit(solution)/shard_map/ppermute | solution.py:340
  40.6 6.7 %collective-permute-start.2 = (bf16[1,3,128,256]{3,2,1,0:T(8,128)(2,1)S(1)}, bf16[1,3,128,256]{3,2,1,0:T(8,128)(2,1)S(1)}, u32[]{:S(2)}, u32[]{:S(2)}) collective-permute-start(bf16[1,3,128,256]{3,2,1,0:T(8,128)(2,1)S(1)} %fusion.11), channel_id=1, source_target_pairs={{0,16},{16,32},{32,48},{48,0},{1,17},{17,33},{33,49},{49,1},{2,18}... | collective-permute-start | bytes 589832 | tf_op jit(solution)/shard_map/ppermute | solution.py:342
  40.6 7.0 %collective-permute-start.4 = (bf16[1,3,128,256]{3,2,1,0:T(8,128)(2,1)S(1)}, bf16[1,3,128,256]{3,2,1,0:T(8,128)(2,1)S(1)}, u32[]{:S(2)}, u32[]{:S(2)}) collective-permute-start(bf16[1,3,128,256]{3,2,1,0:T(8,128)(2,1)S(1)} %fusion.11), channel_id=1, source_target_pairs={{0,48},{16,0},{32,16},{48,32},{1,49},{17,1},{33,17},{49,33},{2,50}... | collective-permute-start | bytes 589832 | tf_op jit(solution)/shard_map/ppermute | solution.py:343
  47.3 6.3 %collective-permute-start.3 = (bf16[1,3,128,256]{3,2,1,0:T(8,128)(2,1)S(1)}, bf16[1,3,128,256]{3,2,1,0:T(8,128)(2,1)S(1)}, u32[]{:S(2)}, u32[]{:S(2)}) collective-permute-start(bf16[1,3,128,256]{3,2,1,0:T(8,128)(2,1)S(1)} %collective-permute-done.2), channel_id=1, source_target_pairs={{0,16},{16,32},{32,48},{48,0},{1,17},{17,33},{33,49},{49,1},{2,18}... | collective-permute-start | bytes 589832 | tf_op jit(solution)/shard_map/ppermute | solution.py:344
  61.1 19.9 %collective-permute-start.5 = (bf16[768,512]{1,0:T(8,128)(2,1)S(1)}, bf16[768,512]{1,0:T(8,128)(2,1)}, u32[]{:S(2)}, u32[]{:S(2)}) collective-permute-start(bf16[768,512]{1,0:T(8,128)(2,1)S(1)} %collective-permute-done.refs_4_), channel_id=1, source_target_pairs={{0,1},{1,2},{2,3},{3,4},{4,5},{5,6},{6,7},{7,0},{8,9},{9,10},{10,1... | collective-permute-start | bytes 2359304 | tf_op jit(solution)/shard_map/ppermute | solution.py:349
  62.0 19.0 %collective-permute-start.6 = (bf16[768,512]{1,0:T(8,128)(2,1)S(1)}, bf16[768,512]{1,0:T(8,128)(2,1)}, u32[]{:S(2)}, u32[]{:S(2)}) collective-permute-start(bf16[768,512]{1,0:T(8,128)(2,1)S(1)} %collective-permute-done.1.refs_1_), channel_id=1, source_target_pairs={{0,7},{1,0},{2,1},{3,2},{4,3},{5,4},{6,5},{7,6},{8,15},{9,8},{10,9... | collective-permute-start | bytes 2359304 | tf_op jit(solution)/shard_map/ppermute | solution.py:350
  66.1 18.0 %collective-permute-start.8 = (bf16[4,3,128,256]{3,2,1,0:T(8,128)(2,1)S(1)}, bf16[4,3,128,256]{3,2,1,0:T(8,128)(2,1)S(1)}, u32[]{:S(2)}, u32[]{:S(2)}) collective-permute-start(bf16[4,3,128,256]{3,2,1,0:T(8,128)(2,1)S(1)} %pad_maximum_fusion.refs_0_), channel_id=1, source_target_pairs={{0,192},{64,0},{128,64},{192,128},{1,193},{65,1},{129,65},{193,129... | collective-permute-start | bytes 2359304 | tf_op jit(solution)/shard_map/ppermute | solution.py:352
  67.3 19.6 %collective-permute-start.7 = (bf16[4,3,128,256]{3,2,1,0:T(8,128)(2,1)S(1)}, bf16[4,3,128,256]{3,2,1,0:T(8,128)(2,1)S(1)}, u32[]{:S(2)}, u32[]{:S(2)}) collective-permute-start(bf16[4,3,128,256]{3,2,1,0:T(8,128)(2,1)S(1)} %pad_maximum_fusion.refs_0_), channel_id=1, source_target_pairs={{0,64},{64,128},{128,192},{192,0},{1,65},{65,129},{129,193},{193,1... | collective-permute-start | bytes 2359304 | tf_op jit(solution)/shard_map/ppermute | solution.py:351
  86.9 22.4 %collective-permute-start.9 = (bf16[768,512]{1,0:T(8,128)(2,1)}, bf16[768,512]{1,0:T(8,128)(2,1)}, u32[]{:S(2)}, u32[]{:S(2)}) collective-permute-start(bf16[768,512]{1,0:T(8,128)(2,1)} %collective-permute-done.5.refs_3_), channel_id=1, source_target_pairs={{0,1},{1,2},{2,3},{3,4},{4,5},{5,6},{6,7},{7,0},{8,9},{9,10},{10,1... | collective-permute-start | bytes 2359304 | tf_op jit(solution)/shard_map/ppermute | solution.py:358
  86.9 22.4 %collective-permute-start.10 = (bf16[768,512]{1,0:T(8,128)(2,1)}, bf16[768,512]{1,0:T(8,128)(2,1)}, u32[]{:S(2)}, u32[]{:S(2)}) collective-permute-start(bf16[768,512]{1,0:T(8,128)(2,1)} %collective-permute-done.6.refs_2_), channel_id=1, source_target_pairs={{0,7},{1,0},{2,1},{3,2},{4,3},{5,4},{6,5},{7,6},{8,15},{9,8},{10,9... | collective-permute-start | bytes 2359304 | tf_op jit(solution)/shard_map/ppermute | solution.py:359
  97.6 8.8 %collective-permute-start.12 = (bf16[2,3,128,256]{3,2,1,0:T(8,128)(2,1)S(1)}, bf16[2,3,128,256]{3,2,1,0:T(8,128)(2,1)S(1)}, u32[]{:S(2)}, u32[]{:S(2)}) collective-permute-start(bf16[2,3,128,256]{3,2,1,0:T(8,128)(2,1)S(1)} %slice.13), channel_id=1, source_target_pairs={{0,192},{64,0},{128,64},{192,128},{1,193},{65,1},{129,65},{193,129... | collective-permute-start | bytes 1179656 | tf_op jit(solution)/shard_map/ppermute | solution.py:363
  98.0 11.2 %collective-permute-start.11 = (bf16[2,3,128,256]{3,2,1,0:T(8,128)(2,1)S(1)}, bf16[2,3,128,256]{3,2,1,0:T(8,128)(2,1)S(1)}, u32[]{:S(2)}, u32[]{:S(2)}) collective-permute-start(bf16[2,3,128,256]{3,2,1,0:T(8,128)(2,1)S(1)} %slice.12), channel_id=1, source_target_pairs={{0,64},{64,128},{128,192},{192,0},{1,65},{65,129},{129,193},{193,1... | collective-permute-start | bytes 1179656 | tf_op jit(solution)/shard_map/ppermute | solution.py:362
  100.0 12.1 %collective-permute-start.15 = (bf16[4,3,128,256]{3,2,1,0:T(8,128)(2,1)S(1)}, bf16[4,3,128,256]{3,2,1,0:T(8,128)(2,1)S(1)}, u32[]{:S(2)}, u32[]{:S(2)}) collective-permute-start(bf16[4,3,128,256]{3,2,1,0:T(8,128)(2,1)S(1)} %pad_maximum_fusion.refs_0_), channel_id=1, source_target_pairs={{0,8},{8,0},{1,9},{9,1},{2,10},{10,2},{3,11},{11,3},{4,12},{12,4},... | collective-permute-start | bytes 2359304 | tf_op jit(solution)/shard_map/ppermute | solution.py:370
  106.4 8.9 %collective-permute-start.16 = (bf16[4,3,128,256]{3,2,1,0:T(8,128)(2,1)S(1)}, bf16[4,3,128,256]{3,2,1,0:T(8,128)(2,1)S(1)}, u32[]{:S(2)}, u32[]{:S(2)}) collective-permute-start(bf16[4,3,128,256]{3,2,1,0:T(8,128)(2,1)S(1)} %collective-permute-done.7.refs_1_), channel_id=1, source_target_pairs={{0,8},{8,0},{1,9},{9,1},{2,10},{10,2},{3,11},{11,3},{4,12},{12,4},... | collective-permute-start | bytes 2359304 | tf_op jit(solution)/shard_map/ppermute | solution.py:370
  109.2 6.1 %collective-permute-start.18 = (bf16[4,3,128,256]{3,2,1,0:T(8,128)(2,1)S(1)}, bf16[4,3,128,256]{3,2,1,0:T(8,128)(2,1)S(1)}, u32[]{:S(2)}, u32[]{:S(2)}) collective-permute-start(bf16[4,3,128,256]{3,2,1,0:T(8,128)(2,1)S(1)} %collective-permute-done.8.refs_3_), channel_id=1, source_target_pairs={{0,8},{8,0},{1,9},{9,1},{2,10},{10,2},{3,11},{11,3},{4,12},{12,4},... | collective-permute-start | bytes 2359304 | tf_op jit(solution)/shard_map/ppermute | solution.py:370
  109.3 6.0 %collective-permute-start.17 = (bf16[4,3,128,256]{3,2,1,0:T(8,128)(2,1)S(1)}, bf16[4,3,128,256]{3,2,1,0:T(8,128)(2,1)S(1)}, u32[]{:S(2)}, u32[]{:S(2)}) collective-permute-start(bf16[4,3,128,256]{3,2,1,0:T(8,128)(2,1)S(1)} %pad_maximum_fusion.1.refs_2_), channel_id=1, source_target_pairs={{0,8},{8,0},{1,9},{9,1},{2,10},{10,2},{3,11},{11,3},{4,12},{12,4},... | collective-permute-start | bytes 2359304 | tf_op jit(solution)/shard_map/ppermute | solution.py:370
  112.0 21.3 %collective-permute-start.13 = (bf16[384,512]{1,0:T(8,128)(2,1)S(1)}, bf16[384,512]{1,0:T(8,128)(2,1)S(1)}, u32[]{:S(2)}, u32[]{:S(2)}) collective-permute-start(bf16[384,512]{1,0:T(8,128)(2,1)S(1)} %slice.14), channel_id=1, source_target_pairs={{0,1},{1,2},{2,3},{3,4},{4,5},{5,6},{6,7},{7,0},{8,9},{9,10},{10,1... | collective-permute-start | bytes 1179656 | tf_op jit(solution)/shard_map/ppermute | solution.py:374
  112.1 21.2 %collective-permute-start.14 = (bf16[384,512]{1,0:T(8,128)(2,1)S(1)}, bf16[384,512]{1,0:T(8,128)(2,1)S(1)}, u32[]{:S(2)}, u32[]{:S(2)}) collective-permute-start(bf16[384,512]{1,0:T(8,128)(2,1)S(1)} %slice.15), channel_id=1, source_target_pairs={{0,7},{1,0},{2,1},{3,2},{4,3},{5,4},{6,5},{7,6},{8,15},{9,8},{10,9... | collective-permute-start | bytes 1179656 | tf_op jit(solution)/shard_map/ppermute | solution.py:375
  148.3 4.7 %collective-permute-start.21 = (f32[8,32]{1,0:T(8,128)}, f32[8,32]{1,0:T(8,128)S(1)}, u32[]{:S(2)}, u32[]{:S(2)}) collective-permute-start(f32[8,32]{1,0:T(8,128)} %shard_map.163), channel_id=1, source_target_pairs={{0,3},{1,0},{2,1},{3,2},{4,7},{5,4},{6,5},{7,6},{8,11},{9,8},{10,9... | collective-permute-start | bytes 3080 | tf_op jit(solution)/shard_map/ppermute | solution.py:387
  151.5 4.7 %collective-permute-start.20 = (f32[8,32]{1,0:T(8,128)}, f32[8,32]{1,0:T(8,128)S(1)}, u32[]{:S(2)}, u32[]{:S(2)}) collective-permute-start(f32[8,32]{1,0:T(8,128)} %shard_map.163), channel_id=1, source_target_pairs={{0,2},{1,3},{2,0},{3,1},{4,6},{5,7},{6,4},{7,5},{8,10},{9,11},{10,... | collective-permute-start | bytes 3080 | tf_op jit(solution)/shard_map/ppermute | solution.py:387
  151.5 5.6 %collective-permute-start.19 = (f32[8,32]{1,0:T(8,128)}, f32[8,32]{1,0:T(8,128)S(1)}, u32[]{:S(2)}, u32[]{:S(2)}) collective-permute-start(f32[8,32]{1,0:T(8,128)} %shard_map.163), channel_id=1, source_target_pairs={{0,1},{1,2},{2,3},{3,0},{4,5},{5,6},{6,7},{7,4},{8,9},{9,10},{10,1... | collective-permute-start | bytes 3080 | tf_op jit(solution)/shard_map/ppermute | solution.py:387
  157.8 7.5 %collective-permute-start.22 = (f32[8,32]{1,0:T(8,128)S(1)}, f32[8,32]{1,0:T(8,128)S(1)}, u32[]{:S(2)}, u32[]{:S(2)}) collective-permute-start(f32[8,32]{1,0:T(8,128)S(1)} %add_add_fusion), channel_id=1, source_target_pairs={{0,4},{1,5},{2,6},{3,7},{4,0},{5,1},{6,2},{7,3},{8,12},{9,13},{10,... | collective-permute-start | bytes 3080 | tf_op jit(solution)/shard_map/ppermute | solution.py:388
  (8 other events, 22.0 us)
Sparse Core Ops, SparseCore 0:
  10.6 59.5 all-gather.1
  97.7 48.6 reduce-scatter.1

commit v6 on v4

--- a/solution.py
+++ b/solution.py
@@ -331,7 +331,7 @@
     y_before = lax.ppermute(strip, "y", ring(NY, 1))
     y_after = lax.ppermute(strip, "y", ring(NY, -1))
     term_rows, token = project(context, columns)
-    lower, upper, y_before, y_after, token = together(lower, upper, y_before, y_after, token)
+    lower, upper, token = together(lower, upper, token)
     blocks.update({2: upper, NZ - 2: lower})
     part_sum = lax.psum_scatter(term_rows, "z", scatter_dimension=0, tiled=True)
 

time: 169 us -> 168 us (level)
  waiting for transfers between devices: 75.2 us -> 72.2 us
    ppermute x2, waiting for transfers between devices: 8.05 us -> 2.42 us  [body(): lower = lax.ppermute(lower, 'z', ring(NZ, 1))]
    reduce_scatter x1, waiting for transfers between devices: 2.43 us -> 7.2 us  [body(): part_sum = lax.psum_scatter(term_rows, 'z', scatter_dimension=0, tiled=True)]
    ppermute x1, waiting for transfers between devices: 4.62 us -> 0.01 us  [body(): y_before = lax.ppermute(strip, 'y', ring(NY, 1))]
    ppermute x2, starting transfers between devices: 1.56 us -> 3.72 us  [body(): lower = lax.ppermute(lower, 'z', ring(NZ, 1))]
    ppermute x1, starting transfers between devices: 3.23 us -> 1.1 us  [body(): y_after = lax.ppermute(strip, 'y', ring(NY, -1))]
    ppermute x1, starting transfers between devices: 1.59 us -> 3.39 us  [body(): lax.ppermute(y_after[2:], 'y', ring(NY, -1))]
  transfers between devices with their start and end apart: 22 -> 22, of which waited for: 13 -> 12; matrix products, arithmetic and copies ran while one was open for 3% -> 3% of each run, Pallas kernels for 11% -> 11%
where the time goes in v6:
time: 168 us; the launch traced here: 166 us
  waiting for transfers between devices  72.2 us (43%)
  starting transfers between devices  33.7 us (20%)
  Pallas kernels  20.1 us (12%)
  between operations  14.3 us (9%)
  blocking collectives  13.5 us (8%)
  local copies, waits for them, and re-layouts  8.35 us (5%)
  other arithmetic  2.37 us (1%)
    all_to_all x1, blocking collectives, body(): votes = lax.all_to_all(votes, 'z', split_axis=0, concat_axis=0, tiled=True)  13.5 us
    all_to_all x1, waiting for transfers between devices, body(): lax.all_to_all(outgoing.reshape(prompts, -1, features), PLANE, split_axis...  10.7 us
    ppermute x1, waiting for transfers between devices, body(): low = lax.ppermute(lower[:half], 'z', ring(NZ, 1))  10.5 us
    all_gather x1, waiting for transfers between devices, body(): columns = lax.all_gather(out_weight.T, PLANE, axis=0, tiled=True)  8.57 us
    ppermute x1, waiting for transfers between devices, body(): lax.ppermute(y_after[2:], 'y', ring(NY, -1))  8.41 us
    all_to_all x1, starting transfers between devices, body(): lax.all_to_all(outgoing.reshape(prompts, -1, features), PLANE, split_axis...  7.62 us
    ppermute x1, waiting for transfers between devices, body(): x_across = lax.ppermute(x_before, 'x', ring(NX, 1))  7.22 us
    reduce_scatter x1, waiting for transfers between devices, body(): part_sum = lax.psum_scatter(term_rows, 'z', scatter_dimension=0, tiled=True)  7.2 us
  transfers between devices with their start and end apart: 22, of which 12 were waited for; matrix products, arithmetic and copies ran while one was open for 3% of the time, Pallas kernels for 11%

profile of v6, /device:TPU:2, one launch (start us, length us, event | category | flops | bytes accessed | tf_op | source)
XLA Modules:
  0.0 165.6 jit_solution(8276393506219964206)
XLA Ops:
  7.9 3.8 %shard_map.157 = bf16[96,8,512]{2,1,0:T(8,128)(2,1)} custom-call(s32[1,32]{1,0:T(1,128)} %owner_ref.1, s32[8,32]{1,0:T(8,128)} %bitcast.72, s32[8,32]{1,0:T(8,128)} %bitcast.73, bf16[256,8,512]{2,1,0:T(8,128)(2,1)} %bitcast.68), custom_call_target="tpu_custom_call" | custom-call | bytes 3145728 | tf_op jit(solution)/shard_map/pallas_call | solution.py:61
  11.7 7.6 %all-to-all-start = ((bf16[32,24,512]{2,1,0:T(8,128)(2,1)}), bf16[32,24,512]{2,1,0:T(8,128)(2,1)S(1)}, u32[]{:S(2)}, u32[]{:S(2)}) async-start(bf16[32,24,512]{2,1,0:T(8,128)(2,1)} %bitcast.67), calls=%async_computation | async-start | bytes 1572864 | tf_op jit(solution)/shard_map/all_to_all | solution.py:302
  23.0 10.7 %all-to-all-done = bf16[32,24,512]{2,1,0:T(8,128)(2,1)S(1)} async-done(((bf16[32,24,512]{2,1,0:T(8,128)(2,1)}), bf16[32,24,512]{2,1,0:T(8,128)(2,1)S(1)}, u32[]{:S(2)}, u32[]{:S(2)}) %all-to-all-start) | async-done | bytes 786464 | tf_op jit(solution)/shard_map/all_to_all | solution.py:302
  33.7 2.0 %collective-permute-start = (bf16[768,512]{1,0:T(8,128)(2,1)S(1)}, bf16[768,512]{1,0:T(8,128)(2,1)}, u32[]{:S(2)}, u32[]{:S(2)}) collective-permute-start(bf16[768,512]{1,0:T(8,128)(2,1)S(1)} %bitcast.64), channel_id=1, source_target_pairs={{0,1},{1,2},{2,3},{3,4},{4,5},{5,6},{6,7},{7,0},{8,9},{9,10},{10,1... | collective-permute-start | bytes 2359304 | tf_op jit(solution)/shard_map/ppermute | solution.py:320
  35.7 4.5 %collective-permute-start.1 = (bf16[768,512]{1,0:T(8,128)(2,1)S(1)}, bf16[768,512]{1,0:T(8,128)(2,1)}, u32[]{:S(2)}, u32[]{:S(2)}) collective-permute-start(bf16[768,512]{1,0:T(8,128)(2,1)S(1)} %bitcast.65), channel_id=1, source_target_pairs={{0,7},{1,0},{2,1},{3,2},{4,3},{5,4},{6,5},{7,6},{8,15},{9,8},{10,9... | collective-permute-start | bytes 2359304 | tf_op jit(solution)/shard_map/ppermute | solution.py:321
  40.3 1.9 %collective-permute-start.4 = (bf16[1,3,128,256]{3,2,1,0:T(8,128)(2,1)S(1)}, bf16[1,3,128,256]{3,2,1,0:T(8,128)(2,1)S(1)}, u32[]{:S(2)}, u32[]{:S(2)}) collective-permute-start(bf16[1,3,128,256]{3,2,1,0:T(8,128)(2,1)S(1)} %fusion.11), channel_id=1, source_target_pairs={{0,48},{16,0},{32,16},{48,32},{1,49},{17,1},{33,17},{49,33},{2,50}... | collective-permute-start | bytes 589832 | tf_op jit(solution)/shard_map/ppermute | solution.py:323
  42.2 5.0 %collective-permute-done.2 = bf16[1,3,128,256]{3,2,1,0:T(8,128)(2,1)S(1)} collective-permute-done((bf16[1,3,128,256]{3,2,1,0:T(8,128)(2,1)S(1)}, bf16[1,3,128,256]{3,2,1,0:T(8,128)(2,1)S(1)}, u32[]{:S(2)}, u32[]{:S(2)}) %collective-permute-start.2) | collective-permute-done | bytes 196640 | tf_op jit(solution)/shard_map/ppermute | solution.py:322
  47.5 7.2 %collective-permute-done.3 = bf16[1,3,128,256]{3,2,1,0:T(8,128)(2,1)S(1)} collective-permute-done((bf16[1,3,128,256]{3,2,1,0:T(8,128)(2,1)S(1)}, bf16[1,3,128,256]{3,2,1,0:T(8,128)(2,1)S(1)}, u32[]{:S(2)}, u32[]{:S(2)}) %collective-permute-start.3) | collective-permute-done | bytes 196640 | tf_op jit(solution)/shard_map/ppermute | solution.py:324
  54.8 3.7 %collective-permute-done.refs_4_ = bf16[768,512]{1,0:T(8,128)(2,1)} collective-permute-done((bf16[768,512]{1,0:T(8,128)(2,1)S(1)}, bf16[768,512]{1,0:T(8,128)(2,1)}, u32[]{:S(2)}, u32[]{:S(2)}) %collective-permute-start) | collective-permute-done | bytes 786464 | tf_op jit(solution)/shard_map/ppermute | solution.py:320
  58.5 3.2 %collective-permute-start.6 = (bf16[768,512]{1,0:T(8,128)(2,1)}, bf16[768,512]{1,0:T(8,128)(2,1)}, u32[]{:S(2)}, u32[]{:S(2)}) collective-permute-start(bf16[768,512]{1,0:T(8,128)(2,1)} %collective-permute-done.1.refs_1_), channel_id=1, source_target_pairs={{0,7},{1,0},{2,1},{3,2},{4,3},{5,4},{6,5},{7,6},{8,15},{9,8},{10,9... | collective-permute-start | bytes 2359304 | tf_op jit(solution)/shard_map/ppermute | solution.py:330
  61.7 1.1 collective-permute-start.11
  63.7 8.6 %all-gather.2.cloned.1.call-done.columns_ref = bf16[5120,640]{1,0:T(8,128)(2,1)} async-done(((bf16[160,640]{1,0:T(8,128)(2,1)}), bf16[5120,640]{1,0:T(8,128)(2,1)}) %all-gather.2.cloned.1.call-update) | async-done | bytes 6553616 | tf_op jit(solution)/shard_map/all_gather | solution.py:296
  72.3 2.9 %copy-done.1 = bf16[5120,640]{1,0:T(8,128)(2,1)S(1)} copy-done((bf16[5120,640]{1,0:T(8,128)(2,1)S(1)}, bf16[5120,640]{1,0:T(8,128)(2,1)}, u32[]{:S(2)}) %copy-start.1) | copy-done | bytes 6553624
  75.2 3.0 %shard_map.158 = (bf16[256,5120]{1,0:T(8,128)(2,1)S(1)}, f32[8,128]{1,0:T(8,128)S(1)}) custom-call(bf16[256,640]{1,0:T(8,128)(2,1)S(1)} %bitcast.63, bf16[5120,640]{1,0:T(8,128)(2,1)S(1)} %copy-done.1), custom_call_target="tpu_custom_call" | custom-call | flops 1677721600 | bytes 9437184 | tf_op jit(solution)/shard_map/pallas_call | solution.py:113
  78.2 1.5 copy-done.2
  79.7 3.7 %collective-permute-start.7 = (bf16[768,512]{1,0:T(8,128)(2,1)}, bf16[768,512]{1,0:T(8,128)(2,1)S(1)}, u32[]{:S(2)}, u32[]{:S(2)}) collective-permute-start(bf16[768,512]{1,0:T(8,128)(2,1)} %collective-permute-done.5.refs_3_), channel_id=1, source_target_pairs={{0,1},{1,2},{2,3},{3,4},{4,5},{5,6},{6,7},{7,0},{8,9},{9,10},{10,1... | collective-permute-start | bytes 2359304 | tf_op jit(solution)/shard_map/ppermute | solution.py:338
  83.4 1.1 collective-permute-start.8
  84.6 3.4 %collective-permute-start.12 = (bf16[2,3,128,256]{3,2,1,0:T(8,128)(2,1)S(1)}, bf16[2,3,128,256]{3,2,1,0:T(8,128)(2,1)S(1)}, u32[]{:S(2)}, u32[]{:S(2)}) collective-permute-start(bf16[2,3,128,256]{3,2,1,0:T(8,128)(2,1)S(1)} %slice.17), channel_id=1, source_target_pairs={{0,192},{64,0},{128,64},{192,128},{1,193},{65,1},{129,65},{193,129... | collective-permute-start | bytes 1179656 | tf_op jit(solution)/shard_map/ppermute | solution.py:343
  88.4 8.4 %collective-permute-done.12 = bf16[2,3,128,256]{3,2,1,0:T(8,128)(2,1)S(1)} collective-permute-done((bf16[2,3,128,256]{3,2,1,0:T(8,128)(2,1)S(1)}, bf16[2,3,128,256]{3,2,1,0:T(8,128)(2,1)S(1)}, u32[]{:S(2)}, u32[]{:S(2)}) %collective-permute-start.12) | collective-permute-done | bytes 393248 | tf_op jit(solution)/shard_map/ppermute | solution.py:343
  96.8 3.4 %collective-permute-done.10 = bf16[2,3,128,256]{3,2,1,0:T(8,128)(2,1)S(1)} collective-permute-done((bf16[2,3,128,256]{3,2,1,0:T(8,128)(2,1)S(1)}, bf16[2,3,128,256]{3,2,1,0:T(8,128)(2,1)S(1)}, u32[]{:S(2)}, u32[]{:S(2)}) %collective-permute-start.10) | collective-permute-done | bytes 393248 | tf_op jit(solution)/shard_map/ppermute | solution.py:342
  100.3 2.4 %collective-permute-done.7.refs_1_ = bf16[768,512]{1,0:T(8,128)(2,1)S(1)} collective-permute-done((bf16[768,512]{1,0:T(8,128)(2,1)}, bf16[768,512]{1,0:T(8,128)(2,1)S(1)}, u32[]{:S(2)}, u32[]{:S(2)}) %collective-permute-start.7) | collective-permute-done | bytes 786464 | tf_op jit(solution)/shard_map/ppermute | solution.py:338
  102.7 2.7 %collective-permute-done.8.refs_0_ = bf16[768,512]{1,0:T(8,128)(2,1)} collective-permute-done((bf16[768,512]{1,0:T(8,128)(2,1)}, bf16[768,512]{1,0:T(8,128)(2,1)}, u32[]{:S(2)}, u32[]{:S(2)}) %collective-permute-start.8) | collective-permute-done | bytes 786464 | tf_op jit(solution)/shard_map/ppermute | solution.py:339
  105.5 1.0 slice.15
  106.6 3.3 %collective-permute-start.14 = (bf16[384,512]{1,0:T(8,128)(2,1)S(1)}, bf16[384,512]{1,0:T(8,128)(2,1)S(1)}, u32[]{:S(2)}, u32[]{:S(2)}) collective-permute-start(bf16[384,512]{1,0:T(8,128)(2,1)S(1)} %slice.15), channel_id=1, source_target_pairs={{0,7},{1,0},{2,1},{3,2},{4,3},{5,4},{6,5},{7,6},{8,15},{9,8},{10,9... | collective-permute-start | bytes 1179656 | tf_op jit(solution)/shard_map/ppermute | solution.py:355
  109.9 1.0 shard_map.159.refs_5_.refs_4_
  110.9 5.4 %shard_map.160 = (f32[3,768,256]{2,1,0:T(8,128)S(1)}, f32[768,128]{1,0:T(8,128)S(1)}) custom-call(bf16[768,512]{1,0:T(8,128)(2,1)S(1)} %bitcast.66, bf16[768,512]{1,0:T(8,128)(2,1)} %collective-permute-done.1.refs_1_, bf16[768,512]{1,0:T(8,128)(2,1)} %collective-permute-done.6.refs_2_, bf16[768,512]{1,0:T(8,128)(2,1)} %collective-permute-done.5.refs_3_, ...), custom_call_target="tpu_custom_call" | custom-call | flops 3019898880 | bytes 12582912 | tf_op jit(solution)/shard_map/pallas_call | solution.py:186
  116.4 10.5 %collective-permute-done.13.refs_2_ = bf16[384,512]{1,0:T(8,128)(2,1)S(1)} collective-permute-done((bf16[384,512]{1,0:T(8,128)(2,1)S(1)}, bf16[384,512]{1,0:T(8,128)(2,1)S(1)}, u32[]{:S(2)}, u32[]{:S(2)}) %collective-permute-start.13) | collective-permute-done | bytes 393248 | tf_op jit(solution)/shard_map/ppermute | solution.py:354
  126.9 1.6 collective-permute-done.14.refs_3_
  128.5 4.8 %shard_map.161 = bf16[32,3,24,256]{3,2,1,0:T(8,128)(2,1)} custom-call(bf16[768,512]{1,0:T(8,128)(2,1)} %collective-permute-done.8.refs_0_, bf16[768,512]{1,0:T(8,128)(2,1)S(1)} %collective-permute-done.7.refs_1_, bf16[384,512]{1,0:T(8,128)(2,1)S(1)} %collective-permute-done.13.refs_2_, bf16[384,512]{1,0:T(8,128)(2,1)S(1)} %collective-permute-done.14.refs_3_, ...), custom_call_target="tpu_custom_call" | custom-call | flops 36238786560 | bytes 12582912 | tf_op jit(solution)/shard_map/pallas_call | solution.py:215
  133.3 7.2 %reduce-scatter.2.cloned.1.call-done.sum_ref = bf16[32,5120]{1,0:T(8,128)(2,1)} async-done(((bf16[256,5120]{1,0:T(8,128)(2,1)}), bf16[32,5120]{1,0:T(8,128)(2,1)}) %reduce-scatter.2.cloned.1.call-update) | async-done | bytes 327696 | tf_op jit(solution)/shard_map/reduce_scatter | solution.py:336
  140.5 2.1 %shard_map.162 = (bf16[32,5120]{1,0:T(8,128)(2,1)}, f32[8,32]{1,0:T(8,128)}) custom-call(s32[1,3]{1,0:T(1,128)} %pair_ref.1, bf16[32,5120]{1,0:T(8,128)(2,1)} %bitcast.70, bf16[1,5120]{1,0:T(2,128)(2,1)} %reshape.51.gain_ref, bf16[1,5120]{1,0:T(2,128)(2,1)} %reshape.52.score_ref, bf16[32,5120]{1,0:T(8,128)(2,1)} %reduce-scatter.2.cloned.1.call-done.sum_ref), custom_call_target="tpu_custom_call" | custom-call | flops 1310720 | bytes 2097152 | tf_op jit(solution)/shard_map/pallas_call | solution.py:257
  143.4 13.5 %all_to_all.10 = f32[8,1,256]{2,1,0:T(1,128)S(1)} all-to-all(f32[8,1,256]{2,1,0:T(1,128)S(1)} %reshape.54), channel_id=1, replica_groups=mesh['y'=4,'x'=4,'core'=2,'z'=8] {'z'}, dimensions={0} | all-to-all | bytes 16384 | tf_op jit(solution)/shard_map/all_to_all | solution.py:373
  (63 shorter events, 9.0 us)
Async XLA Ops:
  7.2 13.0 %copy-start = (bf16[8,32,640]{2,1,0:T(8,128)(2,1)S(1)}, bf16[8,32,640]{2,1,0:T(8,128)(2,1)}, u32[]{:S(2)}) copy-start(bf16[8,32,640]{2,1,0:T(8,128)(2,1)} %param.16) | copy-start | bytes 983044
  7.2 12.2 %copy-start.6 = (bf16[8,32,640]{2,1,0:T(8,128)(2,1)S(1)}, bf16[8,32,640]{2,1,0:T(8,128)(2,1)}, u32[]{:S(2)}) copy-start(bf16[8,32,640]{2,1,0:T(8,128)(2,1)} %param.14) | copy-start | bytes 983044
  7.2 12.2 %copy-start.5 = (bf16[8,32,640]{2,1,0:T(8,128)(2,1)S(1)}, bf16[8,32,640]{2,1,0:T(8,128)(2,1)}, u32[]{:S(2)}) copy-start(bf16[8,32,640]{2,1,0:T(8,128)(2,1)} %param.15) | copy-start | bytes 983044
  7.2 65.1 %all-gather.2.cloned.1.call-start = ((), (), s32[]{:S(2)}) async-start(), calls=%async_computation.3 | async-start | bytes 6758400 | tf_op jit(solution)/shard_map/all_gather | solution.py:296
  11.7 22.0 %all-to-all-start = ((bf16[32,24,512]{2,1,0:T(8,128)(2,1)}), bf16[32,24,512]{2,1,0:T(8,128)(2,1)S(1)}, u32[]{:S(2)}, u32[]{:S(2)}) async-start(bf16[32,24,512]{2,1,0:T(8,128)(2,1)} %bitcast.67), calls=%async_computation | async-start | bytes 1572864 | tf_op jit(solution)/shard_map/all_to_all | solution.py:302
  19.4 121.1 %reduce-scatter.2.cloned.1.call-start = ((), (), s32[]{:S(2)}) async-start(), calls=%async_computation.4 | async-start | bytes 2949120 | tf_op jit(solution)/shard_map/reduce_scatter | solution.py:336
  20.1 0.7 copy-start.8
  20.1 1.3 copy-start.9
  20.1 2.7 %copy-start.7 = (bf16[128,3,256]{2,0,1:T(8,128)(2,1)S(1)}, bf16[128,3,256]{2,0,1:T(8,128)(2,1)}, u32[]{:S(2)}) copy-start(bf16[128,3,256]{2,0,1:T(8,128)(2,1)} %param.27) | copy-start | bytes 589828
  33.7 24.8 %copy-start.3 = (bf16[32,24,512]{2,1,0:T(8,128)(2,1)}, bf16[32,24,512]{2,1,0:T(8,128)(2,1)S(1)}, u32[]{:S(2)}) copy-start(bf16[32,24,512]{2,1,0:T(8,128)(2,1)S(1)} %all-to-all-done) | copy-start | bytes 2359300
  33.7 24.8 %collective-permute-start = (bf16[768,512]{1,0:T(8,128)(2,1)S(1)}, bf16[768,512]{1,0:T(8,128)(2,1)}, u32[]{:S(2)}, u32[]{:S(2)}) collective-permute-start(bf16[768,512]{1,0:T(8,128)(2,1)S(1)} %bitcast.64), channel_id=1, source_target_pairs={{0,1},{1,2},{2,3},{3,4},{4,5},{5,6},{6,7},{7,0},{8,9},{9,10},{10,1... | collective-permute-start | bytes 2359304 | tf_op jit(solution)/shard_map/ppermute | solution.py:320
  35.7 22.8 %collective-permute-start.1 = (bf16[768,512]{1,0:T(8,128)(2,1)S(1)}, bf16[768,512]{1,0:T(8,128)(2,1)}, u32[]{:S(2)}, u32[]{:S(2)}) collective-permute-start(bf16[768,512]{1,0:T(8,128)(2,1)S(1)} %bitcast.65), channel_id=1, source_target_pairs={{0,7},{1,0},{2,1},{3,2},{4,3},{5,4},{6,5},{7,6},{8,15},{9,8},{10,9... | collective-permute-start | bytes 2359304 | tf_op jit(solution)/shard_map/ppermute | solution.py:321
  40.2 7.0 %collective-permute-start.2 = (bf16[1,3,128,256]{3,2,1,0:T(8,128)(2,1)S(1)}, bf16[1,3,128,256]{3,2,1,0:T(8,128)(2,1)S(1)}, u32[]{:S(2)}, u32[]{:S(2)}) collective-permute-start(bf16[1,3,128,256]{3,2,1,0:T(8,128)(2,1)S(1)} %fusion.11), channel_id=1, source_target_pairs={{0,16},{16,32},{32,48},{48,0},{1,17},{17,33},{33,49},{49,1},{2,18}... | collective-permute-start | bytes 589832 | tf_op jit(solution)/shard_map/ppermute | solution.py:322
  40.3 7.1 %collective-permute-start.4 = (bf16[1,3,128,256]{3,2,1,0:T(8,128)(2,1)S(1)}, bf16[1,3,128,256]{3,2,1,0:T(8,128)(2,1)S(1)}, u32[]{:S(2)}, u32[]{:S(2)}) collective-permute-start(bf16[1,3,128,256]{3,2,1,0:T(8,128)(2,1)S(1)} %fusion.11), channel_id=1, source_target_pairs={{0,48},{16,0},{32,16},{48,32},{1,49},{17,1},{33,17},{49,33},{2,50}... | collective-permute-start | bytes 589832 | tf_op jit(solution)/shard_map/ppermute | solution.py:323
  47.2 7.5 %collective-permute-start.3 = (bf16[1,3,128,256]{3,2,1,0:T(8,128)(2,1)S(1)}, bf16[1,3,128,256]{3,2,1,0:T(8,128)(2,1)S(1)}, u32[]{:S(2)}, u32[]{:S(2)}) collective-permute-start(bf16[1,3,128,256]{3,2,1,0:T(8,128)(2,1)S(1)} %collective-permute-done.2), channel_id=1, source_target_pairs={{0,16},{16,32},{32,48},{48,0},{1,17},{17,33},{33,49},{49,1},{2,18}... | collective-permute-start | bytes 589832 | tf_op jit(solution)/shard_map/ppermute | solution.py:324
  58.5 21.2 %collective-permute-start.5 = (bf16[768,512]{1,0:T(8,128)(2,1)}, bf16[768,512]{1,0:T(8,128)(2,1)}, u32[]{:S(2)}, u32[]{:S(2)}) collective-permute-start(bf16[768,512]{1,0:T(8,128)(2,1)} %collective-permute-done.refs_4_), channel_id=1, source_target_pairs={{0,1},{1,2},{2,3},{3,4},{4,5},{5,6},{6,7},{7,0},{8,9},{9,10},{10,1... | collective-permute-start | bytes 2359304 | tf_op jit(solution)/shard_map/ppermute | solution.py:329
  58.5 21.2 %collective-permute-start.6 = (bf16[768,512]{1,0:T(8,128)(2,1)}, bf16[768,512]{1,0:T(8,128)(2,1)}, u32[]{:S(2)}, u32[]{:S(2)}) collective-permute-start(bf16[768,512]{1,0:T(8,128)(2,1)} %collective-permute-done.1.refs_1_), channel_id=1, source_target_pairs={{0,7},{1,0},{2,1},{3,2},{4,3},{5,4},{6,5},{7,6},{8,15},{9,8},{10,9... | collective-permute-start | bytes 2359304 | tf_op jit(solution)/shard_map/ppermute | solution.py:330
  61.7 22.8 %collective-permute-start.11 = (bf16[4,3,128,256]{3,2,1,0:T(8,128)(2,1)S(1)}, bf16[4,3,128,256]{3,2,1,0:T(8,128)(2,1)S(1)}, u32[]{:S(2)}, u32[]{:S(2)}) collective-permute-start(bf16[4,3,128,256]{3,2,1,0:T(8,128)(2,1)S(1)} %pad_maximum_fusion.refs_0_), channel_id=1, source_target_pairs={{0,192},{64,0},{128,64},{192,128},{1,193},{65,1},{129,65},{193,129... | collective-permute-start | bytes 2359304 | tf_op jit(solution)/shard_map/ppermute | solution.py:332
  62.8 25.2 %collective-permute-start.9 = (bf16[4,3,128,256]{3,2,1,0:T(8,128)(2,1)S(1)}, bf16[4,3,128,256]{3,2,1,0:T(8,128)(2,1)S(1)}, u32[]{:S(2)}, u32[]{:S(2)}) collective-permute-start(bf16[4,3,128,256]{3,2,1,0:T(8,128)(2,1)S(1)} %pad_maximum_fusion.refs_0_), channel_id=1, source_target_pairs={{0,64},{64,128},{128,192},{192,0},{1,65},{65,129},{129,193},{193,1... | collective-permute-start | bytes 2359304 | tf_op jit(solution)/shard_map/ppermute | solution.py:331
  72.3 2.9 %copy-start.1 = (bf16[5120,640]{1,0:T(8,128)(2,1)S(1)}, bf16[5120,640]{1,0:T(8,128)(2,1)}, u32[]{:S(2)}) copy-start(bf16[5120,640]{1,0:T(8,128)(2,1)} %all-gather.2.cloned.1.call-done.columns_ref) | copy-start | bytes 19660804
  78.2 1.5 copy-start.2
  79.7 23.0 %collective-permute-start.7 = (bf16[768,512]{1,0:T(8,128)(2,1)}, bf16[768,512]{1,0:T(8,128)(2,1)S(1)}, u32[]{:S(2)}, u32[]{:S(2)}) collective-permute-start(bf16[768,512]{1,0:T(8,128)(2,1)} %collective-permute-done.5.refs_3_), channel_id=1, source_target_pairs={{0,1},{1,2},{2,3},{3,4},{4,5},{5,6},{6,7},{7,0},{8,9},{9,10},{10,1... | collective-permute-start | bytes 2359304 | tf_op jit(solution)/shard_map/ppermute | solution.py:338
  83.4 22.0 %collective-permute-start.8 = (bf16[768,512]{1,0:T(8,128)(2,1)}, bf16[768,512]{1,0:T(8,128)(2,1)}, u32[]{:S(2)}, u32[]{:S(2)}) collective-permute-start(bf16[768,512]{1,0:T(8,128)(2,1)} %collective-permute-done.6.refs_2_), channel_id=1, source_target_pairs={{0,7},{1,0},{2,1},{3,2},{4,3},{5,4},{6,5},{7,6},{8,15},{9,8},{10,9... | collective-permute-start | bytes 2359304 | tf_op jit(solution)/shard_map/ppermute | solution.py:339
  84.6 12.2 %collective-permute-start.12 = (bf16[2,3,128,256]{3,2,1,0:T(8,128)(2,1)S(1)}, bf16[2,3,128,256]{3,2,1,0:T(8,128)(2,1)S(1)}, u32[]{:S(2)}, u32[]{:S(2)}) collective-permute-start(bf16[2,3,128,256]{3,2,1,0:T(8,128)(2,1)S(1)} %slice.17), channel_id=1, source_target_pairs={{0,192},{64,0},{128,64},{192,128},{1,193},{65,1},{129,65},{193,129... | collective-permute-start | bytes 1179656 | tf_op jit(solution)/shard_map/ppermute | solution.py:343
  88.0 12.2 %collective-permute-start.10 = (bf16[2,3,128,256]{3,2,1,0:T(8,128)(2,1)S(1)}, bf16[2,3,128,256]{3,2,1,0:T(8,128)(2,1)S(1)}, u32[]{:S(2)}, u32[]{:S(2)}) collective-permute-start(bf16[2,3,128,256]{3,2,1,0:T(8,128)(2,1)S(1)} %slice.16), channel_id=1, source_target_pairs={{0,64},{64,128},{128,192},{192,0},{1,65},{65,129},{129,193},{193,1... | collective-permute-start | bytes 1179656 | tf_op jit(solution)/shard_map/ppermute | solution.py:342
  88.3 18.3 %collective-permute-start.15 = (bf16[4,3,128,256]{3,2,1,0:T(8,128)(2,1)S(1)}, bf16[4,3,128,256]{3,2,1,0:T(8,128)(2,1)S(1)}, u32[]{:S(2)}, u32[]{:S(2)}) collective-permute-start(bf16[4,3,128,256]{3,2,1,0:T(8,128)(2,1)S(1)} %pad_maximum_fusion.refs_0_), channel_id=1, source_target_pairs={{0,8},{8,0},{1,9},{9,1},{2,10},{10,2},{3,11},{11,3},{4,12},{12,4},... | collective-permute-start | bytes 2359304 | tf_op jit(solution)/shard_map/ppermute | solution.py:350
  96.8 13.1 %collective-permute-start.16 = (bf16[4,3,128,256]{3,2,1,0:T(8,128)(2,1)S(1)}, bf16[4,3,128,256]{3,2,1,0:T(8,128)(2,1)S(1)}, u32[]{:S(2)}, u32[]{:S(2)}) collective-permute-start(bf16[4,3,128,256]{3,2,1,0:T(8,128)(2,1)S(1)} %collective-permute-done.9.refs_1_), channel_id=1, source_target_pairs={{0,8},{8,0},{1,9},{9,1},{2,10},{10,2},{3,11},{11,3},{4,12},{12,4},... | collective-permute-start | bytes 2359304 | tf_op jit(solution)/shard_map/ppermute | solution.py:350
  100.2 9.7 %collective-permute-start.18 = (bf16[4,3,128,256]{3,2,1,0:T(8,128)(2,1)S(1)}, bf16[4,3,128,256]{3,2,1,0:T(8,128)(2,1)S(1)}, u32[]{:S(2)}, u32[]{:S(2)}) collective-permute-start(bf16[4,3,128,256]{3,2,1,0:T(8,128)(2,1)S(1)} %collective-permute-done.11.refs_3_), channel_id=1, source_target_pairs={{0,8},{8,0},{1,9},{9,1},{2,10},{10,2},{3,11},{11,3},{4,12},{12,4},... | collective-permute-start | bytes 2359304 | tf_op jit(solution)/shard_map/ppermute | solution.py:350
  105.4 4.5 %collective-permute-start.17 = (bf16[4,3,128,256]{3,2,1,0:T(8,128)(2,1)S(1)}, bf16[4,3,128,256]{3,2,1,0:T(8,128)(2,1)S(1)}, u32[]{:S(2)}, u32[]{:S(2)}) collective-permute-start(bf16[4,3,128,256]{3,2,1,0:T(8,128)(2,1)S(1)} %pad_maximum_fusion.1.refs_2_), channel_id=1, source_target_pairs={{0,8},{8,0},{1,9},{9,1},{2,10},{10,2},{3,11},{11,3},{4,12},{12,4},... | collective-permute-start | bytes 2359304 | tf_op jit(solution)/shard_map/ppermute | solution.py:350
  105.5 21.4 %collective-permute-start.13 = (bf16[384,512]{1,0:T(8,128)(2,1)S(1)}, bf16[384,512]{1,0:T(8,128)(2,1)S(1)}, u32[]{:S(2)}, u32[]{:S(2)}) collective-permute-start(bf16[384,512]{1,0:T(8,128)(2,1)S(1)} %slice.14), channel_id=1, source_target_pairs={{0,1},{1,2},{2,3},{3,4},{4,5},{5,6},{6,7},{7,0},{8,9},{9,10},{10,1... | collective-permute-start | bytes 1179656 | tf_op jit(solution)/shard_map/ppermute | solution.py:354
  106.6 4.4 %copy-start.4 = (bf16[32,24,512]{2,1,0:T(8,128)(2,1)S(1)}, bf16[32,24,512]{2,1,0:T(8,128)(2,1)}, u32[]{:S(2)}) copy-start(bf16[32,24,512]{2,1,0:T(8,128)(2,1)} %copy-done.3) | copy-start | bytes 2359300
  106.6 21.9 %collective-permute-start.14 = (bf16[384,512]{1,0:T(8,128)(2,1)S(1)}, bf16[384,512]{1,0:T(8,128)(2,1)S(1)}, u32[]{:S(2)}, u32[]{:S(2)}) collective-permute-start(bf16[384,512]{1,0:T(8,128)(2,1)S(1)} %slice.15), channel_id=1, source_target_pairs={{0,7},{1,0},{2,1},{3,2},{4,3},{5,4},{6,5},{7,6},{8,15},{9,8},{10,9... | collective-permute-start | bytes 1179656 | tf_op jit(solution)/shard_map/ppermute | solution.py:355
Sparse Core Ops, SparseCore 0:
  10.6 61.6 all-gather.1
  84.7 55.7 reduce-scatter.1

commit v7 on v6

--- a/solution.py
+++ b/solution.py
@@ -99,37 +99,43 @@
     )(where, token, *slabs)
 
 
-def project_kernel(rows_ref, columns_ref, out_ref, token_ref):
+def project_kernel(own_ref, before_ref, low_ref, high_ref, after_ref, columns_ref, out_ref, token_ref):
+    def project(rows):
+        pairs, length, depth = rows.shape
+        product = lax.dot_general(
+            rows.reshape(pairs * length, depth),
+            columns_ref[...],
+            (((1,), (1,)), ((), ())),
+            preferred_element_type=jnp.float32,
+        )
+        return product.astype(out_ref.dtype).reshape(pairs, length, -1)
+
     token_ref[...] = jnp.zeros_like(token_ref)
-    out_ref[...] = lax.dot_general(
-        rows_ref[...], columns_ref[...], (((1,), (1,)), ((), ())), preferred_element_type=jnp.float32
-    ).astype(out_ref.dtype)
-
-
-def project(rows, columns):
-    count, depth = rows.shape
+    half = low_ref.shape[0]
+    out_ref[:, 0] = project(own_ref[...])
+    out_ref[:, 1] = project(before_ref[...])
+    out_ref[:half, 2] = project(low_ref[...])
+    out_ref[half:, 2] = project(high_ref[...])
+    out_ref[:, 3] = project(after_ref[...])
+
+
+def project(contexts, columns):
+    pairs, length, depth = contexts[0].shape
     width = columns.shape[0]
-    steps = 4
+    vmem = pl.BlockSpec(memory_space=pltpu.VMEM)
     return pl.pallas_call(
         project_kernel,
         out_shape=(
-            jax.ShapeDtypeStruct((count, width), jnp.bfloat16),
+            jax.ShapeDtypeStruct((pairs, NY, length, width), jnp.bfloat16),
             jax.ShapeDtypeStruct((8, 128), jnp.float32),
         ),
-        grid=(steps,),
-        in_specs=[
-            pl.BlockSpec((count, depth), lambda i: (0, 0)),
-            pl.BlockSpec((width // steps, depth), lambda i: (i, 0)),
-        ],
-        out_specs=(
-            pl.BlockSpec((count, width // steps), lambda i: (0, i)),
-            pl.BlockSpec((8, 128), lambda i: (0, 0)),
-        ),
-        compiler_params=pltpu.CompilerParams(vmem_limit_bytes=16 << 20),
+        in_specs=[vmem] * (len(contexts) + 1),
+        out_specs=(vmem, vmem),
+        compiler_params=pltpu.CompilerParams(vmem_limit_bytes=20 << 20),
         cost_estimate=pl.CostEstimate(
-            flops=2 * count * width * depth, bytes_accessed=9 << 20, transcendentals=0
-        ),
-    )(rows, columns)
+            flops=2 * pairs * NY * length * width * depth, bytes_accessed=6 << 20, transcendentals=0
+        ),
+    )(*contexts, columns)
 
 
 def squares_of(values):
@@ -236,13 +242,23 @@
     return out.transpose(0, 2, 1, 3)
 
 
-def norm_kernel(pair_ref, resid_ref, gain_ref, score_ref, sum_ref, hidden_ref, votes_ref):
-    mixed = resid_ref[...].astype(jnp.float32) + sum_ref[...].astype(jnp.float32)
-    squares = jnp.sum(mixed * mixed, axis=-1, keepdims=True)
-    scale = lax.rsqrt(squares * (1.0 / mixed.shape[1]) + 1e-05)
-    normed = mixed * scale * gain_ref[...].astype(jnp.float32)
+def norm_kernel(where_ref, pair_ref, resid_ref, gain_ref, score_ref, *refs):
+    piece_refs = refs[:NY]
+    hidden_ref, votes_ref, mixed_ref = refs[NY:]
+    rows, quarter = piece_refs[0].shape
+    squares = jnp.zeros((rows, 1), jnp.float32)
+    for ahead, piece in enumerate(piece_refs):
+        place = lax.rem(where_ref[0] + ahead, NY)
+        columns = pl.ds(pl.multiple_of(place * quarter, 128), quarter)
+        mixed = resid_ref[:, columns].astype(jnp.float32) + piece[...].astype(jnp.float32)
+        mixed_ref[:, columns] = mixed
+        squares = squares + jnp.sum(mixed * mixed, axis=-1, keepdims=True)
+    scale = lax.rsqrt(squares * (1.0 / (NY * quarter)) + 1e-05)
+    normed = mixed_ref[...] * scale * gain_ref[...].astype(jnp.float32)
     hidden_ref[...] = normed.astype(hidden_ref.dtype)
-    logit = jnp.sum(normed[:1] * score_ref[...].astype(jnp.float32), axis=-1, keepdims=True)
+    logit = jnp.sum(
+        normed[:1] * score_ref[...].astype(jnp.float32), axis=-1, keepdims=True
+    )
     cand = lax.broadcasted_iota(jnp.int32, votes_ref.shape, 0)
     prompt = lax.broadcasted_iota(jnp.int32, votes_ref.shape, 1)
     own = prompt == pair_ref[0, 0]
@@ -251,8 +267,9 @@
     votes_ref[...] = upward - downward
 
 
-def norm_and_vote(pair_index, resid, gain, score, part_sum, prompts, cands):
+def norm_and_vote(where, pair_index, resid, gain, score, pieces, prompts, cands):
     rows, width = resid.shape
+    smem = pl.BlockSpec(memory_space=pltpu.SMEM)
     vmem = pl.BlockSpec(memory_space=pltpu.VMEM)
     return pl.pallas_call(
         norm_kernel,
@@ -260,12 +277,11 @@
             jax.ShapeDtypeStruct((rows, width), jnp.bfloat16),
             jax.ShapeDtypeStruct((cands, prompts), jnp.float32),
         ),
-        in_specs=[pl.BlockSpec(memory_space=pltpu.SMEM)] + [vmem] * 4,
+        in_specs=[smem, smem] + [vmem] * (3 + NY),
         out_specs=(vmem, vmem),
-        cost_estimate=pl.CostEstimate(
-            flops=rows * width * 8, bytes_accessed=2 << 20, transcendentals=rows
-        ),
-    )(pair_index, resid, gain, score, part_sum)
+        scratch_shapes=[pltpu.VMEM((rows, width), jnp.float32)],
+        cost_estimate=pl.CostEstimate(flops=rows * width * 8, bytes_accessed=2 << 20, transcendentals=rows),
+    )(where, pair_index, resid, gain, score, *pieces)
 
 
 def together(*values):
@@ -293,7 +309,7 @@
     my_y, my_x, my_core, my_z = (lax.axis_index(a) for a in ("y", "x", "core", "z"))
 
     where = jnp.stack([my_y, my_x, my_core, my_z]).astype(jnp.int32)
-    columns = lax.all_gather(out_weight.T, PLANE, axis=0, tiled=True)
+    columns = lax.all_gather(out_weight.T, ("x", "core"), axis=0, tiled=True)
 
     outgoing = select_rows(blend_owner, cand_rank, cand_len, blend_rows)
     rank_query, blend_weight, outgoing = together(rank_query, blend_weight, outgoing)
@@ -305,6 +321,10 @@
     own = arrived.reshape(prompts * arrived.shape[1], features)
 
     context = pair_attention(rank_query, rank_key, rank_value, local_heads)
+    context = context.reshape(rank_query.shape[0], length, -1)
+    half_pairs = context.shape[0] // 2
+    c_before = lax.ppermute(context, "y", ring(NY, 1))
+    c_after = lax.ppermute(context, "y", ring(NY, -1))
     depth = blend_weight.shape[0]
     slab = (my_y * NX + my_x) * NC + my_core
     gain = lax.dynamic_slice_in_dim(blend_gain, slab * depth, depth, 0).astype(jnp.float32)
@@ -313,27 +333,33 @@
     )[None]
     gain_row = rank_gain.reshape(1, -1)
     score_row = score_weight.reshape(1, -1)
-    own, context, own_slab, gain_row, score_row, where = together(
-        own, context, own_slab, gain_row, score_row, where
+    own, context, c_before, c_after, own_slab, gain_row, score_row, where = together(
+        own, context, c_before, c_after, own_slab, gain_row, score_row, where
     )
 
     lower = lax.ppermute(own, "z", ring(NZ, 1))
     upper = lax.ppermute(own, "z", ring(NZ, -1))
+    c_low = lax.ppermute(c_before[:half_pairs], "y", ring(NY, 1))
+    c_high = lax.ppermute(c_after[half_pairs:], "y", ring(NY, -1))
     x_before = lax.ppermute(own_slab, "x", ring(NX, 1))
     x_after = lax.ppermute(own_slab, "x", ring(NX, -1))
     x_across = lax.ppermute(x_before, "x", ring(NX, 1))
     strip = jnp.concatenate([own_slab, x_before, x_across, x_after], axis=0)
-    lower, upper, strip, context = together(lower, upper, strip, context)
+    lower, upper, strip, context, c_low, c_high = together(
+        lower, upper, strip, context, c_low, c_high
+    )
     blocks = {1: upper, NZ - 1: lower, 0: own}
+    term_rows, token = project([context, c_before, c_low, c_high, c_after], columns)
+    part_sum = lax.psum_scatter(
+        term_rows.reshape(-1, term_rows.shape[-1]), "z", scatter_dimension=0, tiled=True
+    )
 
     lower = lax.ppermute(lower, "z", ring(NZ, 1))
     upper = lax.ppermute(upper, "z", ring(NZ, -1))
     y_before = lax.ppermute(strip, "y", ring(NY, 1))
     y_after = lax.ppermute(strip, "y", ring(NY, -1))
-    term_rows, token = project(context, columns)
     lower, upper, token = together(lower, upper, token)
     blocks.update({2: upper, NZ - 2: lower})
-    part_sum = lax.psum_scatter(term_rows, "z", scatter_dimension=0, tiled=True)
 
     lower = lax.ppermute(lower, "z", ring(NZ, 1))
     upper = lax.ppermute(upper, "z", ring(NZ, -1))
@@ -344,34 +370,40 @@
         ],
         axis=0,
     )
-    lower, upper, y_across = together(lower, upper, y_across)
-
+    swapped = [lax.ppermute(s, "core", ring(NC, 1)) for s in (strip, y_before, y_after)]
+    lower, upper, part_sum, y_across = together(lower, upper, part_sum, y_across)
+
+    swapped.insert(2, lax.ppermute(y_across, "core", ring(NC, 1)))
     slabs = [strip, y_before, y_across, y_after]
-    weights = arrange(where, token, slabs + [lax.ppermute(s, "core", ring(NC, 1)) for s in slabs])
-    near = (0, 1, 2, NZ - 2, NZ - 1)
     half = own.shape[0] // 2
-    total, squares = encode_first(near, [blocks[i] for i in near], weights)
     low = lax.ppermute(lower[:half], "z", ring(NZ, 1))
     high = lax.ppermute(upper[half:], "z", ring(NZ, -1))
-    blended_qkv = encode_last(
-        (3, NZ - 3, 4), upper, lower, low, high, weights, total, squares, prompts
-    )
-
-    part_sum, blended_qkv = together(part_sum, blended_qkv)
     own_pairs = rank_resid.shape[0]
+    parts = part_sum.reshape(NY, own_pairs * length, -1)
+    pieces = [lax.ppermute(parts[r], "y", ring(NY, -r)) for r in range(1, NY)]
+    weights = arrange(where, token, slabs + swapped)
+    near = (0, 1, 2, NZ - 2, NZ - 1)
+    total, squares = encode_first(near, [blocks[i] for i in near], weights)
+    low, high, squares, *pieces = together(low, high, squares, *pieces)
+    pieces = [parts[0]] + pieces
+
     rank_hidden, votes = norm_and_vote(
+        where,
         pair_index,
         rank_resid.reshape(own_pairs * length, -1),
         gain_row,
         score_row,
-        part_sum,
+        pieces,
         prompts,
         cand_rank.shape[1],
     )
     rank_hidden = rank_hidden.reshape(rank_resid.shape)
-    votes = jnp.broadcast_to(votes[None], (NZ,) + votes.shape)
-    votes = lax.all_to_all(votes, "z", split_axis=0, concat_axis=0, tiled=True)
-    cand_score = jnp.sum(votes, axis=0).T
+    for bit in (1, 2, 4):
+        votes = votes + lax.ppermute(votes, "z", [(i, i ^ bit) for i in range(NZ)])
+    cand_score = votes.T
+    blended_qkv = encode_last(
+        (3, NZ - 3, 4), upper, lower, low, high, weights, total, squares, prompts
+    )
     return (rank_hidden, cand_score, blended_qkv)
 
 

time: 168 us -> 185 us (1.10); the launches traced: 166 us -> 184 us
  starting transfers between devices: 33.7 us -> 48.3 us
  blocking collectives: 13.5 us -> 0 us
  waiting for transfers between devices: 72.2 us -> 83 us
  local copies, waits for them, and re-layouts: 8.35 us -> 14.4 us
    ppermute x0 -> x11, waiting for transfers between devices: none -> 23.6 us  [the longest x1 12.9 us: body(): c_before = lax.ppermute(context, 'y', ring(NY, 1))]
    ppermute x2, waiting for transfers between devices: 2.71 us -> 23.6 us  [body(): upper = lax.ppermute(upper, 'z', ring(NZ, -1))]
    ppermute x2, waiting for transfers between devices: 2.42 us -> 21.3 us  [body(): lower = lax.ppermute(lower, 'z', ring(NZ, 1))]
    ppermute x0 -> x11, starting transfers between devices: none -> 14.2 us  [the longest x3 3.78 us: body(): votes = votes + lax.ppermute(votes, 'z', [(i, i ^ bit) for i in range(NZ)])]
    all_to_all x1 -> x0, blocking collectives: 13.5 us -> none  [body(): votes = lax.all_to_all(votes, 'z', split_axis=0, concat_axis=0, tiled=True)]
    all_to_all x1, waiting for transfers between devices: 10.7 us -> 0.01 us  [body(): lax.all_to_all(outgoing.reshape(prompts, -1, features), PLANE, split_axis...]
    ppermute x1, waiting for transfers between devices: 10.5 us -> 0.01 us  [body(): low = lax.ppermute(lower[:half], 'z', ring(NZ, 1))]
    all_gather x1, waiting for transfers between devices: 8.57 us -> 0.01 us  [body(): columns = lax.all_gather(out_weight.T, ('x', 'core'), axis=0, tiled=True)]
  transfers between devices with their start and end apart: 22 -> 32, of which waited for: 12 -> 11; matrix products, arithmetic and copies ran while one was open for 3% -> 4% of each run, Pallas kernels for 11% -> 9%
where the time goes in v7:
time: 185 us; the launch traced here: 184 us
  waiting for transfers between devices  83 us (45%)
  starting transfers between devices  48.3 us (26%)
  Pallas kernels  21.3 us (12%)
  local copies, waits for them, and re-layouts  14.4 us (8%)
  between operations  14.4 us (8%)
  other arithmetic  2.39 us (1%)
    ppermute x2, waiting for transfers between devices, body(): upper = lax.ppermute(upper, 'z', ring(NZ, -1))  23.6 us
    ppermute x2, waiting for transfers between devices, body(): lower = lax.ppermute(lower, 'z', ring(NZ, 1))  21.3 us
    ppermute x1, waiting for transfers between devices, body(): c_before = lax.ppermute(context, 'y', ring(NY, 1))  12.9 us
    unnamed x48, local copies, waits for them, and re-layouts  9.32 us
    ppermute x3, waiting for transfers between devices, body(): votes = votes + lax.ppermute(votes, 'z', [(i, i ^ bit) for i in range(NZ)])  8.32 us
    all_to_all x1, starting transfers between devices, body(): lax.all_to_all(outgoing.reshape(prompts, -1, features), PLANE, split_axis...  7.62 us
    ppermute x2, starting transfers between devices, body(): upper = lax.ppermute(upper, 'z', ring(NZ, -1))  6.33 us
    ppermute x1, waiting for transfers between devices, body(): lax.ppermute(y_before[:2], 'y', ring(NY, 1))  5.64 us
  transfers between devices with their start and end apart: 32, of which 11 were waited for; matrix products, arithmetic and copies ran while one was open for 4% of the time, Pallas kernels for 9%

profile of v7, /device:TPU:2, one launch (start us, length us, event | category | flops | bytes accessed | tf_op | source)
XLA Modules:
  0.0 184.5 jit_solution(3482523245413953031)
XLA Ops:
  7.9 3.8 %shard_map.157 = bf16[96,8,512]{2,1,0:T(8,128)(2,1)} custom-call(s32[1,32]{1,0:T(1,128)} %owner_ref.1, s32[8,32]{1,0:T(8,128)} %bitcast.72, s32[8,32]{1,0:T(8,128)} %bitcast.73, bf16[256,8,512]{2,1,0:T(8,128)(2,1)} %bitcast.69), custom_call_target="tpu_custom_call" | custom-call | bytes 3145728 | tf_op jit(solution)/shard_map/pallas_call | solution.py:61
  11.7 7.6 %all-to-all-start = ((bf16[32,24,512]{2,1,0:T(8,128)(2,1)}), bf16[32,24,512]{2,1,0:T(8,128)(2,1)S(1)}, u32[]{:S(2)}, u32[]{:S(2)}) async-start(bf16[32,24,512]{2,1,0:T(8,128)(2,1)} %bitcast.68), calls=%async_computation | async-start | bytes 1572864 | tf_op jit(solution)/shard_map/all_to_all | solution.py:318
  20.2 1.5 collective-permute-start
  21.8 1.8 collective-permute-start.1
  25.7 12.9 %collective-permute-done.before_ref = bf16[8,32,640]{2,1,0:T(8,128)(2,1)S(1)} collective-permute-done((bf16[8,32,640]{2,1,0:T(8,128)(2,1)S(1)}, bf16[8,32,640]{2,1,0:T(8,128)(2,1)S(1)}, u32[]{:S(2)}, u32[]{:S(2)}) %collective-permute-start) | collective-permute-done | bytes 327712 | tf_op jit(solution)/shard_map/ppermute | solution.py:326
  38.7 2.0 %collective-permute-start.2 = (bf16[768,512]{1,0:T(8,128)(2,1)S(1)}, bf16[768,512]{1,0:T(8,128)(2,1)}, u32[]{:S(2)}, u32[]{:S(2)}) collective-permute-start(bf16[768,512]{1,0:T(8,128)(2,1)S(1)} %bitcast.62), channel_id=1, source_target_pairs={{0,1},{1,2},{2,3},{3,4},{4,5},{5,6},{6,7},{7,0},{8,9},{9,10},{10,1... | collective-permute-start | bytes 2359304 | tf_op jit(solution)/shard_map/ppermute | solution.py:340
  40.7 4.0 %collective-permute-start.3 = (bf16[768,512]{1,0:T(8,128)(2,1)S(1)}, bf16[768,512]{1,0:T(8,128)(2,1)}, u32[]{:S(2)}, u32[]{:S(2)}) collective-permute-start(bf16[768,512]{1,0:T(8,128)(2,1)S(1)} %bitcast.63), channel_id=1, source_target_pairs={{0,7},{1,0},{2,1},{3,2},{4,3},{5,4},{6,5},{7,6},{8,15},{9,8},{10,9... | collective-permute-start | bytes 2359304 | tf_op jit(solution)/shard_map/ppermute | solution.py:341
  46.7 4.3 %collective-permute-done.4 = bf16[1,3,128,256]{3,2,1,0:T(8,128)(2,1)S(1)} collective-permute-done((bf16[1,3,128,256]{3,2,1,0:T(8,128)(2,1)S(1)}, bf16[1,3,128,256]{3,2,1,0:T(8,128)(2,1)S(1)}, u32[]{:S(2)}, u32[]{:S(2)}) %collective-permute-start.4) | collective-permute-done | bytes 196640 | tf_op jit(solution)/shard_map/ppermute | solution.py:344
  53.2 2.7 %collective-permute-start.8 = (bf16[4,32,640]{2,1,0:T(8,128)(2,1)S(1)}, bf16[4,32,640]{2,1,0:T(8,128)(2,1)S(1)}, u32[]{:S(2)}, u32[]{:S(2)}) collective-permute-start(bf16[4,32,640]{2,1,0:T(8,128)(2,1)S(1)} %slice.35), channel_id=1, source_target_pairs={{0,192},{64,0},{128,64},{192,128},{1,193},{65,1},{129,65},{193,129... | collective-permute-start | bytes 491528 | tf_op jit(solution)/shard_map/ppermute | solution.py:343
  56.8 2.3 %collective-permute-done.7.low_ref = bf16[4,32,640]{2,1,0:T(8,128)(2,1)S(1)} collective-permute-done((bf16[4,32,640]{2,1,0:T(8,128)(2,1)S(1)}, bf16[4,32,640]{2,1,0:T(8,128)(2,1)S(1)}, u32[]{:S(2)}, u32[]{:S(2)}) %collective-permute-start.7) | collective-permute-done | bytes 163872 | tf_op jit(solution)/shard_map/ppermute | solution.py:342
  59.1 3.1 %collective-permute-done.2.refs_4_ = bf16[768,512]{1,0:T(8,128)(2,1)} collective-permute-done((bf16[768,512]{1,0:T(8,128)(2,1)S(1)}, bf16[768,512]{1,0:T(8,128)(2,1)}, u32[]{:S(2)}, u32[]{:S(2)}) %collective-permute-start.2) | collective-permute-done | bytes 786464 | tf_op jit(solution)/shard_map/ppermute | solution.py:340
  63.7 2.6 %shard_map.158 = (bf16[8,4,32,1280]{3,2,1,0:T(8,128)(2,1)S(1)}, f32[8,128]{1,0:T(8,128)S(1)}) custom-call(bf16[8,32,640]{2,1,0:T(8,128)(2,1)S(1)} %bitcast.67, bf16[8,32,640]{2,1,0:T(8,128)(2,1)S(1)} %collective-permute-done.before_ref, bf16[4,32,640]{2,1,0:T(8,128)(2,1)S(1)} %collective-permute-done.7.low_ref, ...), custom_call_target="tpu_custom_call" | custom-call | flops 1677721600 | bytes 6291456 | tf_op jit(solution)/shard_map/pallas_call | solution.py:126
  66.3 1.5 copy-done.3
  67.9 3.1 %collective-permute-start.10 = (bf16[768,512]{1,0:T(8,128)(2,1)}, bf16[768,512]{1,0:T(8,128)(2,1)S(1)}, u32[]{:S(2)}, u32[]{:S(2)}) collective-permute-start(bf16[768,512]{1,0:T(8,128)(2,1)} %collective-permute-done.3.refs_1_), channel_id=1, source_target_pairs={{0,7},{1,0},{2,1},{3,2},{4,3},{5,4},{6,5},{7,6},{8,15},{9,8},{10,9... | collective-permute-start | bytes 2359304 | tf_op jit(solution)/shard_map/ppermute | solution.py:358
  71.8 2.3 %collective-permute-start.15 = (bf16[4,3,128,256]{3,2,1,0:T(8,128)(2,1)S(1)}, bf16[4,3,128,256]{3,2,1,0:T(8,128)(2,1)S(1)}, u32[]{:S(2)}, u32[]{:S(2)}) collective-permute-start(bf16[4,3,128,256]{3,2,1,0:T(8,128)(2,1)S(1)} %pad_maximum_fusion.refs_0_), channel_id=1, source_target_pairs={{0,192},{64,0},{128,64},{192,128},{1,193},{65,1},{129,65},{193,129... | collective-permute-start | bytes 2359304 | tf_op jit(solution)/shard_map/ppermute | solution.py:360
  74.2 23.6 %collective-permute-done.10.refs_2_ = bf16[768,512]{1,0:T(8,128)(2,1)S(1)} collective-permute-done((bf16[768,512]{1,0:T(8,128)(2,1)}, bf16[768,512]{1,0:T(8,128)(2,1)S(1)}, u32[]{:S(2)}, u32[]{:S(2)}) %collective-permute-start.10) | collective-permute-done | bytes 786464 | tf_op jit(solution)/shard_map/ppermute | solution.py:358
  97.8 4.9 %collective-permute-done.9.refs_3_ = bf16[768,512]{1,0:T(8,128)(2,1)S(1)} collective-permute-done((bf16[768,512]{1,0:T(8,128)(2,1)}, bf16[768,512]{1,0:T(8,128)(2,1)S(1)}, u32[]{:S(2)}, u32[]{:S(2)}) %collective-permute-start.9) | collective-permute-done | bytes 786464 | tf_op jit(solution)/shard_map/ppermute | solution.py:357
  102.7 3.2 %collective-permute-start.12 = (bf16[768,512]{1,0:T(8,128)(2,1)S(1)}, bf16[768,512]{1,0:T(8,128)(2,1)}, u32[]{:S(2)}, u32[]{:S(2)}) collective-permute-start(bf16[768,512]{1,0:T(8,128)(2,1)S(1)} %collective-permute-done.10.refs_2_), channel_id=1, source_target_pairs={{0,7},{1,0},{2,1},{3,2},{4,3},{5,4},{6,5},{7,6},{8,15},{9,8},{10,9... | collective-permute-start | bytes 2359304 | tf_op jit(solution)/shard_map/ppermute | solution.py:365
  106.4 3.0 %collective-permute-start.16 = (bf16[2,3,128,256]{3,2,1,0:T(8,128)(2,1)S(1)}, bf16[2,3,128,256]{3,2,1,0:T(8,128)(2,1)S(1)}, u32[]{:S(2)}, u32[]{:S(2)}) collective-permute-start(bf16[2,3,128,256]{3,2,1,0:T(8,128)(2,1)S(1)} %slice.45), channel_id=1, source_target_pairs={{0,192},{64,0},{128,64},{192,128},{1,193},{65,1},{129,65},{193,129... | collective-permute-start | bytes 1179656 | tf_op jit(solution)/shard_map/ppermute | solution.py:369
  109.4 5.6 %collective-permute-done.14 = bf16[2,3,128,256]{3,2,1,0:T(8,128)(2,1)S(1)} collective-permute-done((bf16[2,3,128,256]{3,2,1,0:T(8,128)(2,1)S(1)}, bf16[2,3,128,256]{3,2,1,0:T(8,128)(2,1)S(1)}, u32[]{:S(2)}, u32[]{:S(2)}) %collective-permute-start.14) | collective-permute-done | bytes 393248 | tf_op jit(solution)/shard_map/ppermute | solution.py:368
  115.6 16.4 %collective-permute-done.11.refs_1_ = bf16[768,512]{1,0:T(8,128)(2,1)} collective-permute-done((bf16[768,512]{1,0:T(8,128)(2,1)S(1)}, bf16[768,512]{1,0:T(8,128)(2,1)}, u32[]{:S(2)}, u32[]{:S(2)}) %collective-permute-start.11) | collective-permute-done | bytes 786464 | tf_op jit(solution)/shard_map/ppermute | solution.py:364
  134.2 3.3 %collective-permute-start.18 = (bf16[384,512]{1,0:T(8,128)(2,1)S(1)}, bf16[384,512]{1,0:T(8,128)(2,1)S(1)}, u32[]{:S(2)}, u32[]{:S(2)}) collective-permute-start(bf16[384,512]{1,0:T(8,128)(2,1)S(1)} %slice.40), channel_id=1, source_target_pairs={{0,7},{1,0},{2,1},{3,2},{4,3},{5,4},{6,5},{7,6},{8,15},{9,8},{10,9... | collective-permute-start | bytes 1179656 | tf_op jit(solution)/shard_map/ppermute | solution.py:380
  137.5 1.7 fusion.22
  140.5 2.1 %collective-permute-start.24 = (bf16[32,1280]{1,0:T(8,128)(2,1)S(1)}, bf16[32,1280]{1,0:T(8,128)(2,1)S(1)}, u32[]{:S(2)}, u32[]{:S(2)}) collective-permute-start(bf16[32,1280]{1,0:T(8,128)(2,1)S(1)} %get-tuple-element.76), channel_id=1, source_target_pairs={{0,128},{64,192},{128,0},{192,64},{1,129},{65,193},{129,1},{193,65... | collective-permute-start | bytes 245768 | tf_op jit(solution)/shard_map/ppermute | solution.py:383
  142.9 2.2 %shard_map.159.refs_5_.refs_4_ = bf16[3,4096,256]{2,1,0:T(8,128)(2,1)S(1)} custom-call(s32[4]{0:T(128)S(1)} %pad_add_fusion.where_ref, f32[8,128]{1,0:T(8,128)S(1)} %get-tuple-element.63.token_ref, bf16[4,3,128,256]{3,2,1,0:T(8,128)(2,1)S(1)} %pad_maximum_fusion.refs_0_, bf16[4,3,128,256]{3,2,1,0:T(8,128)(2,1)S(1)} %collective-permute-done.13.refs_1_, ...), custom_call_target="tpu_custom_call" | custom-call | bytes 12582912 | tf_op jit(solution)/shard_map/pallas_call | solution.py:92
  145.2 5.5 %shard_map.160 = (f32[3,768,256]{2,1,0:T(8,128)S(1)}, f32[768,128]{1,0:T(8,128)S(1)}) custom-call(bf16[768,512]{1,0:T(8,128)(2,1)S(1)} %bitcast.64, bf16[768,512]{1,0:T(8,128)(2,1)} %collective-permute-done.3.refs_1_, bf16[768,512]{1,0:T(8,128)(2,1)S(1)} %copy-done.9, bf16[768,512]{1,0:T(8,128)(2,1)S(1)} %copy-done.11, ...), custom_call_target="tpu_custom_call" | custom-call | flops 3019898880 | bytes 12582912 | tf_op jit(solution)/shard_map/pallas_call | solution.py:192
  152.3 2.1 %shard_map.161 = (bf16[32,5120]{1,0:T(8,128)(2,1)}, f32[8,32]{1,0:T(8,128)}) custom-call(s32[4]{0:T(128)} %copy-done.6, s32[1,3]{1,0:T(1,128)} %pair_ref.1, bf16[32,5120]{1,0:T(8,128)(2,1)} %bitcast.70, bf16[1,5120]{1,0:T(2,128)(2,1)} %reshape.57.gain_ref, bf16[1,5120]{1,0:T(2,128)(2,1)} %reshape.58.score_ref, bf16[32,1280]{1,0:T(8,128)(2,1)} %get-tuple-element.78.refs_0_, ...), custom_call_target="tpu_custom_call" | custom-call | flops 1310720 | bytes 2097152 | tf_op jit(solution)/shard_map/pallas_call | solution.py:274
  154.5 3.8 %collective-permute-done.26 = f32[8,32]{1,0:T(8,128)S(1)} collective-permute-done((f32[8,32]{1,0:T(8,128)}, f32[8,32]{1,0:T(8,128)S(1)}, u32[]{:S(2)}, u32[]{:S(2)}) %collective-permute-start.26) | collective-permute-done | bytes 1056 | tf_op jit(solution)/shard_map/ppermute | solution.py:402
  159.0 4.5 %collective-permute-done.27 = f32[8,32]{1,0:T(8,128)S(1)} collective-permute-done((f32[8,32]{1,0:T(8,128)S(1)}, f32[8,32]{1,0:T(8,128)S(1)}, u32[]{:S(2)}, u32[]{:S(2)}) %collective-permute-start.27) | collective-permute-done | bytes 1056 | tf_op jit(solution)/shard_map/ppermute | solution.py:402
  163.5 3.8 %collective-permute-start.28 = (f32[8,32]{1,0:T(8,128)S(1)}, f32[8,32]{1,0:T(8,128)S(1)}, u32[]{:S(2)}, u32[]{:S(2)}) collective-permute-start(f32[8,32]{1,0:T(8,128)S(1)} %add.24), channel_id=1, source_target_pairs={{0,4},{1,5},{2,6},{3,7},{4,0},{5,1},{6,2},{7,3},{8,12},{9,13},{10,... | collective-permute-start | bytes 3080 | tf_op jit(solution)/shard_map/ppermute | solution.py:402
  167.3 2.8 %copy-done.2 = bf16[3,4096,256]{2,1,0:T(8,128)(2,1)S(1)} copy-done((bf16[3,4096,256]{2,1,0:T(8,128)(2,1)S(1)}, bf16[3,4096,256]{2,1,0:T(8,128)(2,1)}, u32[]{:S(2)}) %copy-start.2) | copy-done | bytes 6291480
  172.0 5.0 %shard_map.162 = bf16[32,3,24,256]{3,2,1,0:T(8,128)(2,1)} custom-call(bf16[768,512]{1,0:T(8,128)(2,1)} %collective-permute-done.12.refs_0_, bf16[768,512]{1,0:T(8,128)(2,1)} %collective-permute-done.11.refs_1_, bf16[384,512]{1,0:T(8,128)(2,1)S(1)} %copy-done.13, bf16[384,512]{1,0:T(8,128)(2,1)S(1)} %copy-done.15, bf16[3,4096,256]{2,1,0:T(8,128)(2,1)S(1)} %copy-done.2, ...), custom_call_target="tpu_custom_call" | custom-call | flops 36238786560 | bytes 12582912 | tf_op jit(solution)/shard_map/pallas_call | solution.py:221
  (108 shorter events, 20.7 us)
Async XLA Ops:
  7.2 55.0 %all-gather.2.cloned.1.call-start = ((), (), s32[]{:S(2)}) async-start(), calls=%async_computation.2 | async-start | bytes 1843200 | tf_op jit(solution)/shard_map/all_gather | solution.py:312
  11.7 26.9 %all-to-all-start = ((bf16[32,24,512]{2,1,0:T(8,128)(2,1)}), bf16[32,24,512]{2,1,0:T(8,128)(2,1)S(1)}, u32[]{:S(2)}, u32[]{:S(2)}) async-start(bf16[32,24,512]{2,1,0:T(8,128)(2,1)} %bitcast.68), calls=%async_computation | async-start | bytes 1572864 | tf_op jit(solution)/shard_map/all_to_all | solution.py:318
  19.4 112.6 %reduce-scatter.2.cloned.1.call-start = ((), (), s32[]{:S(2)}) async-start(), calls=%async_computation.3 | async-start | bytes 2949120 | tf_op jit(solution)/shard_map/reduce_scatter | solution.py:353
  20.2 18.4 %collective-permute-start = (bf16[8,32,640]{2,1,0:T(8,128)(2,1)S(1)}, bf16[8,32,640]{2,1,0:T(8,128)(2,1)S(1)}, u32[]{:S(2)}, u32[]{:S(2)}) collective-permute-start(bf16[8,32,640]{2,1,0:T(8,128)(2,1)S(1)} %bitcast.65), channel_id=1, source_target_pairs={{0,64},{64,128},{128,192},{192,0},{1,65},{65,129},{129,193},{193,1... | collective-permute-start | bytes 983048 | tf_op jit(solution)/shard_map/ppermute | solution.py:326
  21.8 16.9 %collective-permute-start.1 = (bf16[8,32,640]{2,1,0:T(8,128)(2,1)S(1)}, bf16[8,32,640]{2,1,0:T(8,128)(2,1)S(1)}, u32[]{:S(2)}, u32[]{:S(2)}) collective-permute-start(bf16[8,32,640]{2,1,0:T(8,128)(2,1)S(1)} %bitcast.66), channel_id=1, source_target_pairs={{0,192},{64,0},{128,64},{192,128},{1,193},{65,1},{129,65},{193,129... | collective-permute-start | bytes 983048 | tf_op jit(solution)/shard_map/ppermute | solution.py:327
  38.7 23.6 %collective-permute-start.2 = (bf16[768,512]{1,0:T(8,128)(2,1)S(1)}, bf16[768,512]{1,0:T(8,128)(2,1)}, u32[]{:S(2)}, u32[]{:S(2)}) collective-permute-start(bf16[768,512]{1,0:T(8,128)(2,1)S(1)} %bitcast.62), channel_id=1, source_target_pairs={{0,1},{1,2},{2,3},{3,4},{4,5},{5,6},{6,7},{7,0},{8,9},{9,10},{10,1... | collective-permute-start | bytes 2359304 | tf_op jit(solution)/shard_map/ppermute | solution.py:340
  40.7 21.6 %collective-permute-start.3 = (bf16[768,512]{1,0:T(8,128)(2,1)S(1)}, bf16[768,512]{1,0:T(8,128)(2,1)}, u32[]{:S(2)}, u32[]{:S(2)}) collective-permute-start(bf16[768,512]{1,0:T(8,128)(2,1)S(1)} %bitcast.63), channel_id=1, source_target_pairs={{0,7},{1,0},{2,1},{3,2},{4,3},{5,4},{6,5},{7,6},{8,15},{9,8},{10,9... | collective-permute-start | bytes 2359304 | tf_op jit(solution)/shard_map/ppermute | solution.py:341
  44.7 6.3 %collective-permute-start.4 = (bf16[1,3,128,256]{3,2,1,0:T(8,128)(2,1)S(1)}, bf16[1,3,128,256]{3,2,1,0:T(8,128)(2,1)S(1)}, u32[]{:S(2)}, u32[]{:S(2)}) collective-permute-start(bf16[1,3,128,256]{3,2,1,0:T(8,128)(2,1)S(1)} %fusion.11), channel_id=1, source_target_pairs={{0,16},{16,32},{32,48},{48,0},{1,17},{17,33},{33,49},{49,1},{2,18}... | collective-permute-start | bytes 589832 | tf_op jit(solution)/shard_map/ppermute | solution.py:344
  46.1 7.1 %collective-permute-start.6 = (bf16[1,3,128,256]{3,2,1,0:T(8,128)(2,1)S(1)}, bf16[1,3,128,256]{3,2,1,0:T(8,128)(2,1)S(1)}, u32[]{:S(2)}, u32[]{:S(2)}) collective-permute-start(bf16[1,3,128,256]{3,2,1,0:T(8,128)(2,1)S(1)} %fusion.11), channel_id=1, source_target_pairs={{0,48},{16,0},{32,16},{48,32},{1,49},{17,1},{33,17},{49,33},{2,50}... | collective-permute-start | bytes 589832 | tf_op jit(solution)/shard_map/ppermute | solution.py:345
  51.0 5.7 %collective-permute-start.5 = (bf16[1,3,128,256]{3,2,1,0:T(8,128)(2,1)S(1)}, bf16[1,3,128,256]{3,2,1,0:T(8,128)(2,1)S(1)}, u32[]{:S(2)}, u32[]{:S(2)}) collective-permute-start(bf16[1,3,128,256]{3,2,1,0:T(8,128)(2,1)S(1)} %collective-permute-done.4), channel_id=1, source_target_pairs={{0,16},{16,32},{32,48},{48,0},{1,17},{17,33},{33,49},{49,1},{2,18}... | collective-permute-start | bytes 589832 | tf_op jit(solution)/shard_map/ppermute | solution.py:346
  52.5 6.6 %collective-permute-start.7 = (bf16[4,32,640]{2,1,0:T(8,128)(2,1)S(1)}, bf16[4,32,640]{2,1,0:T(8,128)(2,1)S(1)}, u32[]{:S(2)}, u32[]{:S(2)}) collective-permute-start(bf16[4,32,640]{2,1,0:T(8,128)(2,1)S(1)} %slice.34), channel_id=1, source_target_pairs={{0,64},{64,128},{128,192},{192,0},{1,65},{65,129},{129,193},{193,1... | collective-permute-start | bytes 491528 | tf_op jit(solution)/shard_map/ppermute | solution.py:342
  53.2 5.9 %collective-permute-start.8 = (bf16[4,32,640]{2,1,0:T(8,128)(2,1)S(1)}, bf16[4,32,640]{2,1,0:T(8,128)(2,1)S(1)}, u32[]{:S(2)}, u32[]{:S(2)}) collective-permute-start(bf16[4,32,640]{2,1,0:T(8,128)(2,1)S(1)} %slice.35), channel_id=1, source_target_pairs={{0,192},{64,0},{128,64},{192,128},{1,193},{65,1},{129,65},{193,129... | collective-permute-start | bytes 491528 | tf_op jit(solution)/shard_map/ppermute | solution.py:343
  67.9 29.9 %collective-permute-start.10 = (bf16[768,512]{1,0:T(8,128)(2,1)}, bf16[768,512]{1,0:T(8,128)(2,1)S(1)}, u32[]{:S(2)}, u32[]{:S(2)}) collective-permute-start(bf16[768,512]{1,0:T(8,128)(2,1)} %collective-permute-done.3.refs_1_), channel_id=1, source_target_pairs={{0,7},{1,0},{2,1},{3,2},{4,3},{5,4},{6,5},{7,6},{8,15},{9,8},{10,9... | collective-permute-start | bytes 2359304 | tf_op jit(solution)/shard_map/ppermute | solution.py:358
  70.9 31.8 %collective-permute-start.9 = (bf16[768,512]{1,0:T(8,128)(2,1)}, bf16[768,512]{1,0:T(8,128)(2,1)S(1)}, u32[]{:S(2)}, u32[]{:S(2)}) collective-permute-start(bf16[768,512]{1,0:T(8,128)(2,1)} %collective-permute-done.2.refs_4_), channel_id=1, source_target_pairs={{0,1},{1,2},{2,3},{3,4},{4,5},{5,6},{6,7},{7,0},{8,9},{9,10},{10,1... | collective-permute-start | bytes 2359304 | tf_op jit(solution)/shard_map/ppermute | solution.py:357
  71.0 35.0 %collective-permute-start.13 = (bf16[4,3,128,256]{3,2,1,0:T(8,128)(2,1)S(1)}, bf16[4,3,128,256]{3,2,1,0:T(8,128)(2,1)S(1)}, u32[]{:S(2)}, u32[]{:S(2)}) collective-permute-start(bf16[4,3,128,256]{3,2,1,0:T(8,128)(2,1)S(1)} %pad_maximum_fusion.refs_0_), channel_id=1, source_target_pairs={{0,64},{64,128},{128,192},{192,0},{1,65},{65,129},{129,193},{193,1... | collective-permute-start | bytes 2359304 | tf_op jit(solution)/shard_map/ppermute | solution.py:359
  71.8 34.5 %collective-permute-start.15 = (bf16[4,3,128,256]{3,2,1,0:T(8,128)(2,1)S(1)}, bf16[4,3,128,256]{3,2,1,0:T(8,128)(2,1)S(1)}, u32[]{:S(2)}, u32[]{:S(2)}) collective-permute-start(bf16[4,3,128,256]{3,2,1,0:T(8,128)(2,1)S(1)} %pad_maximum_fusion.refs_0_), channel_id=1, source_target_pairs={{0,192},{64,0},{128,64},{192,128},{1,193},{65,1},{129,65},{193,129... | collective-permute-start | bytes 2359304 | tf_op jit(solution)/shard_map/ppermute | solution.py:360
  102.7 29.3 %collective-permute-start.11 = (bf16[768,512]{1,0:T(8,128)(2,1)S(1)}, bf16[768,512]{1,0:T(8,128)(2,1)}, u32[]{:S(2)}, u32[]{:S(2)}) collective-permute-start(bf16[768,512]{1,0:T(8,128)(2,1)S(1)} %collective-permute-done.9.refs_3_), channel_id=1, source_target_pairs={{0,1},{1,2},{2,3},{3,4},{4,5},{5,6},{6,7},{7,0},{8,9},{9,10},{10,1... | collective-permute-start | bytes 2359304 | tf_op jit(solution)/shard_map/ppermute | solution.py:364
  102.7 29.3 %collective-permute-start.12 = (bf16[768,512]{1,0:T(8,128)(2,1)S(1)}, bf16[768,512]{1,0:T(8,128)(2,1)}, u32[]{:S(2)}, u32[]{:S(2)}) collective-permute-start(bf16[768,512]{1,0:T(8,128)(2,1)S(1)} %collective-permute-done.10.refs_2_), channel_id=1, source_target_pairs={{0,7},{1,0},{2,1},{3,2},{4,3},{5,4},{6,5},{7,6},{8,15},{9,8},{10,9... | collective-permute-start | bytes 2359304 | tf_op jit(solution)/shard_map/ppermute | solution.py:365
  106.0 9.1 %collective-permute-start.14 = (bf16[2,3,128,256]{3,2,1,0:T(8,128)(2,1)S(1)}, bf16[2,3,128,256]{3,2,1,0:T(8,128)(2,1)S(1)}, u32[]{:S(2)}, u32[]{:S(2)}) collective-permute-start(bf16[2,3,128,256]{3,2,1,0:T(8,128)(2,1)S(1)} %slice.44), channel_id=1, source_target_pairs={{0,64},{64,128},{128,192},{192,0},{1,65},{65,129},{129,193},{193,1... | collective-permute-start | bytes 1179656 | tf_op jit(solution)/shard_map/ppermute | solution.py:368
  106.4 8.7 %collective-permute-start.16 = (bf16[2,3,128,256]{3,2,1,0:T(8,128)(2,1)S(1)}, bf16[2,3,128,256]{3,2,1,0:T(8,128)(2,1)S(1)}, u32[]{:S(2)}, u32[]{:S(2)}) collective-permute-start(bf16[2,3,128,256]{3,2,1,0:T(8,128)(2,1)S(1)} %slice.45), channel_id=1, source_target_pairs={{0,192},{64,0},{128,64},{192,128},{1,193},{65,1},{129,65},{193,129... | collective-permute-start | bytes 1179656 | tf_op jit(solution)/shard_map/ppermute | solution.py:369
  109.4 24.8 %collective-permute-start.19 = (bf16[4,3,128,256]{3,2,1,0:T(8,128)(2,1)S(1)}, bf16[4,3,128,256]{3,2,1,0:T(8,128)(2,1)}, u32[]{:S(2)}, u32[]{:S(2)}) collective-permute-start(bf16[4,3,128,256]{3,2,1,0:T(8,128)(2,1)S(1)} %pad_maximum_fusion.refs_0_), channel_id=1, source_target_pairs={{0,8},{8,0},{1,9},{9,1},{2,10},{10,2},{3,11},{11,3},{4,12},{12,4},... | collective-permute-start | bytes 2359304 | tf_op jit(solution)/shard_map/ppermute | solution.py:373
  115.0 24.1 %collective-permute-start.20 = (bf16[4,3,128,256]{3,2,1,0:T(8,128)(2,1)S(1)}, bf16[4,3,128,256]{3,2,1,0:T(8,128)(2,1)}, u32[]{:S(2)}, u32[]{:S(2)}) collective-permute-start(bf16[4,3,128,256]{3,2,1,0:T(8,128)(2,1)S(1)} %collective-permute-done.13.refs_1_), channel_id=1, source_target_pairs={{0,8},{8,0},{1,9},{9,1},{2,10},{10,2},{3,11},{11,3},{4,12},{12,4},... | collective-permute-start | bytes 2359304 | tf_op jit(solution)/shard_map/ppermute | solution.py:373
  115.1 25.4 %collective-permute-start.22 = (bf16[4,3,128,256]{3,2,1,0:T(8,128)(2,1)S(1)}, bf16[4,3,128,256]{3,2,1,0:T(8,128)(2,1)}, u32[]{:S(2)}, u32[]{:S(2)}) collective-permute-start(bf16[4,3,128,256]{3,2,1,0:T(8,128)(2,1)S(1)} %collective-permute-done.15.refs_3_), channel_id=1, source_target_pairs={{0,8},{8,0},{1,9},{9,1},{2,10},{10,2},{3,11},{11,3},{4,12},{12,4},... | collective-permute-start | bytes 2359304 | tf_op jit(solution)/shard_map/ppermute | solution.py:373
  132.0 10.6 %collective-permute-start.21 = (bf16[4,3,128,256]{3,2,1,0:T(8,128)(2,1)S(1)}, bf16[4,3,128,256]{3,2,1,0:T(8,128)(2,1)S(1)}, u32[]{:S(2)}, u32[]{:S(2)}) collective-permute-start(bf16[4,3,128,256]{3,2,1,0:T(8,128)(2,1)S(1)} %pad_maximum_fusion.1.refs_2_), channel_id=1, source_target_pairs={{0,8},{8,0},{1,9},{9,1},{2,10},{10,2},{3,11},{11,3},{4,12},{12,4},... | collective-permute-start | bytes 2359304 | tf_op jit(solution)/shard_map/ppermute | solution.py:376
  133.1 17.7 %collective-permute-start.17 = (bf16[384,512]{1,0:T(8,128)(2,1)S(1)}, bf16[384,512]{1,0:T(8,128)(2,1)S(1)}, u32[]{:S(2)}, u32[]{:S(2)}) collective-permute-start(bf16[384,512]{1,0:T(8,128)(2,1)S(1)} %slice.39), channel_id=1, source_target_pairs={{0,1},{1,2},{2,3},{3,4},{4,5},{5,6},{6,7},{7,0},{8,9},{9,10},{10,1... | collective-permute-start | bytes 1179656 | tf_op jit(solution)/shard_map/ppermute | solution.py:379
  134.2 17.4 %collective-permute-start.18 = (bf16[384,512]{1,0:T(8,128)(2,1)S(1)}, bf16[384,512]{1,0:T(8,128)(2,1)S(1)}, u32[]{:S(2)}, u32[]{:S(2)}) collective-permute-start(bf16[384,512]{1,0:T(8,128)(2,1)S(1)} %slice.40), channel_id=1, source_target_pairs={{0,7},{1,0},{2,1},{3,2},{4,3},{5,4},{6,5},{7,6},{8,15},{9,8},{10,9... | collective-permute-start | bytes 1179656 | tf_op jit(solution)/shard_map/ppermute | solution.py:380
  139.1 11.6 %collective-permute-start.23 = (bf16[32,1280]{1,0:T(8,128)(2,1)S(1)}, bf16[32,1280]{1,0:T(8,128)(2,1)S(1)}, u32[]{:S(2)}, u32[]{:S(2)}) collective-permute-start(bf16[32,1280]{1,0:T(8,128)(2,1)S(1)} %get-tuple-element.77), channel_id=1, source_target_pairs={{0,192},{64,0},{128,64},{192,128},{1,193},{65,1},{129,65},{193,129... | collective-permute-start | bytes 245768 | tf_op jit(solution)/shard_map/ppermute | solution.py:383
  140.5 10.3 %collective-permute-start.24 = (bf16[32,1280]{1,0:T(8,128)(2,1)S(1)}, bf16[32,1280]{1,0:T(8,128)(2,1)S(1)}, u32[]{:S(2)}, u32[]{:S(2)}) collective-permute-start(bf16[32,1280]{1,0:T(8,128)(2,1)S(1)} %get-tuple-element.76), channel_id=1, source_target_pairs={{0,128},{64,192},{128,0},{192,64},{1,129},{65,193},{129,1},{193,65... | collective-permute-start | bytes 245768 | tf_op jit(solution)/shard_map/ppermute | solution.py:383
  142.6 8.2 %collective-permute-start.25 = (bf16[32,1280]{1,0:T(8,128)(2,1)S(1)}, bf16[32,1280]{1,0:T(8,128)(2,1)S(1)}, u32[]{:S(2)}, u32[]{:S(2)}) collective-permute-start(bf16[32,1280]{1,0:T(8,128)(2,1)S(1)} %get-tuple-element.75), channel_id=1, source_target_pairs={{0,64},{64,128},{128,192},{192,0},{1,65},{65,129},{129,193},{193,1... | collective-permute-start | bytes 245768 | tf_op jit(solution)/shard_map/ppermute | solution.py:383
  154.5 3.8 %collective-permute-start.26 = (f32[8,32]{1,0:T(8,128)}, f32[8,32]{1,0:T(8,128)S(1)}, u32[]{:S(2)}, u32[]{:S(2)}) collective-permute-start(f32[8,32]{1,0:T(8,128)} %get-tuple-element.70), channel_id=1, source_target_pairs={{0,1},{1,0},{2,3},{3,2},{4,5},{5,4},{6,7},{7,6},{8,9},{9,8},{10,11... | collective-permute-start | bytes 3080 | tf_op jit(solution)/shard_map/ppermute | solution.py:402
  159.0 4.5 %collective-permute-start.27 = (f32[8,32]{1,0:T(8,128)S(1)}, f32[8,32]{1,0:T(8,128)S(1)}, u32[]{:S(2)}, u32[]{:S(2)}) collective-permute-start(f32[8,32]{1,0:T(8,128)S(1)} %add.23), channel_id=1, source_target_pairs={{0,2},{1,3},{2,0},{3,1},{4,6},{5,7},{6,4},{7,5},{8,10},{9,11},{10,... | collective-permute-start | bytes 3080 | tf_op jit(solution)/shard_map/ppermute | solution.py:402
  163.5 13.5 %collective-permute-start.28 = (f32[8,32]{1,0:T(8,128)S(1)}, f32[8,32]{1,0:T(8,128)S(1)}, u32[]{:S(2)}, u32[]{:S(2)}) collective-permute-start(f32[8,32]{1,0:T(8,128)S(1)} %add.24), channel_id=1, source_target_pairs={{0,4},{1,5},{2,6},{3,7},{4,0},{5,1},{6,2},{7,3},{8,12},{9,13},{10,... | collective-permute-start | bytes 3080 | tf_op jit(solution)/shard_map/ppermute | solution.py:402
  (24 other events, 254.0 us)
Sparse Core Ops, SparseCore 0:
  9.9 30.5 all-gather.1
  68.0 60.6 reduce-scatter.1

commit v8 on v6

--- a/solution.py
+++ b/solution.py
@@ -35,9 +35,11 @@
     return context.astype(jnp.bfloat16).reshape(pair_count * length, row_width)
 
 
-def select_kernel(owner_ref, rank_ref, len_ref, rows_ref, out_ref, cand_ref, live_ref):
+def select_kernel(owner_ref, rank_ref, len_ref, rows_ref, out_ref, cand_ref, live_ref, mask_ref):
     places = rank_ref.shape[0]
     position = lax.broadcasted_iota(jnp.int32, rows_ref.shape[1:], 0)
+    for live in range(mask_ref.shape[0]):
+        mask_ref[live] = jnp.where(position < live, 1.0, 0.0).astype(mask_ref.dtype)
 
     def one_prompt(prompt, carry):
         owner = owner_ref[0, prompt]
@@ -46,9 +48,8 @@
             cand_ref[prompt, rank] = place
             live_ref[prompt, rank] = len_ref[place, prompt]
         for rank in range(3):
-            picked = rows_ref[prompt * places + cand_ref[prompt, rank]].astype(jnp.float32)
-            chosen = jnp.where(position < live_ref[prompt, rank], picked, 0.0)
-            out_ref[owner * 3 + rank] = chosen.astype(out_ref.dtype)
+            picked = rows_ref[prompt * places + cand_ref[prompt, rank]]
+            out_ref[owner * 3 + rank] = picked * mask_ref[live_ref[prompt, rank]]
         return carry
 
     lax.fori_loop(0, owner_ref.shape[1], one_prompt, 0, unroll=4)
@@ -63,7 +64,8 @@
         out_shape=jax.ShapeDtypeStruct((prompts * 3, length, features), blend_rows.dtype),
         in_specs=[smem, smem, smem, vmem],
         out_specs=vmem,
-        scratch_shapes=[pltpu.SMEM((prompts, cands), jnp.int32)] * 2,
+        scratch_shapes=[pltpu.SMEM((prompts, cands), jnp.int32)] * 2
+        + [pltpu.VMEM((length + 1, length, features), blend_rows.dtype)],
         cost_estimate=pl.CostEstimate(flops=0, bytes_accessed=3 << 20, transcendentals=0),
     )(blend_owner, cand_rank.T, cand_len.T, blend_rows.reshape(prompts * cands, length, features))
 
@@ -228,7 +230,7 @@
         out_specs=pl.BlockSpec((step_prompts, third, length, width), lambda i: (i, 0, 0, 0)),
         compiler_params=pltpu.CompilerParams(vmem_limit_bytes=24 << 20),
         cost_estimate=pl.CostEstimate(
-            flops=40 * rows * 3 * features * third * width,
+            flops=36 * rows * 3 * features * third * width,
             bytes_accessed=12 << 20,
             transcendentals=rows,
         ),

time: 168 us -> 167 us (level)
    ppermute x2, waiting for transfers between devices: 2.42 us -> 5.16 us  [body(): lower = lax.ppermute(lower, 'z', ring(NZ, 1))]
    reduce_scatter x1, waiting for transfers between devices: 7.2 us -> 5.29 us  [body(): part_sum = lax.psum_scatter(term_rows, 'z', scatter_dimension=0, tiled=True)]
  transfers between devices with their start and end apart: 22 -> 22, of which waited for: 12 -> 12; matrix products, arithmetic and copies ran while one was open for 3% -> 2% of each run, Pallas kernels for 11% -> 10%
where the time goes in v8:
time: 167 us; the launch traced here: 166 us
  waiting for transfers between devices  73.2 us (44%)
  starting transfers between devices  34 us (20%)
  Pallas kernels  19 us (11%)
  blocking collectives  14.3 us (9%)
  between operations  14.3 us (9%)
  local copies, waits for them, and re-layouts  7.35 us (4%)
  other arithmetic  2.37 us (1%)
    all_to_all x1, blocking collectives, body(): votes = lax.all_to_all(votes, 'z', split_axis=0, concat_axis=0, tiled=True)  14.3 us
    ppermute x1, waiting for transfers between devices, body(): low = lax.ppermute(lower[:half], 'z', ring(NZ, 1))  11.5 us
    all_to_all x1, waiting for transfers between devices, body(): lax.all_to_all(outgoing.reshape(prompts, -1, features), PLANE, split_axis...  10.8 us
    all_gather x1, waiting for transfers between devices, body(): columns = lax.all_gather(out_weight.T, PLANE, axis=0, tiled=True)  8.66 us
    ppermute x1, waiting for transfers between devices, body(): lax.ppermute(y_after[2:], 'y', ring(NY, -1))  8.35 us
    all_to_all x1, starting transfers between devices, body(): lax.all_to_all(outgoing.reshape(prompts, -1, features), PLANE, split_axis...  7.62 us
    ppermute x1, waiting for transfers between devices, body(): x_across = lax.ppermute(x_before, 'x', ring(NX, 1))  6.78 us
    pallas_call x1, Pallas kernels, encode_first(): pl.pallas_call(lambda *refs: first_kernel(orders, *refs), out_shape=(jax....  5.43 us
  transfers between devices with their start and end apart: 22, of which 12 were waited for; matrix products, arithmetic and copies ran while one was open for 2% of the time, Pallas kernels for 10%

profile of v8, /device:TPU:2, one launch (start us, length us, event | category | flops | bytes accessed | tf_op | source)
XLA Modules:
  0.0 165.6 jit_solution(15088480549344710611)
XLA Ops:
  7.9 3.8 %shard_map.157 = bf16[96,8,512]{2,1,0:T(8,128)(2,1)} custom-call(s32[1,32]{1,0:T(1,128)} %owner_ref.1, s32[8,32]{1,0:T(8,128)} %bitcast.72, s32[8,32]{1,0:T(8,128)} %bitcast.73, bf16[256,8,512]{2,1,0:T(8,128)(2,1)} %bitcast.68), custom_call_target="tpu_custom_call" | custom-call | bytes 3145728 | tf_op jit(solution)/shard_map/pallas_call | solution.py:62
  11.8 7.6 %all-to-all-start = ((bf16[32,24,512]{2,1,0:T(8,128)(2,1)}), bf16[32,24,512]{2,1,0:T(8,128)(2,1)S(1)}, u32[]{:S(2)}, u32[]{:S(2)}) async-start(bf16[32,24,512]{2,1,0:T(8,128)(2,1)} %bitcast.67), calls=%async_computation | async-start | bytes 1572864 | tf_op jit(solution)/shard_map/all_to_all | solution.py:304
  23.0 10.8 %all-to-all-done = bf16[32,24,512]{2,1,0:T(8,128)(2,1)S(1)} async-done(((bf16[32,24,512]{2,1,0:T(8,128)(2,1)}), bf16[32,24,512]{2,1,0:T(8,128)(2,1)S(1)}, u32[]{:S(2)}, u32[]{:S(2)}) %all-to-all-start) | async-done | bytes 786464 | tf_op jit(solution)/shard_map/all_to_all | solution.py:304
  33.8 2.1 %collective-permute-start = (bf16[768,512]{1,0:T(8,128)(2,1)S(1)}, bf16[768,512]{1,0:T(8,128)(2,1)}, u32[]{:S(2)}, u32[]{:S(2)}) collective-permute-start(bf16[768,512]{1,0:T(8,128)(2,1)S(1)} %bitcast.64), channel_id=1, source_target_pairs={{0,1},{1,2},{2,3},{3,4},{4,5},{5,6},{6,7},{7,0},{8,9},{9,10},{10,1... | collective-permute-start | bytes 2359304 | tf_op jit(solution)/shard_map/ppermute | solution.py:322
  35.8 4.5 %collective-permute-start.1 = (bf16[768,512]{1,0:T(8,128)(2,1)S(1)}, bf16[768,512]{1,0:T(8,128)(2,1)}, u32[]{:S(2)}, u32[]{:S(2)}) collective-permute-start(bf16[768,512]{1,0:T(8,128)(2,1)S(1)} %bitcast.65), channel_id=1, source_target_pairs={{0,7},{1,0},{2,1},{3,2},{4,3},{5,4},{6,5},{7,6},{8,15},{9,8},{10,9... | collective-permute-start | bytes 2359304 | tf_op jit(solution)/shard_map/ppermute | solution.py:323
  40.4 2.0 %collective-permute-start.4 = (bf16[1,3,128,256]{3,2,1,0:T(8,128)(2,1)S(1)}, bf16[1,3,128,256]{3,2,1,0:T(8,128)(2,1)S(1)}, u32[]{:S(2)}, u32[]{:S(2)}) collective-permute-start(bf16[1,3,128,256]{3,2,1,0:T(8,128)(2,1)S(1)} %fusion.11), channel_id=1, source_target_pairs={{0,48},{16,0},{32,16},{48,32},{1,49},{17,1},{33,17},{49,33},{2,50}... | collective-permute-start | bytes 589832 | tf_op jit(solution)/shard_map/ppermute | solution.py:325
  42.4 4.9 %collective-permute-done.2 = bf16[1,3,128,256]{3,2,1,0:T(8,128)(2,1)S(1)} collective-permute-done((bf16[1,3,128,256]{3,2,1,0:T(8,128)(2,1)S(1)}, bf16[1,3,128,256]{3,2,1,0:T(8,128)(2,1)S(1)}, u32[]{:S(2)}, u32[]{:S(2)}) %collective-permute-start.2) | collective-permute-done | bytes 196640 | tf_op jit(solution)/shard_map/ppermute | solution.py:324
  47.5 6.8 %collective-permute-done.3 = bf16[1,3,128,256]{3,2,1,0:T(8,128)(2,1)S(1)} collective-permute-done((bf16[1,3,128,256]{3,2,1,0:T(8,128)(2,1)S(1)}, bf16[1,3,128,256]{3,2,1,0:T(8,128)(2,1)S(1)}, u32[]{:S(2)}, u32[]{:S(2)}) %collective-permute-start.3) | collective-permute-done | bytes 196640 | tf_op jit(solution)/shard_map/ppermute | solution.py:326
  54.4 4.1 %collective-permute-done.refs_4_ = bf16[768,512]{1,0:T(8,128)(2,1)} collective-permute-done((bf16[768,512]{1,0:T(8,128)(2,1)S(1)}, bf16[768,512]{1,0:T(8,128)(2,1)}, u32[]{:S(2)}, u32[]{:S(2)}) %collective-permute-start) | collective-permute-done | bytes 786464 | tf_op jit(solution)/shard_map/ppermute | solution.py:322
  58.5 3.2 %collective-permute-start.6 = (bf16[768,512]{1,0:T(8,128)(2,1)}, bf16[768,512]{1,0:T(8,128)(2,1)}, u32[]{:S(2)}, u32[]{:S(2)}) collective-permute-start(bf16[768,512]{1,0:T(8,128)(2,1)} %collective-permute-done.1.refs_1_), channel_id=1, source_target_pairs={{0,7},{1,0},{2,1},{3,2},{4,3},{5,4},{6,5},{7,6},{8,15},{9,8},{10,9... | collective-permute-start | bytes 2359304 | tf_op jit(solution)/shard_map/ppermute | solution.py:332
  61.7 1.1 collective-permute-start.11
  62.8 0.9 collective-permute-start.9
  63.8 8.7 %all-gather.2.cloned.1.call-done.columns_ref = bf16[5120,640]{1,0:T(8,128)(2,1)} async-done(((bf16[160,640]{1,0:T(8,128)(2,1)}), bf16[5120,640]{1,0:T(8,128)(2,1)}) %all-gather.2.cloned.1.call-update) | async-done | bytes 6553616 | tf_op jit(solution)/shard_map/all_gather | solution.py:298
  72.4 2.9 %copy-done.1 = bf16[5120,640]{1,0:T(8,128)(2,1)S(1)} copy-done((bf16[5120,640]{1,0:T(8,128)(2,1)S(1)}, bf16[5120,640]{1,0:T(8,128)(2,1)}, u32[]{:S(2)}) %copy-start.1) | copy-done | bytes 6553624
  75.3 3.0 %shard_map.158 = (bf16[256,5120]{1,0:T(8,128)(2,1)S(1)}, f32[8,128]{1,0:T(8,128)S(1)}) custom-call(bf16[256,640]{1,0:T(8,128)(2,1)S(1)} %bitcast.63, bf16[5120,640]{1,0:T(8,128)(2,1)S(1)} %copy-done.1), custom_call_target="tpu_custom_call" | custom-call | flops 1677721600 | bytes 9437184 | tf_op jit(solution)/shard_map/pallas_call | solution.py:115
  78.4 1.5 copy-done.2
  79.9 3.8 %collective-permute-start.7 = (bf16[768,512]{1,0:T(8,128)(2,1)}, bf16[768,512]{1,0:T(8,128)(2,1)S(1)}, u32[]{:S(2)}, u32[]{:S(2)}) collective-permute-start(bf16[768,512]{1,0:T(8,128)(2,1)} %collective-permute-done.5.refs_3_), channel_id=1, source_target_pairs={{0,1},{1,2},{2,3},{3,4},{4,5},{5,6},{6,7},{7,0},{8,9},{9,10},{10,1... | collective-permute-start | bytes 2359304 | tf_op jit(solution)/shard_map/ppermute | solution.py:340
  83.6 1.2 collective-permute-start.8
  84.8 3.4 %collective-permute-start.12 = (bf16[2,3,128,256]{3,2,1,0:T(8,128)(2,1)S(1)}, bf16[2,3,128,256]{3,2,1,0:T(8,128)(2,1)S(1)}, u32[]{:S(2)}, u32[]{:S(2)}) collective-permute-start(bf16[2,3,128,256]{3,2,1,0:T(8,128)(2,1)S(1)} %slice.17), channel_id=1, source_target_pairs={{0,192},{64,0},{128,64},{192,128},{1,193},{65,1},{129,65},{193,129... | collective-permute-start | bytes 1179656 | tf_op jit(solution)/shard_map/ppermute | solution.py:345
  88.7 8.3 %collective-permute-done.12 = bf16[2,3,128,256]{3,2,1,0:T(8,128)(2,1)S(1)} collective-permute-done((bf16[2,3,128,256]{3,2,1,0:T(8,128)(2,1)S(1)}, bf16[2,3,128,256]{3,2,1,0:T(8,128)(2,1)S(1)}, u32[]{:S(2)}, u32[]{:S(2)}) %collective-permute-start.12) | collective-permute-done | bytes 393248 | tf_op jit(solution)/shard_map/ppermute | solution.py:345
  97.0 3.5 %collective-permute-done.10 = bf16[2,3,128,256]{3,2,1,0:T(8,128)(2,1)S(1)} collective-permute-done((bf16[2,3,128,256]{3,2,1,0:T(8,128)(2,1)S(1)}, bf16[2,3,128,256]{3,2,1,0:T(8,128)(2,1)S(1)}, u32[]{:S(2)}, u32[]{:S(2)}) %collective-permute-start.10) | collective-permute-done | bytes 393248 | tf_op jit(solution)/shard_map/ppermute | solution.py:344
  100.5 5.2 %collective-permute-done.7.refs_1_ = bf16[768,512]{1,0:T(8,128)(2,1)S(1)} collective-permute-done((bf16[768,512]{1,0:T(8,128)(2,1)}, bf16[768,512]{1,0:T(8,128)(2,1)S(1)}, u32[]{:S(2)}, u32[]{:S(2)}) %collective-permute-start.7) | collective-permute-done | bytes 786464 | tf_op jit(solution)/shard_map/ppermute | solution.py:340
  105.7 2.7 %collective-permute-done.8.refs_0_ = bf16[768,512]{1,0:T(8,128)(2,1)S(1)} collective-permute-done((bf16[768,512]{1,0:T(8,128)(2,1)}, bf16[768,512]{1,0:T(8,128)(2,1)S(1)}, u32[]{:S(2)}, u32[]{:S(2)}) %collective-permute-start.8) | collective-permute-done | bytes 786464 | tf_op jit(solution)/shard_map/ppermute | solution.py:341
  108.6 3.4 %collective-permute-start.14 = (bf16[384,512]{1,0:T(8,128)(2,1)S(1)}, bf16[384,512]{1,0:T(8,128)(2,1)S(1)}, u32[]{:S(2)}, u32[]{:S(2)}) collective-permute-start(bf16[384,512]{1,0:T(8,128)(2,1)S(1)} %slice.15), channel_id=1, source_target_pairs={{0,7},{1,0},{2,1},{3,2},{4,3},{5,4},{6,5},{7,6},{8,15},{9,8},{10,9... | collective-permute-start | bytes 1179656 | tf_op jit(solution)/shard_map/ppermute | solution.py:357
  112.0 1.0 shard_map.159.refs_5_.refs_4_
  113.0 5.4 %shard_map.160 = (f32[3,768,256]{2,1,0:T(8,128)S(1)}, f32[768,128]{1,0:T(8,128)S(1)}) custom-call(bf16[768,512]{1,0:T(8,128)(2,1)S(1)} %bitcast.66, bf16[768,512]{1,0:T(8,128)(2,1)} %collective-permute-done.1.refs_1_, bf16[768,512]{1,0:T(8,128)(2,1)} %collective-permute-done.6.refs_2_, bf16[768,512]{1,0:T(8,128)(2,1)} %collective-permute-done.5.refs_3_, ...), custom_call_target="tpu_custom_call" | custom-call | flops 3019898880 | bytes 12582912 | tf_op jit(solution)/shard_map/pallas_call | solution.py:188
  118.5 11.5 %collective-permute-done.13.refs_2_ = bf16[384,512]{1,0:T(8,128)(2,1)S(1)} collective-permute-done((bf16[384,512]{1,0:T(8,128)(2,1)S(1)}, bf16[384,512]{1,0:T(8,128)(2,1)S(1)}, u32[]{:S(2)}, u32[]{:S(2)}) %collective-permute-start.13) | collective-permute-done | bytes 393248 | tf_op jit(solution)/shard_map/ppermute | solution.py:356
  129.9 0.8 collective-permute-done.14.refs_3_
  130.8 3.6 %shard_map.161 = bf16[32,3,24,256]{3,2,1,0:T(8,128)(2,1)} custom-call(bf16[768,512]{1,0:T(8,128)(2,1)S(1)} %collective-permute-done.8.refs_0_, bf16[768,512]{1,0:T(8,128)(2,1)S(1)} %collective-permute-done.7.refs_1_, bf16[384,512]{1,0:T(8,128)(2,1)S(1)} %collective-permute-done.13.refs_2_, bf16[384,512]{1,0:T(8,128)(2,1)S(1)} %collective-permute-done.14.refs_3_, ...), custom_call_target="tpu_custom_call" | custom-call | flops 32614907904 | bytes 12582912 | tf_op jit(solution)/shard_map/pallas_call | solution.py:217
  134.4 5.3 %reduce-scatter.2.cloned.1.call-done.sum_ref = bf16[32,5120]{1,0:T(8,128)(2,1)} async-done(((bf16[256,5120]{1,0:T(8,128)(2,1)}), bf16[32,5120]{1,0:T(8,128)(2,1)}) %reduce-scatter.2.cloned.1.call-update) | async-done | bytes 327696 | tf_op jit(solution)/shard_map/reduce_scatter | solution.py:338
  139.7 2.1 %shard_map.162 = (bf16[32,5120]{1,0:T(8,128)(2,1)}, f32[8,32]{1,0:T(8,128)}) custom-call(s32[1,3]{1,0:T(1,128)} %pair_ref.1, bf16[32,5120]{1,0:T(8,128)(2,1)} %bitcast.70, bf16[1,5120]{1,0:T(2,128)(2,1)} %reshape.51.gain_ref, bf16[1,5120]{1,0:T(2,128)(2,1)} %reshape.52.score_ref, bf16[32,5120]{1,0:T(8,128)(2,1)} %reduce-scatter.2.cloned.1.call-done.sum_ref), custom_call_target="tpu_custom_call" | custom-call | flops 1310720 | bytes 2097152 | tf_op jit(solution)/shard_map/pallas_call | solution.py:259
  142.5 14.3 %all_to_all.10 = f32[8,1,256]{2,1,0:T(1,128)S(1)} all-to-all(f32[8,1,256]{2,1,0:T(1,128)S(1)} %reshape.54), channel_id=1, replica_groups=mesh['y'=4,'x'=4,'core'=2,'z'=8] {'z'}, dimensions={0} | all-to-all | bytes 16384 | tf_op jit(solution)/shard_map/all_to_all | solution.py:375
  (63 shorter events, 8.0 us)
Async XLA Ops:
  7.2 13.0 %copy-start = (bf16[8,32,640]{2,1,0:T(8,128)(2,1)S(1)}, bf16[8,32,640]{2,1,0:T(8,128)(2,1)}, u32[]{:S(2)}) copy-start(bf16[8,32,640]{2,1,0:T(8,128)(2,1)} %param.16) | copy-start | bytes 983044
  7.2 12.3 %copy-start.6 = (bf16[8,32,640]{2,1,0:T(8,128)(2,1)S(1)}, bf16[8,32,640]{2,1,0:T(8,128)(2,1)}, u32[]{:S(2)}) copy-start(bf16[8,32,640]{2,1,0:T(8,128)(2,1)} %param.14) | copy-start | bytes 983044
  7.2 12.3 %copy-start.5 = (bf16[8,32,640]{2,1,0:T(8,128)(2,1)S(1)}, bf16[8,32,640]{2,1,0:T(8,128)(2,1)}, u32[]{:S(2)}) copy-start(bf16[8,32,640]{2,1,0:T(8,128)(2,1)} %param.15) | copy-start | bytes 983044
  7.2 65.2 %all-gather.2.cloned.1.call-start = ((), (), s32[]{:S(2)}) async-start(), calls=%async_computation.3 | async-start | bytes 6758400 | tf_op jit(solution)/shard_map/all_gather | solution.py:298
  11.8 22.0 %all-to-all-start = ((bf16[32,24,512]{2,1,0:T(8,128)(2,1)}), bf16[32,24,512]{2,1,0:T(8,128)(2,1)S(1)}, u32[]{:S(2)}, u32[]{:S(2)}) async-start(bf16[32,24,512]{2,1,0:T(8,128)(2,1)} %bitcast.67), calls=%async_computation | async-start | bytes 1572864 | tf_op jit(solution)/shard_map/all_to_all | solution.py:304
  19.4 120.2 %reduce-scatter.2.cloned.1.call-start = ((), (), s32[]{:S(2)}) async-start(), calls=%async_computation.4 | async-start | bytes 2949120 | tf_op jit(solution)/shard_map/reduce_scatter | solution.py:338
  20.1 0.7 copy-start.8
  20.2 1.3 copy-start.9
  20.2 2.7 %copy-start.7 = (bf16[128,3,256]{2,0,1:T(8,128)(2,1)S(1)}, bf16[128,3,256]{2,0,1:T(8,128)(2,1)}, u32[]{:S(2)}) copy-start(bf16[128,3,256]{2,0,1:T(8,128)(2,1)} %param.27) | copy-start | bytes 589828
  33.8 24.7 %copy-start.3 = (bf16[32,24,512]{2,1,0:T(8,128)(2,1)}, bf16[32,24,512]{2,1,0:T(8,128)(2,1)S(1)}, u32[]{:S(2)}) copy-start(bf16[32,24,512]{2,1,0:T(8,128)(2,1)S(1)} %all-to-all-done) | copy-start | bytes 2359300
  33.8 24.7 %collective-permute-start = (bf16[768,512]{1,0:T(8,128)(2,1)S(1)}, bf16[768,512]{1,0:T(8,128)(2,1)}, u32[]{:S(2)}, u32[]{:S(2)}) collective-permute-start(bf16[768,512]{1,0:T(8,128)(2,1)S(1)} %bitcast.64), channel_id=1, source_target_pairs={{0,1},{1,2},{2,3},{3,4},{4,5},{5,6},{6,7},{7,0},{8,9},{9,10},{10,1... | collective-permute-start | bytes 2359304 | tf_op jit(solution)/shard_map/ppermute | solution.py:322
  35.8 22.7 %collective-permute-start.1 = (bf16[768,512]{1,0:T(8,128)(2,1)S(1)}, bf16[768,512]{1,0:T(8,128)(2,1)}, u32[]{:S(2)}, u32[]{:S(2)}) collective-permute-start(bf16[768,512]{1,0:T(8,128)(2,1)S(1)} %bitcast.65), channel_id=1, source_target_pairs={{0,7},{1,0},{2,1},{3,2},{4,3},{5,4},{6,5},{7,6},{8,15},{9,8},{10,9... | collective-permute-start | bytes 2359304 | tf_op jit(solution)/shard_map/ppermute | solution.py:323
  40.3 6.9 %collective-permute-start.2 = (bf16[1,3,128,256]{3,2,1,0:T(8,128)(2,1)S(1)}, bf16[1,3,128,256]{3,2,1,0:T(8,128)(2,1)S(1)}, u32[]{:S(2)}, u32[]{:S(2)}) collective-permute-start(bf16[1,3,128,256]{3,2,1,0:T(8,128)(2,1)S(1)} %fusion.11), channel_id=1, source_target_pairs={{0,16},{16,32},{32,48},{48,0},{1,17},{17,33},{33,49},{49,1},{2,18}... | collective-permute-start | bytes 589832 | tf_op jit(solution)/shard_map/ppermute | solution.py:324
  40.4 7.1 %collective-permute-start.4 = (bf16[1,3,128,256]{3,2,1,0:T(8,128)(2,1)S(1)}, bf16[1,3,128,256]{3,2,1,0:T(8,128)(2,1)S(1)}, u32[]{:S(2)}, u32[]{:S(2)}) collective-permute-start(bf16[1,3,128,256]{3,2,1,0:T(8,128)(2,1)S(1)} %fusion.11), channel_id=1, source_target_pairs={{0,48},{16,0},{32,16},{48,32},{1,49},{17,1},{33,17},{49,33},{2,50}... | collective-permute-start | bytes 589832 | tf_op jit(solution)/shard_map/ppermute | solution.py:325
  47.2 7.1 %collective-permute-start.3 = (bf16[1,3,128,256]{3,2,1,0:T(8,128)(2,1)S(1)}, bf16[1,3,128,256]{3,2,1,0:T(8,128)(2,1)S(1)}, u32[]{:S(2)}, u32[]{:S(2)}) collective-permute-start(bf16[1,3,128,256]{3,2,1,0:T(8,128)(2,1)S(1)} %collective-permute-done.2), channel_id=1, source_target_pairs={{0,16},{16,32},{32,48},{48,0},{1,17},{17,33},{33,49},{49,1},{2,18}... | collective-permute-start | bytes 589832 | tf_op jit(solution)/shard_map/ppermute | solution.py:326
  58.5 21.4 %collective-permute-start.5 = (bf16[768,512]{1,0:T(8,128)(2,1)}, bf16[768,512]{1,0:T(8,128)(2,1)}, u32[]{:S(2)}, u32[]{:S(2)}) collective-permute-start(bf16[768,512]{1,0:T(8,128)(2,1)} %collective-permute-done.refs_4_), channel_id=1, source_target_pairs={{0,1},{1,2},{2,3},{3,4},{4,5},{5,6},{6,7},{7,0},{8,9},{9,10},{10,1... | collective-permute-start | bytes 2359304 | tf_op jit(solution)/shard_map/ppermute | solution.py:331
  58.5 21.4 %collective-permute-start.6 = (bf16[768,512]{1,0:T(8,128)(2,1)}, bf16[768,512]{1,0:T(8,128)(2,1)}, u32[]{:S(2)}, u32[]{:S(2)}) collective-permute-start(bf16[768,512]{1,0:T(8,128)(2,1)} %collective-permute-done.1.refs_1_), channel_id=1, source_target_pairs={{0,7},{1,0},{2,1},{3,2},{4,3},{5,4},{6,5},{7,6},{8,15},{9,8},{10,9... | collective-permute-start | bytes 2359304 | tf_op jit(solution)/shard_map/ppermute | solution.py:332
  61.7 23.1 %collective-permute-start.11 = (bf16[4,3,128,256]{3,2,1,0:T(8,128)(2,1)S(1)}, bf16[4,3,128,256]{3,2,1,0:T(8,128)(2,1)S(1)}, u32[]{:S(2)}, u32[]{:S(2)}) collective-permute-start(bf16[4,3,128,256]{3,2,1,0:T(8,128)(2,1)S(1)} %pad_maximum_fusion.refs_0_), channel_id=1, source_target_pairs={{0,192},{64,0},{128,64},{192,128},{1,193},{65,1},{129,65},{193,129... | collective-permute-start | bytes 2359304 | tf_op jit(solution)/shard_map/ppermute | solution.py:334
  62.8 25.4 %collective-permute-start.9 = (bf16[4,3,128,256]{3,2,1,0:T(8,128)(2,1)S(1)}, bf16[4,3,128,256]{3,2,1,0:T(8,128)(2,1)S(1)}, u32[]{:S(2)}, u32[]{:S(2)}) collective-permute-start(bf16[4,3,128,256]{3,2,1,0:T(8,128)(2,1)S(1)} %pad_maximum_fusion.refs_0_), channel_id=1, source_target_pairs={{0,64},{64,128},{128,192},{192,0},{1,65},{65,129},{129,193},{193,1... | collective-permute-start | bytes 2359304 | tf_op jit(solution)/shard_map/ppermute | solution.py:333
  72.4 2.9 %copy-start.1 = (bf16[5120,640]{1,0:T(8,128)(2,1)S(1)}, bf16[5120,640]{1,0:T(8,128)(2,1)}, u32[]{:S(2)}) copy-start(bf16[5120,640]{1,0:T(8,128)(2,1)} %all-gather.2.cloned.1.call-done.columns_ref) | copy-start | bytes 19660804
  78.3 1.5 copy-start.2
  79.9 25.8 %collective-permute-start.7 = (bf16[768,512]{1,0:T(8,128)(2,1)}, bf16[768,512]{1,0:T(8,128)(2,1)S(1)}, u32[]{:S(2)}, u32[]{:S(2)}) collective-permute-start(bf16[768,512]{1,0:T(8,128)(2,1)} %collective-permute-done.5.refs_3_), channel_id=1, source_target_pairs={{0,1},{1,2},{2,3},{3,4},{4,5},{5,6},{6,7},{7,0},{8,9},{9,10},{10,1... | collective-permute-start | bytes 2359304 | tf_op jit(solution)/shard_map/ppermute | solution.py:340
  83.6 24.8 %collective-permute-start.8 = (bf16[768,512]{1,0:T(8,128)(2,1)}, bf16[768,512]{1,0:T(8,128)(2,1)S(1)}, u32[]{:S(2)}, u32[]{:S(2)}) collective-permute-start(bf16[768,512]{1,0:T(8,128)(2,1)} %collective-permute-done.6.refs_2_), channel_id=1, source_target_pairs={{0,7},{1,0},{2,1},{3,2},{4,3},{5,4},{6,5},{7,6},{8,15},{9,8},{10,9... | collective-permute-start | bytes 2359304 | tf_op jit(solution)/shard_map/ppermute | solution.py:341
  84.8 12.2 %collective-permute-start.12 = (bf16[2,3,128,256]{3,2,1,0:T(8,128)(2,1)S(1)}, bf16[2,3,128,256]{3,2,1,0:T(8,128)(2,1)S(1)}, u32[]{:S(2)}, u32[]{:S(2)}) collective-permute-start(bf16[2,3,128,256]{3,2,1,0:T(8,128)(2,1)S(1)} %slice.17), channel_id=1, source_target_pairs={{0,192},{64,0},{128,64},{192,128},{1,193},{65,1},{129,65},{193,129... | collective-permute-start | bytes 1179656 | tf_op jit(solution)/shard_map/ppermute | solution.py:345
  88.3 12.2 %collective-permute-start.10 = (bf16[2,3,128,256]{3,2,1,0:T(8,128)(2,1)S(1)}, bf16[2,3,128,256]{3,2,1,0:T(8,128)(2,1)S(1)}, u32[]{:S(2)}, u32[]{:S(2)}) collective-permute-start(bf16[2,3,128,256]{3,2,1,0:T(8,128)(2,1)S(1)} %slice.16), channel_id=1, source_target_pairs={{0,64},{64,128},{128,192},{192,0},{1,65},{65,129},{129,193},{193,1... | collective-permute-start | bytes 1179656 | tf_op jit(solution)/shard_map/ppermute | solution.py:344
  88.6 20.1 %collective-permute-start.15 = (bf16[4,3,128,256]{3,2,1,0:T(8,128)(2,1)S(1)}, bf16[4,3,128,256]{3,2,1,0:T(8,128)(2,1)S(1)}, u32[]{:S(2)}, u32[]{:S(2)}) collective-permute-start(bf16[4,3,128,256]{3,2,1,0:T(8,128)(2,1)S(1)} %pad_maximum_fusion.refs_0_), channel_id=1, source_target_pairs={{0,8},{8,0},{1,9},{9,1},{2,10},{10,2},{3,11},{11,3},{4,12},{12,4},... | collective-permute-start | bytes 2359304 | tf_op jit(solution)/shard_map/ppermute | solution.py:352
  97.0 15.0 %collective-permute-start.16 = (bf16[4,3,128,256]{3,2,1,0:T(8,128)(2,1)S(1)}, bf16[4,3,128,256]{3,2,1,0:T(8,128)(2,1)S(1)}, u32[]{:S(2)}, u32[]{:S(2)}) collective-permute-start(bf16[4,3,128,256]{3,2,1,0:T(8,128)(2,1)S(1)} %collective-permute-done.9.refs_1_), channel_id=1, source_target_pairs={{0,8},{8,0},{1,9},{9,1},{2,10},{10,2},{3,11},{11,3},{4,12},{12,4},... | collective-permute-start | bytes 2359304 | tf_op jit(solution)/shard_map/ppermute | solution.py:352
  100.5 11.5 %collective-permute-start.18 = (bf16[4,3,128,256]{3,2,1,0:T(8,128)(2,1)S(1)}, bf16[4,3,128,256]{3,2,1,0:T(8,128)(2,1)S(1)}, u32[]{:S(2)}, u32[]{:S(2)}) collective-permute-start(bf16[4,3,128,256]{3,2,1,0:T(8,128)(2,1)S(1)} %collective-permute-done.11.refs_3_), channel_id=1, source_target_pairs={{0,8},{8,0},{1,9},{9,1},{2,10},{10,2},{3,11},{11,3},{4,12},{12,4},... | collective-permute-start | bytes 2359304 | tf_op jit(solution)/shard_map/ppermute | solution.py:352
  108.4 3.6 %collective-permute-start.17 = (bf16[4,3,128,256]{3,2,1,0:T(8,128)(2,1)S(1)}, bf16[4,3,128,256]{3,2,1,0:T(8,128)(2,1)S(1)}, u32[]{:S(2)}, u32[]{:S(2)}) collective-permute-start(bf16[4,3,128,256]{3,2,1,0:T(8,128)(2,1)S(1)} %pad_maximum_fusion.1.refs_2_), channel_id=1, source_target_pairs={{0,8},{8,0},{1,9},{9,1},{2,10},{10,2},{3,11},{11,3},{4,12},{12,4},... | collective-permute-start | bytes 2359304 | tf_op jit(solution)/shard_map/ppermute | solution.py:352
  108.5 21.5 %collective-permute-start.13 = (bf16[384,512]{1,0:T(8,128)(2,1)S(1)}, bf16[384,512]{1,0:T(8,128)(2,1)S(1)}, u32[]{:S(2)}, u32[]{:S(2)}) collective-permute-start(bf16[384,512]{1,0:T(8,128)(2,1)S(1)} %slice.14), channel_id=1, source_target_pairs={{0,1},{1,2},{2,3},{3,4},{4,5},{5,6},{6,7},{7,0},{8,9},{9,10},{10,1... | collective-permute-start | bytes 1179656 | tf_op jit(solution)/shard_map/ppermute | solution.py:356
  108.6 4.4 %copy-start.4 = (bf16[32,24,512]{2,1,0:T(8,128)(2,1)S(1)}, bf16[32,24,512]{2,1,0:T(8,128)(2,1)}, u32[]{:S(2)}) copy-start(bf16[32,24,512]{2,1,0:T(8,128)(2,1)} %copy-done.3) | copy-start | bytes 2359300
  108.6 22.2 %collective-permute-start.14 = (bf16[384,512]{1,0:T(8,128)(2,1)S(1)}, bf16[384,512]{1,0:T(8,128)(2,1)S(1)}, u32[]{:S(2)}, u32[]{:S(2)}) collective-permute-start(bf16[384,512]{1,0:T(8,128)(2,1)S(1)} %slice.15), channel_id=1, source_target_pairs={{0,7},{1,0},{2,1},{3,2},{4,3},{5,4},{6,5},{7,6},{8,15},{9,8},{10,9... | collective-permute-start | bytes 1179656 | tf_op jit(solution)/shard_map/ppermute | solution.py:357
Sparse Core Ops, SparseCore 0:
  10.6 61.8 all-gather.1
  80.0 59.6 reduce-scatter.1

commit v9 on v8

--- a/solution.py
+++ b/solution.py
@@ -127,7 +127,7 @@
             pl.BlockSpec((count, width // steps), lambda i: (0, i)),
             pl.BlockSpec((8, 128), lambda i: (0, 0)),
         ),
-        compiler_params=pltpu.CompilerParams(vmem_limit_bytes=16 << 20),
+        compiler_params=pltpu.CompilerParams(vmem_limit_bytes=56 << 20),
         cost_estimate=pl.CostEstimate(
             flops=2 * count * width * depth, bytes_accessed=9 << 20, transcendentals=0
         ),

time: 167 us -> 166 us (level)
  local copies, waits for them, and re-layouts: 7.35 us -> 3.68 us
  Pallas kernels: 19 us -> 22.4 us
    unnamed x23 -> x17, local copies, waits for them, and re-layouts: 4.65 us -> 0.97 us
    pallas_call x1, Pallas kernels: 3.04 us -> 6.34 us  [project(): pl.pallas_call(project_kernel, out_shape=(jax.ShapeDtypeStruct((count, wi...]
  transfers between devices with their start and end apart: 22 -> 22, of which waited for: 12 -> 14; matrix products, arithmetic and copies ran while one was open for 2% -> 3% of each run, Pallas kernels for 10% -> 12%
where the time goes in v9:
time: 166 us; the launch traced here: 165 us
  waiting for transfers between devices  73 us (44%)
  starting transfers between devices  33.4 us (20%)
  Pallas kernels  22.4 us (13%)
  blocking collectives  14.4 us (9%)
  between operations  14.3 us (9%)
  local copies, waits for them, and re-layouts  3.68 us (2%)
  other arithmetic  2.37 us (1%)
    all_to_all x1, blocking collectives, body(): votes = lax.all_to_all(votes, 'z', split_axis=0, concat_axis=0, tiled=True)  14.4 us
    ppermute x1, waiting for transfers between devices, body(): low = lax.ppermute(lower[:half], 'z', ring(NZ, 1))  11.4 us
    all_to_all x1, waiting for transfers between devices, body(): lax.all_to_all(outgoing.reshape(prompts, -1, features), PLANE, split_axis...  10.1 us
    all_gather x1, waiting for transfers between devices, body(): columns = lax.all_gather(out_weight.T, PLANE, axis=0, tiled=True)  8.67 us
    ppermute x1, waiting for transfers between devices, body(): lax.ppermute(y_after[2:], 'y', ring(NY, -1))  8.34 us
    all_to_all x1, starting transfers between devices, body(): lax.all_to_all(outgoing.reshape(prompts, -1, features), PLANE, split_axis...  7.62 us
    ppermute x1, waiting for transfers between devices, body(): x_across = lax.ppermute(x_before, 'x', ring(NX, 1))  6.77 us
    pallas_call x1, Pallas kernels, project(): pl.pallas_call(project_kernel, out_shape=(jax.ShapeDtypeStruct((count, wi...  6.34 us
  transfers between devices with their start and end apart: 22, of which 14 were waited for; matrix products, arithmetic and copies ran while one was open for 3% of the time, Pallas kernels for 12%

profile of v9, /device:TPU:2, one launch (start us, length us, event | category | flops | bytes accessed | tf_op | source)
XLA Modules:
  0.0 164.5 jit_solution(9027913771683566297)
XLA Ops:
  7.9 3.8 %shard_map.157 = bf16[96,8,512]{2,1,0:T(8,128)(2,1)} custom-call(s32[1,32]{1,0:T(1,128)} %owner_ref.1, s32[8,32]{1,0:T(8,128)} %bitcast.72, s32[8,32]{1,0:T(8,128)} %bitcast.73, bf16[256,8,512]{2,1,0:T(8,128)(2,1)} %bitcast.67), custom_call_target="tpu_custom_call" | custom-call | bytes 3145728 | tf_op jit(solution)/shard_map/pallas_call | solution.py:62
  11.8 7.6 %all-to-all-start = ((bf16[32,24,512]{2,1,0:T(8,128)(2,1)}), bf16[32,24,512]{2,1,0:T(8,128)(2,1)S(1)}, u32[]{:S(2)}, u32[]{:S(2)}) async-start(bf16[32,24,512]{2,1,0:T(8,128)(2,1)} %bitcast.66), calls=%async_computation | async-start | bytes 1572864 | tf_op jit(solution)/shard_map/all_to_all | solution.py:304
  20.7 0.8 copy.58
  22.7 0.8 dynamic-slice_convert_fusion
  23.7 10.1 %all-to-all-done = bf16[32,24,512]{2,1,0:T(8,128)(2,1)S(1)} async-done(((bf16[32,24,512]{2,1,0:T(8,128)(2,1)}), bf16[32,24,512]{2,1,0:T(8,128)(2,1)S(1)}, u32[]{:S(2)}, u32[]{:S(2)}) %all-to-all-start) | async-done | bytes 786464 | tf_op jit(solution)/shard_map/all_to_all | solution.py:304
  33.8 2.0 %collective-permute-start = (bf16[768,512]{1,0:T(8,128)(2,1)S(1)}, bf16[768,512]{1,0:T(8,128)(2,1)}, u32[]{:S(2)}, u32[]{:S(2)}) collective-permute-start(bf16[768,512]{1,0:T(8,128)(2,1)S(1)} %bitcast.63), channel_id=1, source_target_pairs={{0,1},{1,2},{2,3},{3,4},{4,5},{5,6},{6,7},{7,0},{8,9},{9,10},{10,1... | collective-permute-start | bytes 2359304 | tf_op jit(solution)/shard_map/ppermute | solution.py:322
  35.8 4.5 %collective-permute-start.1 = (bf16[768,512]{1,0:T(8,128)(2,1)S(1)}, bf16[768,512]{1,0:T(8,128)(2,1)}, u32[]{:S(2)}, u32[]{:S(2)}) collective-permute-start(bf16[768,512]{1,0:T(8,128)(2,1)S(1)} %bitcast.64), channel_id=1, source_target_pairs={{0,7},{1,0},{2,1},{3,2},{4,3},{5,4},{6,5},{7,6},{8,15},{9,8},{10,9... | collective-permute-start | bytes 2359304 | tf_op jit(solution)/shard_map/ppermute | solution.py:323
  40.4 2.0 %collective-permute-start.4 = (bf16[1,3,128,256]{3,2,1,0:T(8,128)(2,1)S(1)}, bf16[1,3,128,256]{3,2,1,0:T(8,128)(2,1)S(1)}, u32[]{:S(2)}, u32[]{:S(2)}) collective-permute-start(bf16[1,3,128,256]{3,2,1,0:T(8,128)(2,1)S(1)} %fusion.11), channel_id=1, source_target_pairs={{0,48},{16,0},{32,16},{48,32},{1,49},{17,1},{33,17},{49,33},{2,50}... | collective-permute-start | bytes 589832 | tf_op jit(solution)/shard_map/ppermute | solution.py:325
  42.4 4.9 %collective-permute-done.2 = bf16[1,3,128,256]{3,2,1,0:T(8,128)(2,1)S(1)} collective-permute-done((bf16[1,3,128,256]{3,2,1,0:T(8,128)(2,1)S(1)}, bf16[1,3,128,256]{3,2,1,0:T(8,128)(2,1)S(1)}, u32[]{:S(2)}, u32[]{:S(2)}) %collective-permute-start.2) | collective-permute-done | bytes 196640 | tf_op jit(solution)/shard_map/ppermute | solution.py:324
  47.5 6.8 %collective-permute-done.3 = bf16[1,3,128,256]{3,2,1,0:T(8,128)(2,1)S(1)} collective-permute-done((bf16[1,3,128,256]{3,2,1,0:T(8,128)(2,1)S(1)}, bf16[1,3,128,256]{3,2,1,0:T(8,128)(2,1)S(1)}, u32[]{:S(2)}, u32[]{:S(2)}) %collective-permute-start.3) | collective-permute-done | bytes 196640 | tf_op jit(solution)/shard_map/ppermute | solution.py:326
  54.4 4.1 %collective-permute-done.refs_4_ = bf16[768,512]{1,0:T(8,128)(2,1)} collective-permute-done((bf16[768,512]{1,0:T(8,128)(2,1)S(1)}, bf16[768,512]{1,0:T(8,128)(2,1)}, u32[]{:S(2)}, u32[]{:S(2)}) %collective-permute-start) | collective-permute-done | bytes 786464 | tf_op jit(solution)/shard_map/ppermute | solution.py:322
  58.5 3.2 %collective-permute-start.6 = (bf16[768,512]{1,0:T(8,128)(2,1)}, bf16[768,512]{1,0:T(8,128)(2,1)}, u32[]{:S(2)}, u32[]{:S(2)}) collective-permute-start(bf16[768,512]{1,0:T(8,128)(2,1)} %collective-permute-done.1.refs_1_), channel_id=1, source_target_pairs={{0,7},{1,0},{2,1},{3,2},{4,3},{5,4},{6,5},{7,6},{8,15},{9,8},{10,9... | collective-permute-start | bytes 2359304 | tf_op jit(solution)/shard_map/ppermute | solution.py:332
  61.7 1.1 collective-permute-start.11
  62.8 0.9 collective-permute-start.9
  63.8 8.7 %all-gather.2.cloned.1.call-done.columns_ref = bf16[5120,640]{1,0:T(8,128)(2,1)} async-done(((bf16[160,640]{1,0:T(8,128)(2,1)}), bf16[5120,640]{1,0:T(8,128)(2,1)}) %all-gather.2.cloned.1.call-update) | async-done | bytes 6553616 | tf_op jit(solution)/shard_map/all_gather | solution.py:298
  72.4 6.3 %shard_map.158 = (bf16[256,5120]{1,0:T(8,128)(2,1)}, f32[8,128]{1,0:T(8,128)}) custom-call(bf16[256,640]{1,0:T(8,128)(2,1)} %bitcast.69, bf16[5120,640]{1,0:T(8,128)(2,1)} %all-gather.2.cloned.1.call-done.columns_ref), custom_call_target="tpu_custom_call" | custom-call | flops 1677721600 | bytes 9437184 | tf_op jit(solution)/shard_map/pallas_call | solution.py:115
  79.3 3.4 %collective-permute-start.7 = (bf16[768,512]{1,0:T(8,128)(2,1)}, bf16[768,512]{1,0:T(8,128)(2,1)S(1)}, u32[]{:S(2)}, u32[]{:S(2)}) collective-permute-start(bf16[768,512]{1,0:T(8,128)(2,1)} %collective-permute-done.5.refs_3_), channel_id=1, source_target_pairs={{0,1},{1,2},{2,3},{3,4},{4,5},{5,6},{6,7},{7,0},{8,9},{9,10},{10,1... | collective-permute-start | bytes 2359304 | tf_op jit(solution)/shard_map/ppermute | solution.py:340
  82.7 1.1 collective-permute-start.8
  83.9 3.3 %collective-permute-start.12 = (bf16[2,3,128,256]{3,2,1,0:T(8,128)(2,1)S(1)}, bf16[2,3,128,256]{3,2,1,0:T(8,128)(2,1)S(1)}, u32[]{:S(2)}, u32[]{:S(2)}) collective-permute-start(bf16[2,3,128,256]{3,2,1,0:T(8,128)(2,1)S(1)} %slice.17), channel_id=1, source_target_pairs={{0,192},{64,0},{128,64},{192,128},{1,193},{65,1},{129,65},{193,129... | collective-permute-start | bytes 1179656 | tf_op jit(solution)/shard_map/ppermute | solution.py:345
  87.6 8.3 %collective-permute-done.12 = bf16[2,3,128,256]{3,2,1,0:T(8,128)(2,1)S(1)} collective-permute-done((bf16[2,3,128,256]{3,2,1,0:T(8,128)(2,1)S(1)}, bf16[2,3,128,256]{3,2,1,0:T(8,128)(2,1)S(1)}, u32[]{:S(2)}, u32[]{:S(2)}) %collective-permute-start.12) | collective-permute-done | bytes 393248 | tf_op jit(solution)/shard_map/ppermute | solution.py:345
  96.0 3.5 %collective-permute-done.10 = bf16[2,3,128,256]{3,2,1,0:T(8,128)(2,1)S(1)} collective-permute-done((bf16[2,3,128,256]{3,2,1,0:T(8,128)(2,1)S(1)}, bf16[2,3,128,256]{3,2,1,0:T(8,128)(2,1)S(1)}, u32[]{:S(2)}, u32[]{:S(2)}) %collective-permute-start.10) | collective-permute-done | bytes 393248 | tf_op jit(solution)/shard_map/ppermute | solution.py:344
  99.5 5.2 %collective-permute-done.7.refs_1_ = bf16[768,512]{1,0:T(8,128)(2,1)S(1)} collective-permute-done((bf16[768,512]{1,0:T(8,128)(2,1)}, bf16[768,512]{1,0:T(8,128)(2,1)S(1)}, u32[]{:S(2)}, u32[]{:S(2)}) %collective-permute-start.7) | collective-permute-done | bytes 786464 | tf_op jit(solution)/shard_map/ppermute | solution.py:340
  104.8 2.8 %collective-permute-done.8.refs_0_ = bf16[768,512]{1,0:T(8,128)(2,1)S(1)} collective-permute-done((bf16[768,512]{1,0:T(8,128)(2,1)}, bf16[768,512]{1,0:T(8,128)(2,1)S(1)}, u32[]{:S(2)}, u32[]{:S(2)}) %collective-permute-start.8) | collective-permute-done | bytes 786464 | tf_op jit(solution)/shard_map/ppermute | solution.py:341
  107.7 3.3 %collective-permute-start.14 = (bf16[384,512]{1,0:T(8,128)(2,1)S(1)}, bf16[384,512]{1,0:T(8,128)(2,1)S(1)}, u32[]{:S(2)}, u32[]{:S(2)}) collective-permute-start(bf16[384,512]{1,0:T(8,128)(2,1)S(1)} %slice.15), channel_id=1, source_target_pairs={{0,7},{1,0},{2,1},{3,2},{4,3},{5,4},{6,5},{7,6},{8,15},{9,8},{10,9... | collective-permute-start | bytes 1179656 | tf_op jit(solution)/shard_map/ppermute | solution.py:357
  111.0 1.0 shard_map.159.refs_5_.refs_4_
  112.1 5.5 %shard_map.160 = (f32[3,768,256]{2,1,0:T(8,128)S(1)}, f32[768,128]{1,0:T(8,128)S(1)}) custom-call(bf16[768,512]{1,0:T(8,128)(2,1)S(1)} %bitcast.65, bf16[768,512]{1,0:T(8,128)(2,1)} %collective-permute-done.1.refs_1_, bf16[768,512]{1,0:T(8,128)(2,1)} %collective-permute-done.6.refs_2_, bf16[768,512]{1,0:T(8,128)(2,1)} %collective-permute-done.5.refs_3_, ...), custom_call_target="tpu_custom_call" | custom-call | flops 3019898880 | bytes 12582912 | tf_op jit(solution)/shard_map/pallas_call | solution.py:188
  117.6 11.4 %collective-permute-done.13.refs_2_ = bf16[384,512]{1,0:T(8,128)(2,1)S(1)} collective-permute-done((bf16[384,512]{1,0:T(8,128)(2,1)S(1)}, bf16[384,512]{1,0:T(8,128)(2,1)S(1)}, u32[]{:S(2)}, u32[]{:S(2)}) %collective-permute-start.13) | collective-permute-done | bytes 393248 | tf_op jit(solution)/shard_map/ppermute | solution.py:356
  128.9 0.8 collective-permute-done.14.refs_3_
  129.8 3.6 %shard_map.161 = bf16[32,3,24,256]{3,2,1,0:T(8,128)(2,1)} custom-call(bf16[768,512]{1,0:T(8,128)(2,1)S(1)} %collective-permute-done.8.refs_0_, bf16[768,512]{1,0:T(8,128)(2,1)S(1)} %collective-permute-done.7.refs_1_, bf16[384,512]{1,0:T(8,128)(2,1)S(1)} %collective-permute-done.13.refs_2_, bf16[384,512]{1,0:T(8,128)(2,1)S(1)} %collective-permute-done.14.refs_3_, ...), custom_call_target="tpu_custom_call" | custom-call | flops 32614907904 | bytes 12582912 | tf_op jit(solution)/shard_map/pallas_call | solution.py:217
  133.4 5.2 %reduce-scatter.2.cloned.1.call-done.sum_ref = bf16[32,5120]{1,0:T(8,128)(2,1)} async-done(((bf16[256,5120]{1,0:T(8,128)(2,1)}), bf16[32,5120]{1,0:T(8,128)(2,1)}) %reduce-scatter.2.cloned.1.call-update) | async-done | bytes 327696 | tf_op jit(solution)/shard_map/reduce_scatter | solution.py:338
  138.6 2.1 %shard_map.162 = (bf16[32,5120]{1,0:T(8,128)(2,1)}, f32[8,32]{1,0:T(8,128)}) custom-call(s32[1,3]{1,0:T(1,128)} %pair_ref.1, bf16[32,5120]{1,0:T(8,128)(2,1)} %bitcast.70, bf16[1,5120]{1,0:T(2,128)(2,1)} %reshape.51.gain_ref, bf16[1,5120]{1,0:T(2,128)(2,1)} %reshape.52.score_ref, bf16[32,5120]{1,0:T(8,128)(2,1)} %reduce-scatter.2.cloned.1.call-done.sum_ref), custom_call_target="tpu_custom_call" | custom-call | flops 1310720 | bytes 2097152 | tf_op jit(solution)/shard_map/pallas_call | solution.py:259
  141.5 14.4 %all_to_all.10 = f32[8,1,256]{2,1,0:T(1,128)S(1)} all-to-all(f32[8,1,256]{2,1,0:T(1,128)S(1)} %reshape.54), channel_id=1, replica_groups=mesh['y'=4,'x'=4,'core'=2,'z'=8] {'z'}, dimensions={0} | all-to-all | bytes 16384 | tf_op jit(solution)/shard_map/all_to_all | solution.py:375
  (57 shorter events, 7.7 us)
Async XLA Ops:
  7.2 13.0 %copy-start = (bf16[8,32,640]{2,1,0:T(8,128)(2,1)S(1)}, bf16[8,32,640]{2,1,0:T(8,128)(2,1)}, u32[]{:S(2)}) copy-start(bf16[8,32,640]{2,1,0:T(8,128)(2,1)} %param.16) | copy-start | bytes 983044
  7.2 12.3 %copy-start.3 = (bf16[8,32,640]{2,1,0:T(8,128)(2,1)S(1)}, bf16[8,32,640]{2,1,0:T(8,128)(2,1)}, u32[]{:S(2)}) copy-start(bf16[8,32,640]{2,1,0:T(8,128)(2,1)} %param.14) | copy-start | bytes 983044
  7.2 12.3 %copy-start.2 = (bf16[8,32,640]{2,1,0:T(8,128)(2,1)S(1)}, bf16[8,32,640]{2,1,0:T(8,128)(2,1)}, u32[]{:S(2)}) copy-start(bf16[8,32,640]{2,1,0:T(8,128)(2,1)} %param.15) | copy-start | bytes 983044
  7.2 65.2 %all-gather.2.cloned.1.call-start = ((), (), s32[]{:S(2)}) async-start(), calls=%async_computation.3 | async-start | bytes 6758400 | tf_op jit(solution)/shard_map/all_gather | solution.py:298
  11.8 22.0 %all-to-all-start = ((bf16[32,24,512]{2,1,0:T(8,128)(2,1)}), bf16[32,24,512]{2,1,0:T(8,128)(2,1)S(1)}, u32[]{:S(2)}, u32[]{:S(2)}) async-start(bf16[32,24,512]{2,1,0:T(8,128)(2,1)} %bitcast.66), calls=%async_computation | async-start | bytes 1572864 | tf_op jit(solution)/shard_map/all_to_all | solution.py:304
  19.4 119.2 %reduce-scatter.2.cloned.1.call-start = ((), (), s32[]{:S(2)}) async-start(), calls=%async_computation.4 | async-start | bytes 2949120 | tf_op jit(solution)/shard_map/reduce_scatter | solution.py:338
  20.1 1.4 copy-start.5
  20.2 2.0 %copy-start.6 = (bf16[5120]{0:T(1024)(128)(2,1)S(1)}, bf16[5120]{0:T(1024)(128)(2,1)}, u32[]{:S(2)}) copy-start(bf16[5120]{0:T(1024)(128)(2,1)} %param.20) | copy-start | bytes 30724
  20.2 3.4 %copy-start.4 = (bf16[128,3,256]{2,0,1:T(8,128)(2,1)S(1)}, bf16[128,3,256]{2,0,1:T(8,128)(2,1)}, u32[]{:S(2)}) copy-start(bf16[128,3,256]{2,0,1:T(8,128)(2,1)} %param.27) | copy-start | bytes 589828
  33.8 24.7 %collective-permute-start = (bf16[768,512]{1,0:T(8,128)(2,1)S(1)}, bf16[768,512]{1,0:T(8,128)(2,1)}, u32[]{:S(2)}, u32[]{:S(2)}) collective-permute-start(bf16[768,512]{1,0:T(8,128)(2,1)S(1)} %bitcast.63), channel_id=1, source_target_pairs={{0,1},{1,2},{2,3},{3,4},{4,5},{5,6},{6,7},{7,0},{8,9},{9,10},{10,1... | collective-permute-start | bytes 2359304 | tf_op jit(solution)/shard_map/ppermute | solution.py:322
  35.8 22.7 %collective-permute-start.1 = (bf16[768,512]{1,0:T(8,128)(2,1)S(1)}, bf16[768,512]{1,0:T(8,128)(2,1)}, u32[]{:S(2)}, u32[]{:S(2)}) collective-permute-start(bf16[768,512]{1,0:T(8,128)(2,1)S(1)} %bitcast.64), channel_id=1, source_target_pairs={{0,7},{1,0},{2,1},{3,2},{4,3},{5,4},{6,5},{7,6},{8,15},{9,8},{10,9... | collective-permute-start | bytes 2359304 | tf_op jit(solution)/shard_map/ppermute | solution.py:323
  40.3 6.9 %collective-permute-start.2 = (bf16[1,3,128,256]{3,2,1,0:T(8,128)(2,1)S(1)}, bf16[1,3,128,256]{3,2,1,0:T(8,128)(2,1)S(1)}, u32[]{:S(2)}, u32[]{:S(2)}) collective-permute-start(bf16[1,3,128,256]{3,2,1,0:T(8,128)(2,1)S(1)} %fusion.11), channel_id=1, source_target_pairs={{0,16},{16,32},{32,48},{48,0},{1,17},{17,33},{33,49},{49,1},{2,18}... | collective-permute-start | bytes 589832 | tf_op jit(solution)/shard_map/ppermute | solution.py:324
  40.4 7.1 %collective-permute-start.4 = (bf16[1,3,128,256]{3,2,1,0:T(8,128)(2,1)S(1)}, bf16[1,3,128,256]{3,2,1,0:T(8,128)(2,1)S(1)}, u32[]{:S(2)}, u32[]{:S(2)}) collective-permute-start(bf16[1,3,128,256]{3,2,1,0:T(8,128)(2,1)S(1)} %fusion.11), channel_id=1, source_target_pairs={{0,48},{16,0},{32,16},{48,32},{1,49},{17,1},{33,17},{49,33},{2,50}... | collective-permute-start | bytes 589832 | tf_op jit(solution)/shard_map/ppermute | solution.py:325
  47.2 7.1 %collective-permute-start.3 = (bf16[1,3,128,256]{3,2,1,0:T(8,128)(2,1)S(1)}, bf16[1,3,128,256]{3,2,1,0:T(8,128)(2,1)S(1)}, u32[]{:S(2)}, u32[]{:S(2)}) collective-permute-start(bf16[1,3,128,256]{3,2,1,0:T(8,128)(2,1)S(1)} %collective-permute-done.2), channel_id=1, source_target_pairs={{0,16},{16,32},{32,48},{48,0},{1,17},{17,33},{33,49},{49,1},{2,18}... | collective-permute-start | bytes 589832 | tf_op jit(solution)/shard_map/ppermute | solution.py:326
  58.5 20.8 %collective-permute-start.5 = (bf16[768,512]{1,0:T(8,128)(2,1)}, bf16[768,512]{1,0:T(8,128)(2,1)}, u32[]{:S(2)}, u32[]{:S(2)}) collective-permute-start(bf16[768,512]{1,0:T(8,128)(2,1)} %collective-permute-done.refs_4_), channel_id=1, source_target_pairs={{0,1},{1,2},{2,3},{3,4},{4,5},{5,6},{6,7},{7,0},{8,9},{9,10},{10,1... | collective-permute-start | bytes 2359304 | tf_op jit(solution)/shard_map/ppermute | solution.py:331
  58.5 20.8 %collective-permute-start.6 = (bf16[768,512]{1,0:T(8,128)(2,1)}, bf16[768,512]{1,0:T(8,128)(2,1)}, u32[]{:S(2)}, u32[]{:S(2)}) collective-permute-start(bf16[768,512]{1,0:T(8,128)(2,1)} %collective-permute-done.1.refs_1_), channel_id=1, source_target_pairs={{0,7},{1,0},{2,1},{3,2},{4,3},{5,4},{6,5},{7,6},{8,15},{9,8},{10,9... | collective-permute-start | bytes 2359304 | tf_op jit(solution)/shard_map/ppermute | solution.py:332
  61.7 22.1 %collective-permute-start.11 = (bf16[4,3,128,256]{3,2,1,0:T(8,128)(2,1)S(1)}, bf16[4,3,128,256]{3,2,1,0:T(8,128)(2,1)S(1)}, u32[]{:S(2)}, u32[]{:S(2)}) collective-permute-start(bf16[4,3,128,256]{3,2,1,0:T(8,128)(2,1)S(1)} %pad_maximum_fusion.refs_0_), channel_id=1, source_target_pairs={{0,192},{64,0},{128,64},{192,128},{1,193},{65,1},{129,65},{193,129... | collective-permute-start | bytes 2359304 | tf_op jit(solution)/shard_map/ppermute | solution.py:334
  62.8 24.4 %collective-permute-start.9 = (bf16[4,3,128,256]{3,2,1,0:T(8,128)(2,1)S(1)}, bf16[4,3,128,256]{3,2,1,0:T(8,128)(2,1)S(1)}, u32[]{:S(2)}, u32[]{:S(2)}) collective-permute-start(bf16[4,3,128,256]{3,2,1,0:T(8,128)(2,1)S(1)} %pad_maximum_fusion.refs_0_), channel_id=1, source_target_pairs={{0,64},{64,128},{128,192},{192,0},{1,65},{65,129},{129,193},{193,1... | collective-permute-start | bytes 2359304 | tf_op jit(solution)/shard_map/ppermute | solution.py:333
  78.8 32.2 %copy-start.1 = (f32[8,128]{1,0:T(8,128)S(1)}, f32[8,128]{1,0:T(8,128)}, u32[]{:S(2)}) copy-start(f32[8,128]{1,0:T(8,128)} %get-tuple-element.49.token_ref) | copy-start | bytes 12292
  79.3 25.5 %collective-permute-start.7 = (bf16[768,512]{1,0:T(8,128)(2,1)}, bf16[768,512]{1,0:T(8,128)(2,1)S(1)}, u32[]{:S(2)}, u32[]{:S(2)}) collective-permute-start(bf16[768,512]{1,0:T(8,128)(2,1)} %collective-permute-done.5.refs_3_), channel_id=1, source_target_pairs={{0,1},{1,2},{2,3},{3,4},{4,5},{5,6},{6,7},{7,0},{8,9},{9,10},{10,1... | collective-permute-start | bytes 2359304 | tf_op jit(solution)/shard_map/ppermute | solution.py:340
  82.7 24.9 %collective-permute-start.8 = (bf16[768,512]{1,0:T(8,128)(2,1)}, bf16[768,512]{1,0:T(8,128)(2,1)S(1)}, u32[]{:S(2)}, u32[]{:S(2)}) collective-permute-start(bf16[768,512]{1,0:T(8,128)(2,1)} %collective-permute-done.6.refs_2_), channel_id=1, source_target_pairs={{0,7},{1,0},{2,1},{3,2},{4,3},{5,4},{6,5},{7,6},{8,15},{9,8},{10,9... | collective-permute-start | bytes 2359304 | tf_op jit(solution)/shard_map/ppermute | solution.py:341
  83.9 12.1 %collective-permute-start.12 = (bf16[2,3,128,256]{3,2,1,0:T(8,128)(2,1)S(1)}, bf16[2,3,128,256]{3,2,1,0:T(8,128)(2,1)S(1)}, u32[]{:S(2)}, u32[]{:S(2)}) collective-permute-start(bf16[2,3,128,256]{3,2,1,0:T(8,128)(2,1)S(1)} %slice.17), channel_id=1, source_target_pairs={{0,192},{64,0},{128,64},{192,128},{1,193},{65,1},{129,65},{193,129... | collective-permute-start | bytes 1179656 | tf_op jit(solution)/shard_map/ppermute | solution.py:345
  87.3 12.2 %collective-permute-start.10 = (bf16[2,3,128,256]{3,2,1,0:T(8,128)(2,1)S(1)}, bf16[2,3,128,256]{3,2,1,0:T(8,128)(2,1)S(1)}, u32[]{:S(2)}, u32[]{:S(2)}) collective-permute-start(bf16[2,3,128,256]{3,2,1,0:T(8,128)(2,1)S(1)} %slice.16), channel_id=1, source_target_pairs={{0,64},{64,128},{128,192},{192,0},{1,65},{65,129},{129,193},{193,1... | collective-permute-start | bytes 1179656 | tf_op jit(solution)/shard_map/ppermute | solution.py:344
  87.5 20.2 %collective-permute-start.15 = (bf16[4,3,128,256]{3,2,1,0:T(8,128)(2,1)S(1)}, bf16[4,3,128,256]{3,2,1,0:T(8,128)(2,1)S(1)}, u32[]{:S(2)}, u32[]{:S(2)}) collective-permute-start(bf16[4,3,128,256]{3,2,1,0:T(8,128)(2,1)S(1)} %pad_maximum_fusion.refs_0_), channel_id=1, source_target_pairs={{0,8},{8,0},{1,9},{9,1},{2,10},{10,2},{3,11},{11,3},{4,12},{12,4},... | collective-permute-start | bytes 2359304 | tf_op jit(solution)/shard_map/ppermute | solution.py:352
  96.0 15.1 %collective-permute-start.16 = (bf16[4,3,128,256]{3,2,1,0:T(8,128)(2,1)S(1)}, bf16[4,3,128,256]{3,2,1,0:T(8,128)(2,1)S(1)}, u32[]{:S(2)}, u32[]{:S(2)}) collective-permute-start(bf16[4,3,128,256]{3,2,1,0:T(8,128)(2,1)S(1)} %collective-permute-done.9.refs_1_), channel_id=1, source_target_pairs={{0,8},{8,0},{1,9},{9,1},{2,10},{10,2},{3,11},{11,3},{4,12},{12,4},... | collective-permute-start | bytes 2359304 | tf_op jit(solution)/shard_map/ppermute | solution.py:352
  99.5 11.6 %collective-permute-start.18 = (bf16[4,3,128,256]{3,2,1,0:T(8,128)(2,1)S(1)}, bf16[4,3,128,256]{3,2,1,0:T(8,128)(2,1)S(1)}, u32[]{:S(2)}, u32[]{:S(2)}) collective-permute-start(bf16[4,3,128,256]{3,2,1,0:T(8,128)(2,1)S(1)} %collective-permute-done.11.refs_3_), channel_id=1, source_target_pairs={{0,8},{8,0},{1,9},{9,1},{2,10},{10,2},{3,11},{11,3},{4,12},{12,4},... | collective-permute-start | bytes 2359304 | tf_op jit(solution)/shard_map/ppermute | solution.py:352
  107.6 3.5 %collective-permute-start.17 = (bf16[4,3,128,256]{3,2,1,0:T(8,128)(2,1)S(1)}, bf16[4,3,128,256]{3,2,1,0:T(8,128)(2,1)S(1)}, u32[]{:S(2)}, u32[]{:S(2)}) collective-permute-start(bf16[4,3,128,256]{3,2,1,0:T(8,128)(2,1)S(1)} %pad_maximum_fusion.1.refs_2_), channel_id=1, source_target_pairs={{0,8},{8,0},{1,9},{9,1},{2,10},{10,2},{3,11},{11,3},{4,12},{12,4},... | collective-permute-start | bytes 2359304 | tf_op jit(solution)/shard_map/ppermute | solution.py:352
  107.6 21.3 %collective-permute-start.13 = (bf16[384,512]{1,0:T(8,128)(2,1)S(1)}, bf16[384,512]{1,0:T(8,128)(2,1)S(1)}, u32[]{:S(2)}, u32[]{:S(2)}) collective-permute-start(bf16[384,512]{1,0:T(8,128)(2,1)S(1)} %slice.14), channel_id=1, source_target_pairs={{0,1},{1,2},{2,3},{3,4},{4,5},{5,6},{6,7},{7,0},{8,9},{9,10},{10,1... | collective-permute-start | bytes 1179656 | tf_op jit(solution)/shard_map/ppermute | solution.py:356
  107.7 22.0 %collective-permute-start.14 = (bf16[384,512]{1,0:T(8,128)(2,1)S(1)}, bf16[384,512]{1,0:T(8,128)(2,1)S(1)}, u32[]{:S(2)}, u32[]{:S(2)}) collective-permute-start(bf16[384,512]{1,0:T(8,128)(2,1)S(1)} %slice.15), channel_id=1, source_target_pairs={{0,7},{1,0},{2,1},{3,2},{4,3},{5,4},{6,5},{7,6},{8,15},{9,8},{10,9... | collective-permute-start | bytes 1179656 | tf_op jit(solution)/shard_map/ppermute | solution.py:357
Sparse Core Ops, SparseCore 0:
  10.6 61.8 all-gather.1
  78.9 59.6 reduce-scatter.1
